TPU v7x, 32 devices: a whole 2x2x4 slice. The times are simulated.
32 devices in a mesh: dp: 8 (over z, y), seq: 4 (over x, core).
Axes of the slice: x: 2, y: 2, z: 4, core: 2. Of those that a mesh axis runs over, the one named last changes fastest.
Arguments:
- signal: bfloat16 [8, 512, 2048], P('dp', 'seq'), may hold values from -6 to 6
- gate_weight: bfloat16 [2048, 2048], P('dp'), may hold values from -0.125 to 0.125
- pos_weight: float32 [33, 64], replicated, may hold values from -4 to 4
- pos_bias: float32 [64], replicated, may hold values from -3.140625 to 3.140625
- filter_weight: float32 [64, 2048], replicated, may hold values from -0.75 to 0.75
- decay_rate: float32 [2048], replicated, as said below
- skip_gain: float32 [2048], replicated, may hold values from -4 to 4
- grad_out: bfloat16 [8, 512, 2048], P('dp', 'seq'), may hold values from -6 to 6
Outputs:
- output: bfloat16 [8, 512, 2048], P('dp', 'seq')
- grad_signal: bfloat16 [8, 512, 2048], P('dp', 'seq')
- grad_gate_weight: float32 [2048, 2048], P('dp')
- grad_pos_weight: float32 [33, 64], replicated
- grad_pos_bias: float32 [64], replicated
- grad_filter_weight: float32 [64, 2048], replicated
- grad_skip: float32 [2048], replicated
Inputs may be any that keep to these rules, and one draw needn't show every extreme that they name: `decay_rate`: every rate is positive and at most 1/30.
All inputs are finite; a program needn't handle non-finite values.
Results may differ from a plain program's by a relative error of at most 0.015.
Values may be sent and summed in bfloat16 or wider, within the bound.
No kernel may reach another device: no remote copies, remote signals or barrier semaphores. Data moves between devices by JAX's collectives and lax.ppermute only.
A program may use at most 192 MiB of HBM per device.

v0:
```python
import functools
import math

import jax
import jax.numpy as jnp
import numpy as np
from jax import lax
from jax.experimental import pallas as pl
from jax.experimental.pallas import tpu as pltpu
from jax.sharding import PartitionSpec as P


f32 = jnp.float32
bf16 = jnp.bfloat16
VMEM = pltpu.VMEM


BASE = 16


@functools.lru_cache(maxsize=None)
def feature_table(length, emb_count):
    positions = np.arange(length)
    bands = np.arange(1, (emb_count - 1) // 2 + 1)
    angle = positions[:, None] * bands[None, :] % length * (2.0 * math.pi / length)
    table = np.concatenate(
        [positions[:, None] / length, np.cos(angle), np.sin(angle), np.ones((length, 1))], axis=1
    )
    rows = -(-table.shape[1] // 8) * 8
    return np.pad(table, ((0, 0), (0, rows - table.shape[1]))).astype(np.float32)


@functools.lru_cache(maxsize=None)
def angle_factors(length):
    step = 4 * length
    lane = np.arange(length)[None, :]
    coarse = np.arange(length // BASE)[:, None]
    fine = np.arange(BASE)[:, None]
    found = []
    for phase in (
        coarse * lane * (4 * BASE),
        (4 * fine + 1) * lane,
        coarse * BASE * (4 * lane + 1),
        fine * (4 * lane + 1),
    ):
        angle = phase % step * (2.0 * math.pi / step)
        found.append(np.stack([np.cos(angle), np.sin(angle)]).astype(np.float32))
    return found


def dot(a, b):
    return jnp.dot(a, b, preferred_element_type=f32)


def dot_first(a, b):
    return lax.dot_general(a, b, (((0,), (0,)), ((), ())), preferred_element_type=f32)


def dot_last(a, b):
    return lax.dot_general(a, b, (((1,), (1,)), ((), ())), preferred_element_type=f32)


def split(x):
    high = x.astype(bf16)
    return high, (x - high.astype(f32)).astype(bf16)


def careful(product, a, b):
    a_high, a_low = split(a)
    b_high, b_low = split(b)
    return product(a_high, b_high) + (product(a_low, b_high) + product(a_high, b_low))


def to_spectrum(a_high, a_low, part, x):
    return dot(a_high[part], x) + dot(a_low[part], x)


def from_spectrum(t_high, re, im, length):
    total = dot(t_high[0], re.astype(bf16)) + dot(t_high[1], im.astype(bf16))
    return total * (1.0 / length)


def struct(shape, kind):
    return jax.ShapeDtypeStruct(shape, kind)


def whole(shape):
    return pl.BlockSpec(shape, lambda i, *_: (0,) * len(shape))


def table_specs(length, block):
    by_row = pl.BlockSpec((2, block, length), lambda i, *_: (0, i, 0))
    by_col = pl.BlockSpec((2, length, block), lambda i, *_: (0, 0, i))
    return by_row, by_col


def spectrum_block(width, block):
    return pl.BlockSpec((2, block, width), lambda i, *_: (0, i, 0))


def generate(place, table, factors, pos_weight, pos_bias, filter_weight, rates, norm, width, block):
    highest = lax.Precision.HIGHEST
    length, _ = table.shape
    order = pos_weight.shape[1]
    emb_count = pos_weight.shape[0]

    def body(
        place_ref, tab, ac, af, tc, tf, pw, pb, fw, rate, norm_ref,
        ah, al, th, spec, env_out, hidden_out, cos_out, filt,
    ):
        step = pl.program_id(0)

        @pl.when(step == 0)
        def _():
            pre = jnp.dot(tab[:, :emb_count], pw[...], precision=highest) + pb[...]
            hidden = jnp.sin(pre)
            hidden_out[...] = hidden
            cos_out[...] = jnp.cos(pre)
            at = lax.broadcasted_iota(jnp.int32, (length, width), 0).astype(f32)
            env = jnp.exp(-rate[...] * at) / norm_ref[...]
            env_out[...] = env
            filt[...] = (jnp.dot(hidden, fw[...], precision=highest) * env).astype(bf16)

        def rows(coarse, fine, store):
            def one(i, carry):
                here = pl.ds(step * (block // BASE) + i, 1)
                out = pl.ds(pl.multiple_of(i * BASE, BASE), BASE)
                cos, sin = coarse[0, here, :], coarse[1, here, :]
                store(out, 0, cos * fine[0] - sin * fine[1])
                store(out, 1, sin * fine[0] + cos * fine[1])
                return carry

            lax.fori_loop(0, block // BASE, one, 0)

        def store_both(out, part, value):
            high, low = split(value)
            ah[part, out, :] = high
            al[part, out, :] = low

        def store_high(out, part, value):
            th[part, out, :] = value.astype(bf16)

        rows(ac, af, store_both)
        rows(tc, tf, store_high)
        spec[0] = to_spectrum(ah, al, 0, filt[...])
        spec[1] = to_spectrum(ah, al, 1, filt[...])

    by_row = pl.BlockSpec((2, block, length), lambda i, *_: (0, i, 0))
    cols = lambda n: pl.BlockSpec((n, width), lambda i, place_ref: (0, place_ref[0]))
    return pl.pallas_call(
        body,
        grid_spec=pltpu.PrefetchScalarGridSpec(
            num_scalar_prefetch=1,
            grid=(length // block,),
            in_specs=[whole(table.shape)]
            + [whole(f.shape) for f in factors]
            + [whole(pos_weight.shape), whole(pos_bias.shape), cols(order), cols(1), cols(1)],
            out_specs=[by_row, by_row, by_row, spectrum_block(width, block)]
            + [whole((length, width)), whole((length, order)), whole((length, order))],
            scratch_shapes=[VMEM((length, width), bf16)],
        ),
        out_shape=[struct((2, length, length), bf16)] * 3
        + [struct((2, length, width), f32), struct((length, width), f32)]
        + [struct((length, order), f32)] * 2,
        name="generate",
    )(place, table, *factors, pos_weight, pos_bias, filter_weight, rates, norm)


def piece(place_ref, r, rows):
    return pl.ds(pl.multiple_of((place_ref[0] ^ r) * rows, rows), rows)


def convolve(place, signal_rel, cot_rel, filt_spec, tables, skip, block):
    a_high, a_low, t_high = tables
    count = len(signal_rel)
    local_len, width = cot_rel[0].shape
    length = local_len * count

    def body(place_ref, *refs):
        sig = refs[:count]
        cot = refs[count : 2 * count]
        fs, ah, al, th, skip_ref = refs[2 * count : 2 * count + 5]
        spec, inner_out, grad_out, x, acc = refs[2 * count + 5 :]
        step = pl.program_id(0)

        @pl.when(step == 0)
        def _():
            for r in range(count):
                x[piece(place_ref, r, local_len), :] = sig[r][...]

        re = to_spectrum(ah, al, 0, x[...])
        im = to_spectrum(ah, al, 1, x[...])
        spec[0] = re
        spec[1] = im
        part = from_spectrum(th, re * fs[0] - im * fs[1], re * fs[1] + im * fs[0], length)

        @pl.when(step == 0)
        def _():
            acc[...] = part

        @pl.when(step != 0)
        def _():
            acc[...] += part

        @pl.when(step == pl.num_programs(0) - 1)
        def _():
            conv = acc[...].astype(bf16).astype(f32)
            inner_out[...] = conv + skip_ref[...] * x[...].astype(f32)
            for r in range(count):
                rows = piece(place_ref, r, local_len)
                grad_out[rows, :] = (cot[r][...].astype(f32) * inner_out[rows, :]).astype(bf16)

    by_row, by_col = table_specs(length, block)
    cols = pl.BlockSpec((local_len, width), lambda i, place_ref: (0, place_ref[0]))
    return pl.pallas_call(
        body,
        grid_spec=pltpu.PrefetchScalarGridSpec(
            num_scalar_prefetch=1,
            grid=(length // block,),
            in_specs=[cols] * count
            + [whole((local_len, width))] * count
            + [spectrum_block(width, block), by_row, by_row, by_col]
            + [pl.BlockSpec((1, width), lambda i, place_ref: (0, place_ref[0]))],
            out_specs=[
                spectrum_block(width, block),
                whole((length, width)),
                whole((length, width)),
            ],
            scratch_shapes=[VMEM((length, width), bf16), VMEM((length, width), f32)],
        ),
        out_shape=[
            struct((2, length, width), f32),
            struct((length, width), f32),
            struct((length, width), bf16),
        ],
        name="convolve",
    )(place, *signal_rel, *cot_rel, filt_spec, a_high, a_low, t_high, skip)


def smem():
    return pl.BlockSpec(memory_space=pltpu.SMEM)


def weight_grads(place, signal_rel, gate_grad, groups):
    count = len(signal_rel)
    local_len, channels = signal_rel[0].shape
    width = gate_grad.shape[1]
    rows = channels // sum(len(group) for group in groups)

    def body(place_ref, *refs):
        sig = refs[:count]
        grad = refs[count]
        outs = refs[count + 1 :]
        right = jnp.concatenate(
            [grad[piece(place_ref, r, local_len), :] for r in range(count)], axis=0
        )
        for out, group in zip(outs, groups):
            for at, k in enumerate(group):
                start = pl.multiple_of((place_ref[1] ^ k) * rows, rows)
                left = jnp.concatenate(
                    [sig[r][:, pl.ds(start, rows)] for r in range(count)], axis=0
                )
                out[at] = dot_first(left, right).astype(bf16)

    return pl.pallas_call(
        body,
        in_specs=[smem()] + [pl.BlockSpec(memory_space=VMEM)] * (count + 1),
        out_specs=[pl.BlockSpec(memory_space=VMEM)] * len(groups),
        out_shape=[struct((len(group), rows, width), bf16) for group in groups],
        name="weight_grads",
    )(place, *signal_rel, gate_grad)


def gating(place, signal_rel, weight_rel, cot_rel, inner):
    count = len(signal_rel)
    dp_count = len(weight_rel)
    local_len, channels = signal_rel[0].shape
    rows, width = weight_rel[0].shape
    length = local_len * count

    def body(place_ref, *refs):
        sig = refs[:count]
        weight = refs[count : count + dp_count]
        cot = refs[count + dp_count : 2 * count + dp_count]
        inner_ref = refs[2 * count + dp_count]
        outs = refs[2 * count + dp_count + 1 : -1]
        full = refs[-1]
        inner_grad_out, conv_grad_out, skip_out = outs[count:]
        for k in range(dp_count):
            start = pl.multiple_of((place_ref[1] ^ k) * rows, rows)
            full[pl.ds(start, rows), :] = weight[k][...]
        left = jnp.concatenate([sig[r][...] for r in range(count)], axis=0)
        gates = dot(left, full[...])
        skip_sum = jnp.zeros((1, width), f32)
        own = pl.multiple_of(place_ref[0] * width, width)
        for r in range(count):
            here = piece(place_ref, r, local_len)
            gate = gates[r * local_len : (r + 1) * local_len]
            outs[r][...] = (gate * inner_ref[here, :]).astype(bf16)
            inner_grad = cot[r][...].astype(f32) * gate
            inner_grad_out[here, :] = inner_grad
            conv_grad_out[here, :] = inner_grad.astype(bf16)
            signal = sig[r][:, pl.ds(own, width)].astype(f32)
            skip_sum += jnp.sum(inner_grad * signal, axis=0, keepdims=True)
        skip_out[...] = jnp.broadcast_to(skip_sum, (8, width))

    return pl.pallas_call(
        body,
        in_specs=[smem()] + [pl.BlockSpec(memory_space=VMEM)] * (2 * count + dp_count + 1),
        out_specs=[pl.BlockSpec(memory_space=VMEM)] * (count + 3),
        out_shape=[struct((local_len, width), bf16)] * count
        + [
            struct((length, width), f32),
            struct((length, width), bf16),
            struct((8, width), f32),
        ],
        scratch_shapes=[VMEM((channels, width), bf16)],
        name="gating",
    )(place, *signal_rel, *weight_rel, *cot_rel, inner)


def packed_rows(order, table_rows, width):
    per_group = width // order
    groups = -(-(table_rows // 8) // per_group)
    return order + 8 + 8 * groups, per_group


def correlate_back(place, conv_grad, inner_grad, filt_spec, tables, skip, block):
    a_high, a_low, t_high = tables
    length, width = conv_grad.shape

    def body(place_ref, cg, ig, fs, ah, al, th, skip_ref, direct_out, spec, back):
        step = pl.program_id(0)
        re = to_spectrum(ah, al, 0, cg[...])
        im = to_spectrum(ah, al, 1, cg[...])
        spec[0] = re
        spec[1] = im
        term = from_spectrum(th, fs[0] * re + fs[1] * im, fs[0] * im - fs[1] * re, length)

        @pl.when(step == 0)
        def _():
            back[...] = term

        @pl.when(step != 0)
        def _():
            back[...] += term

        @pl.when(step == pl.num_programs(0) - 1)
        def _():
            direct_out[...] = ig[...] * skip_ref[...] + back[...].astype(bf16).astype(f32)

    by_row, by_col = table_specs(length, block)
    spec_block = spectrum_block(width, block)
    return pl.pallas_call(
        body,
        grid_spec=pltpu.PrefetchScalarGridSpec(
            num_scalar_prefetch=1,
            grid=(length // block,),
            in_specs=[
                whole((length, width)),
                whole((length, width)),
                spec_block,
                by_row,
                by_row,
                by_col,
                pl.BlockSpec((1, width), lambda i, place_ref: (0, place_ref[0])),
            ],
            out_specs=[whole((length, width)), spec_block],
            scratch_shapes=[VMEM((length, width), f32)],
        ),
        out_shape=[struct((length, width), f32), struct((2, length, width), f32)],
        name="correlate_back",
    )(place, conv_grad, inner_grad, filt_spec, a_high, a_low, t_high, skip)


def correlate_part(
    place, grad_spec, skip_sum, signal_spec, tables, env, hidden, filter_weight, cos_pre, table_t,
    block,
):
    t_high = tables[2]
    length, width = env.shape
    order = filter_weight.shape[0]
    table_rows = table_t.shape[0]
    total_rows, per_group = packed_rows(order, table_rows, width)

    def body(
        place_ref, gs, skip_sum_ref, ss, th, env_ref, hid, fw, cp, tab, packed, part,
    ):
        step = pl.program_id(0)
        term = from_spectrum(
            th, ss[0] * gs[0] + ss[1] * gs[1], ss[0] * gs[1] - ss[1] * gs[0], length
        )

        @pl.when(step == 0)
        def _():
            part[...] = term

        @pl.when(step != 0)
        def _():
            part[...] += term

        @pl.when(step == pl.num_programs(0) - 1)
        def _():
            pre_grad = part[...].astype(bf16).astype(f32) * env_ref[...]
            packed[...] = jnp.zeros((total_rows, width), f32)
            packed[:order, :] = careful(dot_first, hid[...], pre_grad)
            packed[order : order + 8, :] = skip_sum_ref[...]
            act = careful(dot_last, pre_grad, fw[...]) * cp[...]
            small = careful(dot, tab[...], act)
            for b in range(table_rows // 8):
                row = order + 8 + 8 * (b // per_group)
                col = order * (b % per_group)
                packed[row : row + 8, col : col + order] = small[8 * b : 8 * b + 8]

    _, by_col = table_specs(length, block)
    spec_block = spectrum_block(width, block)
    return pl.pallas_call(
        body,
        grid_spec=pltpu.PrefetchScalarGridSpec(
            num_scalar_prefetch=1,
            grid=(length // block,),
            in_specs=[
                spec_block,
                whole((8, width)),
                spec_block,
                by_col,
                whole((length, width)),
                whole(hidden.shape),
                pl.BlockSpec((order, width), lambda i, place_ref: (0, place_ref[0])),
                whole(cos_pre.shape),
                whole(table_t.shape),
            ],
            out_specs=whole((total_rows, width)),
            scratch_shapes=[VMEM((length, width), f32)],
        ),
        out_shape=struct((total_rows, width), f32),
        name="correlate_part",
    )(
        place, grad_spec, skip_sum, signal_spec, t_high, env, hidden, filter_weight, cos_pre,
        table_t,
    )


def through_gate(place, gate_grad, weight_rel, direct, count):
    dp_count = len(weight_rel)
    rows, width = weight_rel[0].shape
    length = gate_grad.shape[0]
    local_len = length // count
    channels = rows * dp_count

    def body(place_ref, *refs):
        grad = refs[0]
        weight = refs[1 : 1 + dp_count]
        direct_ref = refs[1 + dp_count]
        outs = refs[2 + dp_count :]
        left = jnp.concatenate(
            [grad[piece(place_ref, r, local_len), :] for r in range(count)], axis=0
        )
        for k in range(dp_count):
            start = pl.multiple_of((place_ref[1] ^ k) * rows, rows)
            shift = start - place_ref[0] * width
            inside = jnp.logical_and(shift >= 0, shift < width)
            shift = pl.multiple_of(jnp.clip(shift, 0, width - rows), rows)
            scale = jnp.where(inside, 1.0, 0.0).astype(f32)
            terms = dot_last(left, weight[k][...])
            for r in range(count):
                term = terms[r * local_len : (r + 1) * local_len]
                term += scale * direct_ref[piece(place_ref, r, local_len), pl.ds(shift, rows)]
                outs[r][:, pl.ds(start, rows)] = term.astype(bf16)

    return pl.pallas_call(
        body,
        in_specs=[smem()] + [pl.BlockSpec(memory_space=VMEM)] * (dp_count + 2),
        out_specs=[pl.BlockSpec(memory_space=VMEM)] * count,
        out_shape=[struct((local_len, channels), bf16)] * count,
        name="through_gate",
    )(place, gate_grad, *weight_rel, direct)


def assemble(place, pieces, kind):
    count = len(pieces)
    rows, width = pieces[0].shape

    def body(place_ref, *refs):
        out = refs[count]
        for r in range(count):
            start = pl.multiple_of((place_ref[0] ^ r) * width, width)
            out[:, pl.ds(start, width)] = refs[r][...].astype(kind)

    return pl.pallas_call(
        body,
        in_specs=[smem()] + [pl.BlockSpec(memory_space=VMEM)] * count,
        out_specs=pl.BlockSpec(memory_space=VMEM),
        out_shape=struct((rows, width * count), kind),
        name="assemble",
    )(place, *pieces)


def finish(place, pieces, order, emb_count):
    count = len(pieces)
    _, width = pieces[0].shape
    table_rows = -(-(emb_count + 1) // 8) * 8
    _, per_group = packed_rows(order, table_rows, width)

    def body(place_ref, *refs):
        filter_out, skip_out, pos_out, bias_out = refs[count:]
        for r in range(count):
            cols = pl.ds(pl.multiple_of((place_ref[0] ^ r) * width, width), width)
            values = refs[r][...].astype(f32)
            filter_out[:, cols] = values[:order, :]
            skip_out[:, cols] = values[order : order + 1, :]
        tails = [refs[r][...].astype(f32)[order + 8 :, :] for r in range(count)]
        while len(tails) > 1:
            tails = [tails[i] + tails[i + 1] for i in range(0, len(tails), 2)]
        for b in range(table_rows // 8):
            row = 8 * (b // per_group)
            col = order * (b % per_group)
            found = tails[0][row : row + 8, col : col + order]
            low = 8 * b
            high = min(low + 8, emb_count)
            if high > low:
                pos_out[low:high, :] = found[: high - low]
            if low <= emb_count < low + 8:
                bias_out[...] = found[emb_count - low : emb_count - low + 1]

    return pl.pallas_call(
        body,
        in_specs=[smem()] + [pl.BlockSpec(memory_space=VMEM)] * count,
        out_specs=[pl.BlockSpec(memory_space=VMEM)] * 4,
        out_shape=[
            struct((order, width * count), f32),
            struct((1, width * count), f32),
            struct((emb_count, order), f32),
            struct((1, order), f32),
        ],
        name="finish",
    )(place, *pieces)


def swap(value, axis, offset):
    count = lax.axis_size(axis)
    return lax.ppermute(value, axis, [(i, i ^ offset) for i in range(count)])


def gather_rel(own, axis):
    count = lax.axis_size(axis)
    found = {0: own}
    bit = count // 2
    while bit:
        for r in list(found):
            found[r | bit] = swap(found[r], axis, bit)
        bit //= 2
    return [found[r] for r in range(count)]


def add_round(*terms):
    total = terms[0].astype(f32)
    for term in terms[1:]:
        total = total + term.astype(f32)
    return total.astype(bf16)


def shards(
    signal, gate_weight, pos_weight, pos_bias, filter_weight, decay_rate, skip_gain, grad_out
):
    seq_count = lax.axis_size("seq")
    dp_count = lax.axis_size("dp")
    signal_tok = signal[0]
    cot_tok = grad_out[0]
    local_len, channels = signal_tok.shape
    length = local_len * seq_count
    width = channels // seq_count
    emb_count, order = pos_weight.shape
    seq_at = lax.axis_index("seq")
    dp_at = lax.axis_index("dp")
    place = jnp.stack([seq_at, dp_at]).astype(jnp.int32)
    block = min(256, length)

    def own_cols(x, r=0):
        return lax.dynamic_slice_in_dim(x, (seq_at ^ r) * width, width, axis=x.ndim - 1)

    signal_rel = gather_rel(signal_tok, "seq")
    weight_rel = {0: own_cols(gate_weight)}
    for k in range(2, dp_count, 2):
        weight_rel[k] = swap(weight_rel[0], "dp", k)
    for k in range(0, dp_count, 2):
        weight_rel[k + 1] = swap(weight_rel[k], "dp", 1)
    weight_rel = [weight_rel[k] for k in range(dp_count)]
    cot_rel = [own_cols(cot_tok)] + [
        swap(own_cols(cot_tok, r), "seq", r) for r in range(1, seq_count)
    ]

    table = feature_table(length, emb_count)
    rates = decay_rate[None]
    norm = jnp.sqrt(jnp.expm1(-2.0 * rates * length) / jnp.expm1(-2.0 * rates))
    skip = skip_gain[None]
    a_high, a_low, t_high, filt_spec, env, hidden, cos_pre = generate(
        place, jnp.asarray(table), [jnp.asarray(f) for f in angle_factors(length)],
        pos_weight, pos_bias[None], filter_weight, rates, norm, width, block,
    )
    tables = (a_high, a_low, t_high)

    signal_spec, inner, gate_grad = convolve(
        place, signal_rel, cot_rel, filt_spec, tables, skip, block
    )

    far = list(reversed(range(0, dp_count, 2)))
    pairs = [far[i : i + 2] for i in range(0, len(far), 2)]
    groups = [[k + 1 for k in pair] for pair in pairs] + pairs
    weight_parts = weight_grads(place, signal_rel, gate_grad, groups)
    sums = {}
    for i, pair in enumerate(pairs):
        met = swap(weight_parts[i], "dp", 1)
        for at, k in enumerate(pair):
            sums[k] = add_round(weight_parts[len(pairs) + i][at], met[at])
    row_sum = add_round(sums[0], *[swap(sums[k], "dp", k) for k in far[:-1]])
    row_rel = gather_rel(row_sum, "seq")
    grad_gate_weight = assemble(place, row_rel, f32)

    gated = gating(place, signal_rel, weight_rel, cot_rel, inner)
    out_rel = gated[:seq_count]
    inner_grad, conv_grad, skip_sum = gated[seq_count:]
    out_rel = [out_rel[0]] + [swap(out_rel[r], "seq", r) for r in range(1, seq_count)]
    output = assemble(place, out_rel, bf16)

    direct, grad_spec = correlate_back(place, conv_grad, inner_grad, filt_spec, tables, skip, block)
    packed = correlate_part(
        place, grad_spec, skip_sum, signal_spec, tables, env, hidden, filter_weight, cos_pre,
        jnp.asarray(table.T), block,
    )
    back_rel = through_gate(place, gate_grad, weight_rel, direct, seq_count)

    live = {r: back_rel[r] for r in range(seq_count)}
    bit = 1
    while bit < seq_count:
        met = {r: swap(live[r | bit], "seq", bit) for r in live if not r & bit}
        live = {r: add_round(live[r], met[r]) for r in met}
        bit *= 2
    grad_signal = live[0]

    packed = (packed + swap(packed, "dp", 1)).astype(bf16)
    terms = [packed] + [swap(packed, "dp", k) for k in range(2, dp_count, 2)]
    terms = [term.astype(f32) for term in terms]
    while len(terms) > 1:
        terms = [terms[i] + terms[i + 1] for i in range(0, len(terms), 2)]
    packed_rel = gather_rel(terms[0].astype(bf16), "seq")
    grad_filter_weight, grad_skip, grad_pos_weight, grad_pos_bias = finish(
        place, packed_rel, order, emb_count
    )
    return (
        output[None],
        grad_signal[None],
        grad_gate_weight,
        grad_pos_weight,
        grad_pos_bias[0],
        grad_filter_weight,
        grad_skip[0],
    )


def solution(mesh):
    step = mapped(shards, mesh)
    return step


def mapped(body, mesh):
    return jax.shard_map(
        body,
        mesh=mesh,
        in_specs=(
            P("dp", "seq", None),
            P("dp", None),
            P(),
            P(),
            P(),
            P(),
            P(),
            P("dp", "seq", None),
        ),
        out_specs=(P("dp", "seq", None), P("dp", "seq", None), P("dp", None), P(), P(), P(), P()),
        check_vma=False,
    )
```

profile of v0, /device:TPU:0, one launch (start us, length us, event | category | flops | bytes accessed | tf_op | source)
XLA Modules:
  0.0 170.8 jit_solution(15054120206910556681)
XLA Ops:
  0.6 0.0 copy-start
  0.6 3.0 %collective-permute-start.1 = (bf16[128,2048]{1,0:T(8,128)(2,1)}, bf16[128,2048]{1,0:T(8,128)(2,1)S(1)}, u32[]{:S(2)}, u32[]{:S(2)}) collective-permute-start(bf16[128,2048]{1,0:T(8,128)(2,1)} %bitcast.31), channel_id=1, source_target_pairs={{0,2},{1,3},{2,0},{3,1},{4,6},{5,7},{6,4},{7,5},{8,10},{9,11},{10,... | collective-permute-start | bytes 1572872 | tf_op jit(solution)/shard_map/ppermute | solution.py:542
  3.7 0.0 collective-permute-start
  3.7 1.8 %dynamic-slice_bitcast_fusion = (bf16[128,512]{1,0:T(8,128)(2,1)S(1)}, bf16[128,512]{1,0:T(8,128)(2,1)S(1)}, bf16[128,512]{1,0:T(8,128)(2,1)}, bf16[128,512]{1,0:T(8,128)(2,1)S(1)}) fusion(bf16[1,128,2048]{2,1,0:T(8,128)(2,1)} %param.21, s32[]{:T(128)S(6)} %select_n.16, s32[]{:T(128)S(6)} %select_n.14, s32[]{:T(128)S(6)} %select_n.13, s32[]{:T(128)S(6)} %select_n.15), kind=kLoop, calls=%fused_computation.18 | loop fusion | bytes 1048592 | tf_op jit(solution)/shard_map/dynamic_slice | solution.py:580
  5.5 0.2 collective-permute-start.12
  5.7 0.3 collective-permute-start.10
  6.0 1.6 collective-permute-start.11
  7.6 11.4 %collective-permute-done.12.refs_7_.refs_15_ = bf16[128,512]{1,0:T(8,128)(2,1)S(1)} collective-permute-done((bf16[128,512]{1,0:T(8,128)(2,1)S(1)}, bf16[128,512]{1,0:T(8,128)(2,1)S(1)}, u32[]{:S(2)}, u32[]{:S(2)}) %collective-permute-start.12) | collective-permute-done | bytes 131104 | tf_op jit(solution)/shard_map/ppermute | solution.py:542
  19.0 3.6 %collective-permute-start.8 = (bf16[256,512]{1,0:T(8,128)(2,1)S(1)}, bf16[256,512]{1,0:T(8,128)(2,1)S(1)}, u32[]{:S(2)}, u32[]{:S(2)}) collective-permute-start(bf16[256,512]{1,0:T(8,128)(2,1)S(1)} %constant_dynamic-slice_fusion.refs_4_.refs_1_), channel_id=1, source_target_pairs={{0,24},{4,28},{8,16},{12,20},{16,8},{20,12},{24,0},{28,4},{1,25},{... | collective-permute-start | bytes 786440 | tf_op jit(solution)/shard_map/ppermute | solution.py:542
  22.6 0.8 collective-permute-start.4
  23.4 0.0 collective-permute-done.1.refs_2_
  23.4 0.4 collective-permute-start.2
  23.8 6.3 %collective-permute-done.8.refs_10_.refs_7_ = bf16[256,512]{1,0:T(8,128)(2,1)S(1)} collective-permute-done((bf16[256,512]{1,0:T(8,128)(2,1)S(1)}, bf16[256,512]{1,0:T(8,128)(2,1)S(1)}, u32[]{:S(2)}, u32[]{:S(2)}) %collective-permute-start.8) | collective-permute-done | bytes 262176 | tf_op jit(solution)/shard_map/ppermute | solution.py:542
  30.1 1.5 collective-permute-start.3
  31.7 14.2 %collective-permute-done.6.refs_8_.refs_5_ = bf16[256,512]{1,0:T(8,128)(2,1)S(1)} collective-permute-done((bf16[256,512]{1,0:T(8,128)(2,1)S(1)}, bf16[256,512]{1,0:T(8,128)(2,1)S(1)}, u32[]{:S(2)}, u32[]{:S(2)}) %collective-permute-start.6) | collective-permute-done | bytes 262176 | tf_op jit(solution)/shard_map/ppermute | solution.py:542
  45.9 1.5 collective-permute-start.9
  47.4 0.5 collective-permute-start.7
  47.9 1.5 collective-permute-start.5
  49.5 1.3 divide_sqrt_fusion
  50.8 0.6 pad_add_fusion.place_ref
  51.4 8.9 %generate.1 = (bf16[2,512,512]{2,1,0:T(8,128)(2,1)}, bf16[2,512,512]{2,1,0:T(8,128)(2,1)}, bf16[2,512,512]{2,1,0:T(8,128)(2,1)}, f32[2,512,512]{2,1,0:T(8,128)},...) custom-call(s32[2]{0:T(128)} %pad_add_fusion.place_ref, f32[512,40]{1,0:T(8,128)} %constant.42.clone.tab, ...), custom_call_target="tpu_custom_call" | custom-call | tf_op jit(solution)/shard_map/generate/pallas_call | solution.py:150
  60.3 0.0 copy-start.3
  60.3 0.8 copy-done.3
  61.1 7.2 %convolve.1 = (f32[2,512,512]{2,1,0:T(8,128)}, f32[512,512]{1,0:T(8,128)}, bf16[512,512]{1,0:T(8,128)(2,1)}) custom-call(s32[2]{0:T(128)} %pad_add_fusion.place_ref, bf16[128,2048]{1,0:T(8,128)(2,1)} %bitcast.33, bf16[128,2048]{1,0:T(8,128)(2,1)} %copy-done.2, bf16[128,2048]{1,0:T(8,128)(2,1)} %copy-done.1, bf16[128,2048]{1,0:T(8,128)(2,1)} %copy-done.3, ...), custom_call_target="tpu_custom_call" | custom-call | tf_op jit(solution)/shard_map/convolve/pallas_call | solution.py:215
  68.3 4.1 %weight_grads.1 = (bf16[2,256,512]{2,1,0:T(8,128)(2,1)}, bf16[2,256,512]{2,1,0:T(8,128)(2,1)}, bf16[2,256,512]{2,1,0:T(8,128)(2,1)}, bf16[2,256,512]{2,1,0:T(8,128)(2,1)}) custom-call(s32[2]{0:T(128)} %pad_add_fusion.place_ref, bf16[128,2048]{1,0:T(8,128)(2,1)} %bitcast.34, bf16[128,2048]{1,0:T(8,128)(2,1)} %copy-done.2, bf16[128,2048]{1,0:T(8,128)(2,1)} %copy-done.1, ...), custom_call_target="tpu_custom_call" | custom-call | tf_op jit(solution)/shard_map/weight_grads/pallas_call | solution.py:265
  72.4 0.5 collective-permute-start.19
  72.9 0.0 collective-permute-done.3.refs_5_.refs_2_
  72.9 5.4 %gating.1 = (bf16[128,512]{1,0:T(8,128)(2,1)}, bf16[128,512]{1,0:T(8,128)(2,1)}, bf16[128,512]{1,0:T(8,128)(2,1)}, bf16[128,512]{1,0:T(8,128)(2,1)}, f32[512,512...) custom-call(s32[2]{0:T(128)} %pad_add_fusion.place_ref, bf16[128,2048]{1,0:T(8,128)(2,1)} %bitcast.35, ...), custom_call_target="tpu_custom_call" | custom-call | tf_op jit(solution)/shard_map/gating/pallas_call | solution.py:307
  78.3 6.9 %correlate_back.1 = (f32[512,512]{1,0:T(8,128)}, f32[2,512,512]{2,1,0:T(8,128)}) custom-call(s32[2]{0:T(128)} %pad_add_fusion.place_ref, bf16[512,512]{1,0:T(8,128)(2,1)} %get-tuple-element.48.cg, f32[512,512]{1,0:T(8,128)} %get-tuple-element.49.ig, f32[2,512,512]{2,1,0:T(8,128)} %get-tuple-element.38.refs_8_.fs, ...), custom_call_target="tpu_custom_call" | custom-call | tf_op jit(solution)/shard_map/correlate_back/pallas_call | solution.py:354
  85.2 6.3 %correlate_part.1 = f32[80,512]{1,0:T(8,128)} custom-call(s32[2]{0:T(128)} %pad_add_fusion.place_ref, f32[2,512,512]{2,1,0:T(8,128)} %get-tuple-element.59.gs, f32[8,512]{1,0:T(8,128)} %get-tuple-element.60.skip_sum_ref, f32[2,512,512]{2,1,0:T(8,128)} %get-tuple-element.61.ss, bf16[2,512,512]{2,1,0:T(8,128)(2,1)} %get-tuple-element.41.refs_11_.th, ...), custom_call_target="tpu_custom_call" | custom-call | tf_op jit(solution)/shard_map/correlate_part/pallas_call | solution.py:417
  91.5 1.6 collective-permute-start.27
  93.1 0.5 collective-permute-start.20
  93.6 4.6 %through_gate.1 = (bf16[128,2048]{1,0:T(8,128)(2,1)}, bf16[128,2048]{1,0:T(8,128)(2,1)}, bf16[128,2048]{1,0:T(8,128)(2,1)}, bf16[128,2048]{1,0:T(8,128)(2,1)}) custom-call(s32[2]{0:T(128)} %pad_add_fusion.place_ref, bf16[512,512]{1,0:T(8,128)(2,1)} %get-tuple-element.47.refs_0_.refs_4_, bf16[256,512]{1,0:T(8,128)(2,1)} %copy-done.4, ...), custom_call_target="tpu_custom_call" | custom-call | tf_op jit(solution)/shard_map/through_gate/pallas_call | solution.py:471
  98.2 0.5 collective-permute-start.16
  98.7 0.1 collective-permute-done.27
  98.9 0.1 fusion.7
  99.0 0.1 collective-permute-start.23
  99.1 8.9 %collective-permute-done.20 = bf16[2,256,512]{2,1,0:T(8,128)(2,1)S(1)} collective-permute-done((bf16[2,256,512]{2,1,0:T(8,128)(2,1)}, bf16[2,256,512]{2,1,0:T(8,128)(2,1)S(1)}, u32[]{:S(2)}, u32[]{:S(2)}) %collective-permute-start.20) | collective-permute-done | bytes 524320 | tf_op jit(solution)/shard_map/ppermute | solution.py:542
  108.0 0.1 fusion.5
  108.1 2.5 %collective-permute-start.21 = (bf16[256,512]{1,0:T(8,128)(2,1)S(1)}, bf16[256,512]{1,0:T(8,128)(2,1)S(1)}, u32[]{:S(2)}, u32[]{:S(2)}) collective-permute-start(bf16[256,512]{1,0:T(8,128)(2,1)S(1)} %get-tuple-element.69), channel_id=1, source_target_pairs={{0,24},{4,28},{8,16},{12,20},{16,8},{20,12},{24,0},{28,4},{1,25},{... | collective-permute-start | bytes 786440 | tf_op jit(solution)/shard_map/ppermute | solution.py:542
  110.7 0.0 copy-start.14
  110.7 0.1 add_convert_fusion.1
  110.8 1.4 collective-permute-start.30
  112.2 2.0 %collective-permute-start.29 = (bf16[80,512]{1,0:T(8,128)(2,1)S(1)}, bf16[80,512]{1,0:T(8,128)(2,1)S(1)}, u32[]{:S(2)}, u32[]{:S(2)}) collective-permute-start(bf16[80,512]{1,0:T(8,128)(2,1)S(1)} %add_convert_fusion.8), channel_id=1, source_target_pairs={{0,16},{4,20},{8,24},{12,28},{16,0},{20,4},{24,8},{28,12},{1,17},{... | collective-permute-start | bytes 245768 | tf_op jit(solution)/shard_map/ppermute | solution.py:542
  114.2 5.0 %collective-permute-done.21 = bf16[256,512]{1,0:T(8,128)(2,1)S(1)} collective-permute-done((bf16[256,512]{1,0:T(8,128)(2,1)S(1)}, bf16[256,512]{1,0:T(8,128)(2,1)S(1)}, u32[]{:S(2)}, u32[]{:S(2)}) %collective-permute-start.21) | collective-permute-done | bytes 262176 | tf_op jit(solution)/shard_map/ppermute | solution.py:542
  119.2 12.4 %collective-permute-start.28 = (bf16[80,512]{1,0:T(8,128)(2,1)S(1)}, bf16[80,512]{1,0:T(8,128)(2,1)S(1)}, u32[]{:S(2)}, u32[]{:S(2)}) collective-permute-start(bf16[80,512]{1,0:T(8,128)(2,1)S(1)} %add_convert_fusion.8), channel_id=1, source_target_pairs={{0,8},{4,12},{8,0},{12,4},{16,24},{20,28},{24,16},{28,20},{1,9},{5... | collective-permute-start | bytes 245768 | tf_op jit(solution)/shard_map/ppermute | solution.py:542
  131.6 4.1 %collective-permute-done.22 = bf16[256,512]{1,0:T(8,128)(2,1)S(1)} collective-permute-done((bf16[256,512]{1,0:T(8,128)(2,1)S(1)}, bf16[256,512]{1,0:T(8,128)(2,1)S(1)}, u32[]{:S(2)}, u32[]{:S(2)}) %collective-permute-start.22) | collective-permute-done | bytes 262176 | tf_op jit(solution)/shard_map/ppermute | solution.py:542
  135.7 1.8 %collective-permute-start.18 = (bf16[128,2048]{1,0:T(8,128)(2,1)S(1)}, bf16[128,2048]{1,0:T(8,128)(2,1)}, u32[]{:S(2)}, u32[]{:S(2)}) collective-permute-start(bf16[128,2048]{1,0:T(8,128)(2,1)S(1)} %add_convert_fusion.1), channel_id=1, source_target_pairs={{0,2},{1,3},{2,0},{3,1},{4,6},{5,7},{6,4},{7,5},{8,10},{9,11},{10,... | collective-permute-start | bytes 1572872 | tf_op jit(solution)/shard_map/ppermute | solution.py:542
  137.5 0.2 fusion.3.refs_0_
  137.7 0.3 collective-permute-start.14
  138.0 1.9 %collective-permute-start.25 = (bf16[256,512]{1,0:T(8,128)(2,1)S(1)}, bf16[256,512]{1,0:T(8,128)(2,1)S(1)}, u32[]{:S(2)}, u32[]{:S(2)}) collective-permute-start(bf16[256,512]{1,0:T(8,128)(2,1)S(1)} %fusion.3.refs_0_), channel_id=1, source_target_pairs={{0,2},{1,3},{2,0},{3,1},{4,6},{5,7},{6,4},{7,5},{8,10},{9,11},{10,... | collective-permute-start | bytes 786440 | tf_op jit(solution)/shard_map/ppermute | solution.py:542
  139.9 13.3 %collective-permute-done.14.refs_2_ = bf16[128,512]{1,0:T(8,128)(2,1)S(1)} collective-permute-done((bf16[128,512]{1,0:T(8,128)(2,1)S(1)}, bf16[128,512]{1,0:T(8,128)(2,1)S(1)}, u32[]{:S(2)}, u32[]{:S(2)}) %collective-permute-start.14) | collective-permute-done | bytes 131104 | tf_op jit(solution)/shard_map/ppermute | solution.py:542
  153.3 1.8 %collective-permute-start.32 = (bf16[80,512]{1,0:T(8,128)(2,1)S(1)}, bf16[80,512]{1,0:T(8,128)(2,1)S(1)}, u32[]{:S(2)}, u32[]{:S(2)}) collective-permute-start(bf16[80,512]{1,0:T(8,128)(2,1)S(1)} %add_convert_fusion.7.refs_0_), channel_id=1, source_target_pairs={{0,2},{1,3},{2,0},{3,1},{4,6},{5,7},{6,4},{7,5},{8,10},{9,11},{10,... | collective-permute-start | bytes 245768 | tf_op jit(solution)/shard_map/ppermute | solution.py:542
  155.1 3.7 %collective-permute-done.32.refs_2_ = bf16[80,512]{1,0:T(8,128)(2,1)S(1)} collective-permute-done((bf16[80,512]{1,0:T(8,128)(2,1)S(1)}, bf16[80,512]{1,0:T(8,128)(2,1)S(1)}, u32[]{:S(2)}, u32[]{:S(2)}) %collective-permute-start.32) | collective-permute-done | bytes 81952 | tf_op jit(solution)/shard_map/ppermute | solution.py:542
  158.8 2.0 %assemble.2 = bf16[128,2048]{1,0:T(8,128)(2,1)} custom-call(s32[2]{0:T(128)} %pad_add_fusion.place_ref, bf16[128,512]{1,0:T(8,128)(2,1)} %get-tuple-element.43.refs_0_, bf16[128,512]{1,0:T(8,128)(2,1)} %collective-permute-done.13.refs_1_, bf16[128,512]{1,0:T(8,128)(2,1)} %copy-done.19, bf16[128,512]{1,0:T(8,128)(2,1)} %copy-done.20), custom_call_target="tpu_custom_call" | custom-call | tf_op jit(solution)/shard_map/assemble/pallas_call | solution.py:490
  160.8 0.6 copy-done.22
  161.4 0.6 copy-done.23
  162.1 1.9 %finish.1 = (f32[64,2048]{1,0:T(8,128)}, f32[1,2048]{1,0:T(1,128)}, f32[33,64]{1,0:T(8,128)}, f32[1,64]{1,0:T(1,128)}) custom-call(s32[2]{0:T(128)} %pad_add_fusion.place_ref, bf16[80,512]{1,0:T(8,128)(2,1)} %copy-done.15, bf16[80,512]{1,0:T(8,128)(2,1)} %copy-done.22, bf16[80,512]{1,0:T(8,128)(2,1)} %copy-done.21, bf16[80,512]{1,0:T(8,128)(2,1)} %copy-done.23), custom_call_target="tpu_custom_call" | custom-call | tf_op jit(solution)/shard_map/finish/pallas_call | solution.py:526
  163.9 0.5 collective-permute-start.24
  164.4 0.1 collective-permute-start.26
  164.5 2.2 %fusion = bf16[1,128,2048]{2,1,0:T(8,128)(2,1)} fusion(bf16[128,2048]{1,0:T(8,128)(2,1)} %collective-permute-done.18, bf16[128,2048]{1,0:T(8,128)(2,1)} %collective-permute-done.16, bf16[128,2048]{1,0:T(8,128)(2,1)S(1)} %copy-done.14), kind=kLoop, calls=%fused_computation.3 | loop fusion | flops 2097152 | bytes 2097152 | tf_op jit(solution)/shard_map/broadcast_in_dim | solution.py:652
  166.8 0.7 copy-done.17
  167.5 0.7 copy-done.18
  168.2 2.7 %assemble.3 = f32[256,2048]{1,0:T(8,128)} custom-call(s32[2]{0:T(128)} %pad_add_fusion.place_ref, bf16[256,512]{1,0:T(8,128)(2,1)} %copy-done.7, bf16[256,512]{1,0:T(8,128)(2,1)} %copy-done.17, bf16[256,512]{1,0:T(8,128)(2,1)} %copy-done.16, bf16[256,512]{1,0:T(8,128)(2,1)} %copy-done.18), custom_call_target="tpu_custom_call" | custom-call | tf_op jit(solution)/shard_map/assemble/pallas_call | solution.py:490
  (77 shorter events, 0.2 us)
Async XLA Ops:
  0.6 7.0 %copy-start = (bf16[256,2048]{1,0:T(8,128)(2,1)S(1)}, bf16[256,2048]{1,0:T(8,128)(2,1)}, u32[]{:S(2)}) copy-start(bf16[256,2048]{1,0:T(8,128)(2,1)} %param.15) | copy-start | bytes 3145732
  0.6 22.8 %collective-permute-start.1 = (bf16[128,2048]{1,0:T(8,128)(2,1)}, bf16[128,2048]{1,0:T(8,128)(2,1)S(1)}, u32[]{:S(2)}, u32[]{:S(2)}) collective-permute-start(bf16[128,2048]{1,0:T(8,128)(2,1)} %bitcast.31), channel_id=1, source_target_pairs={{0,2},{1,3},{2,0},{3,1},{4,6},{5,7},{6,4},{7,5},{8,10},{9,11},{10,... | collective-permute-start | bytes 1572872 | tf_op jit(solution)/shard_map/ppermute | solution.py:542
  3.7 44.3 %collective-permute-start = (bf16[128,2048]{1,0:T(8,128)(2,1)}, bf16[128,2048]{1,0:T(8,128)(2,1)S(1)}, u32[]{:S(2)}, u32[]{:S(2)}) collective-permute-start(bf16[128,2048]{1,0:T(8,128)(2,1)} %bitcast.32), channel_id=1, source_target_pairs={{0,1},{1,0},{2,3},{3,2},{4,5},{5,4},{6,7},{7,6},{8,9},{9,8},{10,11... | collective-permute-start | bytes 1572872 | tf_op jit(solution)/shard_map/ppermute | solution.py:542
  5.5 13.6 %collective-permute-start.12 = (bf16[128,512]{1,0:T(8,128)(2,1)S(1)}, bf16[128,512]{1,0:T(8,128)(2,1)S(1)}, u32[]{:S(2)}, u32[]{:S(2)}) collective-permute-start(bf16[128,512]{1,0:T(8,128)(2,1)S(1)} %get-tuple-element.71), channel_id=1, source_target_pairs={{0,3},{1,2},{2,1},{3,0},{4,7},{5,6},{6,5},{7,4},{8,11},{9,10},{10,... | collective-permute-start | bytes 393224 | tf_op jit(solution)/shard_map/ppermute | solution.py:542
  5.7 17.0 %collective-permute-start.10 = (bf16[128,512]{1,0:T(8,128)(2,1)S(1)}, bf16[128,512]{1,0:T(8,128)(2,1)}, u32[]{:S(2)}, u32[]{:S(2)}) collective-permute-start(bf16[128,512]{1,0:T(8,128)(2,1)S(1)} %get-tuple-element.72), channel_id=1, source_target_pairs={{0,1},{1,0},{2,3},{3,2},{4,5},{5,4},{6,7},{7,6},{8,9},{9,8},{10,11... | collective-permute-start | bytes 393224 | tf_op jit(solution)/shard_map/ppermute | solution.py:542
  6.0 16.7 %collective-permute-start.11 = (bf16[128,512]{1,0:T(8,128)(2,1)S(1)}, bf16[128,512]{1,0:T(8,128)(2,1)S(1)}, u32[]{:S(2)}, u32[]{:S(2)}) collective-permute-start(bf16[128,512]{1,0:T(8,128)(2,1)S(1)} %get-tuple-element.74), channel_id=1, source_target_pairs={{0,2},{1,3},{2,0},{3,1},{4,6},{5,7},{6,4},{7,5},{8,10},{9,11},{10,... | collective-permute-start | bytes 393224 | tf_op jit(solution)/shard_map/ppermute | solution.py:542
  7.6 65.3 %copy-start.4 = (bf16[256,512]{1,0:T(8,128)(2,1)}, bf16[256,512]{1,0:T(8,128)(2,1)S(1)}, u32[]{:S(2)}) copy-start(bf16[256,512]{1,0:T(8,128)(2,1)S(1)} %constant_dynamic-slice_fusion.refs_4_.refs_1_) | copy-start | bytes 786436
  19.0 41.3 %copy-start.9 = (bf16[128,512]{1,0:T(8,128)(2,1)}, bf16[128,512]{1,0:T(8,128)(2,1)S(1)}, u32[]{:S(2)}) copy-start(bf16[128,512]{1,0:T(8,128)(2,1)S(1)} %collective-permute-done.12.refs_7_.refs_15_) | copy-start | bytes 393220
  19.0 11.1 %collective-permute-start.8 = (bf16[256,512]{1,0:T(8,128)(2,1)S(1)}, bf16[256,512]{1,0:T(8,128)(2,1)S(1)}, u32[]{:S(2)}, u32[]{:S(2)}) collective-permute-start(bf16[256,512]{1,0:T(8,128)(2,1)S(1)} %constant_dynamic-slice_fusion.refs_4_.refs_1_), channel_id=1, source_target_pairs={{0,24},{4,28},{8,16},{12,20},{16,8},{20,12},{24,0},{28,4},{1,25},{... | collective-permute-start | bytes 786440 | tf_op jit(solution)/shard_map/ppermute | solution.py:542
  22.6 23.3 %collective-permute-start.6 = (bf16[256,512]{1,0:T(8,128)(2,1)S(1)}, bf16[256,512]{1,0:T(8,128)(2,1)S(1)}, u32[]{:S(2)}, u32[]{:S(2)}) collective-permute-start(bf16[256,512]{1,0:T(8,128)(2,1)S(1)} %constant_dynamic-slice_fusion.refs_4_.refs_1_), channel_id=1, source_target_pairs={{0,16},{4,20},{8,24},{12,28},{16,0},{20,4},{24,8},{28,12},{1,17},{... | collective-permute-start | bytes 786440 | tf_op jit(solution)/shard_map/ppermute | solution.py:542
  22.6 0.8 copy-start.10
  22.6 24.8 %collective-permute-start.4 = (bf16[256,512]{1,0:T(8,128)(2,1)S(1)}, bf16[256,512]{1,0:T(8,128)(2,1)}, u32[]{:S(2)}, u32[]{:S(2)}) collective-permute-start(bf16[256,512]{1,0:T(8,128)(2,1)S(1)} %constant_dynamic-slice_fusion.refs_4_.refs_1_), channel_id=1, source_target_pairs={{0,8},{4,12},{8,0},{12,4},{16,24},{20,28},{24,16},{28,20},{1,9},{5... | collective-permute-start | bytes 786440 | tf_op jit(solution)/shard_map/ppermute | solution.py:542
  23.4 36.9 %copy-start.1 = (bf16[128,2048]{1,0:T(8,128)(2,1)}, bf16[128,2048]{1,0:T(8,128)(2,1)S(1)}, u32[]{:S(2)}) copy-start(bf16[128,2048]{1,0:T(8,128)(2,1)S(1)} %collective-permute-done.1.refs_2_) | copy-start | bytes 1572868
  23.4 36.8 %collective-permute-start.2 = (bf16[128,2048]{1,0:T(8,128)(2,1)S(1)}, bf16[128,2048]{1,0:T(8,128)(2,1)S(1)}, u32[]{:S(2)}, u32[]{:S(2)}) collective-permute-start(bf16[128,2048]{1,0:T(8,128)(2,1)S(1)} %collective-permute-done.1.refs_2_), channel_id=1, source_target_pairs={{0,1},{1,0},{2,3},{3,2},{4,5},{5,4},{6,7},{7,6},{8,9},{9,8},{10,11... | collective-permute-start | bytes 1572872 | tf_op jit(solution)/shard_map/ppermute | solution.py:542
  30.1 42.8 %copy-start.5 = (bf16[256,512]{1,0:T(8,128)(2,1)}, bf16[256,512]{1,0:T(8,128)(2,1)S(1)}, u32[]{:S(2)}) copy-start(bf16[256,512]{1,0:T(8,128)(2,1)S(1)} %collective-permute-done.8.refs_10_.refs_7_) | copy-start | bytes 786436
  30.1 42.8 %collective-permute-start.3 = (bf16[256,512]{1,0:T(8,128)(2,1)S(1)}, bf16[256,512]{1,0:T(8,128)(2,1)}, u32[]{:S(2)}, u32[]{:S(2)}) collective-permute-start(bf16[256,512]{1,0:T(8,128)(2,1)S(1)} %constant_dynamic-slice_fusion.refs_4_.refs_1_), channel_id=1, source_target_pairs={{0,4},{4,0},{8,12},{12,8},{16,20},{20,16},{24,28},{28,24},{1,5},{5... | collective-permute-start | bytes 786440 | tf_op jit(solution)/shard_map/ppermute | solution.py:542
  45.9 27.0 %copy-start.6 = (bf16[256,512]{1,0:T(8,128)(2,1)}, bf16[256,512]{1,0:T(8,128)(2,1)S(1)}, u32[]{:S(2)}) copy-start(bf16[256,512]{1,0:T(8,128)(2,1)S(1)} %collective-permute-done.6.refs_8_.refs_5_) | copy-start | bytes 786436
  45.9 27.0 %collective-permute-start.9 = (bf16[256,512]{1,0:T(8,128)(2,1)S(1)}, bf16[256,512]{1,0:T(8,128)(2,1)}, u32[]{:S(2)}, u32[]{:S(2)}) collective-permute-start(bf16[256,512]{1,0:T(8,128)(2,1)S(1)} %collective-permute-done.8.refs_10_.refs_7_), channel_id=1, source_target_pairs={{0,4},{4,0},{8,12},{12,8},{16,20},{20,16},{24,28},{28,24},{1,5},{5... | collective-permute-start | bytes 786440 | tf_op jit(solution)/shard_map/ppermute | solution.py:542
  47.4 25.5 %collective-permute-start.7 = (bf16[256,512]{1,0:T(8,128)(2,1)S(1)}, bf16[256,512]{1,0:T(8,128)(2,1)}, u32[]{:S(2)}, u32[]{:S(2)}) collective-permute-start(bf16[256,512]{1,0:T(8,128)(2,1)S(1)} %collective-permute-done.6.refs_8_.refs_5_), channel_id=1, source_target_pairs={{0,4},{4,0},{8,12},{12,8},{16,20},{20,16},{24,28},{28,24},{1,5},{5... | collective-permute-start | bytes 786440 | tf_op jit(solution)/shard_map/ppermute | solution.py:542
  47.9 12.4 %copy-start.2 = (bf16[128,2048]{1,0:T(8,128)(2,1)}, bf16[128,2048]{1,0:T(8,128)(2,1)S(1)}, u32[]{:S(2)}) copy-start(bf16[128,2048]{1,0:T(8,128)(2,1)S(1)} %collective-permute-done.refs_1_) | copy-start | bytes 1572868
  47.9 25.0 %collective-permute-start.5 = (bf16[256,512]{1,0:T(8,128)(2,1)}, bf16[256,512]{1,0:T(8,128)(2,1)}, u32[]{:S(2)}, u32[]{:S(2)}) collective-permute-start(bf16[256,512]{1,0:T(8,128)(2,1)} %collective-permute-done.4.refs_6_.refs_3_), channel_id=1, source_target_pairs={{0,4},{4,0},{8,12},{12,8},{16,20},{20,16},{24,28},{28,24},{1,5},{5... | collective-permute-start | bytes 786440 | tf_op jit(solution)/shard_map/ppermute | solution.py:542
  60.3 0.8 copy-start.3
  72.4 26.5 %collective-permute-start.19 = (bf16[2,256,512]{2,1,0:T(8,128)(2,1)}, bf16[2,256,512]{2,1,0:T(8,128)(2,1)S(1)}, u32[]{:S(2)}, u32[]{:S(2)}) collective-permute-start(bf16[2,256,512]{2,1,0:T(8,128)(2,1)} %get-tuple-element.56), channel_id=1, source_target_pairs={{0,4},{4,0},{8,12},{12,8},{16,20},{20,16},{24,28},{28,24},{1,5},{5... | collective-permute-start | bytes 1572872 | tf_op jit(solution)/shard_map/ppermute | solution.py:542
  91.5 7.4 %copy-start.8 = (f32[80,512]{1,0:T(8,128)S(1)}, f32[80,512]{1,0:T(8,128)}, u32[]{:S(2)}) copy-start(f32[80,512]{1,0:T(8,128)} %correlate_part.1) | copy-start | bytes 491524
  91.5 7.4 %copy-start.13 = (bf16[2,256,512]{2,1,0:T(8,128)(2,1)S(1)}, bf16[2,256,512]{2,1,0:T(8,128)(2,1)}, u32[]{:S(2)}) copy-start(bf16[2,256,512]{2,1,0:T(8,128)(2,1)} %get-tuple-element.55) | copy-start | bytes 1572868
  91.5 7.3 %collective-permute-start.27 = (f32[80,512]{1,0:T(8,128)}, f32[80,512]{1,0:T(8,128)S(1)}, u32[]{:S(2)}, u32[]{:S(2)}) collective-permute-start(f32[80,512]{1,0:T(8,128)} %correlate_part.1), channel_id=1, source_target_pairs={{0,4},{4,0},{8,12},{12,8},{16,20},{20,16},{24,28},{28,24},{1,5},{5... | collective-permute-start | bytes 491528 | tf_op jit(solution)/shard_map/ppermute | solution.py:542
  93.1 14.8 %collective-permute-start.20 = (bf16[2,256,512]{2,1,0:T(8,128)(2,1)}, bf16[2,256,512]{2,1,0:T(8,128)(2,1)S(1)}, u32[]{:S(2)}, u32[]{:S(2)}) collective-permute-start(bf16[2,256,512]{2,1,0:T(8,128)(2,1)} %get-tuple-element.58), channel_id=1, source_target_pairs={{0,4},{4,0},{8,12},{12,8},{16,20},{20,16},{24,28},{28,24},{1,5},{5... | collective-permute-start | bytes 1572872 | tf_op jit(solution)/shard_map/ppermute | solution.py:542
  93.6 17.2 %collective-permute-start.13 = (bf16[128,512]{1,0:T(8,128)(2,1)}, bf16[128,512]{1,0:T(8,128)(2,1)}, u32[]{:S(2)}, u32[]{:S(2)}) collective-permute-start(bf16[128,512]{1,0:T(8,128)(2,1)} %get-tuple-element.44), channel_id=1, source_target_pairs={{0,1},{1,0},{2,3},{3,2},{4,5},{5,4},{6,7},{7,6},{8,9},{9,8},{10,11... | collective-permute-start | bytes 393224 | tf_op jit(solution)/shard_map/ppermute | solution.py:542
  93.6 14.3 %copy-start.11 = (bf16[2,256,512]{2,1,0:T(8,128)(2,1)S(1)}, bf16[2,256,512]{2,1,0:T(8,128)(2,1)}, u32[]{:S(2)}) copy-start(bf16[2,256,512]{2,1,0:T(8,128)(2,1)} %get-tuple-element.57) | copy-start | bytes 1572868
  98.2 12.4 %copy-start.12 = (bf16[128,2048]{1,0:T(8,128)(2,1)S(1)}, bf16[128,2048]{1,0:T(8,128)(2,1)}, u32[]{:S(2)}) copy-start(bf16[128,2048]{1,0:T(8,128)(2,1)} %get-tuple-element.53) | copy-start | bytes 1572868
  98.2 66.3 %collective-permute-start.16 = (bf16[128,2048]{1,0:T(8,128)(2,1)}, bf16[128,2048]{1,0:T(8,128)(2,1)}, u32[]{:S(2)}, u32[]{:S(2)}) collective-permute-start(bf16[128,2048]{1,0:T(8,128)(2,1)} %get-tuple-element.52), channel_id=1, source_target_pairs={{0,1},{1,0},{2,3},{3,2},{4,5},{5,4},{6,7},{7,6},{8,9},{9,8},{10,11... | collective-permute-start | bytes 1572872 | tf_op jit(solution)/shard_map/ppermute | solution.py:542
  98.9 11.8 %collective-permute-start.17 = (bf16[128,2048]{1,0:T(8,128)(2,1)}, bf16[128,2048]{1,0:T(8,128)(2,1)S(1)}, u32[]{:S(2)}, u32[]{:S(2)}) collective-permute-start(bf16[128,2048]{1,0:T(8,128)(2,1)} %get-tuple-element.54), channel_id=1, source_target_pairs={{0,1},{1,0},{2,3},{3,2},{4,5},{5,4},{6,7},{7,6},{8,9},{9,8},{10,11... | collective-permute-start | bytes 1572872 | tf_op jit(solution)/shard_map/ppermute | solution.py:542
  99.0 13.2 %collective-permute-start.23 = (bf16[256,512]{1,0:T(8,128)(2,1)S(1)}, bf16[256,512]{1,0:T(8,128)(2,1)S(1)}, u32[]{:S(2)}, u32[]{:S(2)}) collective-permute-start(bf16[256,512]{1,0:T(8,128)(2,1)S(1)} %fusion.7), channel_id=1, source_target_pairs={{0,8},{4,12},{8,0},{12,4},{16,24},{20,28},{24,16},{28,20},{1,9},{5... | collective-permute-start | bytes 786440 | tf_op jit(solution)/shard_map/ppermute | solution.py:542
  108.0 29.7 %copy-start.25 = (bf16[128,512]{1,0:T(8,128)(2,1)S(1)}, bf16[128,512]{1,0:T(8,128)(2,1)}, u32[]{:S(2)}) copy-start(bf16[128,512]{1,0:T(8,128)(2,1)} %get-tuple-element.45) | copy-start | bytes 393220
  108.0 30.0 %copy-start.24 = (bf16[128,512]{1,0:T(8,128)(2,1)S(1)}, bf16[128,512]{1,0:T(8,128)(2,1)}, u32[]{:S(2)}) copy-start(bf16[128,512]{1,0:T(8,128)(2,1)} %get-tuple-element.46) | copy-start | bytes 393220
  108.1 11.1 %collective-permute-start.21 = (bf16[256,512]{1,0:T(8,128)(2,1)S(1)}, bf16[256,512]{1,0:T(8,128)(2,1)S(1)}, u32[]{:S(2)}, u32[]{:S(2)}) collective-permute-start(bf16[256,512]{1,0:T(8,128)(2,1)S(1)} %get-tuple-element.69), channel_id=1, source_target_pairs={{0,24},{4,28},{8,16},{12,20},{16,8},{20,12},{24,0},{28,4},{1,25},{... | collective-permute-start | bytes 786440 | tf_op jit(solution)/shard_map/ppermute | solution.py:542
  110.6 25.0 %collective-permute-start.22 = (bf16[256,512]{1,0:T(8,128)(2,1)S(1)}, bf16[256,512]{1,0:T(8,128)(2,1)S(1)}, u32[]{:S(2)}, u32[]{:S(2)}) collective-permute-start(bf16[256,512]{1,0:T(8,128)(2,1)S(1)} %get-tuple-element.70), channel_id=1, source_target_pairs={{0,16},{4,20},{8,24},{12,28},{16,0},{20,4},{24,8},{28,12},{1,17},{... | collective-permute-start | bytes 786440 | tf_op jit(solution)/shard_map/ppermute | solution.py:542
  110.7 53.9 %copy-start.14 = (bf16[128,2048]{1,0:T(8,128)(2,1)S(1)}, bf16[128,2048]{1,0:T(8,128)(2,1)}, u32[]{:S(2)}) copy-start(bf16[128,2048]{1,0:T(8,128)(2,1)} %get-tuple-element.51) | copy-start | bytes 1572868
  110.8 26.9 %collective-permute-start.30 = (bf16[80,512]{1,0:T(8,128)(2,1)S(1)}, bf16[80,512]{1,0:T(8,128)(2,1)S(1)}, u32[]{:S(2)}, u32[]{:S(2)}) collective-permute-start(bf16[80,512]{1,0:T(8,128)(2,1)S(1)} %add_convert_fusion.8), channel_id=1, source_target_pairs={{0,24},{4,28},{8,16},{12,20},{16,8},{20,12},{24,0},{28,4},{1,25},{... | collective-permute-start | bytes 245768 | tf_op jit(solution)/shard_map/ppermute | solution.py:542
  112.2 25.7 %collective-permute-start.29 = (bf16[80,512]{1,0:T(8,128)(2,1)S(1)}, bf16[80,512]{1,0:T(8,128)(2,1)S(1)}, u32[]{:S(2)}, u32[]{:S(2)}) collective-permute-start(bf16[80,512]{1,0:T(8,128)(2,1)S(1)} %add_convert_fusion.8), channel_id=1, source_target_pairs={{0,16},{4,20},{8,24},{12,28},{16,0},{20,4},{24,8},{28,12},{1,17},{... | collective-permute-start | bytes 245768 | tf_op jit(solution)/shard_map/ppermute | solution.py:542
  119.2 18.8 %collective-permute-start.28 = (bf16[80,512]{1,0:T(8,128)(2,1)S(1)}, bf16[80,512]{1,0:T(8,128)(2,1)S(1)}, u32[]{:S(2)}, u32[]{:S(2)}) collective-permute-start(bf16[80,512]{1,0:T(8,128)(2,1)S(1)} %add_convert_fusion.8), channel_id=1, source_target_pairs={{0,8},{4,12},{8,0},{12,4},{16,24},{20,28},{24,16},{28,20},{1,9},{5... | collective-permute-start | bytes 245768 | tf_op jit(solution)/shard_map/ppermute | solution.py:542
  135.7 28.8 %collective-permute-start.18 = (bf16[128,2048]{1,0:T(8,128)(2,1)S(1)}, bf16[128,2048]{1,0:T(8,128)(2,1)}, u32[]{:S(2)}, u32[]{:S(2)}) collective-permute-start(bf16[128,2048]{1,0:T(8,128)(2,1)S(1)} %add_convert_fusion.1), channel_id=1, source_target_pairs={{0,2},{1,3},{2,0},{3,1},{4,6},{5,7},{6,4},{7,5},{8,10},{9,11},{10,... | collective-permute-start | bytes 1572872 | tf_op jit(solution)/shard_map/ppermute | solution.py:542
  137.7 29.1 %copy-start.7 = (bf16[256,512]{1,0:T(8,128)(2,1)}, bf16[256,512]{1,0:T(8,128)(2,1)S(1)}, u32[]{:S(2)}) copy-start(bf16[256,512]{1,0:T(8,128)(2,1)S(1)} %fusion.3.refs_0_) | copy-start | bytes 786436
  137.7 15.6 %collective-permute-start.14 = (bf16[128,512]{1,0:T(8,128)(2,1)S(1)}, bf16[128,512]{1,0:T(8,128)(2,1)S(1)}, u32[]{:S(2)}, u32[]{:S(2)}) collective-permute-start(bf16[128,512]{1,0:T(8,128)(2,1)S(1)} %copy-done.25), channel_id=1, source_target_pairs={{0,2},{1,3},{2,0},{3,1},{4,6},{5,7},{6,4},{7,5},{8,10},{9,11},{10,... | collective-permute-start | bytes 393224 | tf_op jit(solution)/shard_map/ppermute | solution.py:542
  138.0 17.1 %collective-permute-start.15 = (bf16[128,512]{1,0:T(8,128)(2,1)S(1)}, bf16[128,512]{1,0:T(8,128)(2,1)S(1)}, u32[]{:S(2)}, u32[]{:S(2)}) collective-permute-start(bf16[128,512]{1,0:T(8,128)(2,1)S(1)} %copy-done.24), channel_id=1, source_target_pairs={{0,3},{1,2},{2,1},{3,0},{4,7},{5,6},{6,5},{7,4},{8,11},{9,10},{10,... | collective-permute-start | bytes 393224 | tf_op jit(solution)/shard_map/ppermute | solution.py:542
  138.0 26.4 %collective-permute-start.25 = (bf16[256,512]{1,0:T(8,128)(2,1)S(1)}, bf16[256,512]{1,0:T(8,128)(2,1)S(1)}, u32[]{:S(2)}, u32[]{:S(2)}) collective-permute-start(bf16[256,512]{1,0:T(8,128)(2,1)S(1)} %fusion.3.refs_0_), channel_id=1, source_target_pairs={{0,2},{1,3},{2,0},{3,1},{4,6},{5,7},{6,4},{7,5},{8,10},{9,11},{10,... | collective-permute-start | bytes 786440 | tf_op jit(solution)/shard_map/ppermute | solution.py:542
  139.9 20.9 %copy-start.15 = (bf16[80,512]{1,0:T(8,128)(2,1)}, bf16[80,512]{1,0:T(8,128)(2,1)S(1)}, u32[]{:S(2)}) copy-start(bf16[80,512]{1,0:T(8,128)(2,1)S(1)} %add_convert_fusion.7.refs_0_) | copy-start | bytes 245764
  153.3 5.6 %copy-start.19 = (bf16[128,512]{1,0:T(8,128)(2,1)}, bf16[128,512]{1,0:T(8,128)(2,1)S(1)}, u32[]{:S(2)}) copy-start(bf16[128,512]{1,0:T(8,128)(2,1)S(1)} %collective-permute-done.14.refs_2_) | copy-start | bytes 393220
  153.3 5.5 %collective-permute-start.32 = (bf16[80,512]{1,0:T(8,128)(2,1)S(1)}, bf16[80,512]{1,0:T(8,128)(2,1)S(1)}, u32[]{:S(2)}, u32[]{:S(2)}) collective-permute-start(bf16[80,512]{1,0:T(8,128)(2,1)S(1)} %add_convert_fusion.7.refs_0_), channel_id=1, source_target_pairs={{0,2},{1,3},{2,0},{3,1},{4,6},{5,7},{6,4},{7,5},{8,10},{9,11},{10,... | collective-permute-start | bytes 245768 | tf_op jit(solution)/shard_map/ppermute | solution.py:542
  155.1 3.7 %copy-start.20 = (bf16[128,512]{1,0:T(8,128)(2,1)}, bf16[128,512]{1,0:T(8,128)(2,1)S(1)}, u32[]{:S(2)}) copy-start(bf16[128,512]{1,0:T(8,128)(2,1)S(1)} %collective-permute-done.15.refs_3_) | copy-start | bytes 393220
  155.1 5.7 %collective-permute-start.31 = (bf16[80,512]{1,0:T(8,128)(2,1)S(1)}, bf16[80,512]{1,0:T(8,128)(2,1)S(1)}, u32[]{:S(2)}, u32[]{:S(2)}) collective-permute-start(bf16[80,512]{1,0:T(8,128)(2,1)S(1)} %add_convert_fusion.7.refs_0_), channel_id=1, source_target_pairs={{0,1},{1,0},{2,3},{3,2},{4,5},{5,4},{6,7},{7,6},{8,9},{9,8},{10,11... | collective-permute-start | bytes 245768 | tf_op jit(solution)/shard_map/ppermute | solution.py:542
  158.8 2.0 %copy-start.21 = (bf16[80,512]{1,0:T(8,128)(2,1)}, bf16[80,512]{1,0:T(8,128)(2,1)S(1)}, u32[]{:S(2)}) copy-start(bf16[80,512]{1,0:T(8,128)(2,1)S(1)} %collective-permute-done.32.refs_2_) | copy-start | bytes 245764
  158.8 2.0 %collective-permute-start.33 = (bf16[80,512]{1,0:T(8,128)(2,1)S(1)}, bf16[80,512]{1,0:T(8,128)(2,1)S(1)}, u32[]{:S(2)}, u32[]{:S(2)}) collective-permute-start(bf16[80,512]{1,0:T(8,128)(2,1)S(1)} %collective-permute-done.32.refs_2_), channel_id=1, source_target_pairs={{0,1},{1,0},{2,3},{3,2},{4,5},{5,4},{6,7},{7,6},{8,9},{9,8},{10,11... | collective-permute-start | bytes 245768 | tf_op jit(solution)/shard_map/ppermute | solution.py:542
  160.8 0.6 copy-start.22
  161.4 0.6 copy-start.23
  163.9 2.8 %collective-permute-start.24 = (bf16[256,512]{1,0:T(8,128)(2,1)S(1)}, bf16[256,512]{1,0:T(8,128)(2,1)S(1)}, u32[]{:S(2)}, u32[]{:S(2)}) collective-permute-start(bf16[256,512]{1,0:T(8,128)(2,1)S(1)} %fusion.3.refs_0_), channel_id=1, source_target_pairs={{0,1},{1,0},{2,3},{3,2},{4,5},{5,4},{6,7},{7,6},{8,9},{9,8},{10,11... | collective-permute-start | bytes 786440 | tf_op jit(solution)/shard_map/ppermute | solution.py:542
  164.4 2.4 %copy-start.16 = (bf16[256,512]{1,0:T(8,128)(2,1)}, bf16[256,512]{1,0:T(8,128)(2,1)S(1)}, u32[]{:S(2)}) copy-start(bf16[256,512]{1,0:T(8,128)(2,1)S(1)} %collective-permute-done.25.refs_2_) | copy-start | bytes 786436
  164.4 2.4 %collective-permute-start.26 = (bf16[256,512]{1,0:T(8,128)(2,1)S(1)}, bf16[256,512]{1,0:T(8,128)(2,1)S(1)}, u32[]{:S(2)}, u32[]{:S(2)}) collective-permute-start(bf16[256,512]{1,0:T(8,128)(2,1)S(1)} %collective-permute-done.25.refs_2_), channel_id=1, source_target_pairs={{0,1},{1,0},{2,3},{3,2},{4,5},{5,4},{6,7},{7,6},{8,9},{9,8},{10,11... | collective-permute-start | bytes 786440 | tf_op jit(solution)/shard_map/ppermute | solution.py:542
  166.8 0.7 copy-start.17
  167.5 0.7 copy-start.18
where the time goes:
time: 171 us
  waiting for transfers between devices  67.1 us (39%)
  Pallas kernels  49.9 us (29%)
  starting transfers between devices  42.9 us (25%)
  local copies, waits for them, and re-layouts  5.28 us (3%)
  other arithmetic  4.71 us (3%)
    ppermute x34, waiting for transfers between devices, swap(): return lax.ppermute(value, axis, [(i, i ^ offset) for i in range(count)])  67.1 us
    ppermute x34, starting transfers between devices, swap(): return lax.ppermute(value, axis, [(i, i ^ offset) for i in range(count)])  42.9 us
    pallas_call x1, Pallas kernels, generate(): pl.pallas_call(body, grid_spec=pltpu.PrefetchScalarGridSpec(num_scalar_pr...  8.9 us
    pallas_call x1, Pallas kernels, convolve(): pl.pallas_call(body, grid_spec=pltpu.PrefetchScalarGridSpec(num_scalar_pr...  7.19 us
    pallas_call x1, Pallas kernels, correlate_back(): pl.pallas_call(body, grid_spec=pltpu.PrefetchScalarGridSpec(num_scalar_pr...  6.89 us
    pallas_call x1, Pallas kernels, correlate_part(): pl.pallas_call(body, grid_spec=pltpu.PrefetchScalarGridSpec(num_scalar_pr...  6.27 us
    pallas_call x1, Pallas kernels, gating(): pl.pallas_call(body, in_specs=[smem()] + [pl.BlockSpec(memory_space=VMEM)...  5.4 us
    pallas_call x2, Pallas kernels, assemble(): pl.pallas_call(body, in_specs=[smem()] + [pl.BlockSpec(memory_space=VMEM)...  4.62 us
  transfers between devices with their start and end apart: 34, of which 9 were waited for; matrix products, arithmetic and copies ran while one was open for 4% of the time, Pallas kernels for 28%

commit v1 on v0

--- a/solution.py
+++ b/solution.py
@@ -163,6 +163,9 @@
         + [struct((2, length, width), f32), struct((length, width), f32)]
         + [struct((length, order), f32)] * 2,
         name="generate",
+        compiler_params=grant(
+            [((6, block, length), 2), ((4, block, width), 4), ((2, length, width), 4)], length, width
+        ),
     )(place, table, *factors, pos_weight, pos_bias, filter_weight, rates, norm)
 
 
@@ -234,7 +237,16 @@
             struct((length, width), bf16),
         ],
         name="convolve",
+        compiler_params=grant(
+            [((6, block, length), 2), ((4, block, width), 4), ((3, length, width), 4)], length, width
+        ),
     )(place, *signal_rel, *cot_rel, filt_spec, a_high, a_low, t_high, skip)
+
+
+def grant(blocks, length, width):
+    held = sum(math.prod(shape) * size for shape, size in blocks)
+    need = 2 * held + 8 * length * width * 4 + (4 << 20)
+    return pltpu.CompilerParams(vmem_limit_bytes=min(need, 60 << 20))
 
 
 def smem():
@@ -246,6 +258,7 @@
     local_len, channels = signal_rel[0].shape
     width = gate_grad.shape[1]
     rows = channels // sum(len(group) for group in groups)
+    length = local_len * count
 
     def body(place_ref, *refs):
         sig = refs[:count]
@@ -268,6 +281,7 @@
         out_specs=[pl.BlockSpec(memory_space=VMEM)] * len(groups),
         out_shape=[struct((len(group), rows, width), bf16) for group in groups],
         name="weight_grads",
+        compiler_params=grant([((length, channels), 2), ((2, channels, width), 2)], length, width),
     )(place, *signal_rel, gate_grad)
 
 
@@ -316,6 +330,7 @@
         ],
         scratch_shapes=[VMEM((channels, width), bf16)],
         name="gating",
+        compiler_params=grant([((length, channels), 2), ((2, channels, width), 2)], length, width),
     )(place, *signal_rel, *weight_rel, *cot_rel, inner)
 
 
@@ -370,6 +385,9 @@
         ),
         out_shape=[struct((length, width), f32), struct((2, length, width), f32)],
         name="correlate_back",
+        compiler_params=grant(
+            [((6, block, length), 2), ((4, block, width), 4), ((3, length, width), 4)], length, width
+        ),
     )(place, conv_grad, inner_grad, filt_spec, a_high, a_low, t_high, skip)
 
 
@@ -435,6 +453,9 @@
         ),
         out_shape=struct((total_rows, width), f32),
         name="correlate_part",
+        compiler_params=grant(
+            [((2, block, length), 2), ((4, block, width), 4), ((2, length, width), 4)], length, width
+        ),
     )(
         place, grad_spec, skip_sum, signal_spec, t_high, env, hidden, filter_weight, cos_pre,
         table_t,
@@ -474,6 +495,7 @@
         out_specs=[pl.BlockSpec(memory_space=VMEM)] * count,
         out_shape=[struct((local_len, channels), bf16)] * count,
         name="through_gate",
+        compiler_params=grant([((length, channels), 2), ((channels, width), 2)], length, width),
     )(place, gate_grad, *weight_rel, direct)
 
 
@@ -493,12 +515,13 @@
         out_specs=pl.BlockSpec(memory_space=VMEM),
         out_shape=struct((rows, width * count), kind),
         name="assemble",
+        compiler_params=grant([((rows, 2 * width * count), 4)], rows, width),
     )(place, *pieces)
 
 
 def finish(place, pieces, order, emb_count):
     count = len(pieces)
-    _, width = pieces[0].shape
+    rows, width = pieces[0].shape
     table_rows = -(-(emb_count + 1) // 8) * 8
     _, per_group = packed_rows(order, table_rows, width)
 
@@ -534,6 +557,7 @@
             struct((1, order), f32),
         ],
         name="finish",
+        compiler_params=grant([((rows, 2 * width * count), 4)], rows, width),
     )(place, *pieces)
 
 

time: 171 us -> 160 us (0.936)
  Pallas kernels: 49.9 us -> 29.9 us
  local copies, waits for them, and re-layouts: 5.28 us -> 13.4 us
  waiting for transfers between devices: 67.1 us -> 69.9 us
  other arithmetic: 4.71 us -> 2.4 us
    unnamed x52 -> x44, local copies, waits for them, and re-layouts: 3.48 us -> 12.3 us
    pallas_call x1, Pallas kernels: 6.89 us -> 3.8 us  [correlate_back(): pl.pallas_call(body, grid_spec=pltpu.PrefetchScalarGridSpec(num_scalar_pr...]
    pallas_call x1, Pallas kernels: 7.19 us -> 4.15 us  [convolve(): pl.pallas_call(body, grid_spec=pltpu.PrefetchScalarGridSpec(num_scalar_pr...]
    pallas_call x1, Pallas kernels: 8.9 us -> 5.87 us  [generate(): pl.pallas_call(body, grid_spec=pltpu.PrefetchScalarGridSpec(num_scalar_pr...]
    ppermute x34, waiting for transfers between devices: 67.1 us -> 69.9 us  [swap(): return lax.ppermute(value, axis, [(i, i ^ offset) for i in range(count)])]
    pallas_call x1, Pallas kernels: 6.27 us -> 3.66 us  [correlate_part(): pl.pallas_call(body, grid_spec=pltpu.PrefetchScalarGridSpec(num_scalar_pr...]
    pallas_call x1, Pallas kernels: 5.4 us -> 2.97 us  [gating(): pl.pallas_call(body, in_specs=[smem()] + [pl.BlockSpec(memory_space=VMEM)...]
    pallas_call x1, Pallas kernels: 4.13 us -> 1.85 us  [weight_grads(): pl.pallas_call(body, in_specs=[smem()] + [pl.BlockSpec(memory_space=VMEM)...]
  transfers between devices with their start and end apart: 34 -> 34, of which waited for: 9 -> 10; matrix products, arithmetic and copies ran while one was open for 4% -> 2% of each run, Pallas kernels for 28% -> 18%
where the time goes in v1:
time: 160 us; the launch traced here: 159 us
  waiting for transfers between devices  69.9 us (44%)
  starting transfers between devices  42.8 us (27%)
  Pallas kernels  29.9 us (19%)
  local copies, waits for them, and re-layouts  13.4 us (8%)
  other arithmetic  2.4 us (2%)
    ppermute x34, waiting for transfers between devices, swap(): return lax.ppermute(value, axis, [(i, i ^ offset) for i in range(count)])  69.9 us
    ppermute x34, starting transfers between devices, swap(): return lax.ppermute(value, axis, [(i, i ^ offset) for i in range(count)])  42.8 us
    unnamed x44, local copies, waits for them, and re-layouts  12.3 us
    pallas_call x1, Pallas kernels, generate(): pl.pallas_call(body, grid_spec=pltpu.PrefetchScalarGridSpec(num_scalar_pr...  5.87 us
    pallas_call x1, Pallas kernels, convolve(): pl.pallas_call(body, grid_spec=pltpu.PrefetchScalarGridSpec(num_scalar_pr...  4.15 us
    pallas_call x1, Pallas kernels, correlate_back(): pl.pallas_call(body, grid_spec=pltpu.PrefetchScalarGridSpec(num_scalar_pr...  3.8 us
    pallas_call x1, Pallas kernels, correlate_part(): pl.pallas_call(body, grid_spec=pltpu.PrefetchScalarGridSpec(num_scalar_pr...  3.66 us
    pallas_call x2, Pallas kernels, assemble(): pl.pallas_call(body, in_specs=[smem()] + [pl.BlockSpec(memory_space=VMEM)...  3.37 us
  transfers between devices with their start and end apart: 34, of which 10 were waited for; matrix products, arithmetic and copies ran while one was open for 2% of the time, Pallas kernels for 18%

profile of v1, /device:TPU:0, one launch (start us, length us, event | category | flops | bytes accessed | tf_op | source)
XLA Modules:
  0.0 159.3 jit_solution(3492003920624643507)
XLA Ops:
  0.7 3.0 %collective-permute-start.1 = (bf16[128,2048]{1,0:T(8,128)(2,1)}, bf16[128,2048]{1,0:T(8,128)(2,1)S(1)}, u32[]{:S(2)}, u32[]{:S(2)}) collective-permute-start(bf16[128,2048]{1,0:T(8,128)(2,1)} %bitcast.31), channel_id=1, source_target_pairs={{0,2},{1,3},{2,0},{3,1},{4,6},{5,7},{6,4},{7,5},{8,10},{9,11},{10,... | collective-permute-start | bytes 1572872 | tf_op jit(solution)/shard_map/ppermute | solution.py:566
  3.7 1.1 dynamic-slice_bitcast_fusion
  4.8 0.3 collective-permute-start.12
  5.1 0.4 collective-permute-start.10
  5.5 1.6 collective-permute-start.11
  7.1 12.0 %collective-permute-done.12.refs_7_.refs_15_ = bf16[128,512]{1,0:T(8,128)(2,1)S(1)} collective-permute-done((bf16[128,512]{1,0:T(8,128)(2,1)S(1)}, bf16[128,512]{1,0:T(8,128)(2,1)S(1)}, u32[]{:S(2)}, u32[]{:S(2)}) %collective-permute-start.12) | collective-permute-done | bytes 131104 | tf_op jit(solution)/shard_map/ppermute | solution.py:566
  19.0 0.7 copy-done.4
  19.7 3.6 %collective-permute-start.8 = (bf16[256,512]{1,0:T(8,128)(2,1)S(1)}, bf16[256,512]{1,0:T(8,128)(2,1)}, u32[]{:S(2)}, u32[]{:S(2)}) collective-permute-start(bf16[256,512]{1,0:T(8,128)(2,1)S(1)} %constant_dynamic-slice_fusion.refs_4_.refs_1_), channel_id=1, source_target_pairs={{0,24},{4,28},{8,16},{12,20},{16,8},{20,12},{24,0},{28,4},{1,25},{... | collective-permute-start | bytes 786440 | tf_op jit(solution)/shard_map/ppermute | solution.py:566
  23.3 0.7 copy-done.6
  24.0 0.7 copy-done.9
  24.6 0.8 collective-permute-start.4
  25.4 5.5 %collective-permute-done.8.refs_10_.refs_7_ = bf16[256,512]{1,0:T(8,128)(2,1)} collective-permute-done((bf16[256,512]{1,0:T(8,128)(2,1)S(1)}, bf16[256,512]{1,0:T(8,128)(2,1)}, u32[]{:S(2)}, u32[]{:S(2)}) %collective-permute-start.8) | collective-permute-done | bytes 262176 | tf_op jit(solution)/shard_map/ppermute | solution.py:566
  30.9 1.5 collective-permute-start.3
  32.4 14.2 %collective-permute-done.6.refs_8_.refs_5_ = bf16[256,512]{1,0:T(8,128)(2,1)} collective-permute-done((bf16[256,512]{1,0:T(8,128)(2,1)S(1)}, bf16[256,512]{1,0:T(8,128)(2,1)}, u32[]{:S(2)}, u32[]{:S(2)}) %collective-permute-start.6) | collective-permute-done | bytes 262176 | tf_op jit(solution)/shard_map/ppermute | solution.py:566
  46.7 1.5 collective-permute-start.9
  48.2 0.5 collective-permute-start.7
  48.7 1.5 collective-permute-start.5
  50.2 0.7 divide_sqrt_fusion
  51.0 1.0 copy-done.2
  52.1 0.9 copy-done.12
  53.0 0.9 copy-done.13
  53.9 0.9 copy-done.14
  54.8 0.8 copy-done.16
  55.7 0.8 copy-done.17
  56.5 0.7 copy-done.19
  57.2 0.7 copy-done.20
  57.9 0.7 copy-done.21
  58.6 5.9 %generate.1 = (bf16[2,512,512]{2,1,0:T(8,128)(2,1)S(1)}, bf16[2,512,512]{2,1,0:T(8,128)(2,1)S(1)}, bf16[2,512,512]{2,1,0:T(8,128)(2,1)S(1)}, f32[2,512,512]{2,1,...) custom-call(s32[2]{0:T(128)S(1)} %pad_add_fusion.place_ref, ...), custom_call_target="tpu_custom_call" | custom-call | tf_op jit(solution)/shard_map/generate/pallas_call | solution.py:150
  64.5 0.9 copy-done.5
  65.4 0.9 copy-done.7
  66.3 0.9 copy-done.10
  67.2 4.1 %convolve.1 = (f32[2,512,512]{2,1,0:T(8,128)S(1)}, f32[512,512]{1,0:T(8,128)S(1)}, bf16[512,512]{1,0:T(8,128)(2,1)S(1)}) custom-call(s32[2]{0:T(128)S(1)} %pad_add_fusion.place_ref, bf16[128,2048]{1,0:T(8,128)(2,1)S(1)} %bitcast.33, bf16[128,2048]{1,0:T(8,128)(2,1)S(1)} %collective-permute-done.refs_1_, ...), custom_call_target="tpu_custom_call" | custom-call | tf_op jit(solution)/shard_map/convolve/pallas_call | solution.py:218
  71.4 1.8 %weight_grads.1 = (bf16[2,256,512]{2,1,0:T(8,128)(2,1)S(1)}, bf16[2,256,512]{2,1,0:T(8,128)(2,1)S(1)}, bf16[2,256,512]{2,1,0:T(8,128)(2,1)S(1)}, bf16[2,256,512]{2,1,0:T(8,128)(2,1)S(1)}) custom-call(s32[2]{0:T(128)S(1)} %pad_add_fusion.place_ref, bf16[128,2048]{1,0:T(8,128)(2,1)S(1)} %bitcast.34, bf16[128,2048]{1,0:T(8,128)(2,1)S(1)} %collective-permute-done.refs_1_, ...), custom_call_target="tpu_custom_call" | custom-call | tf_op jit(solution)/shard_map/weight_grads/pallas_call | solution.py:278
  73.3 0.6 collective-permute-start.19
  73.9 3.0 %gating.1 = (bf16[128,512]{1,0:T(8,128)(2,1)S(1)}, bf16[128,512]{1,0:T(8,128)(2,1)S(1)}, bf16[128,512]{1,0:T(8,128)(2,1)S(1)}, bf16[128,512]{1,0:T(8,128)(2,1)S(...) custom-call(s32[2]{0:T(128)S(1)} %pad_add_fusion.place_ref, ...), custom_call_target="tpu_custom_call" | custom-call | tf_op jit(solution)/shard_map/gating/pallas_call | solution.py:321
  76.9 3.8 %correlate_back.1 = (f32[512,512]{1,0:T(8,128)S(1)}, f32[2,512,512]{2,1,0:T(8,128)S(1)}) custom-call(s32[2]{0:T(128)S(1)} %pad_add_fusion.place_ref, bf16[512,512]{1,0:T(8,128)(2,1)S(1)} %get-tuple-element.48.cg, f32[512,512]{1,0:T(8,128)S(1)} %get-tuple-element.49.ig, f32[2,512,512]{2,1,0:T(8,128)S(1)} %get-tuple-element.38.refs_8_.fs, ...), custom_call_target="tpu_custom_call" | custom-call | tf_op jit(solution)/shard_map/correlate_back/pallas_call | solution.py:369
  80.7 3.7 %correlate_part.1 = f32[80,512]{1,0:T(8,128)S(1)} custom-call(s32[2]{0:T(128)S(1)} %pad_add_fusion.place_ref, f32[2,512,512]{2,1,0:T(8,128)S(1)} %get-tuple-element.59.gs, f32[8,512]{1,0:T(8,128)S(1)} %get-tuple-element.60.skip_sum_ref, f32[2,512,512]{2,1,0:T(8,128)S(1)} %get-tuple-element.61.ss, bf16[2,512,512]{2,1,0:T(8,128)(2,1)S(1)} %get-tuple-element.41.refs_11_.th, ...), custom_call_target="tpu_custom_call" | custom-call | tf_op jit(solution)/shard_map/correlate_part/pallas_call | solution.py:435
  84.4 1.6 collective-permute-start.27
  86.0 0.5 collective-permute-start.20
  86.5 2.8 %through_gate.1 = (bf16[128,2048]{1,0:T(8,128)(2,1)S(1)}, bf16[128,2048]{1,0:T(8,128)(2,1)S(1)}, bf16[128,2048]{1,0:T(8,128)(2,1)S(1)}, bf16[128,2048]{1,0:T(8,128)(2,1)S(1)}) custom-call(s32[2]{0:T(128)S(1)} %pad_add_fusion.place_ref, bf16[512,512]{1,0:T(8,128)(2,1)S(1)} %get-tuple-element.47.refs_0_.refs_4_, ...), custom_call_target="tpu_custom_call" | custom-call | tf_op jit(solution)/shard_map/through_gate/pallas_call | solution.py:492
  89.3 0.6 collective-permute-start.16
  89.9 1.6 %collective-permute-done.27 = f32[80,512]{1,0:T(8,128)S(1)} collective-permute-done((f32[80,512]{1,0:T(8,128)S(1)}, f32[80,512]{1,0:T(8,128)S(1)}, u32[]{:S(2)}, u32[]{:S(2)}) %collective-permute-start.27) | collective-permute-done | bytes 163872 | tf_op jit(solution)/shard_map/ppermute | solution.py:566
  91.7 9.3 %collective-permute-done.20 = bf16[2,256,512]{2,1,0:T(8,128)(2,1)S(1)} collective-permute-done((bf16[2,256,512]{2,1,0:T(8,128)(2,1)S(1)}, bf16[2,256,512]{2,1,0:T(8,128)(2,1)S(1)}, u32[]{:S(2)}, u32[]{:S(2)}) %collective-permute-start.20) | collective-permute-done | bytes 524320 | tf_op jit(solution)/shard_map/ppermute | solution.py:566
  101.0 0.1 fusion.5
  101.2 2.5 %collective-permute-start.21 = (bf16[256,512]{1,0:T(8,128)(2,1)S(1)}, bf16[256,512]{1,0:T(8,128)(2,1)S(1)}, u32[]{:S(2)}, u32[]{:S(2)}) collective-permute-start(bf16[256,512]{1,0:T(8,128)(2,1)S(1)} %get-tuple-element.69), channel_id=1, source_target_pairs={{0,24},{4,28},{8,16},{12,20},{16,8},{20,12},{24,0},{28,4},{1,25},{... | collective-permute-start | bytes 786440 | tf_op jit(solution)/shard_map/ppermute | solution.py:566
  103.9 1.4 collective-permute-start.30
  105.3 2.0 %collective-permute-start.29 = (bf16[80,512]{1,0:T(8,128)(2,1)S(1)}, bf16[80,512]{1,0:T(8,128)(2,1)S(1)}, u32[]{:S(2)}, u32[]{:S(2)}) collective-permute-start(bf16[80,512]{1,0:T(8,128)(2,1)S(1)} %add_convert_fusion.8), channel_id=1, source_target_pairs={{0,16},{4,20},{8,24},{12,28},{16,0},{20,4},{24,8},{28,12},{1,17},{... | collective-permute-start | bytes 245768 | tf_op jit(solution)/shard_map/ppermute | solution.py:566
  107.3 5.0 %collective-permute-done.21 = bf16[256,512]{1,0:T(8,128)(2,1)S(1)} collective-permute-done((bf16[256,512]{1,0:T(8,128)(2,1)S(1)}, bf16[256,512]{1,0:T(8,128)(2,1)S(1)}, u32[]{:S(2)}, u32[]{:S(2)}) %collective-permute-start.21) | collective-permute-done | bytes 262176 | tf_op jit(solution)/shard_map/ppermute | solution.py:566
  112.3 12.4 %collective-permute-start.28 = (bf16[80,512]{1,0:T(8,128)(2,1)S(1)}, bf16[80,512]{1,0:T(8,128)(2,1)S(1)}, u32[]{:S(2)}, u32[]{:S(2)}) collective-permute-start(bf16[80,512]{1,0:T(8,128)(2,1)S(1)} %add_convert_fusion.8), channel_id=1, source_target_pairs={{0,8},{4,12},{8,0},{12,4},{16,24},{20,28},{24,16},{28,20},{1,9},{5... | collective-permute-start | bytes 245768 | tf_op jit(solution)/shard_map/ppermute | solution.py:566
  124.7 4.3 %collective-permute-done.22 = bf16[256,512]{1,0:T(8,128)(2,1)S(1)} collective-permute-done((bf16[256,512]{1,0:T(8,128)(2,1)S(1)}, bf16[256,512]{1,0:T(8,128)(2,1)S(1)}, u32[]{:S(2)}, u32[]{:S(2)}) %collective-permute-start.22) | collective-permute-done | bytes 262176 | tf_op jit(solution)/shard_map/ppermute | solution.py:566
  129.0 1.6 collective-permute-start.18
  130.6 0.2 fusion.3.refs_0_
  130.8 0.5 collective-permute-start.14
  131.3 1.7 %collective-permute-start.25 = (bf16[256,512]{1,0:T(8,128)(2,1)S(1)}, bf16[256,512]{1,0:T(8,128)(2,1)S(1)}, u32[]{:S(2)}, u32[]{:S(2)}) collective-permute-start(bf16[256,512]{1,0:T(8,128)(2,1)S(1)} %fusion.3.refs_0_), channel_id=1, source_target_pairs={{0,2},{1,3},{2,0},{3,1},{4,6},{5,7},{6,4},{7,5},{8,10},{9,11},{10,... | collective-permute-start | bytes 786440 | tf_op jit(solution)/shard_map/ppermute | solution.py:566
  133.0 13.6 %collective-permute-done.14.refs_2_ = bf16[128,512]{1,0:T(8,128)(2,1)S(1)} collective-permute-done((bf16[128,512]{1,0:T(8,128)(2,1)S(1)}, bf16[128,512]{1,0:T(8,128)(2,1)S(1)}, u32[]{:S(2)}, u32[]{:S(2)}) %collective-permute-start.14) | collective-permute-done | bytes 131104 | tf_op jit(solution)/shard_map/ppermute | solution.py:566
  146.6 1.6 collective-permute-start.32
  148.2 0.4 collective-permute-start.31
  148.6 3.9 %collective-permute-done.32.refs_2_ = bf16[80,512]{1,0:T(8,128)(2,1)S(1)} collective-permute-done((bf16[80,512]{1,0:T(8,128)(2,1)S(1)}, bf16[80,512]{1,0:T(8,128)(2,1)S(1)}, u32[]{:S(2)}, u32[]{:S(2)}) %collective-permute-start.32) | collective-permute-done | bytes 81952 | tf_op jit(solution)/shard_map/ppermute | solution.py:566
  152.5 1.4 assemble.2
  153.9 1.4 finish.1
  155.3 0.5 collective-permute-start.24
  155.9 1.0 fusion
  156.9 0.4 collective-permute-done.26.refs_3_
  157.3 2.0 %assemble.3 = f32[256,2048]{1,0:T(8,128)} custom-call(s32[2]{0:T(128)S(1)} %pad_add_fusion.place_ref, bf16[256,512]{1,0:T(8,128)(2,1)S(1)} %fusion.3.refs_0_, bf16[256,512]{1,0:T(8,128)(2,1)S(1)} %collective-permute-done.24.refs_1_, bf16[256,512]{1,0:T(8,128)(2,1)S(1)} %collective-permute-done.25.refs_2_, bf16[256,512]{1,0:T(8,128)(2,1)S(1)} %collective-permute-done.26.refs_3_), custom_call_target="tpu_custom_call" | custom-call | tf_op jit(solution)/shard_map/assemble/pallas_call | solution.py:512
  (69 shorter events, 0.7 us)
Async XLA Ops:
  0.6 6.4 %copy-start = (bf16[256,2048]{1,0:T(8,128)(2,1)S(1)}, bf16[256,2048]{1,0:T(8,128)(2,1)}, u32[]{:S(2)}) copy-start(bf16[256,2048]{1,0:T(8,128)(2,1)} %param.15) | copy-start | bytes 3145732
  0.6 63.8 %copy-start.1 = (bf16[1,128,2048]{2,1,0:T(8,128)(2,1)S(1)}, bf16[1,128,2048]{2,1,0:T(8,128)(2,1)}, u32[]{:S(2)}) copy-start(bf16[1,128,2048]{2,1,0:T(8,128)(2,1)} %param.14) | copy-start | bytes 1572868
  0.7 63.8 %copy-start.18 = (f32[2048]{0:T(1024)S(1)}, f32[2048]{0:T(1024)}, u32[]{:S(2)}) copy-start(f32[2048]{0:T(1024)} %param.20) | copy-start | bytes 24580
  0.7 24.7 %collective-permute-start.1 = (bf16[128,2048]{1,0:T(8,128)(2,1)}, bf16[128,2048]{1,0:T(8,128)(2,1)S(1)}, u32[]{:S(2)}, u32[]{:S(2)}) collective-permute-start(bf16[128,2048]{1,0:T(8,128)(2,1)} %bitcast.31), channel_id=1, source_target_pairs={{0,2},{1,3},{2,0},{3,1},{4,6},{5,7},{6,4},{7,5},{8,10},{9,11},{10,... | collective-permute-start | bytes 1572872 | tf_op jit(solution)/shard_map/ppermute | solution.py:566
  3.7 45.0 %collective-permute-start = (bf16[128,2048]{1,0:T(8,128)(2,1)}, bf16[128,2048]{1,0:T(8,128)(2,1)S(1)}, u32[]{:S(2)}, u32[]{:S(2)}) collective-permute-start(bf16[128,2048]{1,0:T(8,128)(2,1)} %bitcast.32), channel_id=1, source_target_pairs={{0,1},{1,0},{2,3},{3,2},{4,5},{5,4},{6,7},{7,6},{8,9},{9,8},{10,11... | collective-permute-start | bytes 1572872 | tf_op jit(solution)/shard_map/ppermute | solution.py:566
  4.8 14.2 %collective-permute-start.12 = (bf16[128,512]{1,0:T(8,128)(2,1)S(1)}, bf16[128,512]{1,0:T(8,128)(2,1)S(1)}, u32[]{:S(2)}, u32[]{:S(2)}) collective-permute-start(bf16[128,512]{1,0:T(8,128)(2,1)S(1)} %get-tuple-element.71), channel_id=1, source_target_pairs={{0,3},{1,2},{2,1},{3,0},{4,7},{5,6},{6,5},{7,4},{8,11},{9,10},{10,... | collective-permute-start | bytes 393224 | tf_op jit(solution)/shard_map/ppermute | solution.py:566
  5.1 18.2 %collective-permute-start.10 = (bf16[128,512]{1,0:T(8,128)(2,1)S(1)}, bf16[128,512]{1,0:T(8,128)(2,1)S(1)}, u32[]{:S(2)}, u32[]{:S(2)}) collective-permute-start(bf16[128,512]{1,0:T(8,128)(2,1)S(1)} %get-tuple-element.72), channel_id=1, source_target_pairs={{0,1},{1,0},{2,3},{3,2},{4,5},{5,4},{6,7},{7,6},{8,9},{9,8},{10,11... | collective-permute-start | bytes 393224 | tf_op jit(solution)/shard_map/ppermute | solution.py:566
  5.5 18.5 %collective-permute-start.11 = (bf16[128,512]{1,0:T(8,128)(2,1)S(1)}, bf16[128,512]{1,0:T(8,128)(2,1)S(1)}, u32[]{:S(2)}, u32[]{:S(2)}) collective-permute-start(bf16[128,512]{1,0:T(8,128)(2,1)S(1)} %get-tuple-element.74), channel_id=1, source_target_pairs={{0,2},{1,3},{2,0},{3,1},{4,6},{5,7},{6,4},{7,5},{8,10},{9,11},{10,... | collective-permute-start | bytes 393224 | tf_op jit(solution)/shard_map/ppermute | solution.py:566
  19.0 0.7 copy-start.4
  19.7 11.2 %collective-permute-start.8 = (bf16[256,512]{1,0:T(8,128)(2,1)S(1)}, bf16[256,512]{1,0:T(8,128)(2,1)}, u32[]{:S(2)}, u32[]{:S(2)}) collective-permute-start(bf16[256,512]{1,0:T(8,128)(2,1)S(1)} %constant_dynamic-slice_fusion.refs_4_.refs_1_), channel_id=1, source_target_pairs={{0,24},{4,28},{8,16},{12,20},{16,8},{20,12},{24,0},{28,4},{1,25},{... | collective-permute-start | bytes 786440 | tf_op jit(solution)/shard_map/ppermute | solution.py:566
  23.3 0.7 copy-start.6
  23.9 22.7 %collective-permute-start.6 = (bf16[256,512]{1,0:T(8,128)(2,1)S(1)}, bf16[256,512]{1,0:T(8,128)(2,1)}, u32[]{:S(2)}, u32[]{:S(2)}) collective-permute-start(bf16[256,512]{1,0:T(8,128)(2,1)S(1)} %constant_dynamic-slice_fusion.refs_4_.refs_1_), channel_id=1, source_target_pairs={{0,16},{4,20},{8,24},{12,28},{16,0},{20,4},{24,8},{28,12},{1,17},{... | collective-permute-start | bytes 786440 | tf_op jit(solution)/shard_map/ppermute | solution.py:566
  24.0 0.7 copy-start.9
  24.6 23.6 %collective-permute-start.4 = (bf16[256,512]{1,0:T(8,128)(2,1)S(1)}, bf16[256,512]{1,0:T(8,128)(2,1)}, u32[]{:S(2)}, u32[]{:S(2)}) collective-permute-start(bf16[256,512]{1,0:T(8,128)(2,1)S(1)} %constant_dynamic-slice_fusion.refs_4_.refs_1_), channel_id=1, source_target_pairs={{0,8},{4,12},{8,0},{12,4},{16,24},{20,28},{24,16},{28,20},{1,9},{5... | collective-permute-start | bytes 786440 | tf_op jit(solution)/shard_map/ppermute | solution.py:566
  25.4 39.1 %collective-permute-start.2 = (bf16[128,2048]{1,0:T(8,128)(2,1)S(1)}, bf16[128,2048]{1,0:T(8,128)(2,1)S(1)}, u32[]{:S(2)}, u32[]{:S(2)}) collective-permute-start(bf16[128,2048]{1,0:T(8,128)(2,1)S(1)} %collective-permute-done.1.refs_2_), channel_id=1, source_target_pairs={{0,1},{1,0},{2,3},{3,2},{4,5},{5,4},{6,7},{7,6},{8,9},{9,8},{10,11... | collective-permute-start | bytes 1572872 | tf_op jit(solution)/shard_map/ppermute | solution.py:566
  30.9 42.9 %collective-permute-start.3 = (bf16[256,512]{1,0:T(8,128)(2,1)S(1)}, bf16[256,512]{1,0:T(8,128)(2,1)}, u32[]{:S(2)}, u32[]{:S(2)}) collective-permute-start(bf16[256,512]{1,0:T(8,128)(2,1)S(1)} %constant_dynamic-slice_fusion.refs_4_.refs_1_), channel_id=1, source_target_pairs={{0,4},{4,0},{8,12},{12,8},{16,20},{20,16},{24,28},{28,24},{1,5},{5... | collective-permute-start | bytes 786440 | tf_op jit(solution)/shard_map/ppermute | solution.py:566
  46.7 27.2 %collective-permute-start.9 = (bf16[256,512]{1,0:T(8,128)(2,1)}, bf16[256,512]{1,0:T(8,128)(2,1)}, u32[]{:S(2)}, u32[]{:S(2)}) collective-permute-start(bf16[256,512]{1,0:T(8,128)(2,1)} %collective-permute-done.8.refs_10_.refs_7_), channel_id=1, source_target_pairs={{0,4},{4,0},{8,12},{12,8},{16,20},{20,16},{24,28},{28,24},{1,5},{5... | collective-permute-start | bytes 786440 | tf_op jit(solution)/shard_map/ppermute | solution.py:566
  48.2 25.6 %collective-permute-start.7 = (bf16[256,512]{1,0:T(8,128)(2,1)}, bf16[256,512]{1,0:T(8,128)(2,1)}, u32[]{:S(2)}, u32[]{:S(2)}) collective-permute-start(bf16[256,512]{1,0:T(8,128)(2,1)} %collective-permute-done.6.refs_8_.refs_5_), channel_id=1, source_target_pairs={{0,4},{4,0},{8,12},{12,8},{16,20},{20,16},{24,28},{28,24},{1,5},{5... | collective-permute-start | bytes 786440 | tf_op jit(solution)/shard_map/ppermute | solution.py:566
  48.7 25.1 %collective-permute-start.5 = (bf16[256,512]{1,0:T(8,128)(2,1)}, bf16[256,512]{1,0:T(8,128)(2,1)}, u32[]{:S(2)}, u32[]{:S(2)}) collective-permute-start(bf16[256,512]{1,0:T(8,128)(2,1)} %collective-permute-done.4.refs_6_.refs_3_), channel_id=1, source_target_pairs={{0,4},{4,0},{8,12},{12,8},{16,20},{20,16},{24,28},{28,24},{1,5},{5... | collective-permute-start | bytes 786440 | tf_op jit(solution)/shard_map/ppermute | solution.py:566
  51.0 1.0 copy-start.2
  52.1 0.9 copy-start.12
  53.0 0.9 copy-start.13
  53.9 0.9 copy-start.14
  54.8 0.8 copy-start.16
  55.7 0.8 copy-start.17
  56.5 0.7 copy-start.19
  57.2 0.7 copy-start.20
  57.9 0.7 copy-start.21
  64.5 0.9 copy-start.5
  65.4 0.9 copy-start.7
  66.3 0.9 copy-start.10
  71.4 2.5 %copy-start.8 = (bf16[128,512]{1,0:T(8,128)(2,1)S(1)}, bf16[128,512]{1,0:T(8,128)(2,1)}, u32[]{:S(2)}) copy-start(bf16[128,512]{1,0:T(8,128)(2,1)} %copy-done.6) | copy-start | bytes 393220
  71.4 2.5 %copy-start.11 = (bf16[128,512]{1,0:T(8,128)(2,1)S(1)}, bf16[128,512]{1,0:T(8,128)(2,1)}, u32[]{:S(2)}) copy-start(bf16[128,512]{1,0:T(8,128)(2,1)} %copy-done.9) | copy-start | bytes 393220
  73.3 18.3 %collective-permute-start.19 = (bf16[2,256,512]{2,1,0:T(8,128)(2,1)S(1)}, bf16[2,256,512]{2,1,0:T(8,128)(2,1)S(1)}, u32[]{:S(2)}, u32[]{:S(2)}) collective-permute-start(bf16[2,256,512]{2,1,0:T(8,128)(2,1)S(1)} %get-tuple-element.56), channel_id=1, source_target_pairs={{0,4},{4,0},{8,12},{12,8},{16,20},{20,16},{24,28},{28,24},{1,5},{5... | collective-permute-start | bytes 1572872 | tf_op jit(solution)/shard_map/ppermute | solution.py:566
  76.9 3.8 %copy-start.3 = (f32[64,2048]{1,0:T(8,128)S(1)}, f32[64,2048]{1,0:T(8,128)}, u32[]{:S(2)}) copy-start(f32[64,2048]{1,0:T(8,128)} %fw.3) | copy-start | bytes 1572868
  76.9 3.8 %copy-start.15 = (f32[40,512]{1,0:T(8,128)S(1)}, f32[40,512]{1,0:T(8,128)}, u32[]{:S(2)}) copy-start(f32[40,512]{1,0:T(8,128)} %constant.47.clone.tab) | copy-start | bytes 245764
  84.4 7.1 %collective-permute-start.27 = (f32[80,512]{1,0:T(8,128)S(1)}, f32[80,512]{1,0:T(8,128)S(1)}, u32[]{:S(2)}, u32[]{:S(2)}) collective-permute-start(f32[80,512]{1,0:T(8,128)S(1)} %correlate_part.1), channel_id=1, source_target_pairs={{0,4},{4,0},{8,12},{12,8},{16,20},{20,16},{24,28},{28,24},{1,5},{5... | collective-permute-start | bytes 491528 | tf_op jit(solution)/shard_map/ppermute | solution.py:566
  86.0 15.1 %collective-permute-start.20 = (bf16[2,256,512]{2,1,0:T(8,128)(2,1)S(1)}, bf16[2,256,512]{2,1,0:T(8,128)(2,1)S(1)}, u32[]{:S(2)}, u32[]{:S(2)}) collective-permute-start(bf16[2,256,512]{2,1,0:T(8,128)(2,1)S(1)} %get-tuple-element.58), channel_id=1, source_target_pairs={{0,4},{4,0},{8,12},{12,8},{16,20},{20,16},{24,28},{28,24},{1,5},{5... | collective-permute-start | bytes 1572872 | tf_op jit(solution)/shard_map/ppermute | solution.py:566
  86.5 17.4 %collective-permute-start.13 = (bf16[128,512]{1,0:T(8,128)(2,1)S(1)}, bf16[128,512]{1,0:T(8,128)(2,1)S(1)}, u32[]{:S(2)}, u32[]{:S(2)}) collective-permute-start(bf16[128,512]{1,0:T(8,128)(2,1)S(1)} %get-tuple-element.44), channel_id=1, source_target_pairs={{0,1},{1,0},{2,3},{3,2},{4,5},{5,4},{6,7},{7,6},{8,9},{9,8},{10,11... | collective-permute-start | bytes 393224 | tf_op jit(solution)/shard_map/ppermute | solution.py:566
  89.3 66.5 %collective-permute-start.16 = (bf16[128,2048]{1,0:T(8,128)(2,1)S(1)}, bf16[128,2048]{1,0:T(8,128)(2,1)S(1)}, u32[]{:S(2)}, u32[]{:S(2)}) collective-permute-start(bf16[128,2048]{1,0:T(8,128)(2,1)S(1)} %get-tuple-element.52), channel_id=1, source_target_pairs={{0,1},{1,0},{2,3},{3,2},{4,5},{5,4},{6,7},{7,6},{8,9},{9,8},{10,11... | collective-permute-start | bytes 1572872 | tf_op jit(solution)/shard_map/ppermute | solution.py:566
  91.5 12.2 %collective-permute-start.17 = (bf16[128,2048]{1,0:T(8,128)(2,1)S(1)}, bf16[128,2048]{1,0:T(8,128)(2,1)S(1)}, u32[]{:S(2)}, u32[]{:S(2)}) collective-permute-start(bf16[128,2048]{1,0:T(8,128)(2,1)S(1)} %get-tuple-element.54), channel_id=1, source_target_pairs={{0,1},{1,0},{2,3},{3,2},{4,5},{5,4},{6,7},{7,6},{8,9},{9,8},{10,11... | collective-permute-start | bytes 1572872 | tf_op jit(solution)/shard_map/ppermute | solution.py:566
  91.6 13.6 %collective-permute-start.23 = (bf16[256,512]{1,0:T(8,128)(2,1)S(1)}, bf16[256,512]{1,0:T(8,128)(2,1)S(1)}, u32[]{:S(2)}, u32[]{:S(2)}) collective-permute-start(bf16[256,512]{1,0:T(8,128)(2,1)S(1)} %fusion.7), channel_id=1, source_target_pairs={{0,8},{4,12},{8,0},{12,4},{16,24},{20,28},{24,16},{28,20},{1,9},{5... | collective-permute-start | bytes 786440 | tf_op jit(solution)/shard_map/ppermute | solution.py:566
  101.2 11.1 %collective-permute-start.21 = (bf16[256,512]{1,0:T(8,128)(2,1)S(1)}, bf16[256,512]{1,0:T(8,128)(2,1)S(1)}, u32[]{:S(2)}, u32[]{:S(2)}) collective-permute-start(bf16[256,512]{1,0:T(8,128)(2,1)S(1)} %get-tuple-element.69), channel_id=1, source_target_pairs={{0,24},{4,28},{8,16},{12,20},{16,8},{20,12},{24,0},{28,4},{1,25},{... | collective-permute-start | bytes 786440 | tf_op jit(solution)/shard_map/ppermute | solution.py:566
  103.7 25.3 %collective-permute-start.22 = (bf16[256,512]{1,0:T(8,128)(2,1)S(1)}, bf16[256,512]{1,0:T(8,128)(2,1)S(1)}, u32[]{:S(2)}, u32[]{:S(2)}) collective-permute-start(bf16[256,512]{1,0:T(8,128)(2,1)S(1)} %get-tuple-element.70), channel_id=1, source_target_pairs={{0,16},{4,20},{8,24},{12,28},{16,0},{20,4},{24,8},{28,12},{1,17},{... | collective-permute-start | bytes 786440 | tf_op jit(solution)/shard_map/ppermute | solution.py:566
  103.9 26.9 %collective-permute-start.30 = (bf16[80,512]{1,0:T(8,128)(2,1)S(1)}, bf16[80,512]{1,0:T(8,128)(2,1)S(1)}, u32[]{:S(2)}, u32[]{:S(2)}) collective-permute-start(bf16[80,512]{1,0:T(8,128)(2,1)S(1)} %add_convert_fusion.8), channel_id=1, source_target_pairs={{0,24},{4,28},{8,16},{12,20},{16,8},{20,12},{24,0},{28,4},{1,25},{... | collective-permute-start | bytes 245768 | tf_op jit(solution)/shard_map/ppermute | solution.py:566
  105.3 26.0 %collective-permute-start.29 = (bf16[80,512]{1,0:T(8,128)(2,1)S(1)}, bf16[80,512]{1,0:T(8,128)(2,1)S(1)}, u32[]{:S(2)}, u32[]{:S(2)}) collective-permute-start(bf16[80,512]{1,0:T(8,128)(2,1)S(1)} %add_convert_fusion.8), channel_id=1, source_target_pairs={{0,16},{4,20},{8,24},{12,28},{16,0},{20,4},{24,8},{28,12},{1,17},{... | collective-permute-start | bytes 245768 | tf_op jit(solution)/shard_map/ppermute | solution.py:566
  112.3 19.0 %collective-permute-start.28 = (bf16[80,512]{1,0:T(8,128)(2,1)S(1)}, bf16[80,512]{1,0:T(8,128)(2,1)S(1)}, u32[]{:S(2)}, u32[]{:S(2)}) collective-permute-start(bf16[80,512]{1,0:T(8,128)(2,1)S(1)} %add_convert_fusion.8), channel_id=1, source_target_pairs={{0,8},{4,12},{8,0},{12,4},{16,24},{20,28},{24,16},{28,20},{1,9},{5... | collective-permute-start | bytes 245768 | tf_op jit(solution)/shard_map/ppermute | solution.py:566
  129.0 26.8 %collective-permute-start.18 = (bf16[128,2048]{1,0:T(8,128)(2,1)S(1)}, bf16[128,2048]{1,0:T(8,128)(2,1)S(1)}, u32[]{:S(2)}, u32[]{:S(2)}) collective-permute-start(bf16[128,2048]{1,0:T(8,128)(2,1)S(1)} %add_convert_fusion.1), channel_id=1, source_target_pairs={{0,2},{1,3},{2,0},{3,1},{4,6},{5,7},{6,4},{7,5},{8,10},{9,11},{10,... | collective-permute-start | bytes 1572872 | tf_op jit(solution)/shard_map/ppermute | solution.py:566
  130.8 15.8 %collective-permute-start.14 = (bf16[128,512]{1,0:T(8,128)(2,1)S(1)}, bf16[128,512]{1,0:T(8,128)(2,1)S(1)}, u32[]{:S(2)}, u32[]{:S(2)}) collective-permute-start(bf16[128,512]{1,0:T(8,128)(2,1)S(1)} %get-tuple-element.45), channel_id=1, source_target_pairs={{0,2},{1,3},{2,0},{3,1},{4,6},{5,7},{6,4},{7,5},{8,10},{9,11},{10,... | collective-permute-start | bytes 393224 | tf_op jit(solution)/shard_map/ppermute | solution.py:566
  131.3 16.9 %collective-permute-start.15 = (bf16[128,512]{1,0:T(8,128)(2,1)S(1)}, bf16[128,512]{1,0:T(8,128)(2,1)S(1)}, u32[]{:S(2)}, u32[]{:S(2)}) collective-permute-start(bf16[128,512]{1,0:T(8,128)(2,1)S(1)} %get-tuple-element.46), channel_id=1, source_target_pairs={{0,3},{1,2},{2,1},{3,0},{4,7},{5,6},{6,5},{7,4},{8,11},{9,10},{10,... | collective-permute-start | bytes 393224 | tf_op jit(solution)/shard_map/ppermute | solution.py:566
  131.3 24.5 %collective-permute-start.25 = (bf16[256,512]{1,0:T(8,128)(2,1)S(1)}, bf16[256,512]{1,0:T(8,128)(2,1)S(1)}, u32[]{:S(2)}, u32[]{:S(2)}) collective-permute-start(bf16[256,512]{1,0:T(8,128)(2,1)S(1)} %fusion.3.refs_0_), channel_id=1, source_target_pairs={{0,2},{1,3},{2,0},{3,1},{4,6},{5,7},{6,4},{7,5},{8,10},{9,11},{10,... | collective-permute-start | bytes 786440 | tf_op jit(solution)/shard_map/ppermute | solution.py:566
  146.6 5.9 %collective-permute-start.32 = (bf16[80,512]{1,0:T(8,128)(2,1)S(1)}, bf16[80,512]{1,0:T(8,128)(2,1)S(1)}, u32[]{:S(2)}, u32[]{:S(2)}) collective-permute-start(bf16[80,512]{1,0:T(8,128)(2,1)S(1)} %add_convert_fusion.7.refs_0_), channel_id=1, source_target_pairs={{0,2},{1,3},{2,0},{3,1},{4,6},{5,7},{6,4},{7,5},{8,10},{9,11},{10,... | collective-permute-start | bytes 245768 | tf_op jit(solution)/shard_map/ppermute | solution.py:566
  148.2 5.7 %collective-permute-start.31 = (bf16[80,512]{1,0:T(8,128)(2,1)S(1)}, bf16[80,512]{1,0:T(8,128)(2,1)S(1)}, u32[]{:S(2)}, u32[]{:S(2)}) collective-permute-start(bf16[80,512]{1,0:T(8,128)(2,1)S(1)} %add_convert_fusion.7.refs_0_), channel_id=1, source_target_pairs={{0,1},{1,0},{2,3},{3,2},{4,5},{5,4},{6,7},{7,6},{8,9},{9,8},{10,11... | collective-permute-start | bytes 245768 | tf_op jit(solution)/shard_map/ppermute | solution.py:566
  152.5 1.4 collective-permute-start.33
  155.3 1.7 %collective-permute-start.24 = (bf16[256,512]{1,0:T(8,128)(2,1)S(1)}, bf16[256,512]{1,0:T(8,128)(2,1)S(1)}, u32[]{:S(2)}, u32[]{:S(2)}) collective-permute-start(bf16[256,512]{1,0:T(8,128)(2,1)S(1)} %fusion.3.refs_0_), channel_id=1, source_target_pairs={{0,1},{1,0},{2,3},{3,2},{4,5},{5,4},{6,7},{7,6},{8,9},{9,8},{10,11... | collective-permute-start | bytes 786440 | tf_op jit(solution)/shard_map/ppermute | solution.py:566
  155.8 1.5 collective-permute-start.26

commit v2 on v1

--- a/solution.py
+++ b/solution.py
@@ -19,19 +19,7 @@
 
 
 @functools.lru_cache(maxsize=None)
-def feature_table(length, emb_count):
-    positions = np.arange(length)
-    bands = np.arange(1, (emb_count - 1) // 2 + 1)
-    angle = positions[:, None] * bands[None, :] % length * (2.0 * math.pi / length)
-    table = np.concatenate(
-        [positions[:, None] / length, np.cos(angle), np.sin(angle), np.ones((length, 1))], axis=1
-    )
-    rows = -(-table.shape[1] // 8) * 8
-    return np.pad(table, ((0, 0), (0, rows - table.shape[1]))).astype(np.float32)
-
-
-@functools.lru_cache(maxsize=None)
-def angle_factors(length):
+def constants(length, emb_count):
     step = 4 * length
     lane = np.arange(length)[None, :]
     coarse = np.arange(length // BASE)[:, None]
@@ -44,8 +32,19 @@
         fine * (4 * lane + 1),
     ):
         angle = phase % step * (2.0 * math.pi / step)
-        found.append(np.stack([np.cos(angle), np.sin(angle)]).astype(np.float32))
-    return found
+        found += [np.cos(angle), np.sin(angle)]
+    bands = np.arange(1, (emb_count - 1) // 2 + 1)[:, None]
+    angle = bands * lane % length * (2.0 * math.pi / length)
+    rows = 8 * (emb_count // 8 + 1)
+    found += [lane / length, np.cos(angle), np.sin(angle), np.ones((1, length))]
+    found += [np.zeros((rows - emb_count - 1, length))]
+    return np.concatenate(found).astype(np.float32)
+
+
+def constant_rows(length):
+    sizes = [length // BASE, length // BASE, BASE, BASE]
+    starts = np.cumsum([0] + sizes + sizes).tolist()
+    return starts
 
 
 def dot(a, b):
@@ -98,36 +97,44 @@
     return pl.BlockSpec((2, block, width), lambda i, *_: (0, i, 0))
 
 
-def generate(place, table, factors, pos_weight, pos_bias, filter_weight, rates, norm, width, block):
+def generate(place, table, pos_weight, pos_bias, filter_weight, rows_of, width, block):
     highest = lax.Precision.HIGHEST
-    length, _ = table.shape
-    order = pos_weight.shape[1]
-    emb_count = pos_weight.shape[0]
+    length = table.shape[1]
+    emb_count, order = pos_weight.shape
+    starts = constant_rows(length)
 
     def body(
-        place_ref, tab, ac, af, tc, tf, pw, pb, fw, rate, norm_ref,
-        ah, al, th, spec, env_out, hidden_out, cos_out, filt,
+        place_ref, tab, pw, pb, fw, vec, ah, al, th, spec, env_out, hidden_out, cos_out, filt,
     ):
         step = pl.program_id(0)
 
         @pl.when(step == 0)
         def _():
-            pre = jnp.dot(tab[:, :emb_count], pw[...], precision=highest) + pb[...]
+            feat = tab[starts[8] : starts[8] + emb_count, :]
+            pre = pb[...] + lax.dot_general(
+                feat, pw[...], (((0,), (0,)), ((), ())), precision=highest,
+                preferred_element_type=f32,
+            )
             hidden = jnp.sin(pre)
             hidden_out[...] = hidden
             cos_out[...] = jnp.cos(pre)
             at = lax.broadcasted_iota(jnp.int32, (length, width), 0).astype(f32)
-            env = jnp.exp(-rate[...] * at) / norm_ref[...]
+            env = jnp.exp(-vec[0:1, :] * at) / vec[1:2, :]
             env_out[...] = env
             filt[...] = (jnp.dot(hidden, fw[...], precision=highest) * env).astype(bf16)
 
-        def rows(coarse, fine, store):
+        def rows(at, store):
+            cos_start, sin_start, fine_cos, fine_sin = starts[at : at + 4]
+            cos_fine = tab[fine_cos : fine_cos + BASE, :]
+            sin_fine = tab[fine_sin : fine_sin + BASE, :]
+
             def one(i, carry):
-                here = pl.ds(step * (block // BASE) + i, 1)
+                here = step * (block // BASE) + i
                 out = pl.ds(pl.multiple_of(i * BASE, BASE), BASE)
-                cos, sin = coarse[0, here, :], coarse[1, here, :]
-                store(out, 0, cos * fine[0] - sin * fine[1])
-                store(out, 1, sin * fine[0] + cos * fine[1])
+                cos = tab[pl.ds(cos_start + here, 1), :]
+                sin = tab[pl.ds(sin_start + here, 1), :]
+                store(out, 0, cos * cos_fine - sin * sin_fine)
+                store(out, 1, sin * cos_fine + cos * sin_fine)
                 return carry
 
             lax.fori_loop(0, block // BASE, one, 0)
@@ -140,8 +147,8 @@
         def store_high(out, part, value):
             th[part, out, :] = value.astype(bf16)
 
-        rows(ac, af, store_both)
-        rows(tc, tf, store_high)
+        rows(0, store_both)
+        rows(4, store_high)
         spec[0] = to_spectrum(ah, al, 0, filt[...])
         spec[1] = to_spectrum(ah, al, 1, filt[...])
 
@@ -152,9 +159,8 @@
         grid_spec=pltpu.PrefetchScalarGridSpec(
             num_scalar_prefetch=1,
             grid=(length // block,),
-            in_specs=[whole(table.shape)]
-            + [whole(f.shape) for f in factors]
-            + [whole(pos_weight.shape), whole(pos_bias.shape), cols(order), cols(1), cols(1)],
+            in_specs=[whole(table.shape), whole(pos_weight.shape), whole(pos_bias.shape)]
+            + [cols(order), cols(rows_of.shape[0])],
             out_specs=[by_row, by_row, by_row, spectrum_block(width, block)]
             + [whole((length, width)), whole((length, order)), whole((length, order))],
             scratch_shapes=[VMEM((length, width), bf16)],
@@ -164,16 +170,17 @@
         + [struct((length, order), f32)] * 2,
         name="generate",
         compiler_params=grant(
-            [((6, block, length), 2), ((4, block, width), 4), ((2, length, width), 4)], length, width
-        ),
-    )(place, table, *factors, pos_weight, pos_bias, filter_weight, rates, norm)
+            [((6, block, length), 2), ((4, block, width), 4), ((2, length, width), 4)]
+            + [(table.shape, 4)], length, width
+        ),
+    )(place, table, pos_weight, pos_bias, filter_weight, rows_of)
 
 
 def piece(place_ref, r, rows):
     return pl.ds(pl.multiple_of((place_ref[0] ^ r) * rows, rows), rows)
 
 
-def convolve(place, signal_rel, cot_rel, filt_spec, tables, skip, block):
+def convolve(place, signal_rel, cot_rel, filt_spec, tables, rows_of, block):
     a_high, a_low, t_high = tables
     count = len(signal_rel)
     local_len, width = cot_rel[0].shape
@@ -208,7 +215,7 @@
         @pl.when(step == pl.num_programs(0) - 1)
         def _():
             conv = acc[...].astype(bf16).astype(f32)
-            inner_out[...] = conv + skip_ref[...] * x[...].astype(f32)
+            inner_out[...] = conv + skip_ref[2:3, :] * x[...].astype(f32)
             for r in range(count):
                 rows = piece(place_ref, r, local_len)
                 grad_out[rows, :] = (cot[r][...].astype(f32) * inner_out[rows, :]).astype(bf16)
@@ -223,7 +230,7 @@
             in_specs=[cols] * count
             + [whole((local_len, width))] * count
             + [spectrum_block(width, block), by_row, by_row, by_col]
-            + [pl.BlockSpec((1, width), lambda i, place_ref: (0, place_ref[0]))],
+            + [pl.BlockSpec((3, width), lambda i, place_ref: (0, place_ref[0]))],
             out_specs=[
                 spectrum_block(width, block),
                 whole((length, width)),
@@ -240,7 +247,7 @@
         compiler_params=grant(
             [((6, block, length), 2), ((4, block, width), 4), ((3, length, width), 4)], length, width
         ),
-    )(place, *signal_rel, *cot_rel, filt_spec, a_high, a_low, t_high, skip)
+    )(place, *signal_rel, *cot_rel, filt_spec, a_high, a_low, t_high, rows_of)
 
 
 def grant(blocks, length, width):
@@ -340,7 +347,7 @@
     return order + 8 + 8 * groups, per_group
 
 
-def correlate_back(place, conv_grad, inner_grad, filt_spec, tables, skip, block):
+def correlate_back(place, conv_grad, inner_grad, filt_spec, tables, rows_of, block):
     a_high, a_low, t_high = tables
     length, width = conv_grad.shape
 
@@ -362,7 +369,7 @@
 
         @pl.when(step == pl.num_programs(0) - 1)
         def _():
-            direct_out[...] = ig[...] * skip_ref[...] + back[...].astype(bf16).astype(f32)
+            direct_out[...] = ig[...] * skip_ref[2:3, :] + back[...].astype(bf16).astype(f32)
 
     by_row, by_col = table_specs(length, block)
     spec_block = spectrum_block(width, block)
@@ -378,7 +385,7 @@
                 by_row,
                 by_row,
                 by_col,
-                pl.BlockSpec((1, width), lambda i, place_ref: (0, place_ref[0])),
+                pl.BlockSpec((3, width), lambda i, place_ref: (0, place_ref[0])),
             ],
             out_specs=[whole((length, width)), spec_block],
             scratch_shapes=[VMEM((length, width), f32)],
@@ -388,17 +395,18 @@
         compiler_params=grant(
             [((6, block, length), 2), ((4, block, width), 4), ((3, length, width), 4)], length, width
         ),
-    )(place, conv_grad, inner_grad, filt_spec, a_high, a_low, t_high, skip)
+    )(place, conv_grad, inner_grad, filt_spec, a_high, a_low, t_high, rows_of)
 
 
 def correlate_part(
-    place, grad_spec, skip_sum, signal_spec, tables, env, hidden, filter_weight, cos_pre, table_t,
+    place, grad_spec, skip_sum, signal_spec, tables, env, hidden, filter_weight, cos_pre, table,
     block,
 ):
     t_high = tables[2]
     length, width = env.shape
     order = filter_weight.shape[0]
-    table_rows = table_t.shape[0]
+    feature_start = constant_rows(length)[8]
+    table_rows = table.shape[0] - feature_start
     total_rows, per_group = packed_rows(order, table_rows, width)
 
     def body(
@@ -424,7 +432,7 @@
             packed[:order, :] = careful(dot_first, hid[...], pre_grad)
             packed[order : order + 8, :] = skip_sum_ref[...]
             act = careful(dot_last, pre_grad, fw[...]) * cp[...]
-            small = careful(dot, tab[...], act)
+            small = careful(dot, tab[feature_start:, :], act)
             for b in range(table_rows // 8):
                 row = order + 8 + 8 * (b // per_group)
                 col = order * (b % per_group)
@@ -446,7 +454,7 @@
                 whole(hidden.shape),
                 pl.BlockSpec((order, width), lambda i, place_ref: (0, place_ref[0])),
                 whole(cos_pre.shape),
-                whole(table_t.shape),
+                whole(table.shape),
             ],
             out_specs=whole((total_rows, width)),
             scratch_shapes=[VMEM((length, width), f32)],
@@ -458,7 +466,7 @@
         ),
     )(
         place, grad_spec, skip_sum, signal_spec, t_high, env, hidden, filter_weight, cos_pre,
-        table_t,
+        table,
     )
 
 
@@ -522,7 +530,7 @@
 def finish(place, pieces, order, emb_count):
     count = len(pieces)
     rows, width = pieces[0].shape
-    table_rows = -(-(emb_count + 1) // 8) * 8
+    table_rows = 8 * (emb_count // 8 + 1)
     _, per_group = packed_rows(order, table_rows, width)
 
     def body(place_ref, *refs):
@@ -614,22 +622,21 @@
         swap(own_cols(cot_tok, r), "seq", r) for r in range(1, seq_count)
     ]
 
-    table = feature_table(length, emb_count)
+    table = jnp.asarray(constants(length, emb_count))
     rates = decay_rate[None]
     norm = jnp.sqrt(jnp.expm1(-2.0 * rates * length) / jnp.expm1(-2.0 * rates))
-    skip = skip_gain[None]
+    rows_of = jnp.concatenate([rates, norm, skip_gain[None]])
     a_high, a_low, t_high, filt_spec, env, hidden, cos_pre = generate(
-        place, jnp.asarray(table), [jnp.asarray(f) for f in angle_factors(length)],
-        pos_weight, pos_bias[None], filter_weight, rates, norm, width, block,
+        place, table, pos_weight, pos_bias[None], filter_weight, rows_of, width, block
     )
     tables = (a_high, a_low, t_high)
 
     signal_spec, inner, gate_grad = convolve(
-        place, signal_rel, cot_rel, filt_spec, tables, skip, block
+        place, signal_rel, cot_rel, filt_spec, tables, rows_of, block
     )
 
     far = list(reversed(range(0, dp_count, 2)))
-    pairs = [far[i : i + 2] for i in range(0, len(far), 2)]
+    pairs = stages(dp_count)
     groups = [[k + 1 for k in pair] for pair in pairs] + pairs
     weight_parts = weight_grads(place, signal_rel, gate_grad, groups)
     sums = {}
@@ -647,10 +654,12 @@
     out_rel = [out_rel[0]] + [swap(out_rel[r], "seq", r) for r in range(1, seq_count)]
     output = assemble(place, out_rel, bf16)
 
-    direct, grad_spec = correlate_back(place, conv_grad, inner_grad, filt_spec, tables, skip, block)
+    direct, grad_spec = correlate_back(
+        place, conv_grad, inner_grad, filt_spec, tables, rows_of, block
+    )
     packed = correlate_part(
         place, grad_spec, skip_sum, signal_spec, tables, env, hidden, filter_weight, cos_pre,
-        jnp.asarray(table.T), block,
+        table, block,
     )
     back_rel = through_gate(place, gate_grad, weight_rel, direct, seq_count)
 
@@ -662,7 +671,8 @@
         bit *= 2
     grad_signal = live[0]
 
-    packed = (packed + swap(packed, "dp", 1)).astype(bf16)
+    met = swap(packed, "dp", 1)
+    packed = (packed + met).astype(bf16)
     terms = [packed] + [swap(packed, "dp", k) for k in range(2, dp_count, 2)]
     terms = [term.astype(f32) for term in terms]
     while len(terms) > 1:
@@ -682,6 +692,11 @@
     )
 
 
+def stages(dp_count):
+    far = list(reversed(range(0, dp_count, 2)))
+    return [[k] for k in far[:-2]] + [far[-2:]]
+
+
 def solution(mesh):
     step = mapped(shards, mesh)
     return step

time: 160 us -> 154 us (0.963)
  starting transfers between devices: 42.8 us -> 32.2 us
  waiting for transfers between devices: 69.9 us -> 79.4 us
  local copies, waits for them, and re-layouts: 13.4 us -> 9.29 us
    ppermute x34 -> x35, starting transfers between devices: 42.8 us -> 32.2 us  [swap(): return lax.ppermute(value, axis, [(i, i ^ offset) for i in range(count)])]
    ppermute x34 -> x35, waiting for transfers between devices: 69.9 us -> 79.4 us  [swap(): return lax.ppermute(value, axis, [(i, i ^ offset) for i in range(count)])]
    unnamed x44 -> x28, local copies, waits for them, and re-layouts: 12.3 us -> 8.14 us
  transfers between devices with their start and end apart: 34 -> 35, of which waited for: 10 -> 13; matrix products, arithmetic and copies ran while one was open for 2% -> 3% of each run, Pallas kernels for 18% -> 11%
where the time goes in v2:
time: 154 us
  waiting for transfers between devices  79.4 us (52%)
  starting transfers between devices  32.2 us (21%)
  Pallas kernels  28.9 us (19%)
  local copies, waits for them, and re-layouts  9.29 us (6%)
  other arithmetic  3.13 us (2%)
    ppermute x35, waiting for transfers between devices, swap(): return lax.ppermute(value, axis, [(i, i ^ offset) for i in range(count)])  79.4 us
    ppermute x35, starting transfers between devices, swap(): return lax.ppermute(value, axis, [(i, i ^ offset) for i in range(count)])  32.2 us
    unnamed x28, local copies, waits for them, and re-layouts  8.14 us
    pallas_call x1, Pallas kernels, generate(): pl.pallas_call(body, grid_spec=pltpu.PrefetchScalarGridSpec(num_scalar_pr...  5.93 us
    pallas_call x1, Pallas kernels, convolve(): pl.pallas_call(body, grid_spec=pltpu.PrefetchScalarGridSpec(num_scalar_pr...  4.15 us
    pallas_call x1, Pallas kernels, correlate_back(): pl.pallas_call(body, grid_spec=pltpu.PrefetchScalarGridSpec(num_scalar_pr...  3.78 us
    pallas_call x1, Pallas kernels, correlate_part(): pl.pallas_call(body, grid_spec=pltpu.PrefetchScalarGridSpec(num_scalar_pr...  3.65 us
    pallas_call x2, Pallas kernels, assemble(): pl.pallas_call(body, in_specs=[smem()] + [pl.BlockSpec(memory_space=VMEM)...  3.37 us
  transfers between devices with their start and end apart: 35, of which 13 were waited for; matrix products, arithmetic and copies ran while one was open for 3% of the time, Pallas kernels for 11%

profile of v2, /device:TPU:0, one launch (start us, length us, event | category | flops | bytes accessed | tf_op | source)
XLA Modules:
  0.0 153.8 jit_solution(17078046292902940878)
XLA Ops:
  0.7 3.0 %collective-permute-start.1 = (bf16[128,2048]{1,0:T(8,128)(2,1)}, bf16[128,2048]{1,0:T(8,128)(2,1)S(1)}, u32[]{:S(2)}, u32[]{:S(2)}) collective-permute-start(bf16[128,2048]{1,0:T(8,128)(2,1)} %bitcast.31), channel_id=1, source_target_pairs={{0,2},{1,3},{2,0},{3,1},{4,6},{5,7},{6,4},{7,5},{8,10},{9,11},{10,... | collective-permute-start | bytes 1572872 | tf_op jit(solution)/shard_map/ppermute | solution.py:574
  3.7 1.1 dynamic-slice_bitcast_fusion
  4.8 0.3 collective-permute-start.12
  5.1 0.4 collective-permute-start.10
  5.5 1.6 %collective-permute-start.11 = (bf16[128,512]{1,0:T(8,128)(2,1)S(1)}, bf16[128,512]{1,0:T(8,128)(2,1)S(1)}, u32[]{:S(2)}, u32[]{:S(2)}) collective-permute-start(bf16[128,512]{1,0:T(8,128)(2,1)S(1)} %get-tuple-element.76), channel_id=1, source_target_pairs={{0,2},{1,3},{2,0},{3,1},{4,6},{5,7},{6,4},{7,5},{8,10},{9,11},{10,... | collective-permute-start | bytes 393224 | tf_op jit(solution)/shard_map/ppermute | solution.py:574
  7.1 12.0 %collective-permute-done.12.refs_7_.refs_15_ = bf16[128,512]{1,0:T(8,128)(2,1)S(1)} collective-permute-done((bf16[128,512]{1,0:T(8,128)(2,1)S(1)}, bf16[128,512]{1,0:T(8,128)(2,1)S(1)}, u32[]{:S(2)}, u32[]{:S(2)}) %collective-permute-start.12) | collective-permute-done | bytes 131104 | tf_op jit(solution)/shard_map/ppermute | solution.py:574
  19.0 0.7 copy-done.6
  19.7 3.6 %collective-permute-start.8 = (bf16[256,512]{1,0:T(8,128)(2,1)S(1)}, bf16[256,512]{1,0:T(8,128)(2,1)S(1)}, u32[]{:S(2)}, u32[]{:S(2)}) collective-permute-start(bf16[256,512]{1,0:T(8,128)(2,1)S(1)} %constant_dynamic-slice_fusion.refs_4_.refs_1_), channel_id=1, source_target_pairs={{0,24},{4,28},{8,16},{12,20},{16,8},{20,12},{24,0},{28,4},{1,25},{... | collective-permute-start | bytes 786440 | tf_op jit(solution)/shard_map/ppermute | solution.py:574
  23.3 0.7 copy-done.8
  23.9 0.7 copy-done.10
  24.6 0.8 collective-permute-start.4
  25.4 0.7 divide_sqrt_fusion
  26.1 4.7 %collective-permute-done.8.refs_10_.refs_7_ = bf16[256,512]{1,0:T(8,128)(2,1)S(1)} collective-permute-done((bf16[256,512]{1,0:T(8,128)(2,1)S(1)}, bf16[256,512]{1,0:T(8,128)(2,1)S(1)}, u32[]{:S(2)}, u32[]{:S(2)}) %collective-permute-start.8) | collective-permute-done | bytes 262176 | tf_op jit(solution)/shard_map/ppermute | solution.py:574
  30.8 1.5 collective-permute-start.3
  32.3 14.2 %collective-permute-done.6.refs_8_.refs_5_ = bf16[256,512]{1,0:T(8,128)(2,1)S(1)} collective-permute-done((bf16[256,512]{1,0:T(8,128)(2,1)S(1)}, bf16[256,512]{1,0:T(8,128)(2,1)S(1)}, u32[]{:S(2)}, u32[]{:S(2)}) %collective-permute-start.6) | collective-permute-done | bytes 262176 | tf_op jit(solution)/shard_map/ppermute | solution.py:574
  46.6 1.5 collective-permute-start.9
  48.1 0.5 collective-permute-start.7
  48.6 1.5 collective-permute-start.5
  50.2 0.7 pad_maximum_fusion.vec.refs_12_.skip_ref
  51.0 1.0 copy-done.2
  52.0 1.0 copy-done.4
  53.0 0.7 copy-done.12
  53.7 0.7 copy-done.13
  54.4 5.9 %generate.1 = (bf16[2,512,512]{2,1,0:T(8,128)(2,1)S(1)}, bf16[2,512,512]{2,1,0:T(8,128)(2,1)S(1)}, bf16[2,512,512]{2,1,0:T(8,128)(2,1)S(1)}, f32[2,512,512]{2,1,...) custom-call(s32[2]{0:T(128)S(1)} %pad_add_fusion.place_ref, ...), custom_call_target="tpu_custom_call" | custom-call | tf_op jit(solution)/shard_map/generate/pallas_call | solution.py:157
  60.4 0.9 copy-done.7
  61.3 0.9 copy-done.9
  62.2 0.9 copy-done.11
  63.1 4.1 %convolve.1 = (f32[2,512,512]{2,1,0:T(8,128)S(1)}, f32[512,512]{1,0:T(8,128)S(1)}, bf16[512,512]{1,0:T(8,128)(2,1)S(1)}) custom-call(s32[2]{0:T(128)S(1)} %pad_add_fusion.place_ref, bf16[128,2048]{1,0:T(8,128)(2,1)S(1)} %bitcast.33, bf16[128,2048]{1,0:T(8,128)(2,1)S(1)} %collective-permute-done.refs_1_, ...), custom_call_target="tpu_custom_call" | custom-call | tf_op jit(solution)/shard_map/convolve/pallas_call | solution.py:225
  67.3 2.5 %gating.1 = (bf16[128,512]{1,0:T(8,128)(2,1)S(1)}, bf16[128,512]{1,0:T(8,128)(2,1)S(1)}, bf16[128,512]{1,0:T(8,128)(2,1)S(1)}, bf16[128,512]{1,0:T(8,128)(2,1)S(...) custom-call(s32[2]{0:T(128)S(1)} %pad_add_fusion.place_ref, ...), custom_call_target="tpu_custom_call" | custom-call | tf_op jit(solution)/shard_map/gating/pallas_call | solution.py:328
  69.8 3.8 %correlate_back.1 = (f32[512,512]{1,0:T(8,128)S(1)}, f32[2,512,512]{2,1,0:T(8,128)S(1)}) custom-call(s32[2]{0:T(128)S(1)} %pad_add_fusion.place_ref, bf16[512,512]{1,0:T(8,128)(2,1)S(1)} %get-tuple-element.50.cg, f32[512,512]{1,0:T(8,128)S(1)} %get-tuple-element.51.ig, f32[2,512,512]{2,1,0:T(8,128)S(1)} %get-tuple-element.40.refs_8_.fs, ...), custom_call_target="tpu_custom_call" | custom-call | tf_op jit(solution)/shard_map/correlate_back/pallas_call | solution.py:376
  73.6 3.7 %correlate_part.1 = f32[80,512]{1,0:T(8,128)S(1)} custom-call(s32[2]{0:T(128)S(1)} %pad_add_fusion.place_ref, f32[2,512,512]{2,1,0:T(8,128)S(1)} %get-tuple-element.63.gs, f32[8,512]{1,0:T(8,128)S(1)} %get-tuple-element.64.skip_sum_ref, f32[2,512,512]{2,1,0:T(8,128)S(1)} %get-tuple-element.65.ss, bf16[2,512,512]{2,1,0:T(8,128)(2,1)S(1)} %get-tuple-element.43.refs_11_.th, ...), custom_call_target="tpu_custom_call" | custom-call | tf_op jit(solution)/shard_map/correlate_part/pallas_call | solution.py:443
  77.3 0.6 collective-permute-start.28
  77.8 1.8 %weight_grads.1 = (bf16[1,256,512]{2,1,0:T(8,128)(2,1)S(1)}, bf16[1,256,512]{2,1,0:T(8,128)(2,1)S(1)}, bf16[2,256,512]{2,1,0:T(8,128)(2,1)S(1)}, bf16[1,256,512]...) custom-call(s32[2]{0:T(128)S(1)} %pad_add_fusion.place_ref, ...), custom_call_target="tpu_custom_call" | custom-call | tf_op jit(solution)/shard_map/weight_grads/pallas_call | solution.py:285
  79.7 1.6 %collective-permute-start.20 = (bf16[1,256,512]{2,1,0:T(8,128)(2,1)S(1)}, bf16[1,256,512]{2,1,0:T(8,128)(2,1)S(1)}, u32[]{:S(2)}, u32[]{:S(2)}) collective-permute-start(bf16[1,256,512]{2,1,0:T(8,128)(2,1)S(1)} %get-tuple-element.60), channel_id=1, source_target_pairs={{0,4},{4,0},{8,12},{12,8},{16,20},{20,16},{24,28},{28,24},{1,5},{5... | collective-permute-start | bytes 786440 | tf_op jit(solution)/shard_map/ppermute | solution.py:574
  81.3 0.5 collective-permute-start.22
  81.8 1.5 collective-permute-start.19
  83.3 2.3 %through_gate.1 = (bf16[128,2048]{1,0:T(8,128)(2,1)S(1)}, bf16[128,2048]{1,0:T(8,128)(2,1)S(1)}, bf16[128,2048]{1,0:T(8,128)(2,1)S(1)}, bf16[128,2048]{1,0:T(8,128)(2,1)S(1)}) custom-call(s32[2]{0:T(128)S(1)} %pad_add_fusion.place_ref, bf16[512,512]{1,0:T(8,128)(2,1)S(1)} %get-tuple-element.49.refs_0_.refs_4_, ...), custom_call_target="tpu_custom_call" | custom-call | tf_op jit(solution)/shard_map/through_gate/pallas_call | solution.py:500
  85.8 4.0 %collective-permute-done.20 = bf16[1,256,512]{2,1,0:T(8,128)(2,1)S(1)} collective-permute-done((bf16[1,256,512]{2,1,0:T(8,128)(2,1)S(1)}, bf16[1,256,512]{2,1,0:T(8,128)(2,1)S(1)}, u32[]{:S(2)}, u32[]{:S(2)}) %collective-permute-start.20) | collective-permute-done | bytes 262176 | tf_op jit(solution)/shard_map/ppermute | solution.py:574
  89.8 5.5 %collective-permute-done.22 = bf16[1,256,512]{2,1,0:T(8,128)(2,1)S(1)} collective-permute-done((bf16[1,256,512]{2,1,0:T(8,128)(2,1)S(1)}, bf16[1,256,512]{2,1,0:T(8,128)(2,1)S(1)}, u32[]{:S(2)}, u32[]{:S(2)}) %collective-permute-start.22) | collective-permute-done | bytes 262176 | tf_op jit(solution)/shard_map/ppermute | solution.py:574
  95.3 2.5 %collective-permute-start.21 = (bf16[256,512]{1,0:T(8,128)(2,1)S(1)}, bf16[256,512]{1,0:T(8,128)(2,1)S(1)}, u32[]{:S(2)}, u32[]{:S(2)}) collective-permute-start(bf16[256,512]{1,0:T(8,128)(2,1)S(1)} %fusion.5), channel_id=1, source_target_pairs={{0,24},{4,28},{8,16},{12,20},{16,8},{20,12},{24,0},{28,4},{1,25},{... | collective-permute-start | bytes 786440 | tf_op jit(solution)/shard_map/ppermute | solution.py:574
  97.9 7.2 %collective-permute-done.19 = bf16[2,256,512]{2,1,0:T(8,128)(2,1)S(1)} collective-permute-done((bf16[2,256,512]{2,1,0:T(8,128)(2,1)S(1)}, bf16[2,256,512]{2,1,0:T(8,128)(2,1)S(1)}, u32[]{:S(2)}, u32[]{:S(2)}) %collective-permute-start.19) | collective-permute-done | bytes 524320 | tf_op jit(solution)/shard_map/ppermute | solution.py:574
  105.1 0.4 collective-permute-start.23
  105.6 2.7 %collective-permute-start.24 = (bf16[256,512]{1,0:T(8,128)(2,1)S(1)}, bf16[256,512]{1,0:T(8,128)(2,1)S(1)}, u32[]{:S(2)}, u32[]{:S(2)}) collective-permute-start(bf16[256,512]{1,0:T(8,128)(2,1)S(1)} %fusion.7), channel_id=1, source_target_pairs={{0,8},{4,12},{8,0},{12,4},{16,24},{20,28},{24,16},{28,20},{1,9},{5... | collective-permute-start | bytes 786440 | tf_op jit(solution)/shard_map/ppermute | solution.py:574
  108.5 1.4 collective-permute-start.31
  109.9 0.1 collective-permute-start.30
  110.0 10.2 %collective-permute-done.23 = bf16[256,512]{1,0:T(8,128)(2,1)S(1)} collective-permute-done((bf16[256,512]{1,0:T(8,128)(2,1)S(1)}, bf16[256,512]{1,0:T(8,128)(2,1)S(1)}, u32[]{:S(2)}, u32[]{:S(2)}) %collective-permute-start.23) | collective-permute-done | bytes 262176 | tf_op jit(solution)/shard_map/ppermute | solution.py:574
  120.3 1.0 collective-permute-start.18
  121.3 0.2 fusion.3.refs_0_
  121.5 1.2 collective-permute-start.14
  122.6 2.9 %collective-permute-done.30 = bf16[80,512]{1,0:T(8,128)(2,1)S(1)} collective-permute-done((bf16[80,512]{1,0:T(8,128)(2,1)S(1)}, bf16[80,512]{1,0:T(8,128)(2,1)S(1)}, u32[]{:S(2)}, u32[]{:S(2)}) %collective-permute-start.30) | collective-permute-done | bytes 81952 | tf_op jit(solution)/shard_map/ppermute | solution.py:574
  125.5 0.1 collective-permute-start.15
  125.7 0.6 collective-permute-done.29
  126.3 0.8 collective-permute-start.26
  127.2 10.7 %collective-permute-done.14.refs_2_ = bf16[128,512]{1,0:T(8,128)(2,1)S(1)} collective-permute-done((bf16[128,512]{1,0:T(8,128)(2,1)S(1)}, bf16[128,512]{1,0:T(8,128)(2,1)S(1)}, u32[]{:S(2)}, u32[]{:S(2)}) %collective-permute-start.14) | collective-permute-done | bytes 131104 | tf_op jit(solution)/shard_map/ppermute | solution.py:574
  137.9 1.0 collective-permute-start.33
  138.9 0.3 collective-permute-done.15.refs_3_
  139.2 1.3 collective-permute-start.32
  140.5 6.5 %collective-permute-done.33.refs_2_ = bf16[80,512]{1,0:T(8,128)(2,1)S(1)} collective-permute-done((bf16[80,512]{1,0:T(8,128)(2,1)S(1)}, bf16[80,512]{1,0:T(8,128)(2,1)S(1)}, u32[]{:S(2)}, u32[]{:S(2)}) %collective-permute-start.33) | collective-permute-done | bytes 81952 | tf_op jit(solution)/shard_map/ppermute | solution.py:574
  147.0 1.4 assemble.2
  148.4 1.4 finish.1
  149.8 0.5 collective-permute-start.25
  150.4 1.0 fusion
  151.4 0.4 collective-permute-done.27.refs_3_
  151.8 2.0 %assemble.3 = f32[256,2048]{1,0:T(8,128)} custom-call(s32[2]{0:T(128)S(1)} %pad_add_fusion.place_ref, bf16[256,512]{1,0:T(8,128)(2,1)S(1)} %fusion.3.refs_0_, bf16[256,512]{1,0:T(8,128)(2,1)S(1)} %collective-permute-done.25.refs_1_, bf16[256,512]{1,0:T(8,128)(2,1)S(1)} %collective-permute-done.26.refs_2_, bf16[256,512]{1,0:T(8,128)(2,1)S(1)} %collective-permute-done.27.refs_3_), custom_call_target="tpu_custom_call" | custom-call | tf_op jit(solution)/shard_map/assemble/pallas_call | solution.py:520
  (57 shorter events, 0.8 us)
Async XLA Ops:
  0.6 6.4 %copy-start = (bf16[256,2048]{1,0:T(8,128)(2,1)S(1)}, bf16[256,2048]{1,0:T(8,128)(2,1)}, u32[]{:S(2)}) copy-start(bf16[256,2048]{1,0:T(8,128)(2,1)} %param.10) | copy-start | bytes 3145732
  0.6 59.7 %copy-start.1 = (bf16[1,128,2048]{2,1,0:T(8,128)(2,1)S(1)}, bf16[1,128,2048]{2,1,0:T(8,128)(2,1)}, u32[]{:S(2)}) copy-start(bf16[1,128,2048]{2,1,0:T(8,128)(2,1)} %param.9) | copy-start | bytes 1572868
  0.7 24.7 %collective-permute-start.1 = (bf16[128,2048]{1,0:T(8,128)(2,1)}, bf16[128,2048]{1,0:T(8,128)(2,1)S(1)}, u32[]{:S(2)}, u32[]{:S(2)}) collective-permute-start(bf16[128,2048]{1,0:T(8,128)(2,1)} %bitcast.31), channel_id=1, source_target_pairs={{0,2},{1,3},{2,0},{3,1},{4,6},{5,7},{6,4},{7,5},{8,10},{9,11},{10,... | collective-permute-start | bytes 1572872 | tf_op jit(solution)/shard_map/ppermute | solution.py:574
  3.7 44.9 %collective-permute-start = (bf16[128,2048]{1,0:T(8,128)(2,1)}, bf16[128,2048]{1,0:T(8,128)(2,1)S(1)}, u32[]{:S(2)}, u32[]{:S(2)}) collective-permute-start(bf16[128,2048]{1,0:T(8,128)(2,1)} %bitcast.32), channel_id=1, source_target_pairs={{0,1},{1,0},{2,3},{3,2},{4,5},{5,4},{6,7},{7,6},{8,9},{9,8},{10,11... | collective-permute-start | bytes 1572872 | tf_op jit(solution)/shard_map/ppermute | solution.py:574
  4.8 14.2 %collective-permute-start.12 = (bf16[128,512]{1,0:T(8,128)(2,1)S(1)}, bf16[128,512]{1,0:T(8,128)(2,1)S(1)}, u32[]{:S(2)}, u32[]{:S(2)}) collective-permute-start(bf16[128,512]{1,0:T(8,128)(2,1)S(1)} %get-tuple-element.73), channel_id=1, source_target_pairs={{0,3},{1,2},{2,1},{3,0},{4,7},{5,6},{6,5},{7,4},{8,11},{9,10},{10,... | collective-permute-start | bytes 393224 | tf_op jit(solution)/shard_map/ppermute | solution.py:574
  5.1 18.2 %collective-permute-start.10 = (bf16[128,512]{1,0:T(8,128)(2,1)S(1)}, bf16[128,512]{1,0:T(8,128)(2,1)S(1)}, u32[]{:S(2)}, u32[]{:S(2)}) collective-permute-start(bf16[128,512]{1,0:T(8,128)(2,1)S(1)} %get-tuple-element.74), channel_id=1, source_target_pairs={{0,1},{1,0},{2,3},{3,2},{4,5},{5,4},{6,7},{7,6},{8,9},{9,8},{10,11... | collective-permute-start | bytes 393224 | tf_op jit(solution)/shard_map/ppermute | solution.py:574
  5.5 18.5 %collective-permute-start.11 = (bf16[128,512]{1,0:T(8,128)(2,1)S(1)}, bf16[128,512]{1,0:T(8,128)(2,1)S(1)}, u32[]{:S(2)}, u32[]{:S(2)}) collective-permute-start(bf16[128,512]{1,0:T(8,128)(2,1)S(1)} %get-tuple-element.76), channel_id=1, source_target_pairs={{0,2},{1,3},{2,0},{3,1},{4,6},{5,7},{6,4},{7,5},{8,10},{9,11},{10,... | collective-permute-start | bytes 393224 | tf_op jit(solution)/shard_map/ppermute | solution.py:574
  19.0 0.7 copy-start.6
  19.7 11.1 %collective-permute-start.8 = (bf16[256,512]{1,0:T(8,128)(2,1)S(1)}, bf16[256,512]{1,0:T(8,128)(2,1)S(1)}, u32[]{:S(2)}, u32[]{:S(2)}) collective-permute-start(bf16[256,512]{1,0:T(8,128)(2,1)S(1)} %constant_dynamic-slice_fusion.refs_4_.refs_1_), channel_id=1, source_target_pairs={{0,24},{4,28},{8,16},{12,20},{16,8},{20,12},{24,0},{28,4},{1,25},{... | collective-permute-start | bytes 786440 | tf_op jit(solution)/shard_map/ppermute | solution.py:574
  23.3 0.7 copy-start.8
  23.9 22.6 %collective-permute-start.6 = (bf16[256,512]{1,0:T(8,128)(2,1)S(1)}, bf16[256,512]{1,0:T(8,128)(2,1)S(1)}, u32[]{:S(2)}, u32[]{:S(2)}) collective-permute-start(bf16[256,512]{1,0:T(8,128)(2,1)S(1)} %constant_dynamic-slice_fusion.refs_4_.refs_1_), channel_id=1, source_target_pairs={{0,16},{4,20},{8,24},{12,28},{16,0},{20,4},{24,8},{28,12},{1,17},{... | collective-permute-start | bytes 786440 | tf_op jit(solution)/shard_map/ppermute | solution.py:574
  23.9 0.7 copy-start.10
  24.6 23.5 %collective-permute-start.4 = (bf16[256,512]{1,0:T(8,128)(2,1)S(1)}, bf16[256,512]{1,0:T(8,128)(2,1)}, u32[]{:S(2)}, u32[]{:S(2)}) collective-permute-start(bf16[256,512]{1,0:T(8,128)(2,1)S(1)} %constant_dynamic-slice_fusion.refs_4_.refs_1_), channel_id=1, source_target_pairs={{0,8},{4,12},{8,0},{12,4},{16,24},{20,28},{24,16},{28,20},{1,9},{5... | collective-permute-start | bytes 786440 | tf_op jit(solution)/shard_map/ppermute | solution.py:574
  25.4 34.9 %collective-permute-start.2 = (bf16[128,2048]{1,0:T(8,128)(2,1)S(1)}, bf16[128,2048]{1,0:T(8,128)(2,1)S(1)}, u32[]{:S(2)}, u32[]{:S(2)}) collective-permute-start(bf16[128,2048]{1,0:T(8,128)(2,1)S(1)} %collective-permute-done.1.refs_2_), channel_id=1, source_target_pairs={{0,1},{1,0},{2,3},{3,2},{4,5},{5,4},{6,7},{7,6},{8,9},{9,8},{10,11... | collective-permute-start | bytes 1572872 | tf_op jit(solution)/shard_map/ppermute | solution.py:574
  30.8 36.4 %collective-permute-start.3 = (bf16[256,512]{1,0:T(8,128)(2,1)S(1)}, bf16[256,512]{1,0:T(8,128)(2,1)S(1)}, u32[]{:S(2)}, u32[]{:S(2)}) collective-permute-start(bf16[256,512]{1,0:T(8,128)(2,1)S(1)} %constant_dynamic-slice_fusion.refs_4_.refs_1_), channel_id=1, source_target_pairs={{0,4},{4,0},{8,12},{12,8},{16,20},{20,16},{24,28},{28,24},{1,5},{5... | collective-permute-start | bytes 786440 | tf_op jit(solution)/shard_map/ppermute | solution.py:574
  46.6 20.7 %collective-permute-start.9 = (bf16[256,512]{1,0:T(8,128)(2,1)S(1)}, bf16[256,512]{1,0:T(8,128)(2,1)S(1)}, u32[]{:S(2)}, u32[]{:S(2)}) collective-permute-start(bf16[256,512]{1,0:T(8,128)(2,1)S(1)} %collective-permute-done.8.refs_10_.refs_7_), channel_id=1, source_target_pairs={{0,4},{4,0},{8,12},{12,8},{16,20},{20,16},{24,28},{28,24},{1,5},{5... | collective-permute-start | bytes 786440 | tf_op jit(solution)/shard_map/ppermute | solution.py:574
  48.1 19.2 %collective-permute-start.7 = (bf16[256,512]{1,0:T(8,128)(2,1)S(1)}, bf16[256,512]{1,0:T(8,128)(2,1)S(1)}, u32[]{:S(2)}, u32[]{:S(2)}) collective-permute-start(bf16[256,512]{1,0:T(8,128)(2,1)S(1)} %collective-permute-done.6.refs_8_.refs_5_), channel_id=1, source_target_pairs={{0,4},{4,0},{8,12},{12,8},{16,20},{20,16},{24,28},{28,24},{1,5},{5... | collective-permute-start | bytes 786440 | tf_op jit(solution)/shard_map/ppermute | solution.py:574
  48.6 18.7 %collective-permute-start.5 = (bf16[256,512]{1,0:T(8,128)(2,1)}, bf16[256,512]{1,0:T(8,128)(2,1)S(1)}, u32[]{:S(2)}, u32[]{:S(2)}) collective-permute-start(bf16[256,512]{1,0:T(8,128)(2,1)} %collective-permute-done.4.refs_6_.refs_3_), channel_id=1, source_target_pairs={{0,4},{4,0},{8,12},{12,8},{16,20},{20,16},{24,28},{28,24},{1,5},{5... | collective-permute-start | bytes 786440 | tf_op jit(solution)/shard_map/ppermute | solution.py:574
  50.9 1.0 copy-start.2
  52.0 1.0 copy-start.4
  53.0 0.7 copy-start.12
  53.7 0.7 copy-start.13
  60.4 0.9 copy-start.7
  61.3 0.9 copy-start.9
  62.2 0.9 copy-start.11
  69.8 3.8 %copy-start.3 = (f32[64,2048]{1,0:T(8,128)S(1)}, f32[64,2048]{1,0:T(8,128)}, u32[]{:S(2)}) copy-start(f32[64,2048]{1,0:T(8,128)} %fw.3) | copy-start | bytes 1572868
  69.8 3.8 %copy-start.5 = (f32[232,512]{1,0:T(8,128)S(1)}, f32[232,512]{1,0:T(8,128)}, u32[]{:S(2)}) copy-start(f32[232,512]{1,0:T(8,128)} %constant.32.clone.tab) | copy-start | bytes 1425412
  77.3 8.4 %collective-permute-start.28 = (f32[80,512]{1,0:T(8,128)S(1)}, f32[80,512]{1,0:T(8,128)S(1)}, u32[]{:S(2)}, u32[]{:S(2)}) collective-permute-start(f32[80,512]{1,0:T(8,128)S(1)} %correlate_part.1), channel_id=1, source_target_pairs={{0,4},{4,0},{8,12},{12,8},{16,20},{20,16},{24,28},{28,24},{1,5},{5... | collective-permute-start | bytes 491528 | tf_op jit(solution)/shard_map/ppermute | solution.py:574
  79.7 10.0 %collective-permute-start.20 = (bf16[1,256,512]{2,1,0:T(8,128)(2,1)S(1)}, bf16[1,256,512]{2,1,0:T(8,128)(2,1)S(1)}, u32[]{:S(2)}, u32[]{:S(2)}) collective-permute-start(bf16[1,256,512]{2,1,0:T(8,128)(2,1)S(1)} %get-tuple-element.60), channel_id=1, source_target_pairs={{0,4},{4,0},{8,12},{12,8},{16,20},{20,16},{24,28},{28,24},{1,5},{5... | collective-permute-start | bytes 786440 | tf_op jit(solution)/shard_map/ppermute | solution.py:574
  81.3 27.2 %collective-permute-start.13 = (bf16[128,512]{1,0:T(8,128)(2,1)S(1)}, bf16[128,512]{1,0:T(8,128)(2,1)S(1)}, u32[]{:S(2)}, u32[]{:S(2)}) collective-permute-start(bf16[128,512]{1,0:T(8,128)(2,1)S(1)} %get-tuple-element.46), channel_id=1, source_target_pairs={{0,1},{1,0},{2,3},{3,2},{4,5},{5,4},{6,7},{7,6},{8,9},{9,8},{10,11... | collective-permute-start | bytes 393224 | tf_op jit(solution)/shard_map/ppermute | solution.py:574
  81.3 14.0 %collective-permute-start.22 = (bf16[1,256,512]{2,1,0:T(8,128)(2,1)S(1)}, bf16[1,256,512]{2,1,0:T(8,128)(2,1)S(1)}, u32[]{:S(2)}, u32[]{:S(2)}) collective-permute-start(bf16[1,256,512]{2,1,0:T(8,128)(2,1)S(1)} %get-tuple-element.62), channel_id=1, source_target_pairs={{0,4},{4,0},{8,12},{12,8},{16,20},{20,16},{24,28},{28,24},{1,5},{5... | collective-permute-start | bytes 786440 | tf_op jit(solution)/shard_map/ppermute | solution.py:574
  81.8 23.3 %collective-permute-start.19 = (bf16[2,256,512]{2,1,0:T(8,128)(2,1)S(1)}, bf16[2,256,512]{2,1,0:T(8,128)(2,1)S(1)}, u32[]{:S(2)}, u32[]{:S(2)}) collective-permute-start(bf16[2,256,512]{2,1,0:T(8,128)(2,1)S(1)} %get-tuple-element.58), channel_id=1, source_target_pairs={{0,4},{4,0},{8,12},{12,8},{16,20},{20,16},{24,28},{28,24},{1,5},{5... | collective-permute-start | bytes 1572872 | tf_op jit(solution)/shard_map/ppermute | solution.py:574
  85.7 64.7 %collective-permute-start.16 = (bf16[128,2048]{1,0:T(8,128)(2,1)S(1)}, bf16[128,2048]{1,0:T(8,128)(2,1)S(1)}, u32[]{:S(2)}, u32[]{:S(2)}) collective-permute-start(bf16[128,2048]{1,0:T(8,128)(2,1)S(1)} %get-tuple-element.54), channel_id=1, source_target_pairs={{0,1},{1,0},{2,3},{3,2},{4,5},{5,4},{6,7},{7,6},{8,9},{9,8},{10,11... | collective-permute-start | bytes 1572872 | tf_op jit(solution)/shard_map/ppermute | solution.py:574
  89.7 15.8 %collective-permute-start.17 = (bf16[128,2048]{1,0:T(8,128)(2,1)S(1)}, bf16[128,2048]{1,0:T(8,128)(2,1)S(1)}, u32[]{:S(2)}, u32[]{:S(2)}) collective-permute-start(bf16[128,2048]{1,0:T(8,128)(2,1)S(1)} %get-tuple-element.56), channel_id=1, source_target_pairs={{0,1},{1,0},{2,3},{3,2},{4,5},{5,4},{6,7},{7,6},{8,9},{9,8},{10,11... | collective-permute-start | bytes 1572872 | tf_op jit(solution)/shard_map/ppermute | solution.py:574
  95.3 14.5 %collective-permute-start.21 = (bf16[256,512]{1,0:T(8,128)(2,1)S(1)}, bf16[256,512]{1,0:T(8,128)(2,1)S(1)}, u32[]{:S(2)}, u32[]{:S(2)}) collective-permute-start(bf16[256,512]{1,0:T(8,128)(2,1)S(1)} %fusion.5), channel_id=1, source_target_pairs={{0,24},{4,28},{8,16},{12,20},{16,8},{20,12},{24,0},{28,4},{1,25},{... | collective-permute-start | bytes 786440 | tf_op jit(solution)/shard_map/ppermute | solution.py:574
  105.1 15.1 %collective-permute-start.23 = (bf16[256,512]{1,0:T(8,128)(2,1)S(1)}, bf16[256,512]{1,0:T(8,128)(2,1)S(1)}, u32[]{:S(2)}, u32[]{:S(2)}) collective-permute-start(bf16[256,512]{1,0:T(8,128)(2,1)S(1)} %fusion.6), channel_id=1, source_target_pairs={{0,16},{4,20},{8,24},{12,28},{16,0},{20,4},{24,8},{28,12},{1,17},{... | collective-permute-start | bytes 786440 | tf_op jit(solution)/shard_map/ppermute | solution.py:574
  105.6 14.7 %collective-permute-start.24 = (bf16[256,512]{1,0:T(8,128)(2,1)S(1)}, bf16[256,512]{1,0:T(8,128)(2,1)S(1)}, u32[]{:S(2)}, u32[]{:S(2)}) collective-permute-start(bf16[256,512]{1,0:T(8,128)(2,1)S(1)} %fusion.7), channel_id=1, source_target_pairs={{0,8},{4,12},{8,0},{12,4},{16,24},{20,28},{24,16},{28,20},{1,9},{5... | collective-permute-start | bytes 786440 | tf_op jit(solution)/shard_map/ppermute | solution.py:574
  108.5 13.0 %collective-permute-start.31 = (bf16[80,512]{1,0:T(8,128)(2,1)S(1)}, bf16[80,512]{1,0:T(8,128)(2,1)S(1)}, u32[]{:S(2)}, u32[]{:S(2)}) collective-permute-start(bf16[80,512]{1,0:T(8,128)(2,1)S(1)} %add_convert_fusion.8), channel_id=1, source_target_pairs={{0,24},{4,28},{8,16},{12,20},{16,8},{20,12},{24,0},{28,4},{1,25},{... | collective-permute-start | bytes 245768 | tf_op jit(solution)/shard_map/ppermute | solution.py:574
  109.9 15.6 %collective-permute-start.30 = (bf16[80,512]{1,0:T(8,128)(2,1)S(1)}, bf16[80,512]{1,0:T(8,128)(2,1)S(1)}, u32[]{:S(2)}, u32[]{:S(2)}) collective-permute-start(bf16[80,512]{1,0:T(8,128)(2,1)S(1)} %add_convert_fusion.8), channel_id=1, source_target_pairs={{0,16},{4,20},{8,24},{12,28},{16,0},{20,4},{24,8},{28,12},{1,17},{... | collective-permute-start | bytes 245768 | tf_op jit(solution)/shard_map/ppermute | solution.py:574
  120.3 6.0 %collective-permute-start.29 = (bf16[80,512]{1,0:T(8,128)(2,1)S(1)}, bf16[80,512]{1,0:T(8,128)(2,1)S(1)}, u32[]{:S(2)}, u32[]{:S(2)}) collective-permute-start(bf16[80,512]{1,0:T(8,128)(2,1)S(1)} %add_convert_fusion.8), channel_id=1, source_target_pairs={{0,8},{4,12},{8,0},{12,4},{16,24},{20,28},{24,16},{28,20},{1,9},{5... | collective-permute-start | bytes 245768 | tf_op jit(solution)/shard_map/ppermute | solution.py:574
  120.3 30.1 %collective-permute-start.18 = (bf16[128,2048]{1,0:T(8,128)(2,1)S(1)}, bf16[128,2048]{1,0:T(8,128)(2,1)S(1)}, u32[]{:S(2)}, u32[]{:S(2)}) collective-permute-start(bf16[128,2048]{1,0:T(8,128)(2,1)S(1)} %add_convert_fusion.1), channel_id=1, source_target_pairs={{0,2},{1,3},{2,0},{3,1},{4,6},{5,7},{6,4},{7,5},{8,10},{9,11},{10,... | collective-permute-start | bytes 1572872 | tf_op jit(solution)/shard_map/ppermute | solution.py:574
  121.5 16.4 %collective-permute-start.14 = (bf16[128,512]{1,0:T(8,128)(2,1)S(1)}, bf16[128,512]{1,0:T(8,128)(2,1)S(1)}, u32[]{:S(2)}, u32[]{:S(2)}) collective-permute-start(bf16[128,512]{1,0:T(8,128)(2,1)S(1)} %get-tuple-element.47), channel_id=1, source_target_pairs={{0,2},{1,3},{2,0},{3,1},{4,6},{5,7},{6,4},{7,5},{8,10},{9,11},{10,... | collective-permute-start | bytes 393224 | tf_op jit(solution)/shard_map/ppermute | solution.py:574
  125.5 13.7 %collective-permute-start.15 = (bf16[128,512]{1,0:T(8,128)(2,1)S(1)}, bf16[128,512]{1,0:T(8,128)(2,1)S(1)}, u32[]{:S(2)}, u32[]{:S(2)}) collective-permute-start(bf16[128,512]{1,0:T(8,128)(2,1)S(1)} %get-tuple-element.48), channel_id=1, source_target_pairs={{0,3},{1,2},{2,1},{3,0},{4,7},{5,6},{6,5},{7,4},{8,11},{9,10},{10,... | collective-permute-start | bytes 393224 | tf_op jit(solution)/shard_map/ppermute | solution.py:574
  126.3 24.0 %collective-permute-start.26 = (bf16[256,512]{1,0:T(8,128)(2,1)S(1)}, bf16[256,512]{1,0:T(8,128)(2,1)S(1)}, u32[]{:S(2)}, u32[]{:S(2)}) collective-permute-start(bf16[256,512]{1,0:T(8,128)(2,1)S(1)} %fusion.3.refs_0_), channel_id=1, source_target_pairs={{0,2},{1,3},{2,0},{3,1},{4,6},{5,7},{6,4},{7,5},{8,10},{9,11},{10,... | collective-permute-start | bytes 786440 | tf_op jit(solution)/shard_map/ppermute | solution.py:574
  137.9 9.1 %collective-permute-start.33 = (bf16[80,512]{1,0:T(8,128)(2,1)S(1)}, bf16[80,512]{1,0:T(8,128)(2,1)S(1)}, u32[]{:S(2)}, u32[]{:S(2)}) collective-permute-start(bf16[80,512]{1,0:T(8,128)(2,1)S(1)} %add_convert_fusion.7.refs_0_), channel_id=1, source_target_pairs={{0,2},{1,3},{2,0},{3,1},{4,6},{5,7},{6,4},{7,5},{8,10},{9,11},{10,... | collective-permute-start | bytes 245768 | tf_op jit(solution)/shard_map/ppermute | solution.py:574
  139.2 9.2 %collective-permute-start.32 = (bf16[80,512]{1,0:T(8,128)(2,1)S(1)}, bf16[80,512]{1,0:T(8,128)(2,1)S(1)}, u32[]{:S(2)}, u32[]{:S(2)}) collective-permute-start(bf16[80,512]{1,0:T(8,128)(2,1)S(1)} %add_convert_fusion.7.refs_0_), channel_id=1, source_target_pairs={{0,1},{1,0},{2,3},{3,2},{4,5},{5,4},{6,7},{7,6},{8,9},{9,8},{10,11... | collective-permute-start | bytes 245768 | tf_op jit(solution)/shard_map/ppermute | solution.py:574
  147.0 1.4 collective-permute-start.34
  149.8 1.7 %collective-permute-start.25 = (bf16[256,512]{1,0:T(8,128)(2,1)S(1)}, bf16[256,512]{1,0:T(8,128)(2,1)S(1)}, u32[]{:S(2)}, u32[]{:S(2)}) collective-permute-start(bf16[256,512]{1,0:T(8,128)(2,1)S(1)} %fusion.3.refs_0_), channel_id=1, source_target_pairs={{0,1},{1,0},{2,3},{3,2},{4,5},{5,4},{6,7},{7,6},{8,9},{9,8},{10,11... | collective-permute-start | bytes 786440 | tf_op jit(solution)/shard_map/ppermute | solution.py:574
  150.3 1.5 collective-permute-start.27

commit v3 on v2

--- a/solution.py
+++ b/solution.py
@@ -103,13 +103,26 @@
     emb_count, order = pos_weight.shape
     starts = constant_rows(length)
 
-    def body(
-        place_ref, tab, pw, pb, fw, vec, ah, al, th, spec, env_out, hidden_out, cos_out, filt,
-    ):
+    def body(place_ref, *refs):
+        sources = refs[:5]
+        ah, al, th, spec, env_out, hidden_out, cos_out, rows_out, filt, *held, done = refs[5:]
+        tab, pw, pb, fw, vec = held
         step = pl.program_id(0)
 
         @pl.when(step == 0)
         def _():
+            mine = pl.ds(pl.multiple_of(place_ref[0] * width, width), width)
+            copies = [
+                pltpu.make_async_copy(
+                    source if i < 3 else source.at[:, mine], target, done.at[i]
+                )
+                for i, (source, target) in enumerate(zip(sources, held))
+            ]
+            for copy in copies:
+                copy.start()
+            for copy in copies:
+                copy.wait()
+            rows_out[...] = vec[...]
             feat = tab[starts[8] : starts[8] + emb_count, :]
             pre = pb[...] + lax.dot_general(
                 feat, pw[...], (((0,), (0,)), ((), ())), precision=highest,
@@ -153,27 +166,36 @@
         spec[1] = to_spectrum(ah, al, 1, filt[...])
 
     by_row = pl.BlockSpec((2, block, length), lambda i, *_: (0, i, 0))
-    cols = lambda n: pl.BlockSpec((n, width), lambda i, place_ref: (0, place_ref[0]))
     return pl.pallas_call(
         body,
         grid_spec=pltpu.PrefetchScalarGridSpec(
             num_scalar_prefetch=1,
             grid=(length // block,),
-            in_specs=[whole(table.shape), whole(pos_weight.shape), whole(pos_bias.shape)]
-            + [cols(order), cols(rows_of.shape[0])],
+            in_specs=[pl.BlockSpec(memory_space=pltpu.HBM)] * 5,
             out_specs=[by_row, by_row, by_row, spectrum_block(width, block)]
-            + [whole((length, width)), whole((length, order)), whole((length, order))],
-            scratch_shapes=[VMEM((length, width), bf16)],
+            + [whole((length, width)), whole((length, order)), whole((length, order))]
+            + [whole((rows_of.shape[0], width))],
+            scratch_shapes=[VMEM((length, width), bf16)]
+            + [VMEM(x.shape, f32) for x in (table, pos_weight, pos_bias)]
+            + [VMEM((order, width), f32), VMEM((rows_of.shape[0], width), f32)]
+            + [pltpu.SemaphoreType.DMA((5,))],
         ),
         out_shape=[struct((2, length, length), bf16)] * 3
         + [struct((2, length, width), f32), struct((length, width), f32)]
-        + [struct((length, order), f32)] * 2,
+        + [struct((length, order), f32)] * 2
+        + [struct((rows_of.shape[0], width), f32)],
         name="generate",
         compiler_params=grant(
             [((6, block, length), 2), ((4, block, width), 4), ((2, length, width), 4)]
             + [(table.shape, 4)], length, width
         ),
-    )(place, table, pos_weight, pos_bias, filter_weight, rows_of)
+    )(
+        place,
+        *[
+            pltpu.with_memory_space_constraint(x, pltpu.HBM)
+            for x in (table, pos_weight, pos_bias, filter_weight, rows_of)
+        ],
+    )
 
 
 def piece(place_ref, r, rows):
@@ -230,7 +252,7 @@
             in_specs=[cols] * count
             + [whole((local_len, width))] * count
             + [spectrum_block(width, block), by_row, by_row, by_col]
-            + [pl.BlockSpec((3, width), lambda i, place_ref: (0, place_ref[0]))],
+            + [whole(rows_of.shape)],
             out_specs=[
                 spectrum_block(width, block),
                 whole((length, width)),
@@ -385,7 +407,7 @@
                 by_row,
                 by_row,
                 by_col,
-                pl.BlockSpec((3, width), lambda i, place_ref: (0, place_ref[0])),
+                whole(rows_of.shape),
             ],
             out_specs=[whole((length, width)), spec_block],
             scratch_shapes=[VMEM((length, width), f32)],
@@ -626,7 +648,7 @@
     rates = decay_rate[None]
     norm = jnp.sqrt(jnp.expm1(-2.0 * rates * length) / jnp.expm1(-2.0 * rates))
     rows_of = jnp.concatenate([rates, norm, skip_gain[None]])
-    a_high, a_low, t_high, filt_spec, env, hidden, cos_pre = generate(
+    a_high, a_low, t_high, filt_spec, env, hidden, cos_pre, rows_of = generate(
         place, table, pos_weight, pos_bias[None], filter_weight, rows_of, width, block
     )
     tables = (a_high, a_low, t_high)

time: 154 us -> 153 us (level)
  local copies, waits for them, and re-layouts: 9.29 us -> 5.85 us
  starting transfers between devices: 32.2 us -> 35.5 us
  waiting for transfers between devices: 79.4 us -> 76.3 us
    unnamed x28 -> x20, local copies, waits for them, and re-layouts: 8.14 us -> 4.7 us
    ppermute x35, starting transfers between devices: 32.2 us -> 35.5 us  [swap(): return lax.ppermute(value, axis, [(i, i ^ offset) for i in range(count)])]
    ppermute x35, waiting for transfers between devices: 79.4 us -> 76.3 us  [swap(): return lax.ppermute(value, axis, [(i, i ^ offset) for i in range(count)])]
  transfers between devices with their start and end apart: 35 -> 35, of which waited for: 13 -> 14; matrix products, arithmetic and copies ran while one was open for 3% -> 3% of each run, Pallas kernels for 11% -> 12%
where the time goes in v3:
time: 153 us; the launch traced here: 152 us
  waiting for transfers between devices  76.3 us (50%)
  starting transfers between devices  35.5 us (23%)
  Pallas kernels  30 us (20%)
  local copies, waits for them, and re-layouts  5.85 us (4%)
  other arithmetic  3.78 us (2%)
    ppermute x35, waiting for transfers between devices, swap(): return lax.ppermute(value, axis, [(i, i ^ offset) for i in range(count)])  76.3 us
    ppermute x35, starting transfers between devices, swap(): return lax.ppermute(value, axis, [(i, i ^ offset) for i in range(count)])  35.5 us
    pallas_call x1, Pallas kernels, generate(): pl.pallas_call(body, grid_spec=pltpu.PrefetchScalarGridSpec(num_scalar_pr...  7.03 us
    unnamed x20, local copies, waits for them, and re-layouts  4.7 us
    pallas_call x1, Pallas kernels, convolve(): pl.pallas_call(body, grid_spec=pltpu.PrefetchScalarGridSpec(num_scalar_pr...  4.15 us
    pallas_call x1, Pallas kernels, correlate_back(): pl.pallas_call(body, grid_spec=pltpu.PrefetchScalarGridSpec(num_scalar_pr...  3.8 us
    pallas_call x1, Pallas kernels, correlate_part(): pl.pallas_call(body, grid_spec=pltpu.PrefetchScalarGridSpec(num_scalar_pr...  3.66 us
    pallas_call x2, Pallas kernels, assemble(): pl.pallas_call(body, in_specs=[smem()] + [pl.BlockSpec(memory_space=VMEM)...  3.37 us
  transfers between devices with their start and end apart: 35, of which 14 were waited for; matrix products, arithmetic and copies ran while one was open for 3% of the time, Pallas kernels for 12%

profile of v3, /device:TPU:0, one launch (start us, length us, event | category | flops | bytes accessed | tf_op | source)
XLA Modules:
  0.0 152.4 jit_solution(14366477877160026467)
XLA Ops:
  0.7 3.0 %collective-permute-start.1 = (bf16[128,2048]{1,0:T(8,128)(2,1)}, bf16[128,2048]{1,0:T(8,128)(2,1)S(1)}, u32[]{:S(2)}, u32[]{:S(2)}) collective-permute-start(bf16[128,2048]{1,0:T(8,128)(2,1)} %bitcast.31), channel_id=1, source_target_pairs={{0,2},{1,3},{2,0},{3,1},{4,6},{5,7},{6,4},{7,5},{8,10},{9,11},{10,... | collective-permute-start | bytes 1572872 | tf_op jit(solution)/shard_map/ppermute | solution.py:596
  3.7 1.1 dynamic-slice_bitcast_fusion
  4.8 0.3 collective-permute-start.12
  5.1 0.4 collective-permute-start.10
  5.5 1.6 %collective-permute-start.11 = (bf16[128,512]{1,0:T(8,128)(2,1)S(1)}, bf16[128,512]{1,0:T(8,128)(2,1)S(1)}, u32[]{:S(2)}, u32[]{:S(2)}) collective-permute-start(bf16[128,512]{1,0:T(8,128)(2,1)S(1)} %get-tuple-element.78), channel_id=1, source_target_pairs={{0,2},{1,3},{2,0},{3,1},{4,6},{5,7},{6,4},{7,5},{8,10},{9,11},{10,... | collective-permute-start | bytes 393224 | tf_op jit(solution)/shard_map/ppermute | solution.py:596
  7.1 12.0 %collective-permute-done.12.refs_7_.refs_15_ = bf16[128,512]{1,0:T(8,128)(2,1)S(1)} collective-permute-done((bf16[128,512]{1,0:T(8,128)(2,1)S(1)}, bf16[128,512]{1,0:T(8,128)(2,1)S(1)}, u32[]{:S(2)}, u32[]{:S(2)}) %collective-permute-start.12) | collective-permute-done | bytes 131104 | tf_op jit(solution)/shard_map/ppermute | solution.py:596
  19.0 0.7 copy-done.4
  19.7 3.6 %collective-permute-start.8 = (bf16[256,512]{1,0:T(8,128)(2,1)S(1)}, bf16[256,512]{1,0:T(8,128)(2,1)S(1)}, u32[]{:S(2)}, u32[]{:S(2)}) collective-permute-start(bf16[256,512]{1,0:T(8,128)(2,1)S(1)} %constant_dynamic-slice_fusion.refs_4_.refs_1_), channel_id=1, source_target_pairs={{0,24},{4,28},{8,16},{12,20},{16,8},{20,12},{24,0},{28,4},{1,25},{... | collective-permute-start | bytes 786440 | tf_op jit(solution)/shard_map/ppermute | solution.py:596
  23.3 0.7 copy-done.6
  23.9 0.7 copy-done.8
  24.6 0.8 collective-permute-start.4
  25.4 0.7 divide_sqrt_fusion
  26.1 4.7 %collective-permute-done.8.refs_10_.refs_7_ = bf16[256,512]{1,0:T(8,128)(2,1)S(1)} collective-permute-done((bf16[256,512]{1,0:T(8,128)(2,1)S(1)}, bf16[256,512]{1,0:T(8,128)(2,1)S(1)}, u32[]{:S(2)}, u32[]{:S(2)}) %collective-permute-start.8) | collective-permute-done | bytes 262176 | tf_op jit(solution)/shard_map/ppermute | solution.py:596
  30.8 1.5 collective-permute-start.3
  32.3 14.2 %collective-permute-done.6.refs_8_.refs_5_ = bf16[256,512]{1,0:T(8,128)(2,1)S(1)} collective-permute-done((bf16[256,512]{1,0:T(8,128)(2,1)S(1)}, bf16[256,512]{1,0:T(8,128)(2,1)S(1)}, u32[]{:S(2)}, u32[]{:S(2)}) %collective-permute-start.6) | collective-permute-done | bytes 262176 | tf_op jit(solution)/shard_map/ppermute | solution.py:596
  46.6 1.5 collective-permute-start.9
  48.1 0.5 collective-permute-start.7
  48.6 1.5 collective-permute-start.5
  50.1 0.1 pad_add_fusion.place_ref
  50.2 1.4 pad_maximum_fusion.refs_4_
  51.6 7.0 %generate.1 = (bf16[2,512,512]{2,1,0:T(8,128)(2,1)S(1)}, bf16[2,512,512]{2,1,0:T(8,128)(2,1)S(1)}, bf16[2,512,512]{2,1,0:T(8,128)(2,1)S(1)}, f32[2,512,512]{2,1,...) custom-call(s32[2]{0:T(128)S(1)} %pad_add_fusion.place_ref, ...), custom_call_target="tpu_custom_call" | custom-call | tf_op jit(solution)/shard_map/generate/pallas_call | solution.py:169
  58.6 0.9 copy-done.5
  59.5 0.9 copy-done.7
  60.4 0.9 copy-done.9
  61.3 4.1 %convolve.1 = (f32[2,512,512]{2,1,0:T(8,128)S(1)}, f32[512,512]{1,0:T(8,128)S(1)}, bf16[512,512]{1,0:T(8,128)(2,1)S(1)}) custom-call(s32[2]{0:T(128)S(1)} %pad_add_fusion.place_ref, bf16[128,2048]{1,0:T(8,128)(2,1)S(1)} %bitcast.33, bf16[128,2048]{1,0:T(8,128)(2,1)S(1)} %collective-permute-done.refs_1_, ...), custom_call_target="tpu_custom_call" | custom-call | tf_op jit(solution)/shard_map/convolve/pallas_call | solution.py:247
  65.5 0.4 collective-permute-done.5.refs_7_.refs_4_
  66.0 2.5 %gating.1 = (bf16[128,512]{1,0:T(8,128)(2,1)S(1)}, bf16[128,512]{1,0:T(8,128)(2,1)S(1)}, bf16[128,512]{1,0:T(8,128)(2,1)S(1)}, bf16[128,512]{1,0:T(8,128)(2,1)S(...) custom-call(s32[2]{0:T(128)S(1)} %pad_add_fusion.place_ref, ...), custom_call_target="tpu_custom_call" | custom-call | tf_op jit(solution)/shard_map/gating/pallas_call | solution.py:350
  68.5 3.8 %correlate_back.1 = (f32[512,512]{1,0:T(8,128)S(1)}, f32[2,512,512]{2,1,0:T(8,128)S(1)}) custom-call(s32[2]{0:T(128)S(1)} %pad_add_fusion.place_ref, bf16[512,512]{1,0:T(8,128)(2,1)S(1)} %get-tuple-element.52.cg, f32[512,512]{1,0:T(8,128)S(1)} %get-tuple-element.53.ig, f32[2,512,512]{2,1,0:T(8,128)S(1)} %get-tuple-element.41.refs_8_.fs, ...), custom_call_target="tpu_custom_call" | custom-call | tf_op jit(solution)/shard_map/correlate_back/pallas_call | solution.py:398
  72.3 3.7 %correlate_part.1 = f32[80,512]{1,0:T(8,128)S(1)} custom-call(s32[2]{0:T(128)S(1)} %pad_add_fusion.place_ref, f32[2,512,512]{2,1,0:T(8,128)S(1)} %get-tuple-element.65.gs, f32[8,512]{1,0:T(8,128)S(1)} %get-tuple-element.66.skip_sum_ref, f32[2,512,512]{2,1,0:T(8,128)S(1)} %get-tuple-element.67.ss, bf16[2,512,512]{2,1,0:T(8,128)(2,1)S(1)} %get-tuple-element.44.refs_11_.th, ...), custom_call_target="tpu_custom_call" | custom-call | tf_op jit(solution)/shard_map/correlate_part/pallas_call | solution.py:465
  76.0 1.6 %collective-permute-start.28 = (f32[80,512]{1,0:T(8,128)S(1)}, f32[80,512]{1,0:T(8,128)S(1)}, u32[]{:S(2)}, u32[]{:S(2)}) collective-permute-start(f32[80,512]{1,0:T(8,128)S(1)} %correlate_part.1), channel_id=1, source_target_pairs={{0,4},{4,0},{8,12},{12,8},{16,20},{20,16},{24,28},{28,24},{1,5},{5... | collective-permute-start | bytes 491528 | tf_op jit(solution)/shard_map/ppermute | solution.py:596
  77.6 1.8 %weight_grads.1 = (bf16[1,256,512]{2,1,0:T(8,128)(2,1)S(1)}, bf16[1,256,512]{2,1,0:T(8,128)(2,1)S(1)}, bf16[2,256,512]{2,1,0:T(8,128)(2,1)S(1)}, bf16[1,256,512]...) custom-call(s32[2]{0:T(128)S(1)} %pad_add_fusion.place_ref, ...), custom_call_target="tpu_custom_call" | custom-call | tf_op jit(solution)/shard_map/weight_grads/pallas_call | solution.py:307
  79.4 0.6 collective-permute-start.20
  80.0 1.5 collective-permute-start.22
  81.5 0.5 collective-permute-start.19
  82.0 2.3 %through_gate.1 = (bf16[128,2048]{1,0:T(8,128)(2,1)S(1)}, bf16[128,2048]{1,0:T(8,128)(2,1)S(1)}, bf16[128,2048]{1,0:T(8,128)(2,1)S(1)}, bf16[128,2048]{1,0:T(8,128)(2,1)S(1)}) custom-call(s32[2]{0:T(128)S(1)} %pad_add_fusion.place_ref, bf16[512,512]{1,0:T(8,128)(2,1)S(1)} %get-tuple-element.51.refs_0_.refs_4_, ...), custom_call_target="tpu_custom_call" | custom-call | tf_op jit(solution)/shard_map/through_gate/pallas_call | solution.py:522
  84.4 0.1 collective-permute-start.16
  84.5 4.2 %collective-permute-done.20 = bf16[1,256,512]{2,1,0:T(8,128)(2,1)S(1)} collective-permute-done((bf16[1,256,512]{2,1,0:T(8,128)(2,1)S(1)}, bf16[1,256,512]{2,1,0:T(8,128)(2,1)S(1)}, u32[]{:S(2)}, u32[]{:S(2)}) %collective-permute-start.20) | collective-permute-done | bytes 262176 | tf_op jit(solution)/shard_map/ppermute | solution.py:596
  88.7 5.5 %collective-permute-done.22 = bf16[1,256,512]{2,1,0:T(8,128)(2,1)S(1)} collective-permute-done((bf16[1,256,512]{2,1,0:T(8,128)(2,1)S(1)}, bf16[1,256,512]{2,1,0:T(8,128)(2,1)S(1)}, u32[]{:S(2)}, u32[]{:S(2)}) %collective-permute-start.22) | collective-permute-done | bytes 262176 | tf_op jit(solution)/shard_map/ppermute | solution.py:596
  94.3 2.5 %collective-permute-start.21 = (bf16[256,512]{1,0:T(8,128)(2,1)S(1)}, bf16[256,512]{1,0:T(8,128)(2,1)S(1)}, u32[]{:S(2)}, u32[]{:S(2)}) collective-permute-start(bf16[256,512]{1,0:T(8,128)(2,1)S(1)} %fusion.5), channel_id=1, source_target_pairs={{0,24},{4,28},{8,16},{12,20},{16,8},{20,12},{24,0},{28,4},{1,25},{... | collective-permute-start | bytes 786440 | tf_op jit(solution)/shard_map/ppermute | solution.py:596
  96.8 7.0 %collective-permute-done.19 = bf16[2,256,512]{2,1,0:T(8,128)(2,1)S(1)} collective-permute-done((bf16[2,256,512]{2,1,0:T(8,128)(2,1)S(1)}, bf16[2,256,512]{2,1,0:T(8,128)(2,1)S(1)}, u32[]{:S(2)}, u32[]{:S(2)}) %collective-permute-start.19) | collective-permute-done | bytes 524320 | tf_op jit(solution)/shard_map/ppermute | solution.py:596
  103.8 1.7 %collective-permute-start.23 = (bf16[256,512]{1,0:T(8,128)(2,1)S(1)}, bf16[256,512]{1,0:T(8,128)(2,1)S(1)}, u32[]{:S(2)}, u32[]{:S(2)}) collective-permute-start(bf16[256,512]{1,0:T(8,128)(2,1)S(1)} %fusion.6), channel_id=1, source_target_pairs={{0,16},{4,20},{8,24},{12,28},{16,0},{20,4},{24,8},{28,12},{1,17},{... | collective-permute-start | bytes 786440 | tf_op jit(solution)/shard_map/ppermute | solution.py:596
  105.6 1.4 collective-permute-start.24
  107.0 0.2 add_convert_fusion.1
  107.2 1.4 collective-permute-start.31
  108.6 0.8 collective-permute-start.30
  109.4 9.6 %collective-permute-done.23 = bf16[256,512]{1,0:T(8,128)(2,1)S(1)} collective-permute-done((bf16[256,512]{1,0:T(8,128)(2,1)S(1)}, bf16[256,512]{1,0:T(8,128)(2,1)S(1)}, u32[]{:S(2)}, u32[]{:S(2)}) %collective-permute-start.23) | collective-permute-done | bytes 262176 | tf_op jit(solution)/shard_map/ppermute | solution.py:596
  119.0 2.3 %collective-permute-start.18 = (bf16[128,2048]{1,0:T(8,128)(2,1)S(1)}, bf16[128,2048]{1,0:T(8,128)(2,1)S(1)}, u32[]{:S(2)}, u32[]{:S(2)}) collective-permute-start(bf16[128,2048]{1,0:T(8,128)(2,1)S(1)} %add_convert_fusion.1), channel_id=1, source_target_pairs={{0,2},{1,3},{2,0},{3,1},{4,6},{5,7},{6,4},{7,5},{8,10},{9,11},{10,... | collective-permute-start | bytes 1572872 | tf_op jit(solution)/shard_map/ppermute | solution.py:596
  121.3 0.2 fusion.3.refs_0_
  121.5 1.5 collective-permute-start.14
  122.9 1.2 collective-permute-done.30
  124.2 0.3 collective-permute-start.15
  124.4 0.5 collective-permute-done.29
  124.9 1.7 %collective-permute-start.26 = (bf16[256,512]{1,0:T(8,128)(2,1)S(1)}, bf16[256,512]{1,0:T(8,128)(2,1)S(1)}, u32[]{:S(2)}, u32[]{:S(2)}) collective-permute-start(bf16[256,512]{1,0:T(8,128)(2,1)S(1)} %fusion.3.refs_0_), channel_id=1, source_target_pairs={{0,2},{1,3},{2,0},{3,1},{4,6},{5,7},{6,4},{7,5},{8,10},{9,11},{10,... | collective-permute-start | bytes 786440 | tf_op jit(solution)/shard_map/ppermute | solution.py:596
  126.7 10.1 %collective-permute-done.14.refs_2_ = bf16[128,512]{1,0:T(8,128)(2,1)S(1)} collective-permute-done((bf16[128,512]{1,0:T(8,128)(2,1)S(1)}, bf16[128,512]{1,0:T(8,128)(2,1)S(1)}, u32[]{:S(2)}, u32[]{:S(2)}) %collective-permute-start.14) | collective-permute-done | bytes 131104 | tf_op jit(solution)/shard_map/ppermute | solution.py:596
  136.9 2.0 %collective-permute-start.33 = (bf16[80,512]{1,0:T(8,128)(2,1)S(1)}, bf16[80,512]{1,0:T(8,128)(2,1)S(1)}, u32[]{:S(2)}, u32[]{:S(2)}) collective-permute-start(bf16[80,512]{1,0:T(8,128)(2,1)S(1)} %add_convert_fusion.7.refs_0_), channel_id=1, source_target_pairs={{0,2},{1,3},{2,0},{3,1},{4,6},{5,7},{6,4},{7,5},{8,10},{9,11},{10,... | collective-permute-start | bytes 245768 | tf_op jit(solution)/shard_map/ppermute | solution.py:596
  138.9 0.3 collective-permute-done.15.refs_3_
  139.2 0.3 collective-permute-start.32
  139.5 6.0 %collective-permute-done.33.refs_2_ = bf16[80,512]{1,0:T(8,128)(2,1)S(1)} collective-permute-done((bf16[80,512]{1,0:T(8,128)(2,1)S(1)}, bf16[80,512]{1,0:T(8,128)(2,1)S(1)}, u32[]{:S(2)}, u32[]{:S(2)}) %collective-permute-start.33) | collective-permute-done | bytes 81952 | tf_op jit(solution)/shard_map/ppermute | solution.py:596
  145.6 1.4 assemble.2
  146.9 1.4 finish.1
  148.3 0.5 collective-permute-start.25
  148.9 1.0 fusion
  150.0 0.4 collective-permute-done.27.refs_3_
  150.4 2.0 %assemble.3 = f32[256,2048]{1,0:T(8,128)} custom-call(s32[2]{0:T(128)S(1)} %pad_add_fusion.place_ref, bf16[256,512]{1,0:T(8,128)(2,1)S(1)} %fusion.3.refs_0_, bf16[256,512]{1,0:T(8,128)(2,1)S(1)} %collective-permute-done.25.refs_1_, bf16[256,512]{1,0:T(8,128)(2,1)S(1)} %collective-permute-done.26.refs_2_, bf16[256,512]{1,0:T(8,128)(2,1)S(1)} %collective-permute-done.27.refs_3_), custom_call_target="tpu_custom_call" | custom-call | tf_op jit(solution)/shard_map/assemble/pallas_call | solution.py:542
  (49 shorter events, 0.5 us)
Async XLA Ops:
  0.6 6.4 %copy-start = (bf16[256,2048]{1,0:T(8,128)(2,1)S(1)}, bf16[256,2048]{1,0:T(8,128)(2,1)}, u32[]{:S(2)}) copy-start(bf16[256,2048]{1,0:T(8,128)(2,1)} %param.10) | copy-start | bytes 3145732
  0.6 58.0 %copy-start.1 = (bf16[1,128,2048]{2,1,0:T(8,128)(2,1)S(1)}, bf16[1,128,2048]{2,1,0:T(8,128)(2,1)}, u32[]{:S(2)}) copy-start(bf16[1,128,2048]{2,1,0:T(8,128)(2,1)} %param.9) | copy-start | bytes 1572868
  0.7 24.7 %collective-permute-start.1 = (bf16[128,2048]{1,0:T(8,128)(2,1)}, bf16[128,2048]{1,0:T(8,128)(2,1)S(1)}, u32[]{:S(2)}, u32[]{:S(2)}) collective-permute-start(bf16[128,2048]{1,0:T(8,128)(2,1)} %bitcast.31), channel_id=1, source_target_pairs={{0,2},{1,3},{2,0},{3,1},{4,6},{5,7},{6,4},{7,5},{8,10},{9,11},{10,... | collective-permute-start | bytes 1572872 | tf_op jit(solution)/shard_map/ppermute | solution.py:596
  3.7 44.9 %collective-permute-start = (bf16[128,2048]{1,0:T(8,128)(2,1)}, bf16[128,2048]{1,0:T(8,128)(2,1)S(1)}, u32[]{:S(2)}, u32[]{:S(2)}) collective-permute-start(bf16[128,2048]{1,0:T(8,128)(2,1)} %bitcast.32), channel_id=1, source_target_pairs={{0,1},{1,0},{2,3},{3,2},{4,5},{5,4},{6,7},{7,6},{8,9},{9,8},{10,11... | collective-permute-start | bytes 1572872 | tf_op jit(solution)/shard_map/ppermute | solution.py:596
  4.8 14.2 %collective-permute-start.12 = (bf16[128,512]{1,0:T(8,128)(2,1)S(1)}, bf16[128,512]{1,0:T(8,128)(2,1)S(1)}, u32[]{:S(2)}, u32[]{:S(2)}) collective-permute-start(bf16[128,512]{1,0:T(8,128)(2,1)S(1)} %get-tuple-element.75), channel_id=1, source_target_pairs={{0,3},{1,2},{2,1},{3,0},{4,7},{5,6},{6,5},{7,4},{8,11},{9,10},{10,... | collective-permute-start | bytes 393224 | tf_op jit(solution)/shard_map/ppermute | solution.py:596
  5.1 18.2 %collective-permute-start.10 = (bf16[128,512]{1,0:T(8,128)(2,1)S(1)}, bf16[128,512]{1,0:T(8,128)(2,1)S(1)}, u32[]{:S(2)}, u32[]{:S(2)}) collective-permute-start(bf16[128,512]{1,0:T(8,128)(2,1)S(1)} %get-tuple-element.76), channel_id=1, source_target_pairs={{0,1},{1,0},{2,3},{3,2},{4,5},{5,4},{6,7},{7,6},{8,9},{9,8},{10,11... | collective-permute-start | bytes 393224 | tf_op jit(solution)/shard_map/ppermute | solution.py:596
  5.5 18.5 %collective-permute-start.11 = (bf16[128,512]{1,0:T(8,128)(2,1)S(1)}, bf16[128,512]{1,0:T(8,128)(2,1)S(1)}, u32[]{:S(2)}, u32[]{:S(2)}) collective-permute-start(bf16[128,512]{1,0:T(8,128)(2,1)S(1)} %get-tuple-element.78), channel_id=1, source_target_pairs={{0,2},{1,3},{2,0},{3,1},{4,6},{5,7},{6,4},{7,5},{8,10},{9,11},{10,... | collective-permute-start | bytes 393224 | tf_op jit(solution)/shard_map/ppermute | solution.py:596
  19.0 0.7 copy-start.4
  19.7 11.1 %collective-permute-start.8 = (bf16[256,512]{1,0:T(8,128)(2,1)S(1)}, bf16[256,512]{1,0:T(8,128)(2,1)S(1)}, u32[]{:S(2)}, u32[]{:S(2)}) collective-permute-start(bf16[256,512]{1,0:T(8,128)(2,1)S(1)} %constant_dynamic-slice_fusion.refs_4_.refs_1_), channel_id=1, source_target_pairs={{0,24},{4,28},{8,16},{12,20},{16,8},{20,12},{24,0},{28,4},{1,25},{... | collective-permute-start | bytes 786440 | tf_op jit(solution)/shard_map/ppermute | solution.py:596
  23.3 0.7 copy-start.6
  23.9 22.6 %collective-permute-start.6 = (bf16[256,512]{1,0:T(8,128)(2,1)S(1)}, bf16[256,512]{1,0:T(8,128)(2,1)S(1)}, u32[]{:S(2)}, u32[]{:S(2)}) collective-permute-start(bf16[256,512]{1,0:T(8,128)(2,1)S(1)} %constant_dynamic-slice_fusion.refs_4_.refs_1_), channel_id=1, source_target_pairs={{0,16},{4,20},{8,24},{12,28},{16,0},{20,4},{24,8},{28,12},{1,17},{... | collective-permute-start | bytes 786440 | tf_op jit(solution)/shard_map/ppermute | solution.py:596
  23.9 0.7 copy-start.8
  24.6 23.5 %collective-permute-start.4 = (bf16[256,512]{1,0:T(8,128)(2,1)S(1)}, bf16[256,512]{1,0:T(8,128)(2,1)}, u32[]{:S(2)}, u32[]{:S(2)}) collective-permute-start(bf16[256,512]{1,0:T(8,128)(2,1)S(1)} %constant_dynamic-slice_fusion.refs_4_.refs_1_), channel_id=1, source_target_pairs={{0,8},{4,12},{8,0},{12,4},{16,24},{20,28},{24,16},{28,20},{1,9},{5... | collective-permute-start | bytes 786440 | tf_op jit(solution)/shard_map/ppermute | solution.py:596
  25.4 33.2 %collective-permute-start.2 = (bf16[128,2048]{1,0:T(8,128)(2,1)S(1)}, bf16[128,2048]{1,0:T(8,128)(2,1)S(1)}, u32[]{:S(2)}, u32[]{:S(2)}) collective-permute-start(bf16[128,2048]{1,0:T(8,128)(2,1)S(1)} %collective-permute-done.1.refs_2_), channel_id=1, source_target_pairs={{0,1},{1,0},{2,3},{3,2},{4,5},{5,4},{6,7},{7,6},{8,9},{9,8},{10,11... | collective-permute-start | bytes 1572872 | tf_op jit(solution)/shard_map/ppermute | solution.py:596
  30.8 34.7 %collective-permute-start.3 = (bf16[256,512]{1,0:T(8,128)(2,1)S(1)}, bf16[256,512]{1,0:T(8,128)(2,1)S(1)}, u32[]{:S(2)}, u32[]{:S(2)}) collective-permute-start(bf16[256,512]{1,0:T(8,128)(2,1)S(1)} %constant_dynamic-slice_fusion.refs_4_.refs_1_), channel_id=1, source_target_pairs={{0,4},{4,0},{8,12},{12,8},{16,20},{20,16},{24,28},{28,24},{1,5},{5... | collective-permute-start | bytes 786440 | tf_op jit(solution)/shard_map/ppermute | solution.py:596
  46.6 18.9 %collective-permute-start.9 = (bf16[256,512]{1,0:T(8,128)(2,1)S(1)}, bf16[256,512]{1,0:T(8,128)(2,1)S(1)}, u32[]{:S(2)}, u32[]{:S(2)}) collective-permute-start(bf16[256,512]{1,0:T(8,128)(2,1)S(1)} %collective-permute-done.8.refs_10_.refs_7_), channel_id=1, source_target_pairs={{0,4},{4,0},{8,12},{12,8},{16,20},{20,16},{24,28},{28,24},{1,5},{5... | collective-permute-start | bytes 786440 | tf_op jit(solution)/shard_map/ppermute | solution.py:596
  48.1 17.4 %collective-permute-start.7 = (bf16[256,512]{1,0:T(8,128)(2,1)S(1)}, bf16[256,512]{1,0:T(8,128)(2,1)S(1)}, u32[]{:S(2)}, u32[]{:S(2)}) collective-permute-start(bf16[256,512]{1,0:T(8,128)(2,1)S(1)} %collective-permute-done.6.refs_8_.refs_5_), channel_id=1, source_target_pairs={{0,4},{4,0},{8,12},{12,8},{16,20},{20,16},{24,28},{28,24},{1,5},{5... | collective-permute-start | bytes 786440 | tf_op jit(solution)/shard_map/ppermute | solution.py:596
  48.6 17.4 %collective-permute-start.5 = (bf16[256,512]{1,0:T(8,128)(2,1)}, bf16[256,512]{1,0:T(8,128)(2,1)S(1)}, u32[]{:S(2)}, u32[]{:S(2)}) collective-permute-start(bf16[256,512]{1,0:T(8,128)(2,1)} %collective-permute-done.4.refs_6_.refs_3_), channel_id=1, source_target_pairs={{0,4},{4,0},{8,12},{12,8},{16,20},{20,16},{24,28},{28,24},{1,5},{5... | collective-permute-start | bytes 786440 | tf_op jit(solution)/shard_map/ppermute | solution.py:596
  58.6 0.9 copy-start.5
  59.5 0.9 copy-start.7
  60.4 0.9 copy-start.9
  68.5 3.8 %copy-start.2 = (f32[64,2048]{1,0:T(8,128)S(1)}, f32[64,2048]{1,0:T(8,128)}, u32[]{:S(2)}) copy-start(f32[64,2048]{1,0:T(8,128)} %fw.1) | copy-start | bytes 1572868
  68.5 3.8 %copy-start.3 = (f32[232,512]{1,0:T(8,128)S(1)}, f32[232,512]{1,0:T(8,128)}, u32[]{:S(2)}) copy-start(f32[232,512]{1,0:T(8,128)} %constant.32.clone.refs_0_.tab) | copy-start | bytes 1425412
  76.0 8.4 %collective-permute-start.28 = (f32[80,512]{1,0:T(8,128)S(1)}, f32[80,512]{1,0:T(8,128)S(1)}, u32[]{:S(2)}, u32[]{:S(2)}) collective-permute-start(f32[80,512]{1,0:T(8,128)S(1)} %correlate_part.1), channel_id=1, source_target_pairs={{0,4},{4,0},{8,12},{12,8},{16,20},{20,16},{24,28},{28,24},{1,5},{5... | collective-permute-start | bytes 491528 | tf_op jit(solution)/shard_map/ppermute | solution.py:596
  79.4 9.2 %collective-permute-start.20 = (bf16[1,256,512]{2,1,0:T(8,128)(2,1)S(1)}, bf16[1,256,512]{2,1,0:T(8,128)(2,1)S(1)}, u32[]{:S(2)}, u32[]{:S(2)}) collective-permute-start(bf16[1,256,512]{2,1,0:T(8,128)(2,1)S(1)} %get-tuple-element.62), channel_id=1, source_target_pairs={{0,4},{4,0},{8,12},{12,8},{16,20},{20,16},{24,28},{28,24},{1,5},{5... | collective-permute-start | bytes 786440 | tf_op jit(solution)/shard_map/ppermute | solution.py:596
  80.0 27.2 %collective-permute-start.13 = (bf16[128,512]{1,0:T(8,128)(2,1)S(1)}, bf16[128,512]{1,0:T(8,128)(2,1)S(1)}, u32[]{:S(2)}, u32[]{:S(2)}) collective-permute-start(bf16[128,512]{1,0:T(8,128)(2,1)S(1)} %get-tuple-element.48), channel_id=1, source_target_pairs={{0,1},{1,0},{2,3},{3,2},{4,5},{5,4},{6,7},{7,6},{8,9},{9,8},{10,11... | collective-permute-start | bytes 393224 | tf_op jit(solution)/shard_map/ppermute | solution.py:596
  80.0 14.3 %collective-permute-start.22 = (bf16[1,256,512]{2,1,0:T(8,128)(2,1)S(1)}, bf16[1,256,512]{2,1,0:T(8,128)(2,1)S(1)}, u32[]{:S(2)}, u32[]{:S(2)}) collective-permute-start(bf16[1,256,512]{2,1,0:T(8,128)(2,1)S(1)} %get-tuple-element.64), channel_id=1, source_target_pairs={{0,4},{4,0},{8,12},{12,8},{16,20},{20,16},{24,28},{28,24},{1,5},{5... | collective-permute-start | bytes 786440 | tf_op jit(solution)/shard_map/ppermute | solution.py:596
  81.5 22.3 %collective-permute-start.19 = (bf16[2,256,512]{2,1,0:T(8,128)(2,1)S(1)}, bf16[2,256,512]{2,1,0:T(8,128)(2,1)S(1)}, u32[]{:S(2)}, u32[]{:S(2)}) collective-permute-start(bf16[2,256,512]{2,1,0:T(8,128)(2,1)S(1)} %get-tuple-element.60), channel_id=1, source_target_pairs={{0,4},{4,0},{8,12},{12,8},{16,20},{20,16},{24,28},{28,24},{1,5},{5... | collective-permute-start | bytes 1572872 | tf_op jit(solution)/shard_map/ppermute | solution.py:596
  84.4 64.5 %collective-permute-start.16 = (bf16[128,2048]{1,0:T(8,128)(2,1)S(1)}, bf16[128,2048]{1,0:T(8,128)(2,1)S(1)}, u32[]{:S(2)}, u32[]{:S(2)}) collective-permute-start(bf16[128,2048]{1,0:T(8,128)(2,1)S(1)} %get-tuple-element.56), channel_id=1, source_target_pairs={{0,1},{1,0},{2,3},{3,2},{4,5},{5,4},{6,7},{7,6},{8,9},{9,8},{10,11... | collective-permute-start | bytes 1572872 | tf_op jit(solution)/shard_map/ppermute | solution.py:596
  88.7 16.9 %collective-permute-start.17 = (bf16[128,2048]{1,0:T(8,128)(2,1)S(1)}, bf16[128,2048]{1,0:T(8,128)(2,1)S(1)}, u32[]{:S(2)}, u32[]{:S(2)}) collective-permute-start(bf16[128,2048]{1,0:T(8,128)(2,1)S(1)} %get-tuple-element.58), channel_id=1, source_target_pairs={{0,1},{1,0},{2,3},{3,2},{4,5},{5,4},{6,7},{7,6},{8,9},{9,8},{10,11... | collective-permute-start | bytes 1572872 | tf_op jit(solution)/shard_map/ppermute | solution.py:596
  94.3 14.3 %collective-permute-start.21 = (bf16[256,512]{1,0:T(8,128)(2,1)S(1)}, bf16[256,512]{1,0:T(8,128)(2,1)S(1)}, u32[]{:S(2)}, u32[]{:S(2)}) collective-permute-start(bf16[256,512]{1,0:T(8,128)(2,1)S(1)} %fusion.5), channel_id=1, source_target_pairs={{0,24},{4,28},{8,16},{12,20},{16,8},{20,12},{24,0},{28,4},{1,25},{... | collective-permute-start | bytes 786440 | tf_op jit(solution)/shard_map/ppermute | solution.py:596
  103.8 15.2 %collective-permute-start.23 = (bf16[256,512]{1,0:T(8,128)(2,1)S(1)}, bf16[256,512]{1,0:T(8,128)(2,1)S(1)}, u32[]{:S(2)}, u32[]{:S(2)}) collective-permute-start(bf16[256,512]{1,0:T(8,128)(2,1)S(1)} %fusion.6), channel_id=1, source_target_pairs={{0,16},{4,20},{8,24},{12,28},{16,0},{20,4},{24,8},{28,12},{1,17},{... | collective-permute-start | bytes 786440 | tf_op jit(solution)/shard_map/ppermute | solution.py:596
  105.6 13.4 %collective-permute-start.24 = (bf16[256,512]{1,0:T(8,128)(2,1)S(1)}, bf16[256,512]{1,0:T(8,128)(2,1)S(1)}, u32[]{:S(2)}, u32[]{:S(2)}) collective-permute-start(bf16[256,512]{1,0:T(8,128)(2,1)S(1)} %fusion.7), channel_id=1, source_target_pairs={{0,8},{4,12},{8,0},{12,4},{16,24},{20,28},{24,16},{28,20},{1,9},{5... | collective-permute-start | bytes 786440 | tf_op jit(solution)/shard_map/ppermute | solution.py:596
  107.2 14.3 %collective-permute-start.31 = (bf16[80,512]{1,0:T(8,128)(2,1)S(1)}, bf16[80,512]{1,0:T(8,128)(2,1)S(1)}, u32[]{:S(2)}, u32[]{:S(2)}) collective-permute-start(bf16[80,512]{1,0:T(8,128)(2,1)S(1)} %add_convert_fusion.8), channel_id=1, source_target_pairs={{0,24},{4,28},{8,16},{12,20},{16,8},{20,12},{24,0},{28,4},{1,25},{... | collective-permute-start | bytes 245768 | tf_op jit(solution)/shard_map/ppermute | solution.py:596
  108.6 15.6 %collective-permute-start.30 = (bf16[80,512]{1,0:T(8,128)(2,1)S(1)}, bf16[80,512]{1,0:T(8,128)(2,1)S(1)}, u32[]{:S(2)}, u32[]{:S(2)}) collective-permute-start(bf16[80,512]{1,0:T(8,128)(2,1)S(1)} %add_convert_fusion.8), channel_id=1, source_target_pairs={{0,16},{4,20},{8,24},{12,28},{16,0},{20,4},{24,8},{28,12},{1,17},{... | collective-permute-start | bytes 245768 | tf_op jit(solution)/shard_map/ppermute | solution.py:596
  119.0 5.9 %collective-permute-start.29 = (bf16[80,512]{1,0:T(8,128)(2,1)S(1)}, bf16[80,512]{1,0:T(8,128)(2,1)S(1)}, u32[]{:S(2)}, u32[]{:S(2)}) collective-permute-start(bf16[80,512]{1,0:T(8,128)(2,1)S(1)} %add_convert_fusion.8), channel_id=1, source_target_pairs={{0,8},{4,12},{8,0},{12,4},{16,24},{20,28},{24,16},{28,20},{1,9},{5... | collective-permute-start | bytes 245768 | tf_op jit(solution)/shard_map/ppermute | solution.py:596
  119.0 29.9 %collective-permute-start.18 = (bf16[128,2048]{1,0:T(8,128)(2,1)S(1)}, bf16[128,2048]{1,0:T(8,128)(2,1)S(1)}, u32[]{:S(2)}, u32[]{:S(2)}) collective-permute-start(bf16[128,2048]{1,0:T(8,128)(2,1)S(1)} %add_convert_fusion.1), channel_id=1, source_target_pairs={{0,2},{1,3},{2,0},{3,1},{4,6},{5,7},{6,4},{7,5},{8,10},{9,11},{10,... | collective-permute-start | bytes 1572872 | tf_op jit(solution)/shard_map/ppermute | solution.py:596
  121.5 15.4 %collective-permute-start.14 = (bf16[128,512]{1,0:T(8,128)(2,1)S(1)}, bf16[128,512]{1,0:T(8,128)(2,1)S(1)}, u32[]{:S(2)}, u32[]{:S(2)}) collective-permute-start(bf16[128,512]{1,0:T(8,128)(2,1)S(1)} %get-tuple-element.49), channel_id=1, source_target_pairs={{0,2},{1,3},{2,0},{3,1},{4,6},{5,7},{6,4},{7,5},{8,10},{9,11},{10,... | collective-permute-start | bytes 393224 | tf_op jit(solution)/shard_map/ppermute | solution.py:596
  124.2 15.1 %collective-permute-start.15 = (bf16[128,512]{1,0:T(8,128)(2,1)S(1)}, bf16[128,512]{1,0:T(8,128)(2,1)S(1)}, u32[]{:S(2)}, u32[]{:S(2)}) collective-permute-start(bf16[128,512]{1,0:T(8,128)(2,1)S(1)} %get-tuple-element.50), channel_id=1, source_target_pairs={{0,3},{1,2},{2,1},{3,0},{4,7},{5,6},{6,5},{7,4},{8,11},{9,10},{10,... | collective-permute-start | bytes 393224 | tf_op jit(solution)/shard_map/ppermute | solution.py:596
  124.9 23.9 %collective-permute-start.26 = (bf16[256,512]{1,0:T(8,128)(2,1)S(1)}, bf16[256,512]{1,0:T(8,128)(2,1)S(1)}, u32[]{:S(2)}, u32[]{:S(2)}) collective-permute-start(bf16[256,512]{1,0:T(8,128)(2,1)S(1)} %fusion.3.refs_0_), channel_id=1, source_target_pairs={{0,2},{1,3},{2,0},{3,1},{4,6},{5,7},{6,4},{7,5},{8,10},{9,11},{10,... | collective-permute-start | bytes 786440 | tf_op jit(solution)/shard_map/ppermute | solution.py:596
  136.9 8.7 %collective-permute-start.33 = (bf16[80,512]{1,0:T(8,128)(2,1)S(1)}, bf16[80,512]{1,0:T(8,128)(2,1)S(1)}, u32[]{:S(2)}, u32[]{:S(2)}) collective-permute-start(bf16[80,512]{1,0:T(8,128)(2,1)S(1)} %add_convert_fusion.7.refs_0_), channel_id=1, source_target_pairs={{0,2},{1,3},{2,0},{3,1},{4,6},{5,7},{6,4},{7,5},{8,10},{9,11},{10,... | collective-permute-start | bytes 245768 | tf_op jit(solution)/shard_map/ppermute | solution.py:596
  139.2 7.7 %collective-permute-start.32 = (bf16[80,512]{1,0:T(8,128)(2,1)S(1)}, bf16[80,512]{1,0:T(8,128)(2,1)S(1)}, u32[]{:S(2)}, u32[]{:S(2)}) collective-permute-start(bf16[80,512]{1,0:T(8,128)(2,1)S(1)} %add_convert_fusion.7.refs_0_), channel_id=1, source_target_pairs={{0,1},{1,0},{2,3},{3,2},{4,5},{5,4},{6,7},{7,6},{8,9},{9,8},{10,11... | collective-permute-start | bytes 245768 | tf_op jit(solution)/shard_map/ppermute | solution.py:596
  145.6 1.4 collective-permute-start.34
  148.3 1.7 %collective-permute-start.25 = (bf16[256,512]{1,0:T(8,128)(2,1)S(1)}, bf16[256,512]{1,0:T(8,128)(2,1)S(1)}, u32[]{:S(2)}, u32[]{:S(2)}) collective-permute-start(bf16[256,512]{1,0:T(8,128)(2,1)S(1)} %fusion.3.refs_0_), channel_id=1, source_target_pairs={{0,1},{1,0},{2,3},{3,2},{4,5},{5,4},{6,7},{7,6},{8,9},{9,8},{10,11... | collective-permute-start | bytes 786440 | tf_op jit(solution)/shard_map/ppermute | solution.py:596
  148.8 1.5 %collective-permute-start.27 = (bf16[256,512]{1,0:T(8,128)(2,1)S(1)}, bf16[256,512]{1,0:T(8,128)(2,1)S(1)}, u32[]{:S(2)}, u32[]{:S(2)}) collective-permute-start(bf16[256,512]{1,0:T(8,128)(2,1)S(1)} %collective-permute-done.26.refs_2_), channel_id=1, source_target_pairs={{0,1},{1,0},{2,3},{3,2},{4,5},{5,4},{6,7},{7,6},{8,9},{9,8},{10,11... | collective-permute-start | bytes 786440 | tf_op jit(solution)/shard_map/ppermute | solution.py:596

commit v4 on v3

--- a/solution.py
+++ b/solution.py
@@ -105,7 +105,7 @@
 
     def body(place_ref, *refs):
         sources = refs[:5]
-        ah, al, th, spec, env_out, hidden_out, cos_out, rows_out, filt, *held, done = refs[5:]
+        ah, al, th, spec, env_out, hidden_out, pre_out, rows_out, filt, *held, done = refs[5:]
         tab, pw, pb, fw, vec = held
         step = pl.program_id(0)
 
@@ -130,9 +130,9 @@
             )
             hidden = jnp.sin(pre)
             hidden_out[...] = hidden
-            cos_out[...] = jnp.cos(pre)
+            pre_out[...] = pre
             at = lax.broadcasted_iota(jnp.int32, (length, width), 0).astype(f32)
-            env = jnp.exp(-vec[0:1, :] * at) / vec[1:2, :]
+            env = jnp.exp(-vec[0:1, :] * at) * (1.0 / vec[1:2, :])
             env_out[...] = env
             filt[...] = (jnp.dot(hidden, fw[...], precision=highest) * env).astype(bf16)
 
@@ -421,7 +421,7 @@
 
 
 def correlate_part(
-    place, grad_spec, skip_sum, signal_spec, tables, env, hidden, filter_weight, cos_pre, table,
+    place, grad_spec, skip_sum, signal_spec, tables, env, hidden, filter_weight, pre, table,
     block,
 ):
     t_high = tables[2]
@@ -432,7 +432,7 @@
     total_rows, per_group = packed_rows(order, table_rows, width)
 
     def body(
-        place_ref, gs, skip_sum_ref, ss, th, env_ref, hid, fw, cp, tab, packed, part,
+        place_ref, gs, skip_sum_ref, ss, th, env_ref, hid, fw, pre_ref, tab, packed, part,
     ):
         step = pl.program_id(0)
         term = from_spectrum(
@@ -453,7 +453,7 @@
             packed[...] = jnp.zeros((total_rows, width), f32)
             packed[:order, :] = careful(dot_first, hid[...], pre_grad)
             packed[order : order + 8, :] = skip_sum_ref[...]
-            act = careful(dot_last, pre_grad, fw[...]) * cp[...]
+            act = careful(dot_last, pre_grad, fw[...]) * jnp.cos(pre_ref[...])
             small = careful(dot, tab[feature_start:, :], act)
             for b in range(table_rows // 8):
                 row = order + 8 + 8 * (b // per_group)
@@ -475,7 +475,7 @@
                 whole((length, width)),
                 whole(hidden.shape),
                 pl.BlockSpec((order, width), lambda i, place_ref: (0, place_ref[0])),
-                whole(cos_pre.shape),
+                whole(pre.shape),
                 whole(table.shape),
             ],
             out_specs=whole((total_rows, width)),
@@ -487,7 +487,7 @@
             [((2, block, length), 2), ((4, block, width), 4), ((2, length, width), 4)], length, width
         ),
     )(
-        place, grad_spec, skip_sum, signal_spec, t_high, env, hidden, filter_weight, cos_pre,
+        place, grad_spec, skip_sum, signal_spec, t_high, env, hidden, filter_weight, pre,
         table,
     )
 
@@ -648,7 +648,7 @@
     rates = decay_rate[None]
     norm = jnp.sqrt(jnp.expm1(-2.0 * rates * length) / jnp.expm1(-2.0 * rates))
     rows_of = jnp.concatenate([rates, norm, skip_gain[None]])
-    a_high, a_low, t_high, filt_spec, env, hidden, cos_pre, rows_of = generate(
+    a_high, a_low, t_high, filt_spec, env, hidden, pre, rows_of = generate(
         place, table, pos_weight, pos_bias[None], filter_weight, rows_of, width, block
     )
     tables = (a_high, a_low, t_high)
@@ -680,7 +680,7 @@
         place, conv_grad, inner_grad, filt_spec, tables, rows_of, block
     )
     packed = correlate_part(
-        place, grad_spec, skip_sum, signal_spec, tables, env, hidden, filter_weight, cos_pre,
+        place, grad_spec, skip_sum, signal_spec, tables, env, hidden, filter_weight, pre,
         table, block,
     )
     back_rel = through_gate(place, gate_grad, weight_rel, direct, seq_count)

time: 153 us -> 153 us (level)
  no operation moved by 1% of the time
where the time goes in v4:
time: 153 us
  waiting for transfers between devices  76.4 us (50%)
  starting transfers between devices  35.5 us (23%)
  Pallas kernels  30.6 us (20%)
  local copies, waits for them, and re-layouts  5.85 us (4%)
  other arithmetic  3.78 us (2%)
    ppermute x35, waiting for transfers between devices, swap(): return lax.ppermute(value, axis, [(i, i ^ offset) for i in range(count)])  76.4 us
    ppermute x35, starting transfers between devices, swap(): return lax.ppermute(value, axis, [(i, i ^ offset) for i in range(count)])  35.5 us
    pallas_call x1, Pallas kernels, generate(): pl.pallas_call(body, grid_spec=pltpu.PrefetchScalarGridSpec(num_scalar_pr...  6.96 us
    unnamed x20, local copies, waits for them, and re-layouts  4.7 us
    pallas_call x1, Pallas kernels, correlate_part(): pl.pallas_call(body, grid_spec=pltpu.PrefetchScalarGridSpec(num_scalar_pr...  4.31 us
    pallas_call x1, Pallas kernels, convolve(): pl.pallas_call(body, grid_spec=pltpu.PrefetchScalarGridSpec(num_scalar_pr...  4.15 us
    pallas_call x1, Pallas kernels, correlate_back(): pl.pallas_call(body, grid_spec=pltpu.PrefetchScalarGridSpec(num_scalar_pr...  3.8 us
    pallas_call x2, Pallas kernels, assemble(): pl.pallas_call(body, in_specs=[smem()] + [pl.BlockSpec(memory_space=VMEM)...  3.37 us
  transfers between devices with their start and end apart: 35, of which 14 were waited for; matrix products, arithmetic and copies ran while one was open for 3% of the time, Pallas kernels for 12%

profile of v4, /device:TPU:0, one launch (start us, length us, event | category | flops | bytes accessed | tf_op | source)
XLA Modules:
  0.0 153.0 jit_solution(8474780363754767858)
XLA Ops:
  0.7 3.0 %collective-permute-start.1 = (bf16[128,2048]{1,0:T(8,128)(2,1)}, bf16[128,2048]{1,0:T(8,128)(2,1)S(1)}, u32[]{:S(2)}, u32[]{:S(2)}) collective-permute-start(bf16[128,2048]{1,0:T(8,128)(2,1)} %bitcast.31), channel_id=1, source_target_pairs={{0,2},{1,3},{2,0},{3,1},{4,6},{5,7},{6,4},{7,5},{8,10},{9,11},{10,... | collective-permute-start | bytes 1572872 | tf_op jit(solution)/shard_map/ppermute | solution.py:596
  3.7 1.1 dynamic-slice_bitcast_fusion
  4.8 0.3 collective-permute-start.12
  5.1 0.4 collective-permute-start.10
  5.5 1.6 %collective-permute-start.11 = (bf16[128,512]{1,0:T(8,128)(2,1)S(1)}, bf16[128,512]{1,0:T(8,128)(2,1)S(1)}, u32[]{:S(2)}, u32[]{:S(2)}) collective-permute-start(bf16[128,512]{1,0:T(8,128)(2,1)S(1)} %get-tuple-element.78), channel_id=1, source_target_pairs={{0,2},{1,3},{2,0},{3,1},{4,6},{5,7},{6,4},{7,5},{8,10},{9,11},{10,... | collective-permute-start | bytes 393224 | tf_op jit(solution)/shard_map/ppermute | solution.py:596
  7.1 12.0 %collective-permute-done.12.refs_7_.refs_15_ = bf16[128,512]{1,0:T(8,128)(2,1)S(1)} collective-permute-done((bf16[128,512]{1,0:T(8,128)(2,1)S(1)}, bf16[128,512]{1,0:T(8,128)(2,1)S(1)}, u32[]{:S(2)}, u32[]{:S(2)}) %collective-permute-start.12) | collective-permute-done | bytes 131104 | tf_op jit(solution)/shard_map/ppermute | solution.py:596
  19.0 0.7 copy-done.4
  19.7 3.6 %collective-permute-start.8 = (bf16[256,512]{1,0:T(8,128)(2,1)S(1)}, bf16[256,512]{1,0:T(8,128)(2,1)S(1)}, u32[]{:S(2)}, u32[]{:S(2)}) collective-permute-start(bf16[256,512]{1,0:T(8,128)(2,1)S(1)} %constant_dynamic-slice_fusion.refs_4_.refs_1_), channel_id=1, source_target_pairs={{0,24},{4,28},{8,16},{12,20},{16,8},{20,12},{24,0},{28,4},{1,25},{... | collective-permute-start | bytes 786440 | tf_op jit(solution)/shard_map/ppermute | solution.py:596
  23.3 0.7 copy-done.6
  23.9 0.7 copy-done.8
  24.6 0.8 collective-permute-start.4
  25.4 0.7 divide_sqrt_fusion
  26.1 4.7 %collective-permute-done.8.refs_10_.refs_7_ = bf16[256,512]{1,0:T(8,128)(2,1)S(1)} collective-permute-done((bf16[256,512]{1,0:T(8,128)(2,1)S(1)}, bf16[256,512]{1,0:T(8,128)(2,1)S(1)}, u32[]{:S(2)}, u32[]{:S(2)}) %collective-permute-start.8) | collective-permute-done | bytes 262176 | tf_op jit(solution)/shard_map/ppermute | solution.py:596
  30.8 1.5 collective-permute-start.3
  32.3 14.2 %collective-permute-done.6.refs_8_.refs_5_ = bf16[256,512]{1,0:T(8,128)(2,1)S(1)} collective-permute-done((bf16[256,512]{1,0:T(8,128)(2,1)S(1)}, bf16[256,512]{1,0:T(8,128)(2,1)S(1)}, u32[]{:S(2)}, u32[]{:S(2)}) %collective-permute-start.6) | collective-permute-done | bytes 262176 | tf_op jit(solution)/shard_map/ppermute | solution.py:596
  46.6 1.5 collective-permute-start.9
  48.1 0.5 collective-permute-start.7
  48.6 1.5 collective-permute-start.5
  50.1 0.1 pad_add_fusion.place_ref
  50.2 1.4 pad_maximum_fusion.refs_4_
  51.6 7.0 %generate.1 = (bf16[2,512,512]{2,1,0:T(8,128)(2,1)S(1)}, bf16[2,512,512]{2,1,0:T(8,128)(2,1)S(1)}, bf16[2,512,512]{2,1,0:T(8,128)(2,1)S(1)}, f32[2,512,512]{2,1,...) custom-call(s32[2]{0:T(128)S(1)} %pad_add_fusion.place_ref, ...), custom_call_target="tpu_custom_call" | custom-call | tf_op jit(solution)/shard_map/generate/pallas_call | solution.py:169
  58.6 0.9 copy-done.5
  59.5 0.9 copy-done.7
  60.4 0.9 copy-done.9
  61.3 4.1 %convolve.1 = (f32[2,512,512]{2,1,0:T(8,128)S(1)}, f32[512,512]{1,0:T(8,128)S(1)}, bf16[512,512]{1,0:T(8,128)(2,1)S(1)}) custom-call(s32[2]{0:T(128)S(1)} %pad_add_fusion.place_ref, bf16[128,2048]{1,0:T(8,128)(2,1)S(1)} %bitcast.33, bf16[128,2048]{1,0:T(8,128)(2,1)S(1)} %collective-permute-done.refs_1_, ...), custom_call_target="tpu_custom_call" | custom-call | tf_op jit(solution)/shard_map/convolve/pallas_call | solution.py:247
  65.4 0.5 collective-permute-done.5.refs_7_.refs_4_
  66.0 2.5 %gating.1 = (bf16[128,512]{1,0:T(8,128)(2,1)S(1)}, bf16[128,512]{1,0:T(8,128)(2,1)S(1)}, bf16[128,512]{1,0:T(8,128)(2,1)S(1)}, bf16[128,512]{1,0:T(8,128)(2,1)S(...) custom-call(s32[2]{0:T(128)S(1)} %pad_add_fusion.place_ref, ...), custom_call_target="tpu_custom_call" | custom-call | tf_op jit(solution)/shard_map/gating/pallas_call | solution.py:350
  68.5 3.8 %correlate_back.1 = (f32[512,512]{1,0:T(8,128)S(1)}, f32[2,512,512]{2,1,0:T(8,128)S(1)}) custom-call(s32[2]{0:T(128)S(1)} %pad_add_fusion.place_ref, bf16[512,512]{1,0:T(8,128)(2,1)S(1)} %get-tuple-element.52.cg, f32[512,512]{1,0:T(8,128)S(1)} %get-tuple-element.53.ig, f32[2,512,512]{2,1,0:T(8,128)S(1)} %get-tuple-element.41.refs_8_.fs, ...), custom_call_target="tpu_custom_call" | custom-call | tf_op jit(solution)/shard_map/correlate_back/pallas_call | solution.py:398
  72.3 4.3 %correlate_part.1 = f32[80,512]{1,0:T(8,128)S(1)} custom-call(s32[2]{0:T(128)S(1)} %pad_add_fusion.place_ref, f32[2,512,512]{2,1,0:T(8,128)S(1)} %get-tuple-element.65.gs, f32[8,512]{1,0:T(8,128)S(1)} %get-tuple-element.66.skip_sum_ref, f32[2,512,512]{2,1,0:T(8,128)S(1)} %get-tuple-element.67.ss, bf16[2,512,512]{2,1,0:T(8,128)(2,1)S(1)} %get-tuple-element.44.refs_11_.th, ...), custom_call_target="tpu_custom_call" | custom-call | tf_op jit(solution)/shard_map/correlate_part/pallas_call | solution.py:465
  76.6 1.6 %collective-permute-start.28 = (f32[80,512]{1,0:T(8,128)S(1)}, f32[80,512]{1,0:T(8,128)S(1)}, u32[]{:S(2)}, u32[]{:S(2)}) collective-permute-start(f32[80,512]{1,0:T(8,128)S(1)} %correlate_part.1), channel_id=1, source_target_pairs={{0,4},{4,0},{8,12},{12,8},{16,20},{20,16},{24,28},{28,24},{1,5},{5... | collective-permute-start | bytes 491528 | tf_op jit(solution)/shard_map/ppermute | solution.py:596
  78.2 1.8 %weight_grads.1 = (bf16[1,256,512]{2,1,0:T(8,128)(2,1)S(1)}, bf16[1,256,512]{2,1,0:T(8,128)(2,1)S(1)}, bf16[2,256,512]{2,1,0:T(8,128)(2,1)S(1)}, bf16[1,256,512]...) custom-call(s32[2]{0:T(128)S(1)} %pad_add_fusion.place_ref, ...), custom_call_target="tpu_custom_call" | custom-call | tf_op jit(solution)/shard_map/weight_grads/pallas_call | solution.py:307
  80.1 0.6 collective-permute-start.20
  80.7 1.5 collective-permute-start.22
  82.2 0.5 collective-permute-start.19
  82.7 2.3 %through_gate.1 = (bf16[128,2048]{1,0:T(8,128)(2,1)S(1)}, bf16[128,2048]{1,0:T(8,128)(2,1)S(1)}, bf16[128,2048]{1,0:T(8,128)(2,1)S(1)}, bf16[128,2048]{1,0:T(8,128)(2,1)S(1)}) custom-call(s32[2]{0:T(128)S(1)} %pad_add_fusion.place_ref, bf16[512,512]{1,0:T(8,128)(2,1)S(1)} %get-tuple-element.51.refs_0_.refs_4_, ...), custom_call_target="tpu_custom_call" | custom-call | tf_op jit(solution)/shard_map/through_gate/pallas_call | solution.py:522
  85.0 0.1 collective-permute-start.16
  85.1 4.2 %collective-permute-done.20 = bf16[1,256,512]{2,1,0:T(8,128)(2,1)S(1)} collective-permute-done((bf16[1,256,512]{2,1,0:T(8,128)(2,1)S(1)}, bf16[1,256,512]{2,1,0:T(8,128)(2,1)S(1)}, u32[]{:S(2)}, u32[]{:S(2)}) %collective-permute-start.20) | collective-permute-done | bytes 262176 | tf_op jit(solution)/shard_map/ppermute | solution.py:596
  89.4 5.5 %collective-permute-done.22 = bf16[1,256,512]{2,1,0:T(8,128)(2,1)S(1)} collective-permute-done((bf16[1,256,512]{2,1,0:T(8,128)(2,1)S(1)}, bf16[1,256,512]{2,1,0:T(8,128)(2,1)S(1)}, u32[]{:S(2)}, u32[]{:S(2)}) %collective-permute-start.22) | collective-permute-done | bytes 262176 | tf_op jit(solution)/shard_map/ppermute | solution.py:596
  94.9 2.5 %collective-permute-start.21 = (bf16[256,512]{1,0:T(8,128)(2,1)S(1)}, bf16[256,512]{1,0:T(8,128)(2,1)S(1)}, u32[]{:S(2)}, u32[]{:S(2)}) collective-permute-start(bf16[256,512]{1,0:T(8,128)(2,1)S(1)} %fusion.5), channel_id=1, source_target_pairs={{0,24},{4,28},{8,16},{12,20},{16,8},{20,12},{24,0},{28,4},{1,25},{... | collective-permute-start | bytes 786440 | tf_op jit(solution)/shard_map/ppermute | solution.py:596
  97.5 7.0 %collective-permute-done.19 = bf16[2,256,512]{2,1,0:T(8,128)(2,1)S(1)} collective-permute-done((bf16[2,256,512]{2,1,0:T(8,128)(2,1)S(1)}, bf16[2,256,512]{2,1,0:T(8,128)(2,1)S(1)}, u32[]{:S(2)}, u32[]{:S(2)}) %collective-permute-start.19) | collective-permute-done | bytes 524320 | tf_op jit(solution)/shard_map/ppermute | solution.py:596
  104.5 1.7 %collective-permute-start.23 = (bf16[256,512]{1,0:T(8,128)(2,1)S(1)}, bf16[256,512]{1,0:T(8,128)(2,1)S(1)}, u32[]{:S(2)}, u32[]{:S(2)}) collective-permute-start(bf16[256,512]{1,0:T(8,128)(2,1)S(1)} %fusion.6), channel_id=1, source_target_pairs={{0,16},{4,20},{8,24},{12,28},{16,0},{20,4},{24,8},{28,12},{1,17},{... | collective-permute-start | bytes 786440 | tf_op jit(solution)/shard_map/ppermute | solution.py:596
  106.2 1.4 collective-permute-start.24
  107.7 0.2 add_convert_fusion.1
  107.8 1.4 collective-permute-start.31
  109.3 0.8 collective-permute-start.30
  110.0 9.6 %collective-permute-done.23 = bf16[256,512]{1,0:T(8,128)(2,1)S(1)} collective-permute-done((bf16[256,512]{1,0:T(8,128)(2,1)S(1)}, bf16[256,512]{1,0:T(8,128)(2,1)S(1)}, u32[]{:S(2)}, u32[]{:S(2)}) %collective-permute-start.23) | collective-permute-done | bytes 262176 | tf_op jit(solution)/shard_map/ppermute | solution.py:596
  119.7 2.3 %collective-permute-start.18 = (bf16[128,2048]{1,0:T(8,128)(2,1)S(1)}, bf16[128,2048]{1,0:T(8,128)(2,1)S(1)}, u32[]{:S(2)}, u32[]{:S(2)}) collective-permute-start(bf16[128,2048]{1,0:T(8,128)(2,1)S(1)} %add_convert_fusion.1), channel_id=1, source_target_pairs={{0,2},{1,3},{2,0},{3,1},{4,6},{5,7},{6,4},{7,5},{8,10},{9,11},{10,... | collective-permute-start | bytes 1572872 | tf_op jit(solution)/shard_map/ppermute | solution.py:596
  122.0 0.2 fusion.3.refs_0_
  122.1 1.5 collective-permute-start.14
  123.6 1.2 collective-permute-done.30
  124.8 0.3 collective-permute-start.15
  125.1 0.5 collective-permute-done.29
  125.6 1.8 %collective-permute-start.26 = (bf16[256,512]{1,0:T(8,128)(2,1)S(1)}, bf16[256,512]{1,0:T(8,128)(2,1)S(1)}, u32[]{:S(2)}, u32[]{:S(2)}) collective-permute-start(bf16[256,512]{1,0:T(8,128)(2,1)S(1)} %fusion.3.refs_0_), channel_id=1, source_target_pairs={{0,2},{1,3},{2,0},{3,1},{4,6},{5,7},{6,4},{7,5},{8,10},{9,11},{10,... | collective-permute-start | bytes 786440 | tf_op jit(solution)/shard_map/ppermute | solution.py:596
  127.4 10.1 %collective-permute-done.14.refs_2_ = bf16[128,512]{1,0:T(8,128)(2,1)S(1)} collective-permute-done((bf16[128,512]{1,0:T(8,128)(2,1)S(1)}, bf16[128,512]{1,0:T(8,128)(2,1)S(1)}, u32[]{:S(2)}, u32[]{:S(2)}) %collective-permute-start.14) | collective-permute-done | bytes 131104 | tf_op jit(solution)/shard_map/ppermute | solution.py:596
  137.5 2.0 %collective-permute-start.33 = (bf16[80,512]{1,0:T(8,128)(2,1)S(1)}, bf16[80,512]{1,0:T(8,128)(2,1)S(1)}, u32[]{:S(2)}, u32[]{:S(2)}) collective-permute-start(bf16[80,512]{1,0:T(8,128)(2,1)S(1)} %add_convert_fusion.7.refs_0_), channel_id=1, source_target_pairs={{0,2},{1,3},{2,0},{3,1},{4,6},{5,7},{6,4},{7,5},{8,10},{9,11},{10,... | collective-permute-start | bytes 245768 | tf_op jit(solution)/shard_map/ppermute | solution.py:596
  139.6 0.3 collective-permute-done.15.refs_3_
  139.9 0.3 collective-permute-start.32
  140.2 6.0 %collective-permute-done.33.refs_2_ = bf16[80,512]{1,0:T(8,128)(2,1)S(1)} collective-permute-done((bf16[80,512]{1,0:T(8,128)(2,1)S(1)}, bf16[80,512]{1,0:T(8,128)(2,1)S(1)}, u32[]{:S(2)}, u32[]{:S(2)}) %collective-permute-start.33) | collective-permute-done | bytes 81952 | tf_op jit(solution)/shard_map/ppermute | solution.py:596
  146.2 1.4 assemble.2
  147.6 1.4 finish.1
  149.0 0.5 collective-permute-start.25
  149.5 1.0 fusion
  150.6 0.4 collective-permute-done.27.refs_3_
  151.0 2.0 %assemble.3 = f32[256,2048]{1,0:T(8,128)} custom-call(s32[2]{0:T(128)S(1)} %pad_add_fusion.place_ref, bf16[256,512]{1,0:T(8,128)(2,1)S(1)} %fusion.3.refs_0_, bf16[256,512]{1,0:T(8,128)(2,1)S(1)} %collective-permute-done.25.refs_1_, bf16[256,512]{1,0:T(8,128)(2,1)S(1)} %collective-permute-done.26.refs_2_, bf16[256,512]{1,0:T(8,128)(2,1)S(1)} %collective-permute-done.27.refs_3_), custom_call_target="tpu_custom_call" | custom-call | tf_op jit(solution)/shard_map/assemble/pallas_call | solution.py:542
  (49 shorter events, 0.5 us)
Async XLA Ops:
  0.6 6.4 %copy-start = (bf16[256,2048]{1,0:T(8,128)(2,1)S(1)}, bf16[256,2048]{1,0:T(8,128)(2,1)}, u32[]{:S(2)}) copy-start(bf16[256,2048]{1,0:T(8,128)(2,1)} %param.10) | copy-start | bytes 3145732
  0.6 57.9 %copy-start.1 = (bf16[1,128,2048]{2,1,0:T(8,128)(2,1)S(1)}, bf16[1,128,2048]{2,1,0:T(8,128)(2,1)}, u32[]{:S(2)}) copy-start(bf16[1,128,2048]{2,1,0:T(8,128)(2,1)} %param.9) | copy-start | bytes 1572868
  0.7 24.7 %collective-permute-start.1 = (bf16[128,2048]{1,0:T(8,128)(2,1)}, bf16[128,2048]{1,0:T(8,128)(2,1)S(1)}, u32[]{:S(2)}, u32[]{:S(2)}) collective-permute-start(bf16[128,2048]{1,0:T(8,128)(2,1)} %bitcast.31), channel_id=1, source_target_pairs={{0,2},{1,3},{2,0},{3,1},{4,6},{5,7},{6,4},{7,5},{8,10},{9,11},{10,... | collective-permute-start | bytes 1572872 | tf_op jit(solution)/shard_map/ppermute | solution.py:596
  3.7 44.9 %collective-permute-start = (bf16[128,2048]{1,0:T(8,128)(2,1)}, bf16[128,2048]{1,0:T(8,128)(2,1)S(1)}, u32[]{:S(2)}, u32[]{:S(2)}) collective-permute-start(bf16[128,2048]{1,0:T(8,128)(2,1)} %bitcast.32), channel_id=1, source_target_pairs={{0,1},{1,0},{2,3},{3,2},{4,5},{5,4},{6,7},{7,6},{8,9},{9,8},{10,11... | collective-permute-start | bytes 1572872 | tf_op jit(solution)/shard_map/ppermute | solution.py:596
  4.8 14.2 %collective-permute-start.12 = (bf16[128,512]{1,0:T(8,128)(2,1)S(1)}, bf16[128,512]{1,0:T(8,128)(2,1)S(1)}, u32[]{:S(2)}, u32[]{:S(2)}) collective-permute-start(bf16[128,512]{1,0:T(8,128)(2,1)S(1)} %get-tuple-element.75), channel_id=1, source_target_pairs={{0,3},{1,2},{2,1},{3,0},{4,7},{5,6},{6,5},{7,4},{8,11},{9,10},{10,... | collective-permute-start | bytes 393224 | tf_op jit(solution)/shard_map/ppermute | solution.py:596
  5.1 18.2 %collective-permute-start.10 = (bf16[128,512]{1,0:T(8,128)(2,1)S(1)}, bf16[128,512]{1,0:T(8,128)(2,1)S(1)}, u32[]{:S(2)}, u32[]{:S(2)}) collective-permute-start(bf16[128,512]{1,0:T(8,128)(2,1)S(1)} %get-tuple-element.76), channel_id=1, source_target_pairs={{0,1},{1,0},{2,3},{3,2},{4,5},{5,4},{6,7},{7,6},{8,9},{9,8},{10,11... | collective-permute-start | bytes 393224 | tf_op jit(solution)/shard_map/ppermute | solution.py:596
  5.5 18.5 %collective-permute-start.11 = (bf16[128,512]{1,0:T(8,128)(2,1)S(1)}, bf16[128,512]{1,0:T(8,128)(2,1)S(1)}, u32[]{:S(2)}, u32[]{:S(2)}) collective-permute-start(bf16[128,512]{1,0:T(8,128)(2,1)S(1)} %get-tuple-element.78), channel_id=1, source_target_pairs={{0,2},{1,3},{2,0},{3,1},{4,6},{5,7},{6,4},{7,5},{8,10},{9,11},{10,... | collective-permute-start | bytes 393224 | tf_op jit(solution)/shard_map/ppermute | solution.py:596
  19.0 0.7 copy-start.4
  19.7 11.1 %collective-permute-start.8 = (bf16[256,512]{1,0:T(8,128)(2,1)S(1)}, bf16[256,512]{1,0:T(8,128)(2,1)S(1)}, u32[]{:S(2)}, u32[]{:S(2)}) collective-permute-start(bf16[256,512]{1,0:T(8,128)(2,1)S(1)} %constant_dynamic-slice_fusion.refs_4_.refs_1_), channel_id=1, source_target_pairs={{0,24},{4,28},{8,16},{12,20},{16,8},{20,12},{24,0},{28,4},{1,25},{... | collective-permute-start | bytes 786440 | tf_op jit(solution)/shard_map/ppermute | solution.py:596
  23.3 0.7 copy-start.6
  23.9 22.6 %collective-permute-start.6 = (bf16[256,512]{1,0:T(8,128)(2,1)S(1)}, bf16[256,512]{1,0:T(8,128)(2,1)S(1)}, u32[]{:S(2)}, u32[]{:S(2)}) collective-permute-start(bf16[256,512]{1,0:T(8,128)(2,1)S(1)} %constant_dynamic-slice_fusion.refs_4_.refs_1_), channel_id=1, source_target_pairs={{0,16},{4,20},{8,24},{12,28},{16,0},{20,4},{24,8},{28,12},{1,17},{... | collective-permute-start | bytes 786440 | tf_op jit(solution)/shard_map/ppermute | solution.py:596
  23.9 0.7 copy-start.8
  24.6 23.5 %collective-permute-start.4 = (bf16[256,512]{1,0:T(8,128)(2,1)S(1)}, bf16[256,512]{1,0:T(8,128)(2,1)}, u32[]{:S(2)}, u32[]{:S(2)}) collective-permute-start(bf16[256,512]{1,0:T(8,128)(2,1)S(1)} %constant_dynamic-slice_fusion.refs_4_.refs_1_), channel_id=1, source_target_pairs={{0,8},{4,12},{8,0},{12,4},{16,24},{20,28},{24,16},{28,20},{1,9},{5... | collective-permute-start | bytes 786440 | tf_op jit(solution)/shard_map/ppermute | solution.py:596
  25.4 33.1 %collective-permute-start.2 = (bf16[128,2048]{1,0:T(8,128)(2,1)S(1)}, bf16[128,2048]{1,0:T(8,128)(2,1)S(1)}, u32[]{:S(2)}, u32[]{:S(2)}) collective-permute-start(bf16[128,2048]{1,0:T(8,128)(2,1)S(1)} %collective-permute-done.1.refs_2_), channel_id=1, source_target_pairs={{0,1},{1,0},{2,3},{3,2},{4,5},{5,4},{6,7},{7,6},{8,9},{9,8},{10,11... | collective-permute-start | bytes 1572872 | tf_op jit(solution)/shard_map/ppermute | solution.py:596
  30.8 34.6 %collective-permute-start.3 = (bf16[256,512]{1,0:T(8,128)(2,1)S(1)}, bf16[256,512]{1,0:T(8,128)(2,1)S(1)}, u32[]{:S(2)}, u32[]{:S(2)}) collective-permute-start(bf16[256,512]{1,0:T(8,128)(2,1)S(1)} %constant_dynamic-slice_fusion.refs_4_.refs_1_), channel_id=1, source_target_pairs={{0,4},{4,0},{8,12},{12,8},{16,20},{20,16},{24,28},{28,24},{1,5},{5... | collective-permute-start | bytes 786440 | tf_op jit(solution)/shard_map/ppermute | solution.py:596
  46.6 18.9 %collective-permute-start.9 = (bf16[256,512]{1,0:T(8,128)(2,1)S(1)}, bf16[256,512]{1,0:T(8,128)(2,1)S(1)}, u32[]{:S(2)}, u32[]{:S(2)}) collective-permute-start(bf16[256,512]{1,0:T(8,128)(2,1)S(1)} %collective-permute-done.8.refs_10_.refs_7_), channel_id=1, source_target_pairs={{0,4},{4,0},{8,12},{12,8},{16,20},{20,16},{24,28},{28,24},{1,5},{5... | collective-permute-start | bytes 786440 | tf_op jit(solution)/shard_map/ppermute | solution.py:596
  48.1 17.4 %collective-permute-start.7 = (bf16[256,512]{1,0:T(8,128)(2,1)S(1)}, bf16[256,512]{1,0:T(8,128)(2,1)S(1)}, u32[]{:S(2)}, u32[]{:S(2)}) collective-permute-start(bf16[256,512]{1,0:T(8,128)(2,1)S(1)} %collective-permute-done.6.refs_8_.refs_5_), channel_id=1, source_target_pairs={{0,4},{4,0},{8,12},{12,8},{16,20},{20,16},{24,28},{28,24},{1,5},{5... | collective-permute-start | bytes 786440 | tf_op jit(solution)/shard_map/ppermute | solution.py:596
  48.6 17.4 %collective-permute-start.5 = (bf16[256,512]{1,0:T(8,128)(2,1)}, bf16[256,512]{1,0:T(8,128)(2,1)S(1)}, u32[]{:S(2)}, u32[]{:S(2)}) collective-permute-start(bf16[256,512]{1,0:T(8,128)(2,1)} %collective-permute-done.4.refs_6_.refs_3_), channel_id=1, source_target_pairs={{0,4},{4,0},{8,12},{12,8},{16,20},{20,16},{24,28},{28,24},{1,5},{5... | collective-permute-start | bytes 786440 | tf_op jit(solution)/shard_map/ppermute | solution.py:596
  58.5 0.9 copy-start.5
  59.5 0.9 copy-start.7
  60.4 0.9 copy-start.9
  68.5 3.8 %copy-start.2 = (f32[64,2048]{1,0:T(8,128)S(1)}, f32[64,2048]{1,0:T(8,128)}, u32[]{:S(2)}) copy-start(f32[64,2048]{1,0:T(8,128)} %fw.1) | copy-start | bytes 1572868
  68.5 3.8 %copy-start.3 = (f32[232,512]{1,0:T(8,128)S(1)}, f32[232,512]{1,0:T(8,128)}, u32[]{:S(2)}) copy-start(f32[232,512]{1,0:T(8,128)} %constant.32.clone.refs_0_.tab) | copy-start | bytes 1425412
  76.6 8.4 %collective-permute-start.28 = (f32[80,512]{1,0:T(8,128)S(1)}, f32[80,512]{1,0:T(8,128)S(1)}, u32[]{:S(2)}, u32[]{:S(2)}) collective-permute-start(f32[80,512]{1,0:T(8,128)S(1)} %correlate_part.1), channel_id=1, source_target_pairs={{0,4},{4,0},{8,12},{12,8},{16,20},{20,16},{24,28},{28,24},{1,5},{5... | collective-permute-start | bytes 491528 | tf_op jit(solution)/shard_map/ppermute | solution.py:596
  80.1 9.2 %collective-permute-start.20 = (bf16[1,256,512]{2,1,0:T(8,128)(2,1)S(1)}, bf16[1,256,512]{2,1,0:T(8,128)(2,1)S(1)}, u32[]{:S(2)}, u32[]{:S(2)}) collective-permute-start(bf16[1,256,512]{2,1,0:T(8,128)(2,1)S(1)} %get-tuple-element.62), channel_id=1, source_target_pairs={{0,4},{4,0},{8,12},{12,8},{16,20},{20,16},{24,28},{28,24},{1,5},{5... | collective-permute-start | bytes 786440 | tf_op jit(solution)/shard_map/ppermute | solution.py:596
  80.7 27.2 %collective-permute-start.13 = (bf16[128,512]{1,0:T(8,128)(2,1)S(1)}, bf16[128,512]{1,0:T(8,128)(2,1)S(1)}, u32[]{:S(2)}, u32[]{:S(2)}) collective-permute-start(bf16[128,512]{1,0:T(8,128)(2,1)S(1)} %get-tuple-element.48), channel_id=1, source_target_pairs={{0,1},{1,0},{2,3},{3,2},{4,5},{5,4},{6,7},{7,6},{8,9},{9,8},{10,11... | collective-permute-start | bytes 393224 | tf_op jit(solution)/shard_map/ppermute | solution.py:596
  80.7 14.3 %collective-permute-start.22 = (bf16[1,256,512]{2,1,0:T(8,128)(2,1)S(1)}, bf16[1,256,512]{2,1,0:T(8,128)(2,1)S(1)}, u32[]{:S(2)}, u32[]{:S(2)}) collective-permute-start(bf16[1,256,512]{2,1,0:T(8,128)(2,1)S(1)} %get-tuple-element.64), channel_id=1, source_target_pairs={{0,4},{4,0},{8,12},{12,8},{16,20},{20,16},{24,28},{28,24},{1,5},{5... | collective-permute-start | bytes 786440 | tf_op jit(solution)/shard_map/ppermute | solution.py:596
  82.2 22.3 %collective-permute-start.19 = (bf16[2,256,512]{2,1,0:T(8,128)(2,1)S(1)}, bf16[2,256,512]{2,1,0:T(8,128)(2,1)S(1)}, u32[]{:S(2)}, u32[]{:S(2)}) collective-permute-start(bf16[2,256,512]{2,1,0:T(8,128)(2,1)S(1)} %get-tuple-element.60), channel_id=1, source_target_pairs={{0,4},{4,0},{8,12},{12,8},{16,20},{20,16},{24,28},{28,24},{1,5},{5... | collective-permute-start | bytes 1572872 | tf_op jit(solution)/shard_map/ppermute | solution.py:596
  85.0 64.5 %collective-permute-start.16 = (bf16[128,2048]{1,0:T(8,128)(2,1)S(1)}, bf16[128,2048]{1,0:T(8,128)(2,1)S(1)}, u32[]{:S(2)}, u32[]{:S(2)}) collective-permute-start(bf16[128,2048]{1,0:T(8,128)(2,1)S(1)} %get-tuple-element.56), channel_id=1, source_target_pairs={{0,1},{1,0},{2,3},{3,2},{4,5},{5,4},{6,7},{7,6},{8,9},{9,8},{10,11... | collective-permute-start | bytes 1572872 | tf_op jit(solution)/shard_map/ppermute | solution.py:596
  89.3 16.9 %collective-permute-start.17 = (bf16[128,2048]{1,0:T(8,128)(2,1)S(1)}, bf16[128,2048]{1,0:T(8,128)(2,1)S(1)}, u32[]{:S(2)}, u32[]{:S(2)}) collective-permute-start(bf16[128,2048]{1,0:T(8,128)(2,1)S(1)} %get-tuple-element.58), channel_id=1, source_target_pairs={{0,1},{1,0},{2,3},{3,2},{4,5},{5,4},{6,7},{7,6},{8,9},{9,8},{10,11... | collective-permute-start | bytes 1572872 | tf_op jit(solution)/shard_map/ppermute | solution.py:596
  94.9 14.3 %collective-permute-start.21 = (bf16[256,512]{1,0:T(8,128)(2,1)S(1)}, bf16[256,512]{1,0:T(8,128)(2,1)S(1)}, u32[]{:S(2)}, u32[]{:S(2)}) collective-permute-start(bf16[256,512]{1,0:T(8,128)(2,1)S(1)} %fusion.5), channel_id=1, source_target_pairs={{0,24},{4,28},{8,16},{12,20},{16,8},{20,12},{24,0},{28,4},{1,25},{... | collective-permute-start | bytes 786440 | tf_op jit(solution)/shard_map/ppermute | solution.py:596
  104.5 15.2 %collective-permute-start.23 = (bf16[256,512]{1,0:T(8,128)(2,1)S(1)}, bf16[256,512]{1,0:T(8,128)(2,1)S(1)}, u32[]{:S(2)}, u32[]{:S(2)}) collective-permute-start(bf16[256,512]{1,0:T(8,128)(2,1)S(1)} %fusion.6), channel_id=1, source_target_pairs={{0,16},{4,20},{8,24},{12,28},{16,0},{20,4},{24,8},{28,12},{1,17},{... | collective-permute-start | bytes 786440 | tf_op jit(solution)/shard_map/ppermute | solution.py:596
  106.2 13.4 %collective-permute-start.24 = (bf16[256,512]{1,0:T(8,128)(2,1)S(1)}, bf16[256,512]{1,0:T(8,128)(2,1)S(1)}, u32[]{:S(2)}, u32[]{:S(2)}) collective-permute-start(bf16[256,512]{1,0:T(8,128)(2,1)S(1)} %fusion.7), channel_id=1, source_target_pairs={{0,8},{4,12},{8,0},{12,4},{16,24},{20,28},{24,16},{28,20},{1,9},{5... | collective-permute-start | bytes 786440 | tf_op jit(solution)/shard_map/ppermute | solution.py:596
  107.8 14.3 %collective-permute-start.31 = (bf16[80,512]{1,0:T(8,128)(2,1)S(1)}, bf16[80,512]{1,0:T(8,128)(2,1)S(1)}, u32[]{:S(2)}, u32[]{:S(2)}) collective-permute-start(bf16[80,512]{1,0:T(8,128)(2,1)S(1)} %add_convert_fusion.8), channel_id=1, source_target_pairs={{0,24},{4,28},{8,16},{12,20},{16,8},{20,12},{24,0},{28,4},{1,25},{... | collective-permute-start | bytes 245768 | tf_op jit(solution)/shard_map/ppermute | solution.py:596
  109.3 15.6 %collective-permute-start.30 = (bf16[80,512]{1,0:T(8,128)(2,1)S(1)}, bf16[80,512]{1,0:T(8,128)(2,1)S(1)}, u32[]{:S(2)}, u32[]{:S(2)}) collective-permute-start(bf16[80,512]{1,0:T(8,128)(2,1)S(1)} %add_convert_fusion.8), channel_id=1, source_target_pairs={{0,16},{4,20},{8,24},{12,28},{16,0},{20,4},{24,8},{28,12},{1,17},{... | collective-permute-start | bytes 245768 | tf_op jit(solution)/shard_map/ppermute | solution.py:596
  119.6 5.9 %collective-permute-start.29 = (bf16[80,512]{1,0:T(8,128)(2,1)S(1)}, bf16[80,512]{1,0:T(8,128)(2,1)S(1)}, u32[]{:S(2)}, u32[]{:S(2)}) collective-permute-start(bf16[80,512]{1,0:T(8,128)(2,1)S(1)} %add_convert_fusion.8), channel_id=1, source_target_pairs={{0,8},{4,12},{8,0},{12,4},{16,24},{20,28},{24,16},{28,20},{1,9},{5... | collective-permute-start | bytes 245768 | tf_op jit(solution)/shard_map/ppermute | solution.py:596
  119.7 29.9 %collective-permute-start.18 = (bf16[128,2048]{1,0:T(8,128)(2,1)S(1)}, bf16[128,2048]{1,0:T(8,128)(2,1)S(1)}, u32[]{:S(2)}, u32[]{:S(2)}) collective-permute-start(bf16[128,2048]{1,0:T(8,128)(2,1)S(1)} %add_convert_fusion.1), channel_id=1, source_target_pairs={{0,2},{1,3},{2,0},{3,1},{4,6},{5,7},{6,4},{7,5},{8,10},{9,11},{10,... | collective-permute-start | bytes 1572872 | tf_op jit(solution)/shard_map/ppermute | solution.py:596
  122.1 15.4 %collective-permute-start.14 = (bf16[128,512]{1,0:T(8,128)(2,1)S(1)}, bf16[128,512]{1,0:T(8,128)(2,1)S(1)}, u32[]{:S(2)}, u32[]{:S(2)}) collective-permute-start(bf16[128,512]{1,0:T(8,128)(2,1)S(1)} %get-tuple-element.49), channel_id=1, source_target_pairs={{0,2},{1,3},{2,0},{3,1},{4,6},{5,7},{6,4},{7,5},{8,10},{9,11},{10,... | collective-permute-start | bytes 393224 | tf_op jit(solution)/shard_map/ppermute | solution.py:596
  124.8 15.1 %collective-permute-start.15 = (bf16[128,512]{1,0:T(8,128)(2,1)S(1)}, bf16[128,512]{1,0:T(8,128)(2,1)S(1)}, u32[]{:S(2)}, u32[]{:S(2)}) collective-permute-start(bf16[128,512]{1,0:T(8,128)(2,1)S(1)} %get-tuple-element.50), channel_id=1, source_target_pairs={{0,3},{1,2},{2,1},{3,0},{4,7},{5,6},{6,5},{7,4},{8,11},{9,10},{10,... | collective-permute-start | bytes 393224 | tf_op jit(solution)/shard_map/ppermute | solution.py:596
  125.6 23.9 %collective-permute-start.26 = (bf16[256,512]{1,0:T(8,128)(2,1)S(1)}, bf16[256,512]{1,0:T(8,128)(2,1)S(1)}, u32[]{:S(2)}, u32[]{:S(2)}) collective-permute-start(bf16[256,512]{1,0:T(8,128)(2,1)S(1)} %fusion.3.refs_0_), channel_id=1, source_target_pairs={{0,2},{1,3},{2,0},{3,1},{4,6},{5,7},{6,4},{7,5},{8,10},{9,11},{10,... | collective-permute-start | bytes 786440 | tf_op jit(solution)/shard_map/ppermute | solution.py:596
  137.5 8.7 %collective-permute-start.33 = (bf16[80,512]{1,0:T(8,128)(2,1)S(1)}, bf16[80,512]{1,0:T(8,128)(2,1)S(1)}, u32[]{:S(2)}, u32[]{:S(2)}) collective-permute-start(bf16[80,512]{1,0:T(8,128)(2,1)S(1)} %add_convert_fusion.7.refs_0_), channel_id=1, source_target_pairs={{0,2},{1,3},{2,0},{3,1},{4,6},{5,7},{6,4},{7,5},{8,10},{9,11},{10,... | collective-permute-start | bytes 245768 | tf_op jit(solution)/shard_map/ppermute | solution.py:596
  139.9 7.7 %collective-permute-start.32 = (bf16[80,512]{1,0:T(8,128)(2,1)S(1)}, bf16[80,512]{1,0:T(8,128)(2,1)S(1)}, u32[]{:S(2)}, u32[]{:S(2)}) collective-permute-start(bf16[80,512]{1,0:T(8,128)(2,1)S(1)} %add_convert_fusion.7.refs_0_), channel_id=1, source_target_pairs={{0,1},{1,0},{2,3},{3,2},{4,5},{5,4},{6,7},{7,6},{8,9},{9,8},{10,11... | collective-permute-start | bytes 245768 | tf_op jit(solution)/shard_map/ppermute | solution.py:596
  146.2 1.4 collective-permute-start.34
  149.0 1.7 %collective-permute-start.25 = (bf16[256,512]{1,0:T(8,128)(2,1)S(1)}, bf16[256,512]{1,0:T(8,128)(2,1)S(1)}, u32[]{:S(2)}, u32[]{:S(2)}) collective-permute-start(bf16[256,512]{1,0:T(8,128)(2,1)S(1)} %fusion.3.refs_0_), channel_id=1, source_target_pairs={{0,1},{1,0},{2,3},{3,2},{4,5},{5,4},{6,7},{7,6},{8,9},{9,8},{10,11... | collective-permute-start | bytes 786440 | tf_op jit(solution)/shard_map/ppermute | solution.py:596
  149.5 1.5 %collective-permute-start.27 = (bf16[256,512]{1,0:T(8,128)(2,1)S(1)}, bf16[256,512]{1,0:T(8,128)(2,1)S(1)}, u32[]{:S(2)}, u32[]{:S(2)}) collective-permute-start(bf16[256,512]{1,0:T(8,128)(2,1)S(1)} %collective-permute-done.26.refs_2_), channel_id=1, source_target_pairs={{0,1},{1,0},{2,3},{3,2},{4,5},{5,4},{6,7},{7,6},{8,9},{9,8},{10,11... | collective-permute-start | bytes 786440 | tf_op jit(solution)/shard_map/ppermute | solution.py:596

commit v5 on v3

--- a/solution.py
+++ b/solution.py
@@ -132,7 +132,7 @@
             hidden_out[...] = hidden
             cos_out[...] = jnp.cos(pre)
             at = lax.broadcasted_iota(jnp.int32, (length, width), 0).astype(f32)
-            env = jnp.exp(-vec[0:1, :] * at) / vec[1:2, :]
+            env = jnp.exp(-vec[0:1, :] * at) * (1.0 / vec[1:2, :])
             env_out[...] = env
             filt[...] = (jnp.dot(hidden, fw[...], precision=highest) * env).astype(bf16)
 
@@ -150,7 +150,7 @@
                 store(out, 1, sin * cos_fine + cos * sin_fine)
                 return carry
 
-            lax.fori_loop(0, block // BASE, one, 0)
+            lax.fori_loop(0, block // BASE, one, 0, unroll=4)
 
         def store_both(out, part, value):
             high, low = split(value)
@@ -691,7 +691,7 @@
         met = {r: swap(live[r | bit], "seq", bit) for r in live if not r & bit}
         live = {r: add_round(live[r], met[r]) for r in met}
         bit *= 2
-    grad_signal = live[0]
+    grad_signal = live[0][None]
 
     met = swap(packed, "dp", 1)
     packed = (packed + met).astype(bf16)
@@ -699,13 +699,14 @@
     terms = [term.astype(f32) for term in terms]
     while len(terms) > 1:
         terms = [terms[i] + terms[i + 1] for i in range(0, len(terms), 2)]
-    packed_rel = gather_rel(terms[0].astype(bf16), "seq")
+    packed = terms[0].astype(bf16)
+    packed_rel = [packed] + [swap(packed, "seq", r) for r in range(1, seq_count)]
     grad_filter_weight, grad_skip, grad_pos_weight, grad_pos_bias = finish(
         place, packed_rel, order, emb_count
     )
     return (
         output[None],
-        grad_signal[None],
+        grad_signal,
         grad_gate_weight,
         grad_pos_weight,
         grad_pos_bias[0],

time: 153 us -> 153 us (level)
  no operation moved by 1% of the time
where the time goes in v5:
time: 153 us
  waiting for transfers between devices  77 us (50%)
  starting transfers between devices  35.5 us (23%)
  Pallas kernels  29.8 us (19%)
  local copies, waits for them, and re-layouts  5.85 us (4%)
  other arithmetic  3.78 us (2%)
    ppermute x35, waiting for transfers between devices, swap(): return lax.ppermute(value, axis, [(i, i ^ offset) for i in range(count)])  77 us
    ppermute x35, starting transfers between devices, swap(): return lax.ppermute(value, axis, [(i, i ^ offset) for i in range(count)])  35.5 us
    pallas_call x1, Pallas kernels, generate(): pl.pallas_call(body, grid_spec=pltpu.PrefetchScalarGridSpec(num_scalar_pr...  6.8 us
    unnamed x20, local copies, waits for them, and re-layouts  4.7 us
    pallas_call x1, Pallas kernels, convolve(): pl.pallas_call(body, grid_spec=pltpu.PrefetchScalarGridSpec(num_scalar_pr...  4.14 us
    pallas_call x1, Pallas kernels, correlate_back(): pl.pallas_call(body, grid_spec=pltpu.PrefetchScalarGridSpec(num_scalar_pr...  3.8 us
    pallas_call x1, Pallas kernels, correlate_part(): pl.pallas_call(body, grid_spec=pltpu.PrefetchScalarGridSpec(num_scalar_pr...  3.66 us
    pallas_call x2, Pallas kernels, assemble(): pl.pallas_call(body, in_specs=[smem()] + [pl.BlockSpec(memory_space=VMEM)...  3.37 us
  transfers between devices with their start and end apart: 35, of which 14 were waited for; matrix products, arithmetic and copies ran while one was open for 3% of the time, Pallas kernels for 12%

profile of v5, /device:TPU:0, one launch (start us, length us, event | category | flops | bytes accessed | tf_op | source)
XLA Modules:
  0.0 152.9 jit_solution(12062184383809028139)
XLA Ops:
  0.7 3.0 %collective-permute-start.1 = (bf16[128,2048]{1,0:T(8,128)(2,1)}, bf16[128,2048]{1,0:T(8,128)(2,1)S(1)}, u32[]{:S(2)}, u32[]{:S(2)}) collective-permute-start(bf16[128,2048]{1,0:T(8,128)(2,1)} %bitcast.31), channel_id=1, source_target_pairs={{0,2},{1,3},{2,0},{3,1},{4,6},{5,7},{6,4},{7,5},{8,10},{9,11},{10,... | collective-permute-start | bytes 1572872 | tf_op jit(solution)/shard_map/ppermute | solution.py:596
  3.7 1.1 dynamic-slice_bitcast_fusion
  4.8 0.3 collective-permute-start.12
  5.1 0.4 collective-permute-start.10
  5.5 1.6 %collective-permute-start.11 = (bf16[128,512]{1,0:T(8,128)(2,1)S(1)}, bf16[128,512]{1,0:T(8,128)(2,1)S(1)}, u32[]{:S(2)}, u32[]{:S(2)}) collective-permute-start(bf16[128,512]{1,0:T(8,128)(2,1)S(1)} %get-tuple-element.78), channel_id=1, source_target_pairs={{0,2},{1,3},{2,0},{3,1},{4,6},{5,7},{6,4},{7,5},{8,10},{9,11},{10,... | collective-permute-start | bytes 393224 | tf_op jit(solution)/shard_map/ppermute | solution.py:596
  7.1 12.0 %collective-permute-done.12.refs_7_.refs_15_ = bf16[128,512]{1,0:T(8,128)(2,1)S(1)} collective-permute-done((bf16[128,512]{1,0:T(8,128)(2,1)S(1)}, bf16[128,512]{1,0:T(8,128)(2,1)S(1)}, u32[]{:S(2)}, u32[]{:S(2)}) %collective-permute-start.12) | collective-permute-done | bytes 131104 | tf_op jit(solution)/shard_map/ppermute | solution.py:596
  19.0 0.7 copy-done.4
  19.7 3.6 %collective-permute-start.8 = (bf16[256,512]{1,0:T(8,128)(2,1)S(1)}, bf16[256,512]{1,0:T(8,128)(2,1)S(1)}, u32[]{:S(2)}, u32[]{:S(2)}) collective-permute-start(bf16[256,512]{1,0:T(8,128)(2,1)S(1)} %constant_dynamic-slice_fusion.refs_4_.refs_1_), channel_id=1, source_target_pairs={{0,24},{4,28},{8,16},{12,20},{16,8},{20,12},{24,0},{28,4},{1,25},{... | collective-permute-start | bytes 786440 | tf_op jit(solution)/shard_map/ppermute | solution.py:596
  23.3 0.7 copy-done.6
  23.9 0.7 copy-done.8
  24.6 0.8 collective-permute-start.4
  25.4 0.7 divide_sqrt_fusion
  26.1 4.7 %collective-permute-done.8.refs_10_.refs_7_ = bf16[256,512]{1,0:T(8,128)(2,1)S(1)} collective-permute-done((bf16[256,512]{1,0:T(8,128)(2,1)S(1)}, bf16[256,512]{1,0:T(8,128)(2,1)S(1)}, u32[]{:S(2)}, u32[]{:S(2)}) %collective-permute-start.8) | collective-permute-done | bytes 262176 | tf_op jit(solution)/shard_map/ppermute | solution.py:596
  30.8 1.5 collective-permute-start.3
  32.3 14.2 %collective-permute-done.6.refs_8_.refs_5_ = bf16[256,512]{1,0:T(8,128)(2,1)S(1)} collective-permute-done((bf16[256,512]{1,0:T(8,128)(2,1)S(1)}, bf16[256,512]{1,0:T(8,128)(2,1)S(1)}, u32[]{:S(2)}, u32[]{:S(2)}) %collective-permute-start.6) | collective-permute-done | bytes 262176 | tf_op jit(solution)/shard_map/ppermute | solution.py:596
  46.6 1.5 collective-permute-start.9
  48.1 0.5 collective-permute-start.7
  48.6 1.5 collective-permute-start.5
  50.1 0.1 pad_add_fusion.place_ref
  50.2 1.4 pad_maximum_fusion.refs_4_
  51.6 6.8 %generate.1 = (bf16[2,512,512]{2,1,0:T(8,128)(2,1)S(1)}, bf16[2,512,512]{2,1,0:T(8,128)(2,1)S(1)}, bf16[2,512,512]{2,1,0:T(8,128)(2,1)S(1)}, f32[2,512,512]{2,1,...) custom-call(s32[2]{0:T(128)S(1)} %pad_add_fusion.place_ref, ...), custom_call_target="tpu_custom_call" | custom-call | tf_op jit(solution)/shard_map/generate/pallas_call | solution.py:169
  58.4 0.9 copy-done.5
  59.3 0.9 copy-done.7
  60.2 0.9 copy-done.9
  61.1 4.1 %convolve.1 = (f32[2,512,512]{2,1,0:T(8,128)S(1)}, f32[512,512]{1,0:T(8,128)S(1)}, bf16[512,512]{1,0:T(8,128)(2,1)S(1)}) custom-call(s32[2]{0:T(128)S(1)} %pad_add_fusion.place_ref, bf16[128,2048]{1,0:T(8,128)(2,1)S(1)} %bitcast.33, bf16[128,2048]{1,0:T(8,128)(2,1)S(1)} %collective-permute-done.refs_1_, ...), custom_call_target="tpu_custom_call" | custom-call | tf_op jit(solution)/shard_map/convolve/pallas_call | solution.py:247
  65.3 0.7 collective-permute-done.5.refs_7_.refs_4_
  66.0 2.5 %gating.1 = (bf16[128,512]{1,0:T(8,128)(2,1)S(1)}, bf16[128,512]{1,0:T(8,128)(2,1)S(1)}, bf16[128,512]{1,0:T(8,128)(2,1)S(1)}, bf16[128,512]{1,0:T(8,128)(2,1)S(...) custom-call(s32[2]{0:T(128)S(1)} %pad_add_fusion.place_ref, ...), custom_call_target="tpu_custom_call" | custom-call | tf_op jit(solution)/shard_map/gating/pallas_call | solution.py:350
  68.5 3.8 %correlate_back.1 = (f32[512,512]{1,0:T(8,128)S(1)}, f32[2,512,512]{2,1,0:T(8,128)S(1)}) custom-call(s32[2]{0:T(128)S(1)} %pad_add_fusion.place_ref, bf16[512,512]{1,0:T(8,128)(2,1)S(1)} %get-tuple-element.52.cg, f32[512,512]{1,0:T(8,128)S(1)} %get-tuple-element.53.ig, f32[2,512,512]{2,1,0:T(8,128)S(1)} %get-tuple-element.41.refs_8_.fs, ...), custom_call_target="tpu_custom_call" | custom-call | tf_op jit(solution)/shard_map/correlate_back/pallas_call | solution.py:398
  72.3 3.7 %correlate_part.1 = f32[80,512]{1,0:T(8,128)S(1)} custom-call(s32[2]{0:T(128)S(1)} %pad_add_fusion.place_ref, f32[2,512,512]{2,1,0:T(8,128)S(1)} %get-tuple-element.65.gs, f32[8,512]{1,0:T(8,128)S(1)} %get-tuple-element.66.skip_sum_ref, f32[2,512,512]{2,1,0:T(8,128)S(1)} %get-tuple-element.67.ss, bf16[2,512,512]{2,1,0:T(8,128)(2,1)S(1)} %get-tuple-element.44.refs_11_.th, ...), custom_call_target="tpu_custom_call" | custom-call | tf_op jit(solution)/shard_map/correlate_part/pallas_call | solution.py:465
  76.0 1.6 %collective-permute-start.28 = (f32[80,512]{1,0:T(8,128)S(1)}, f32[80,512]{1,0:T(8,128)S(1)}, u32[]{:S(2)}, u32[]{:S(2)}) collective-permute-start(f32[80,512]{1,0:T(8,128)S(1)} %correlate_part.1), channel_id=1, source_target_pairs={{0,4},{4,0},{8,12},{12,8},{16,20},{20,16},{24,28},{28,24},{1,5},{5... | collective-permute-start | bytes 491528 | tf_op jit(solution)/shard_map/ppermute | solution.py:596
  77.6 1.8 %weight_grads.1 = (bf16[1,256,512]{2,1,0:T(8,128)(2,1)S(1)}, bf16[1,256,512]{2,1,0:T(8,128)(2,1)S(1)}, bf16[2,256,512]{2,1,0:T(8,128)(2,1)S(1)}, bf16[1,256,512]...) custom-call(s32[2]{0:T(128)S(1)} %pad_add_fusion.place_ref, ...), custom_call_target="tpu_custom_call" | custom-call | tf_op jit(solution)/shard_map/weight_grads/pallas_call | solution.py:307
  79.4 0.6 collective-permute-start.20
  80.0 1.5 collective-permute-start.22
  81.5 0.5 collective-permute-start.19
  82.0 2.3 %through_gate.1 = (bf16[128,2048]{1,0:T(8,128)(2,1)S(1)}, bf16[128,2048]{1,0:T(8,128)(2,1)S(1)}, bf16[128,2048]{1,0:T(8,128)(2,1)S(1)}, bf16[128,2048]{1,0:T(8,128)(2,1)S(1)}) custom-call(s32[2]{0:T(128)S(1)} %pad_add_fusion.place_ref, bf16[512,512]{1,0:T(8,128)(2,1)S(1)} %get-tuple-element.51.refs_0_.refs_4_, ...), custom_call_target="tpu_custom_call" | custom-call | tf_op jit(solution)/shard_map/through_gate/pallas_call | solution.py:522
  84.4 0.1 collective-permute-start.16
  84.5 4.2 %collective-permute-done.20 = bf16[1,256,512]{2,1,0:T(8,128)(2,1)S(1)} collective-permute-done((bf16[1,256,512]{2,1,0:T(8,128)(2,1)S(1)}, bf16[1,256,512]{2,1,0:T(8,128)(2,1)S(1)}, u32[]{:S(2)}, u32[]{:S(2)}) %collective-permute-start.20) | collective-permute-done | bytes 262176 | tf_op jit(solution)/shard_map/ppermute | solution.py:596
  88.7 5.5 %collective-permute-done.22 = bf16[1,256,512]{2,1,0:T(8,128)(2,1)S(1)} collective-permute-done((bf16[1,256,512]{2,1,0:T(8,128)(2,1)S(1)}, bf16[1,256,512]{2,1,0:T(8,128)(2,1)S(1)}, u32[]{:S(2)}, u32[]{:S(2)}) %collective-permute-start.22) | collective-permute-done | bytes 262176 | tf_op jit(solution)/shard_map/ppermute | solution.py:596
  94.3 2.5 %collective-permute-start.21 = (bf16[256,512]{1,0:T(8,128)(2,1)S(1)}, bf16[256,512]{1,0:T(8,128)(2,1)S(1)}, u32[]{:S(2)}, u32[]{:S(2)}) collective-permute-start(bf16[256,512]{1,0:T(8,128)(2,1)S(1)} %fusion.5), channel_id=1, source_target_pairs={{0,24},{4,28},{8,16},{12,20},{16,8},{20,12},{24,0},{28,4},{1,25},{... | collective-permute-start | bytes 786440 | tf_op jit(solution)/shard_map/ppermute | solution.py:596
  96.8 7.0 %collective-permute-done.19 = bf16[2,256,512]{2,1,0:T(8,128)(2,1)S(1)} collective-permute-done((bf16[2,256,512]{2,1,0:T(8,128)(2,1)S(1)}, bf16[2,256,512]{2,1,0:T(8,128)(2,1)S(1)}, u32[]{:S(2)}, u32[]{:S(2)}) %collective-permute-start.19) | collective-permute-done | bytes 524320 | tf_op jit(solution)/shard_map/ppermute | solution.py:596
  103.8 1.7 %collective-permute-start.23 = (bf16[256,512]{1,0:T(8,128)(2,1)S(1)}, bf16[256,512]{1,0:T(8,128)(2,1)S(1)}, u32[]{:S(2)}, u32[]{:S(2)}) collective-permute-start(bf16[256,512]{1,0:T(8,128)(2,1)S(1)} %fusion.6), channel_id=1, source_target_pairs={{0,16},{4,20},{8,24},{12,28},{16,0},{20,4},{24,8},{28,12},{1,17},{... | collective-permute-start | bytes 786440 | tf_op jit(solution)/shard_map/ppermute | solution.py:596
  105.6 1.4 collective-permute-start.24
  107.0 0.2 add_convert_fusion.1
  107.2 1.4 collective-permute-start.31
  108.6 0.8 collective-permute-start.30
  109.4 9.6 %collective-permute-done.23 = bf16[256,512]{1,0:T(8,128)(2,1)S(1)} collective-permute-done((bf16[256,512]{1,0:T(8,128)(2,1)S(1)}, bf16[256,512]{1,0:T(8,128)(2,1)S(1)}, u32[]{:S(2)}, u32[]{:S(2)}) %collective-permute-start.23) | collective-permute-done | bytes 262176 | tf_op jit(solution)/shard_map/ppermute | solution.py:596
  119.0 2.3 %collective-permute-start.18 = (bf16[128,2048]{1,0:T(8,128)(2,1)S(1)}, bf16[128,2048]{1,0:T(8,128)(2,1)S(1)}, u32[]{:S(2)}, u32[]{:S(2)}) collective-permute-start(bf16[128,2048]{1,0:T(8,128)(2,1)S(1)} %add_convert_fusion.1), channel_id=1, source_target_pairs={{0,2},{1,3},{2,0},{3,1},{4,6},{5,7},{6,4},{7,5},{8,10},{9,11},{10,... | collective-permute-start | bytes 1572872 | tf_op jit(solution)/shard_map/ppermute | solution.py:596
  121.3 0.2 fusion.3.refs_0_
  121.5 1.5 collective-permute-start.14
  122.9 1.2 collective-permute-done.30
  124.2 0.3 collective-permute-start.15
  124.4 0.5 collective-permute-done.29
  124.9 1.7 %collective-permute-start.26 = (bf16[256,512]{1,0:T(8,128)(2,1)S(1)}, bf16[256,512]{1,0:T(8,128)(2,1)S(1)}, u32[]{:S(2)}, u32[]{:S(2)}) collective-permute-start(bf16[256,512]{1,0:T(8,128)(2,1)S(1)} %fusion.3.refs_0_), channel_id=1, source_target_pairs={{0,2},{1,3},{2,0},{3,1},{4,6},{5,7},{6,4},{7,5},{8,10},{9,11},{10,... | collective-permute-start | bytes 786440 | tf_op jit(solution)/shard_map/ppermute | solution.py:596
  126.7 10.1 %collective-permute-done.14.refs_2_ = bf16[128,512]{1,0:T(8,128)(2,1)S(1)} collective-permute-done((bf16[128,512]{1,0:T(8,128)(2,1)S(1)}, bf16[128,512]{1,0:T(8,128)(2,1)S(1)}, u32[]{:S(2)}, u32[]{:S(2)}) %collective-permute-start.14) | collective-permute-done | bytes 131104 | tf_op jit(solution)/shard_map/ppermute | solution.py:596
  136.9 1.9 %collective-permute-done.15.refs_3_ = bf16[128,512]{1,0:T(8,128)(2,1)S(1)} collective-permute-done((bf16[128,512]{1,0:T(8,128)(2,1)S(1)}, bf16[128,512]{1,0:T(8,128)(2,1)S(1)}, u32[]{:S(2)}, u32[]{:S(2)}) %collective-permute-start.15) | collective-permute-done | bytes 131104 | tf_op jit(solution)/shard_map/ppermute | solution.py:596
  138.8 0.4 collective-permute-start.33
  139.2 5.0 %collective-permute-done.34.refs_3_ = bf16[80,512]{1,0:T(8,128)(2,1)S(1)} collective-permute-done((bf16[80,512]{1,0:T(8,128)(2,1)S(1)}, bf16[80,512]{1,0:T(8,128)(2,1)S(1)}, u32[]{:S(2)}, u32[]{:S(2)}) %collective-permute-start.34) | collective-permute-done | bytes 81952 | tf_op jit(solution)/shard_map/ppermute | solution.py:596
  144.2 2.0 %collective-permute-start.32 = (bf16[80,512]{1,0:T(8,128)(2,1)S(1)}, bf16[80,512]{1,0:T(8,128)(2,1)S(1)}, u32[]{:S(2)}, u32[]{:S(2)}) collective-permute-start(bf16[80,512]{1,0:T(8,128)(2,1)S(1)} %add_convert_fusion.7.refs_0_), channel_id=1, source_target_pairs={{0,1},{1,0},{2,3},{3,2},{4,5},{5,4},{6,7},{7,6},{8,9},{9,8},{10,11... | collective-permute-start | bytes 245768 | tf_op jit(solution)/shard_map/ppermute | solution.py:596
  146.3 1.4 assemble.2
  147.6 1.4 finish.1
  149.0 0.5 collective-permute-start.27
  149.5 1.0 fusion
  150.6 0.4 collective-permute-done.27.refs_3_
  150.9 2.0 %assemble.3 = f32[256,2048]{1,0:T(8,128)} custom-call(s32[2]{0:T(128)S(1)} %pad_add_fusion.place_ref, bf16[256,512]{1,0:T(8,128)(2,1)S(1)} %fusion.3.refs_0_, bf16[256,512]{1,0:T(8,128)(2,1)S(1)} %collective-permute-done.25.refs_1_, bf16[256,512]{1,0:T(8,128)(2,1)S(1)} %collective-permute-done.26.refs_2_, bf16[256,512]{1,0:T(8,128)(2,1)S(1)} %collective-permute-done.27.refs_3_), custom_call_target="tpu_custom_call" | custom-call | tf_op jit(solution)/shard_map/assemble/pallas_call | solution.py:542
  (49 shorter events, 0.4 us)
Async XLA Ops:
  0.6 6.4 %copy-start = (bf16[256,2048]{1,0:T(8,128)(2,1)S(1)}, bf16[256,2048]{1,0:T(8,128)(2,1)}, u32[]{:S(2)}) copy-start(bf16[256,2048]{1,0:T(8,128)(2,1)} %param.10) | copy-start | bytes 3145732
  0.6 57.7 %copy-start.1 = (bf16[1,128,2048]{2,1,0:T(8,128)(2,1)S(1)}, bf16[1,128,2048]{2,1,0:T(8,128)(2,1)}, u32[]{:S(2)}) copy-start(bf16[1,128,2048]{2,1,0:T(8,128)(2,1)} %param.9) | copy-start | bytes 1572868
  0.7 24.7 %collective-permute-start.1 = (bf16[128,2048]{1,0:T(8,128)(2,1)}, bf16[128,2048]{1,0:T(8,128)(2,1)S(1)}, u32[]{:S(2)}, u32[]{:S(2)}) collective-permute-start(bf16[128,2048]{1,0:T(8,128)(2,1)} %bitcast.31), channel_id=1, source_target_pairs={{0,2},{1,3},{2,0},{3,1},{4,6},{5,7},{6,4},{7,5},{8,10},{9,11},{10,... | collective-permute-start | bytes 1572872 | tf_op jit(solution)/shard_map/ppermute | solution.py:596
  3.7 44.9 %collective-permute-start = (bf16[128,2048]{1,0:T(8,128)(2,1)}, bf16[128,2048]{1,0:T(8,128)(2,1)S(1)}, u32[]{:S(2)}, u32[]{:S(2)}) collective-permute-start(bf16[128,2048]{1,0:T(8,128)(2,1)} %bitcast.32), channel_id=1, source_target_pairs={{0,1},{1,0},{2,3},{3,2},{4,5},{5,4},{6,7},{7,6},{8,9},{9,8},{10,11... | collective-permute-start | bytes 1572872 | tf_op jit(solution)/shard_map/ppermute | solution.py:596
  4.8 14.2 %collective-permute-start.12 = (bf16[128,512]{1,0:T(8,128)(2,1)S(1)}, bf16[128,512]{1,0:T(8,128)(2,1)S(1)}, u32[]{:S(2)}, u32[]{:S(2)}) collective-permute-start(bf16[128,512]{1,0:T(8,128)(2,1)S(1)} %get-tuple-element.75), channel_id=1, source_target_pairs={{0,3},{1,2},{2,1},{3,0},{4,7},{5,6},{6,5},{7,4},{8,11},{9,10},{10,... | collective-permute-start | bytes 393224 | tf_op jit(solution)/shard_map/ppermute | solution.py:596
  5.1 18.2 %collective-permute-start.10 = (bf16[128,512]{1,0:T(8,128)(2,1)S(1)}, bf16[128,512]{1,0:T(8,128)(2,1)S(1)}, u32[]{:S(2)}, u32[]{:S(2)}) collective-permute-start(bf16[128,512]{1,0:T(8,128)(2,1)S(1)} %get-tuple-element.76), channel_id=1, source_target_pairs={{0,1},{1,0},{2,3},{3,2},{4,5},{5,4},{6,7},{7,6},{8,9},{9,8},{10,11... | collective-permute-start | bytes 393224 | tf_op jit(solution)/shard_map/ppermute | solution.py:596
  5.5 18.5 %collective-permute-start.11 = (bf16[128,512]{1,0:T(8,128)(2,1)S(1)}, bf16[128,512]{1,0:T(8,128)(2,1)S(1)}, u32[]{:S(2)}, u32[]{:S(2)}) collective-permute-start(bf16[128,512]{1,0:T(8,128)(2,1)S(1)} %get-tuple-element.78), channel_id=1, source_target_pairs={{0,2},{1,3},{2,0},{3,1},{4,6},{5,7},{6,4},{7,5},{8,10},{9,11},{10,... | collective-permute-start | bytes 393224 | tf_op jit(solution)/shard_map/ppermute | solution.py:596
  19.0 0.7 copy-start.4
  19.7 11.1 %collective-permute-start.8 = (bf16[256,512]{1,0:T(8,128)(2,1)S(1)}, bf16[256,512]{1,0:T(8,128)(2,1)S(1)}, u32[]{:S(2)}, u32[]{:S(2)}) collective-permute-start(bf16[256,512]{1,0:T(8,128)(2,1)S(1)} %constant_dynamic-slice_fusion.refs_4_.refs_1_), channel_id=1, source_target_pairs={{0,24},{4,28},{8,16},{12,20},{16,8},{20,12},{24,0},{28,4},{1,25},{... | collective-permute-start | bytes 786440 | tf_op jit(solution)/shard_map/ppermute | solution.py:596
  23.3 0.7 copy-start.6
  23.9 22.6 %collective-permute-start.6 = (bf16[256,512]{1,0:T(8,128)(2,1)S(1)}, bf16[256,512]{1,0:T(8,128)(2,1)S(1)}, u32[]{:S(2)}, u32[]{:S(2)}) collective-permute-start(bf16[256,512]{1,0:T(8,128)(2,1)S(1)} %constant_dynamic-slice_fusion.refs_4_.refs_1_), channel_id=1, source_target_pairs={{0,16},{4,20},{8,24},{12,28},{16,0},{20,4},{24,8},{28,12},{1,17},{... | collective-permute-start | bytes 786440 | tf_op jit(solution)/shard_map/ppermute | solution.py:596
  23.9 0.7 copy-start.8
  24.6 23.5 %collective-permute-start.4 = (bf16[256,512]{1,0:T(8,128)(2,1)S(1)}, bf16[256,512]{1,0:T(8,128)(2,1)}, u32[]{:S(2)}, u32[]{:S(2)}) collective-permute-start(bf16[256,512]{1,0:T(8,128)(2,1)S(1)} %constant_dynamic-slice_fusion.refs_4_.refs_1_), channel_id=1, source_target_pairs={{0,8},{4,12},{8,0},{12,4},{16,24},{20,28},{24,16},{28,20},{1,9},{5... | collective-permute-start | bytes 786440 | tf_op jit(solution)/shard_map/ppermute | solution.py:596
  25.4 33.0 %collective-permute-start.2 = (bf16[128,2048]{1,0:T(8,128)(2,1)S(1)}, bf16[128,2048]{1,0:T(8,128)(2,1)S(1)}, u32[]{:S(2)}, u32[]{:S(2)}) collective-permute-start(bf16[128,2048]{1,0:T(8,128)(2,1)S(1)} %collective-permute-done.1.refs_2_), channel_id=1, source_target_pairs={{0,1},{1,0},{2,3},{3,2},{4,5},{5,4},{6,7},{7,6},{8,9},{9,8},{10,11... | collective-permute-start | bytes 1572872 | tf_op jit(solution)/shard_map/ppermute | solution.py:596
  30.8 34.5 %collective-permute-start.3 = (bf16[256,512]{1,0:T(8,128)(2,1)S(1)}, bf16[256,512]{1,0:T(8,128)(2,1)S(1)}, u32[]{:S(2)}, u32[]{:S(2)}) collective-permute-start(bf16[256,512]{1,0:T(8,128)(2,1)S(1)} %constant_dynamic-slice_fusion.refs_4_.refs_1_), channel_id=1, source_target_pairs={{0,4},{4,0},{8,12},{12,8},{16,20},{20,16},{24,28},{28,24},{1,5},{5... | collective-permute-start | bytes 786440 | tf_op jit(solution)/shard_map/ppermute | solution.py:596
  46.6 18.7 %collective-permute-start.9 = (bf16[256,512]{1,0:T(8,128)(2,1)S(1)}, bf16[256,512]{1,0:T(8,128)(2,1)S(1)}, u32[]{:S(2)}, u32[]{:S(2)}) collective-permute-start(bf16[256,512]{1,0:T(8,128)(2,1)S(1)} %collective-permute-done.8.refs_10_.refs_7_), channel_id=1, source_target_pairs={{0,4},{4,0},{8,12},{12,8},{16,20},{20,16},{24,28},{28,24},{1,5},{5... | collective-permute-start | bytes 786440 | tf_op jit(solution)/shard_map/ppermute | solution.py:596
  48.1 17.2 %collective-permute-start.7 = (bf16[256,512]{1,0:T(8,128)(2,1)S(1)}, bf16[256,512]{1,0:T(8,128)(2,1)S(1)}, u32[]{:S(2)}, u32[]{:S(2)}) collective-permute-start(bf16[256,512]{1,0:T(8,128)(2,1)S(1)} %collective-permute-done.6.refs_8_.refs_5_), channel_id=1, source_target_pairs={{0,4},{4,0},{8,12},{12,8},{16,20},{20,16},{24,28},{28,24},{1,5},{5... | collective-permute-start | bytes 786440 | tf_op jit(solution)/shard_map/ppermute | solution.py:596
  48.6 17.4 %collective-permute-start.5 = (bf16[256,512]{1,0:T(8,128)(2,1)}, bf16[256,512]{1,0:T(8,128)(2,1)S(1)}, u32[]{:S(2)}, u32[]{:S(2)}) collective-permute-start(bf16[256,512]{1,0:T(8,128)(2,1)} %collective-permute-done.4.refs_6_.refs_3_), channel_id=1, source_target_pairs={{0,4},{4,0},{8,12},{12,8},{16,20},{20,16},{24,28},{28,24},{1,5},{5... | collective-permute-start | bytes 786440 | tf_op jit(solution)/shard_map/ppermute | solution.py:596
  58.4 0.9 copy-start.5
  59.3 0.9 copy-start.7
  60.2 0.9 copy-start.9
  68.5 3.8 %copy-start.2 = (f32[64,2048]{1,0:T(8,128)S(1)}, f32[64,2048]{1,0:T(8,128)}, u32[]{:S(2)}) copy-start(f32[64,2048]{1,0:T(8,128)} %fw.1) | copy-start | bytes 1572868
  68.5 3.8 %copy-start.3 = (f32[232,512]{1,0:T(8,128)S(1)}, f32[232,512]{1,0:T(8,128)}, u32[]{:S(2)}) copy-start(f32[232,512]{1,0:T(8,128)} %constant.32.clone.refs_0_.tab) | copy-start | bytes 1425412
  76.0 8.4 %collective-permute-start.28 = (f32[80,512]{1,0:T(8,128)S(1)}, f32[80,512]{1,0:T(8,128)S(1)}, u32[]{:S(2)}, u32[]{:S(2)}) collective-permute-start(f32[80,512]{1,0:T(8,128)S(1)} %correlate_part.1), channel_id=1, source_target_pairs={{0,4},{4,0},{8,12},{12,8},{16,20},{20,16},{24,28},{28,24},{1,5},{5... | collective-permute-start | bytes 491528 | tf_op jit(solution)/shard_map/ppermute | solution.py:596
  79.4 9.2 %collective-permute-start.20 = (bf16[1,256,512]{2,1,0:T(8,128)(2,1)S(1)}, bf16[1,256,512]{2,1,0:T(8,128)(2,1)S(1)}, u32[]{:S(2)}, u32[]{:S(2)}) collective-permute-start(bf16[1,256,512]{2,1,0:T(8,128)(2,1)S(1)} %get-tuple-element.62), channel_id=1, source_target_pairs={{0,4},{4,0},{8,12},{12,8},{16,20},{20,16},{24,28},{28,24},{1,5},{5... | collective-permute-start | bytes 786440 | tf_op jit(solution)/shard_map/ppermute | solution.py:596
  80.0 27.2 %collective-permute-start.13 = (bf16[128,512]{1,0:T(8,128)(2,1)S(1)}, bf16[128,512]{1,0:T(8,128)(2,1)S(1)}, u32[]{:S(2)}, u32[]{:S(2)}) collective-permute-start(bf16[128,512]{1,0:T(8,128)(2,1)S(1)} %get-tuple-element.48), channel_id=1, source_target_pairs={{0,1},{1,0},{2,3},{3,2},{4,5},{5,4},{6,7},{7,6},{8,9},{9,8},{10,11... | collective-permute-start | bytes 393224 | tf_op jit(solution)/shard_map/ppermute | solution.py:596
  80.0 14.3 %collective-permute-start.22 = (bf16[1,256,512]{2,1,0:T(8,128)(2,1)S(1)}, bf16[1,256,512]{2,1,0:T(8,128)(2,1)S(1)}, u32[]{:S(2)}, u32[]{:S(2)}) collective-permute-start(bf16[1,256,512]{2,1,0:T(8,128)(2,1)S(1)} %get-tuple-element.64), channel_id=1, source_target_pairs={{0,4},{4,0},{8,12},{12,8},{16,20},{20,16},{24,28},{28,24},{1,5},{5... | collective-permute-start | bytes 786440 | tf_op jit(solution)/shard_map/ppermute | solution.py:596
  81.5 22.3 %collective-permute-start.19 = (bf16[2,256,512]{2,1,0:T(8,128)(2,1)S(1)}, bf16[2,256,512]{2,1,0:T(8,128)(2,1)S(1)}, u32[]{:S(2)}, u32[]{:S(2)}) collective-permute-start(bf16[2,256,512]{2,1,0:T(8,128)(2,1)S(1)} %get-tuple-element.60), channel_id=1, source_target_pairs={{0,4},{4,0},{8,12},{12,8},{16,20},{20,16},{24,28},{28,24},{1,5},{5... | collective-permute-start | bytes 1572872 | tf_op jit(solution)/shard_map/ppermute | solution.py:596
  84.4 65.2 %collective-permute-start.16 = (bf16[128,2048]{1,0:T(8,128)(2,1)S(1)}, bf16[128,2048]{1,0:T(8,128)(2,1)S(1)}, u32[]{:S(2)}, u32[]{:S(2)}) collective-permute-start(bf16[128,2048]{1,0:T(8,128)(2,1)S(1)} %get-tuple-element.56), channel_id=1, source_target_pairs={{0,1},{1,0},{2,3},{3,2},{4,5},{5,4},{6,7},{7,6},{8,9},{9,8},{10,11... | collective-permute-start | bytes 1572872 | tf_op jit(solution)/shard_map/ppermute | solution.py:596
  88.7 16.9 %collective-permute-start.17 = (bf16[128,2048]{1,0:T(8,128)(2,1)S(1)}, bf16[128,2048]{1,0:T(8,128)(2,1)S(1)}, u32[]{:S(2)}, u32[]{:S(2)}) collective-permute-start(bf16[128,2048]{1,0:T(8,128)(2,1)S(1)} %get-tuple-element.58), channel_id=1, source_target_pairs={{0,1},{1,0},{2,3},{3,2},{4,5},{5,4},{6,7},{7,6},{8,9},{9,8},{10,11... | collective-permute-start | bytes 1572872 | tf_op jit(solution)/shard_map/ppermute | solution.py:596
  94.3 14.3 %collective-permute-start.21 = (bf16[256,512]{1,0:T(8,128)(2,1)S(1)}, bf16[256,512]{1,0:T(8,128)(2,1)S(1)}, u32[]{:S(2)}, u32[]{:S(2)}) collective-permute-start(bf16[256,512]{1,0:T(8,128)(2,1)S(1)} %fusion.5), channel_id=1, source_target_pairs={{0,24},{4,28},{8,16},{12,20},{16,8},{20,12},{24,0},{28,4},{1,25},{... | collective-permute-start | bytes 786440 | tf_op jit(solution)/shard_map/ppermute | solution.py:596
  103.8 15.2 %collective-permute-start.23 = (bf16[256,512]{1,0:T(8,128)(2,1)S(1)}, bf16[256,512]{1,0:T(8,128)(2,1)S(1)}, u32[]{:S(2)}, u32[]{:S(2)}) collective-permute-start(bf16[256,512]{1,0:T(8,128)(2,1)S(1)} %fusion.6), channel_id=1, source_target_pairs={{0,16},{4,20},{8,24},{12,28},{16,0},{20,4},{24,8},{28,12},{1,17},{... | collective-permute-start | bytes 786440 | tf_op jit(solution)/shard_map/ppermute | solution.py:596
  105.6 13.4 %collective-permute-start.24 = (bf16[256,512]{1,0:T(8,128)(2,1)S(1)}, bf16[256,512]{1,0:T(8,128)(2,1)S(1)}, u32[]{:S(2)}, u32[]{:S(2)}) collective-permute-start(bf16[256,512]{1,0:T(8,128)(2,1)S(1)} %fusion.7), channel_id=1, source_target_pairs={{0,8},{4,12},{8,0},{12,4},{16,24},{20,28},{24,16},{28,20},{1,9},{5... | collective-permute-start | bytes 786440 | tf_op jit(solution)/shard_map/ppermute | solution.py:596
  107.2 14.3 %collective-permute-start.31 = (bf16[80,512]{1,0:T(8,128)(2,1)S(1)}, bf16[80,512]{1,0:T(8,128)(2,1)S(1)}, u32[]{:S(2)}, u32[]{:S(2)}) collective-permute-start(bf16[80,512]{1,0:T(8,128)(2,1)S(1)} %add_convert_fusion.8), channel_id=1, source_target_pairs={{0,24},{4,28},{8,16},{12,20},{16,8},{20,12},{24,0},{28,4},{1,25},{... | collective-permute-start | bytes 245768 | tf_op jit(solution)/shard_map/ppermute | solution.py:596
  108.6 15.6 %collective-permute-start.30 = (bf16[80,512]{1,0:T(8,128)(2,1)S(1)}, bf16[80,512]{1,0:T(8,128)(2,1)S(1)}, u32[]{:S(2)}, u32[]{:S(2)}) collective-permute-start(bf16[80,512]{1,0:T(8,128)(2,1)S(1)} %add_convert_fusion.8), channel_id=1, source_target_pairs={{0,16},{4,20},{8,24},{12,28},{16,0},{20,4},{24,8},{28,12},{1,17},{... | collective-permute-start | bytes 245768 | tf_op jit(solution)/shard_map/ppermute | solution.py:596
  119.0 5.9 %collective-permute-start.29 = (bf16[80,512]{1,0:T(8,128)(2,1)S(1)}, bf16[80,512]{1,0:T(8,128)(2,1)S(1)}, u32[]{:S(2)}, u32[]{:S(2)}) collective-permute-start(bf16[80,512]{1,0:T(8,128)(2,1)S(1)} %add_convert_fusion.8), channel_id=1, source_target_pairs={{0,8},{4,12},{8,0},{12,4},{16,24},{20,28},{24,16},{28,20},{1,9},{5... | collective-permute-start | bytes 245768 | tf_op jit(solution)/shard_map/ppermute | solution.py:596
  119.0 30.5 %collective-permute-start.18 = (bf16[128,2048]{1,0:T(8,128)(2,1)S(1)}, bf16[128,2048]{1,0:T(8,128)(2,1)S(1)}, u32[]{:S(2)}, u32[]{:S(2)}) collective-permute-start(bf16[128,2048]{1,0:T(8,128)(2,1)S(1)} %add_convert_fusion.1), channel_id=1, source_target_pairs={{0,2},{1,3},{2,0},{3,1},{4,6},{5,7},{6,4},{7,5},{8,10},{9,11},{10,... | collective-permute-start | bytes 1572872 | tf_op jit(solution)/shard_map/ppermute | solution.py:596
  121.5 15.4 %collective-permute-start.14 = (bf16[128,512]{1,0:T(8,128)(2,1)S(1)}, bf16[128,512]{1,0:T(8,128)(2,1)S(1)}, u32[]{:S(2)}, u32[]{:S(2)}) collective-permute-start(bf16[128,512]{1,0:T(8,128)(2,1)S(1)} %get-tuple-element.49), channel_id=1, source_target_pairs={{0,2},{1,3},{2,0},{3,1},{4,6},{5,7},{6,4},{7,5},{8,10},{9,11},{10,... | collective-permute-start | bytes 393224 | tf_op jit(solution)/shard_map/ppermute | solution.py:596
  124.2 14.6 %collective-permute-start.15 = (bf16[128,512]{1,0:T(8,128)(2,1)S(1)}, bf16[128,512]{1,0:T(8,128)(2,1)S(1)}, u32[]{:S(2)}, u32[]{:S(2)}) collective-permute-start(bf16[128,512]{1,0:T(8,128)(2,1)S(1)} %get-tuple-element.50), channel_id=1, source_target_pairs={{0,3},{1,2},{2,1},{3,0},{4,7},{5,6},{6,5},{7,4},{8,11},{9,10},{10,... | collective-permute-start | bytes 393224 | tf_op jit(solution)/shard_map/ppermute | solution.py:596
  124.9 24.1 %collective-permute-start.26 = (bf16[256,512]{1,0:T(8,128)(2,1)S(1)}, bf16[256,512]{1,0:T(8,128)(2,1)S(1)}, u32[]{:S(2)}, u32[]{:S(2)}) collective-permute-start(bf16[256,512]{1,0:T(8,128)(2,1)S(1)} %fusion.3.refs_0_), channel_id=1, source_target_pairs={{0,2},{1,3},{2,0},{3,1},{4,6},{5,7},{6,4},{7,5},{8,10},{9,11},{10,... | collective-permute-start | bytes 786440 | tf_op jit(solution)/shard_map/ppermute | solution.py:596
  136.9 7.3 %collective-permute-start.34 = (bf16[80,512]{1,0:T(8,128)(2,1)S(1)}, bf16[80,512]{1,0:T(8,128)(2,1)S(1)}, u32[]{:S(2)}, u32[]{:S(2)}) collective-permute-start(bf16[80,512]{1,0:T(8,128)(2,1)S(1)} %add_convert_fusion.7.refs_0_), channel_id=1, source_target_pairs={{0,3},{1,2},{2,1},{3,0},{4,7},{5,6},{6,5},{7,4},{8,11},{9,10},{10,... | collective-permute-start | bytes 245768 | tf_op jit(solution)/shard_map/ppermute | solution.py:596
  138.8 8.8 %collective-permute-start.33 = (bf16[80,512]{1,0:T(8,128)(2,1)S(1)}, bf16[80,512]{1,0:T(8,128)(2,1)S(1)}, u32[]{:S(2)}, u32[]{:S(2)}) collective-permute-start(bf16[80,512]{1,0:T(8,128)(2,1)S(1)} %add_convert_fusion.7.refs_0_), channel_id=1, source_target_pairs={{0,2},{1,3},{2,0},{3,1},{4,6},{5,7},{6,4},{7,5},{8,10},{9,11},{10,... | collective-permute-start | bytes 245768 | tf_op jit(solution)/shard_map/ppermute | solution.py:596
  144.2 3.4 %collective-permute-start.32 = (bf16[80,512]{1,0:T(8,128)(2,1)S(1)}, bf16[80,512]{1,0:T(8,128)(2,1)S(1)}, u32[]{:S(2)}, u32[]{:S(2)}) collective-permute-start(bf16[80,512]{1,0:T(8,128)(2,1)S(1)} %add_convert_fusion.7.refs_0_), channel_id=1, source_target_pairs={{0,1},{1,0},{2,3},{3,2},{4,5},{5,4},{6,7},{7,6},{8,9},{9,8},{10,11... | collective-permute-start | bytes 245768 | tf_op jit(solution)/shard_map/ppermute | solution.py:596
  149.0 1.6 %collective-permute-start.25 = (bf16[256,512]{1,0:T(8,128)(2,1)S(1)}, bf16[256,512]{1,0:T(8,128)(2,1)S(1)}, u32[]{:S(2)}, u32[]{:S(2)}) collective-permute-start(bf16[256,512]{1,0:T(8,128)(2,1)S(1)} %fusion.3.refs_0_), channel_id=1, source_target_pairs={{0,1},{1,0},{2,3},{3,2},{4,5},{5,4},{6,7},{7,6},{8,9},{9,8},{10,11... | collective-permute-start | bytes 786440 | tf_op jit(solution)/shard_map/ppermute | solution.py:596
  149.0 1.9 %collective-permute-start.27 = (bf16[256,512]{1,0:T(8,128)(2,1)S(1)}, bf16[256,512]{1,0:T(8,128)(2,1)S(1)}, u32[]{:S(2)}, u32[]{:S(2)}) collective-permute-start(bf16[256,512]{1,0:T(8,128)(2,1)S(1)} %collective-permute-done.26.refs_2_), channel_id=1, source_target_pairs={{0,1},{1,0},{2,3},{3,2},{4,5},{5,4},{6,7},{7,6},{8,9},{9,8},{10,11... | collective-permute-start | bytes 786440 | tf_op jit(solution)/shard_map/ppermute | solution.py:596

commit v6 on v5

--- a/solution.py
+++ b/solution.py
@@ -328,7 +328,7 @@
         inner_ref = refs[2 * count + dp_count]
         outs = refs[2 * count + dp_count + 1 : -1]
         full = refs[-1]
-        inner_grad_out, conv_grad_out, skip_out = outs[count:]
+        out, inner_grad_out, conv_grad_out, skip_out = outs
         for k in range(dp_count):
             start = pl.multiple_of((place_ref[1] ^ k) * rows, rows)
             full[pl.ds(start, rows), :] = weight[k][...]
@@ -339,7 +339,7 @@
         for r in range(count):
             here = piece(place_ref, r, local_len)
             gate = gates[r * local_len : (r + 1) * local_len]
-            outs[r][...] = (gate * inner_ref[here, :]).astype(bf16)
+            out[here, :] = (gate * inner_ref[here, :]).astype(bf16)
             inner_grad = cot[r][...].astype(f32) * gate
             inner_grad_out[here, :] = inner_grad
             conv_grad_out[here, :] = inner_grad.astype(bf16)
@@ -350,9 +350,9 @@
     return pl.pallas_call(
         body,
         in_specs=[smem()] + [pl.BlockSpec(memory_space=VMEM)] * (2 * count + dp_count + 1),
-        out_specs=[pl.BlockSpec(memory_space=VMEM)] * (count + 3),
-        out_shape=[struct((local_len, width), bf16)] * count
-        + [
+        out_specs=[pl.BlockSpec(memory_space=VMEM)] * 4,
+        out_shape=[
+            struct((length, width), bf16),
             struct((length, width), f32),
             struct((length, width), bf16),
             struct((8, width), f32),
@@ -369,11 +369,16 @@
     return order + 8 + 8 * groups, per_group
 
 
-def correlate_back(place, conv_grad, inner_grad, filt_spec, tables, rows_of, block):
+def correlate_back(
+    place, out, conv_grad, inner_grad, filt_spec, tables, rows_of, count, block
+):
     a_high, a_low, t_high = tables
     length, width = conv_grad.shape
-
-    def body(place_ref, cg, ig, fs, ah, al, th, skip_ref, direct_out, spec, back):
+    local_len = length // count
+
+    def body(place_ref, out_ref, cg, ig, fs, ah, al, th, skip_ref, *refs):
+        pieces = refs[:count]
+        spec, back = refs[count:]
         step = pl.program_id(0)
         re = to_spectrum(ah, al, 0, cg[...])
         im = to_spectrum(ah, al, 1, cg[...])
@@ -391,7 +396,11 @@
 
         @pl.when(step == pl.num_programs(0) - 1)
         def _():
-            direct_out[...] = ig[...] * skip_ref[2:3, :] + back[...].astype(bf16).astype(f32)
+            for r in range(count):
+                rows = piece(place_ref, r, local_len)
+                direct = ig[rows, :] * skip_ref[2:3, :]
+                pieces[r][0] = out_ref[rows, :]
+                pieces[r][1] = (direct + back[rows, :].astype(bf16).astype(f32)).astype(bf16)
 
     by_row, by_col = table_specs(length, block)
     spec_block = spectrum_block(width, block)
@@ -401,6 +410,7 @@
             num_scalar_prefetch=1,
             grid=(length // block,),
             in_specs=[
+                whole((length, width)),
                 whole((length, width)),
                 whole((length, width)),
                 spec_block,
@@ -409,15 +419,16 @@
                 by_col,
                 whole(rows_of.shape),
             ],
-            out_specs=[whole((length, width)), spec_block],
+            out_specs=[whole((2, local_len, width))] * count + [spec_block],
             scratch_shapes=[VMEM((length, width), f32)],
         ),
-        out_shape=[struct((length, width), f32), struct((2, length, width), f32)],
+        out_shape=[struct((2, local_len, width), bf16)] * count
+        + [struct((2, length, width), f32)],
         name="correlate_back",
         compiler_params=grant(
             [((6, block, length), 2), ((4, block, width), 4), ((3, length, width), 4)], length, width
         ),
-    )(place, conv_grad, inner_grad, filt_spec, a_high, a_low, t_high, rows_of)
+    )(place, out, conv_grad, inner_grad, filt_spec, a_high, a_low, t_high, rows_of)
 
 
 def correlate_part(
@@ -492,7 +503,7 @@
     )
 
 
-def through_gate(place, gate_grad, weight_rel, direct, count):
+def through_gate(place, gate_grad, weight_rel, count):
     dp_count = len(weight_rel)
     rows, width = weight_rel[0].shape
     length = gate_grad.shape[0]
@@ -502,31 +513,47 @@
     def body(place_ref, *refs):
         grad = refs[0]
         weight = refs[1 : 1 + dp_count]
-        direct_ref = refs[1 + dp_count]
-        outs = refs[2 + dp_count :]
+        outs = refs[1 + dp_count :]
         left = jnp.concatenate(
             [grad[piece(place_ref, r, local_len), :] for r in range(count)], axis=0
         )
         for k in range(dp_count):
             start = pl.multiple_of((place_ref[1] ^ k) * rows, rows)
-            shift = start - place_ref[0] * width
-            inside = jnp.logical_and(shift >= 0, shift < width)
-            shift = pl.multiple_of(jnp.clip(shift, 0, width - rows), rows)
-            scale = jnp.where(inside, 1.0, 0.0).astype(f32)
             terms = dot_last(left, weight[k][...])
             for r in range(count):
                 term = terms[r * local_len : (r + 1) * local_len]
-                term += scale * direct_ref[piece(place_ref, r, local_len), pl.ds(shift, rows)]
                 outs[r][:, pl.ds(start, rows)] = term.astype(bf16)
 
     return pl.pallas_call(
         body,
-        in_specs=[smem()] + [pl.BlockSpec(memory_space=VMEM)] * (dp_count + 2),
+        in_specs=[smem()] + [pl.BlockSpec(memory_space=VMEM)] * (dp_count + 1),
         out_specs=[pl.BlockSpec(memory_space=VMEM)] * count,
         out_shape=[struct((local_len, channels), bf16)] * count,
         name="through_gate",
         compiler_params=grant([((length, channels), 2), ((channels, width), 2)], length, width),
-    )(place, gate_grad, *weight_rel, direct)
+    )(place, gate_grad, *weight_rel)
+
+
+def combine(place, pieces, near_part, far_part):
+    count = len(pieces)
+    _, rows, width = pieces[0].shape
+
+    def body(place_ref, *refs):
+        near, far, out, grad = refs[count:]
+        for r in range(count):
+            cols = pl.ds(pl.multiple_of((place_ref[0] ^ r) * width, width), width)
+            out[:, cols] = refs[r][0]
+            total = near[:, cols].astype(f32) + far[:, cols].astype(f32)
+            grad[:, cols] = (total + refs[r][1].astype(f32)).astype(bf16)
+
+    return pl.pallas_call(
+        body,
+        in_specs=[smem()] + [pl.BlockSpec(memory_space=VMEM)] * (count + 2),
+        out_specs=[pl.BlockSpec(memory_space=VMEM)] * 2,
+        out_shape=[struct((rows, width * count), bf16)] * 2,
+        name="combine",
+        compiler_params=grant([((rows, 6 * width * count), 2)], rows, width),
+    )(place, *pieces, near_part, far_part)
 
 
 def assemble(place, pieces, kind):
@@ -670,28 +697,27 @@
     row_rel = gather_rel(row_sum, "seq")
     grad_gate_weight = assemble(place, row_rel, f32)
 
-    gated = gating(place, signal_rel, weight_rel, cot_rel, inner)
-    out_rel = gated[:seq_count]
-    inner_grad, conv_grad, skip_sum = gated[seq_count:]
-    out_rel = [out_rel[0]] + [swap(out_rel[r], "seq", r) for r in range(1, seq_count)]
-    output = assemble(place, out_rel, bf16)
-
-    direct, grad_spec = correlate_back(
-        place, conv_grad, inner_grad, filt_spec, tables, rows_of, block
-    )
-    packed = correlate_part(
-        place, grad_spec, skip_sum, signal_spec, tables, env, hidden, filter_weight, cos_pre,
-        table, block,
-    )
-    back_rel = through_gate(place, gate_grad, weight_rel, direct, seq_count)
-
+    back_rel = through_gate(place, gate_grad, weight_rel, seq_count)
     live = {r: back_rel[r] for r in range(seq_count)}
     bit = 1
     while bit < seq_count:
         met = {r: swap(live[r | bit], "seq", bit) for r in live if not r & bit}
-        live = {r: add_round(live[r], met[r]) for r in met}
         bit *= 2
-    grad_signal = live[0][None]
+        if bit < seq_count:
+            live = {r: add_round(live[r], met[r]) for r in met}
+
+    out, inner_grad, conv_grad, skip_sum = gating(
+        place, signal_rel, weight_rel, cot_rel, inner
+    )
+    *pieces, grad_spec = correlate_back(
+        place, out, conv_grad, inner_grad, filt_spec, tables, rows_of, seq_count, block
+    )
+    pieces = [pieces[0]] + [swap(pieces[r], "seq", r) for r in range(1, seq_count)]
+    packed = correlate_part(
+        place, grad_spec, skip_sum, signal_spec, tables, env, hidden, filter_weight, cos_pre,
+        table, block,
+    )
+    output, grad_signal = combine(place, pieces, live[0], met[0])
 
     met = swap(packed, "dp", 1)
     packed = (packed + met).astype(bf16)
@@ -706,7 +732,7 @@
     )
     return (
         output[None],
-        grad_signal,
+        grad_signal[None],
         grad_gate_weight,
         grad_pos_weight,
         grad_pos_bias[0],

time: 153 us -> 156 us (1.020)
  waiting for transfers between devices: 77 us -> 80.9 us
    ppermute x35, waiting for transfers between devices: 77 us -> 80.9 us  [swap(): return lax.ppermute(value, axis, [(i, i ^ offset) for i in range(count)])]
    pallas_call x0 -> x1, Pallas kernels: none -> 1.61 us  [combine(): pl.pallas_call(body, in_specs=[smem()] + [pl.BlockSpec(memory_space=VMEM)...]
    pallas_call x2 -> x1, Pallas kernels: 3.37 us -> 2 us  [assemble(): pl.pallas_call(body, in_specs=[smem()] + [pl.BlockSpec(memory_space=VMEM)...]
  transfers between devices with their start and end apart: 35 -> 35, of which waited for: 14 -> 13; matrix products, arithmetic and copies ran while one was open for 3% -> 3% of each run, Pallas kernels for 12% -> 12%
where the time goes in v6:
time: 156 us
  waiting for transfers between devices  80.9 us (52%)
  starting transfers between devices  35.4 us (23%)
  Pallas kernels  30.1 us (19%)
  local copies, waits for them, and re-layouts  5.85 us (4%)
  other arithmetic  2.84 us (2%)
    ppermute x35, waiting for transfers between devices, swap(): return lax.ppermute(value, axis, [(i, i ^ offset) for i in range(count)])  80.9 us
    ppermute x35, starting transfers between devices, swap(): return lax.ppermute(value, axis, [(i, i ^ offset) for i in range(count)])  35.4 us
    pallas_call x1, Pallas kernels, generate(): pl.pallas_call(body, grid_spec=pltpu.PrefetchScalarGridSpec(num_scalar_pr...  6.8 us
    unnamed x20, local copies, waits for them, and re-layouts  4.7 us
    pallas_call x1, Pallas kernels, convolve(): pl.pallas_call(body, grid_spec=pltpu.PrefetchScalarGridSpec(num_scalar_pr...  4.14 us
    pallas_call x1, Pallas kernels, correlate_back(): pl.pallas_call(body, grid_spec=pltpu.PrefetchScalarGridSpec(num_scalar_pr...  3.85 us
    pallas_call x1, Pallas kernels, correlate_part(): pl.pallas_call(body, grid_spec=pltpu.PrefetchScalarGridSpec(num_scalar_pr...  3.67 us
  transfers between devices with their start and end apart: 35, of which 13 were waited for; matrix products, arithmetic and copies ran while one was open for 3% of the time, Pallas kernels for 12%

profile of v6, /device:TPU:0, one launch (start us, length us, event | category | flops | bytes accessed | tf_op | source)
XLA Modules:
  0.0 156.0 jit_solution(9055359351357767269)
XLA Ops:
  0.7 3.0 %collective-permute-start.1 = (bf16[128,2048]{1,0:T(8,128)(2,1)}, bf16[128,2048]{1,0:T(8,128)(2,1)S(1)}, u32[]{:S(2)}, u32[]{:S(2)}) collective-permute-start(bf16[128,2048]{1,0:T(8,128)(2,1)} %bitcast.30), channel_id=1, source_target_pairs={{0,2},{1,3},{2,0},{3,1},{4,6},{5,7},{6,4},{7,5},{8,10},{9,11},{10,... | collective-permute-start | bytes 1572872 | tf_op jit(solution)/shard_map/ppermute | solution.py:623
  3.7 1.1 dynamic-slice_bitcast_fusion
  4.8 0.3 collective-permute-start.12
  5.1 0.4 collective-permute-start.10
  5.5 1.6 collective-permute-start.11
  7.1 12.0 %collective-permute-done.12.refs_7_.refs_15_ = bf16[128,512]{1,0:T(8,128)(2,1)S(1)} collective-permute-done((bf16[128,512]{1,0:T(8,128)(2,1)S(1)}, bf16[128,512]{1,0:T(8,128)(2,1)S(1)}, u32[]{:S(2)}, u32[]{:S(2)}) %collective-permute-start.12) | collective-permute-done | bytes 131104 | tf_op jit(solution)/shard_map/ppermute | solution.py:623
  19.0 0.7 copy-done.4
  19.7 3.6 %collective-permute-start.8 = (bf16[256,512]{1,0:T(8,128)(2,1)S(1)}, bf16[256,512]{1,0:T(8,128)(2,1)S(1)}, u32[]{:S(2)}, u32[]{:S(2)}) collective-permute-start(bf16[256,512]{1,0:T(8,128)(2,1)S(1)} %constant_dynamic-slice_fusion.refs_4_.refs_1_), channel_id=1, source_target_pairs={{0,24},{4,28},{8,16},{12,20},{16,8},{20,12},{24,0},{28,4},{1,25},{... | collective-permute-start | bytes 786440 | tf_op jit(solution)/shard_map/ppermute | solution.py:623
  23.3 0.7 copy-done.6
  23.9 0.7 copy-done.8
  24.6 0.8 collective-permute-start.4
  25.4 0.7 divide_sqrt_fusion
  26.1 4.7 %collective-permute-done.8.refs_10_.refs_7_ = bf16[256,512]{1,0:T(8,128)(2,1)S(1)} collective-permute-done((bf16[256,512]{1,0:T(8,128)(2,1)S(1)}, bf16[256,512]{1,0:T(8,128)(2,1)S(1)}, u32[]{:S(2)}, u32[]{:S(2)}) %collective-permute-start.8) | collective-permute-done | bytes 262176 | tf_op jit(solution)/shard_map/ppermute | solution.py:623
  30.8 1.5 collective-permute-start.3
  32.3 14.2 %collective-permute-done.6.refs_8_.refs_5_ = bf16[256,512]{1,0:T(8,128)(2,1)S(1)} collective-permute-done((bf16[256,512]{1,0:T(8,128)(2,1)S(1)}, bf16[256,512]{1,0:T(8,128)(2,1)S(1)}, u32[]{:S(2)}, u32[]{:S(2)}) %collective-permute-start.6) | collective-permute-done | bytes 262176 | tf_op jit(solution)/shard_map/ppermute | solution.py:623
  46.6 1.5 collective-permute-start.9
  48.1 0.5 collective-permute-start.7
  48.6 1.5 collective-permute-start.5
  50.1 0.1 pad_add_fusion.place_ref
  50.2 1.4 pad_maximum_fusion.refs_4_
  51.6 6.8 %generate.1 = (bf16[2,512,512]{2,1,0:T(8,128)(2,1)S(1)}, bf16[2,512,512]{2,1,0:T(8,128)(2,1)S(1)}, bf16[2,512,512]{2,1,0:T(8,128)(2,1)S(1)}, f32[2,512,512]{2,1,...) custom-call(s32[2]{0:T(128)S(1)} %pad_add_fusion.place_ref, ...), custom_call_target="tpu_custom_call" | custom-call | tf_op jit(solution)/shard_map/generate/pallas_call | solution.py:169
  58.4 0.9 copy-done.5
  59.3 0.9 copy-done.7
  60.2 0.9 copy-done.9
  61.1 4.1 %convolve.1 = (f32[2,512,512]{2,1,0:T(8,128)S(1)}, f32[512,512]{1,0:T(8,128)S(1)}, bf16[512,512]{1,0:T(8,128)(2,1)S(1)}) custom-call(s32[2]{0:T(128)S(1)} %pad_add_fusion.place_ref, bf16[128,2048]{1,0:T(8,128)(2,1)S(1)} %bitcast.32, bf16[128,2048]{1,0:T(8,128)(2,1)S(1)} %collective-permute-done.refs_1_, ...), custom_call_target="tpu_custom_call" | custom-call | tf_op jit(solution)/shard_map/convolve/pallas_call | solution.py:247
  65.3 0.7 collective-permute-done.5.refs_7_.refs_4_
  66.0 2.5 %gating.1 = (bf16[512,512]{1,0:T(8,128)(2,1)S(1)}, f32[512,512]{1,0:T(8,128)S(1)}, bf16[512,512]{1,0:T(8,128)(2,1)S(1)}, f32[8,512]{1,0:T(8,128)S(1)}) custom-call(s32[2]{0:T(128)S(1)} %pad_add_fusion.place_ref, bf16[128,2048]{1,0:T(8,128)(2,1)S(1)} %bitcast.33, bf16[128,2048]{1,0:T(8,128)(2,1)S(1)} %collective-permute-done.refs_1_, ...), custom_call_target="tpu_custom_call" | custom-call | tf_op jit(solution)/shard_map/gating/pallas_call | solution.py:350
  68.5 3.9 %correlate_back.1 = (bf16[2,128,512]{2,1,0:T(8,128)(2,1)S(1)}, bf16[2,128,512]{2,1,0:T(8,128)(2,1)S(1)}, bf16[2,128,512]{2,1,0:T(8,128)(2,1)S(1)}, bf16[2,128,512]{2,1,0:T(8,128)(2,1)S(1)}, f32[2,512,512]{2,1,0:T(8,128)S(1)}) custom-call(s32[2]{0:T(128)S(1)} %pad_add_fusion.place_ref, bf16[512,512]{1,0:T(8,128)(2,1)S(1)} %get-tuple-element.49.out_ref, ...), custom_call_target="tpu_custom_call" | custom-call | tf_op jit(solution)/shard_map/correlate_back/pallas_call | solution.py:407
  72.4 3.7 %correlate_part.1 = f32[80,512]{1,0:T(8,128)S(1)} custom-call(s32[2]{0:T(128)S(1)} %pad_add_fusion.place_ref, f32[2,512,512]{2,1,0:T(8,128)S(1)} %get-tuple-element.69.gs, f32[8,512]{1,0:T(8,128)S(1)} %get-tuple-element.70.skip_sum_ref, f32[2,512,512]{2,1,0:T(8,128)S(1)} %get-tuple-element.71.ss, bf16[2,512,512]{2,1,0:T(8,128)(2,1)S(1)} %get-tuple-element.46.refs_11_.th, ...), custom_call_target="tpu_custom_call" | custom-call | tf_op jit(solution)/shard_map/correlate_part/pallas_call | solution.py:476
  76.0 1.6 %collective-permute-start.28 = (f32[80,512]{1,0:T(8,128)S(1)}, f32[80,512]{1,0:T(8,128)S(1)}, u32[]{:S(2)}, u32[]{:S(2)}) collective-permute-start(f32[80,512]{1,0:T(8,128)S(1)} %correlate_part.1), channel_id=1, source_target_pairs={{0,4},{4,0},{8,12},{12,8},{16,20},{20,16},{24,28},{28,24},{1,5},{5... | collective-permute-start | bytes 491528 | tf_op jit(solution)/shard_map/ppermute | solution.py:623
  77.6 1.8 %weight_grads.1 = (bf16[1,256,512]{2,1,0:T(8,128)(2,1)S(1)}, bf16[1,256,512]{2,1,0:T(8,128)(2,1)S(1)}, bf16[2,256,512]{2,1,0:T(8,128)(2,1)S(1)}, bf16[1,256,512]...) custom-call(s32[2]{0:T(128)S(1)} %pad_add_fusion.place_ref, ...), custom_call_target="tpu_custom_call" | custom-call | tf_op jit(solution)/shard_map/weight_grads/pallas_call | solution.py:307
  79.5 0.6 collective-permute-start.20
  80.1 1.5 collective-permute-start.22
  81.6 0.5 collective-permute-start.19
  82.1 2.5 %collective-permute-start.31 = (bf16[80,512]{1,0:T(8,128)(2,1)S(1)}, bf16[80,512]{1,0:T(8,128)(2,1)S(1)}, u32[]{:S(2)}, u32[]{:S(2)}) collective-permute-start(bf16[80,512]{1,0:T(8,128)(2,1)S(1)} %add_convert_fusion.7), channel_id=1, source_target_pairs={{0,24},{4,28},{8,16},{12,20},{16,8},{20,12},{24,0},{28,4},{1,25},{... | collective-permute-start | bytes 245768 | tf_op jit(solution)/shard_map/ppermute | solution.py:623
  84.7 4.0 %collective-permute-done.20 = bf16[1,256,512]{2,1,0:T(8,128)(2,1)S(1)} collective-permute-done((bf16[1,256,512]{2,1,0:T(8,128)(2,1)S(1)}, bf16[1,256,512]{2,1,0:T(8,128)(2,1)S(1)}, u32[]{:S(2)}, u32[]{:S(2)}) %collective-permute-start.20) | collective-permute-done | bytes 262176 | tf_op jit(solution)/shard_map/ppermute | solution.py:623
  88.7 0.7 collective-permute-start.29
  89.5 4.9 %collective-permute-done.22 = bf16[1,256,512]{2,1,0:T(8,128)(2,1)S(1)} collective-permute-done((bf16[1,256,512]{2,1,0:T(8,128)(2,1)S(1)}, bf16[1,256,512]{2,1,0:T(8,128)(2,1)S(1)}, u32[]{:S(2)}, u32[]{:S(2)}) %collective-permute-start.22) | collective-permute-done | bytes 262176 | tf_op jit(solution)/shard_map/ppermute | solution.py:623
  94.3 2.5 %collective-permute-start.21 = (bf16[256,512]{1,0:T(8,128)(2,1)S(1)}, bf16[256,512]{1,0:T(8,128)(2,1)S(1)}, u32[]{:S(2)}, u32[]{:S(2)}) collective-permute-start(bf16[256,512]{1,0:T(8,128)(2,1)S(1)} %fusion.4), channel_id=1, source_target_pairs={{0,24},{4,28},{8,16},{12,20},{16,8},{20,12},{24,0},{28,4},{1,25},{... | collective-permute-start | bytes 786440 | tf_op jit(solution)/shard_map/ppermute | solution.py:623
  96.9 7.0 %collective-permute-done.19 = bf16[2,256,512]{2,1,0:T(8,128)(2,1)S(1)} collective-permute-done((bf16[2,256,512]{2,1,0:T(8,128)(2,1)S(1)}, bf16[2,256,512]{2,1,0:T(8,128)(2,1)S(1)}, u32[]{:S(2)}, u32[]{:S(2)}) %collective-permute-start.19) | collective-permute-done | bytes 524320 | tf_op jit(solution)/shard_map/ppermute | solution.py:623
  103.9 1.7 %collective-permute-start.23 = (bf16[256,512]{1,0:T(8,128)(2,1)S(1)}, bf16[256,512]{1,0:T(8,128)(2,1)S(1)}, u32[]{:S(2)}, u32[]{:S(2)}) collective-permute-start(bf16[256,512]{1,0:T(8,128)(2,1)S(1)} %fusion.5), channel_id=1, source_target_pairs={{0,16},{4,20},{8,24},{12,28},{16,0},{20,4},{24,8},{28,12},{1,17},{... | collective-permute-start | bytes 786440 | tf_op jit(solution)/shard_map/ppermute | solution.py:623
  105.7 1.4 collective-permute-start.24
  107.1 2.3 %through_gate.1 = (bf16[128,2048]{1,0:T(8,128)(2,1)S(1)}, bf16[128,2048]{1,0:T(8,128)(2,1)S(1)}, bf16[128,2048]{1,0:T(8,128)(2,1)S(1)}, bf16[128,2048]{1,0:T(8,128)(2,1)S(1)}) custom-call(s32[2]{0:T(128)S(1)} %pad_add_fusion.place_ref, bf16[512,512]{1,0:T(8,128)(2,1)S(1)} %get-tuple-element.56.refs_0_.refs_4_, ...), custom_call_target="tpu_custom_call" | custom-call | tf_op jit(solution)/shard_map/through_gate/pallas_call | solution.py:527
  109.4 0.1 collective-permute-start.17
  109.5 0.5 collective-permute-start.13
  110.0 0.2 collective-permute-start.16
  110.2 7.0 %collective-permute-done.23 = bf16[256,512]{1,0:T(8,128)(2,1)S(1)} collective-permute-done((bf16[256,512]{1,0:T(8,128)(2,1)S(1)}, bf16[256,512]{1,0:T(8,128)(2,1)S(1)}, u32[]{:S(2)}, u32[]{:S(2)}) %collective-permute-start.23) | collective-permute-done | bytes 262176 | tf_op jit(solution)/shard_map/ppermute | solution.py:623
  117.2 0.6 collective-permute-start.34
  117.8 1.4 collective-permute-start.33
  119.2 0.2 fusion.2.refs_0_
  119.3 2.1 %collective-permute-done.34.refs_3_ = bf16[80,512]{1,0:T(8,128)(2,1)S(1)} collective-permute-done((bf16[80,512]{1,0:T(8,128)(2,1)S(1)}, bf16[80,512]{1,0:T(8,128)(2,1)S(1)}, u32[]{:S(2)}, u32[]{:S(2)}) %collective-permute-start.34) | collective-permute-done | bytes 81952 | tf_op jit(solution)/shard_map/ppermute | solution.py:623
  121.4 0.4 collective-permute-start.32
  121.8 1.6 %collective-permute-start.26 = (bf16[256,512]{1,0:T(8,128)(2,1)S(1)}, bf16[256,512]{1,0:T(8,128)(2,1)S(1)}, u32[]{:S(2)}, u32[]{:S(2)}) collective-permute-start(bf16[256,512]{1,0:T(8,128)(2,1)S(1)} %fusion.2.refs_0_), channel_id=1, source_target_pairs={{0,2},{1,3},{2,0},{3,1},{4,6},{5,7},{6,4},{7,5},{8,10},{9,11},{10,... | collective-permute-start | bytes 786440 | tf_op jit(solution)/shard_map/ppermute | solution.py:623
  123.5 0.1 add_convert_fusion
  123.7 0.8 collective-permute-start.18
  124.5 1.2 collective-permute-start.14
  125.7 1.4 finish.1
  127.1 0.9 collective-permute-start.25
  128.0 3.0 %collective-permute-done.26.refs_2_ = bf16[256,512]{1,0:T(8,128)(2,1)S(1)} collective-permute-done((bf16[256,512]{1,0:T(8,128)(2,1)S(1)}, bf16[256,512]{1,0:T(8,128)(2,1)S(1)}, u32[]{:S(2)}, u32[]{:S(2)}) %collective-permute-start.26) | collective-permute-done | bytes 262176 | tf_op jit(solution)/shard_map/ppermute | solution.py:623
  131.0 0.1 add_convert_fusion.1.refs_4_
  131.1 16.7 %collective-permute-done.14.refs_2_ = bf16[2,128,512]{2,1,0:T(8,128)(2,1)S(1)} collective-permute-done((bf16[2,128,512]{2,1,0:T(8,128)(2,1)S(1)}, bf16[2,128,512]{2,1,0:T(8,128)(2,1)S(1)}, u32[]{:S(2)}, u32[]{:S(2)}) %collective-permute-start.14) | collective-permute-done | bytes 262176 | tf_op jit(solution)/shard_map/ppermute | solution.py:623
  147.9 4.5 %collective-permute-done.15.refs_3_ = bf16[2,128,512]{2,1,0:T(8,128)(2,1)S(1)} collective-permute-done((bf16[2,128,512]{2,1,0:T(8,128)(2,1)S(1)}, bf16[2,128,512]{2,1,0:T(8,128)(2,1)S(1)}, u32[]{:S(2)}, u32[]{:S(2)}) %collective-permute-start.15) | collective-permute-done | bytes 262176 | tf_op jit(solution)/shard_map/ppermute | solution.py:623
  152.3 1.6 %combine.1 = (bf16[128,2048]{1,0:T(8,128)(2,1)}, bf16[128,2048]{1,0:T(8,128)(2,1)}) custom-call(s32[2]{0:T(128)S(1)} %pad_add_fusion.place_ref, bf16[2,128,512]{2,1,0:T(8,128)(2,1)S(1)} %get-tuple-element.52.refs_0_, bf16[2,128,512]{2,1,0:T(8,128)(2,1)S(1)} %collective-permute-done.13.refs_1_, bf16[2,128,512]{2,1,0:T(8,128)(2,1)S(1)} %collective-permute-done.14.refs_2_, ...), custom_call_target="tpu_custom_call" | custom-call | tf_op jit(solution)/shard_map/combine/pallas_call | solution.py:549
  154.0 2.0 %assemble.1 = f32[256,2048]{1,0:T(8,128)} custom-call(s32[2]{0:T(128)S(1)} %pad_add_fusion.place_ref, bf16[256,512]{1,0:T(8,128)(2,1)S(1)} %fusion.2.refs_0_, bf16[256,512]{1,0:T(8,128)(2,1)S(1)} %collective-permute-done.25.refs_1_, bf16[256,512]{1,0:T(8,128)(2,1)S(1)} %collective-permute-done.26.refs_2_, bf16[256,512]{1,0:T(8,128)(2,1)S(1)} %collective-permute-done.27.refs_3_), custom_call_target="tpu_custom_call" | custom-call | tf_op jit(solution)/shard_map/assemble/pallas_call | solution.py:569
  (49 shorter events, 0.5 us)
Async XLA Ops:
  0.6 6.4 %copy-start = (bf16[256,2048]{1,0:T(8,128)(2,1)S(1)}, bf16[256,2048]{1,0:T(8,128)(2,1)}, u32[]{:S(2)}) copy-start(bf16[256,2048]{1,0:T(8,128)(2,1)} %param.10) | copy-start | bytes 3145732
  0.6 57.7 %copy-start.1 = (bf16[1,128,2048]{2,1,0:T(8,128)(2,1)S(1)}, bf16[1,128,2048]{2,1,0:T(8,128)(2,1)}, u32[]{:S(2)}) copy-start(bf16[1,128,2048]{2,1,0:T(8,128)(2,1)} %param.9) | copy-start | bytes 1572868
  0.7 24.7 %collective-permute-start.1 = (bf16[128,2048]{1,0:T(8,128)(2,1)}, bf16[128,2048]{1,0:T(8,128)(2,1)S(1)}, u32[]{:S(2)}, u32[]{:S(2)}) collective-permute-start(bf16[128,2048]{1,0:T(8,128)(2,1)} %bitcast.30), channel_id=1, source_target_pairs={{0,2},{1,3},{2,0},{3,1},{4,6},{5,7},{6,4},{7,5},{8,10},{9,11},{10,... | collective-permute-start | bytes 1572872 | tf_op jit(solution)/shard_map/ppermute | solution.py:623
  3.7 44.9 %collective-permute-start = (bf16[128,2048]{1,0:T(8,128)(2,1)}, bf16[128,2048]{1,0:T(8,128)(2,1)S(1)}, u32[]{:S(2)}, u32[]{:S(2)}) collective-permute-start(bf16[128,2048]{1,0:T(8,128)(2,1)} %bitcast.31), channel_id=1, source_target_pairs={{0,1},{1,0},{2,3},{3,2},{4,5},{5,4},{6,7},{7,6},{8,9},{9,8},{10,11... | collective-permute-start | bytes 1572872 | tf_op jit(solution)/shard_map/ppermute | solution.py:623
  4.8 14.2 %collective-permute-start.12 = (bf16[128,512]{1,0:T(8,128)(2,1)S(1)}, bf16[128,512]{1,0:T(8,128)(2,1)S(1)}, u32[]{:S(2)}, u32[]{:S(2)}) collective-permute-start(bf16[128,512]{1,0:T(8,128)(2,1)S(1)} %get-tuple-element.79), channel_id=1, source_target_pairs={{0,3},{1,2},{2,1},{3,0},{4,7},{5,6},{6,5},{7,4},{8,11},{9,10},{10,... | collective-permute-start | bytes 393224 | tf_op jit(solution)/shard_map/ppermute | solution.py:623
  5.1 18.2 %collective-permute-start.10 = (bf16[128,512]{1,0:T(8,128)(2,1)S(1)}, bf16[128,512]{1,0:T(8,128)(2,1)S(1)}, u32[]{:S(2)}, u32[]{:S(2)}) collective-permute-start(bf16[128,512]{1,0:T(8,128)(2,1)S(1)} %get-tuple-element.80), channel_id=1, source_target_pairs={{0,1},{1,0},{2,3},{3,2},{4,5},{5,4},{6,7},{7,6},{8,9},{9,8},{10,11... | collective-permute-start | bytes 393224 | tf_op jit(solution)/shard_map/ppermute | solution.py:623
  5.5 18.5 %collective-permute-start.11 = (bf16[128,512]{1,0:T(8,128)(2,1)S(1)}, bf16[128,512]{1,0:T(8,128)(2,1)S(1)}, u32[]{:S(2)}, u32[]{:S(2)}) collective-permute-start(bf16[128,512]{1,0:T(8,128)(2,1)S(1)} %get-tuple-element.82), channel_id=1, source_target_pairs={{0,2},{1,3},{2,0},{3,1},{4,6},{5,7},{6,4},{7,5},{8,10},{9,11},{10,... | collective-permute-start | bytes 393224 | tf_op jit(solution)/shard_map/ppermute | solution.py:623
  19.0 0.7 copy-start.4
  19.7 11.1 %collective-permute-start.8 = (bf16[256,512]{1,0:T(8,128)(2,1)S(1)}, bf16[256,512]{1,0:T(8,128)(2,1)S(1)}, u32[]{:S(2)}, u32[]{:S(2)}) collective-permute-start(bf16[256,512]{1,0:T(8,128)(2,1)S(1)} %constant_dynamic-slice_fusion.refs_4_.refs_1_), channel_id=1, source_target_pairs={{0,24},{4,28},{8,16},{12,20},{16,8},{20,12},{24,0},{28,4},{1,25},{... | collective-permute-start | bytes 786440 | tf_op jit(solution)/shard_map/ppermute | solution.py:623
  23.3 0.7 copy-start.6
  23.9 22.6 %collective-permute-start.6 = (bf16[256,512]{1,0:T(8,128)(2,1)S(1)}, bf16[256,512]{1,0:T(8,128)(2,1)S(1)}, u32[]{:S(2)}, u32[]{:S(2)}) collective-permute-start(bf16[256,512]{1,0:T(8,128)(2,1)S(1)} %constant_dynamic-slice_fusion.refs_4_.refs_1_), channel_id=1, source_target_pairs={{0,16},{4,20},{8,24},{12,28},{16,0},{20,4},{24,8},{28,12},{1,17},{... | collective-permute-start | bytes 786440 | tf_op jit(solution)/shard_map/ppermute | solution.py:623
  23.9 0.7 copy-start.8
  24.6 23.5 %collective-permute-start.4 = (bf16[256,512]{1,0:T(8,128)(2,1)S(1)}, bf16[256,512]{1,0:T(8,128)(2,1)}, u32[]{:S(2)}, u32[]{:S(2)}) collective-permute-start(bf16[256,512]{1,0:T(8,128)(2,1)S(1)} %constant_dynamic-slice_fusion.refs_4_.refs_1_), channel_id=1, source_target_pairs={{0,8},{4,12},{8,0},{12,4},{16,24},{20,28},{24,16},{28,20},{1,9},{5... | collective-permute-start | bytes 786440 | tf_op jit(solution)/shard_map/ppermute | solution.py:623
  25.4 33.0 %collective-permute-start.2 = (bf16[128,2048]{1,0:T(8,128)(2,1)S(1)}, bf16[128,2048]{1,0:T(8,128)(2,1)S(1)}, u32[]{:S(2)}, u32[]{:S(2)}) collective-permute-start(bf16[128,2048]{1,0:T(8,128)(2,1)S(1)} %collective-permute-done.1.refs_2_), channel_id=1, source_target_pairs={{0,1},{1,0},{2,3},{3,2},{4,5},{5,4},{6,7},{7,6},{8,9},{9,8},{10,11... | collective-permute-start | bytes 1572872 | tf_op jit(solution)/shard_map/ppermute | solution.py:623
  30.8 34.5 %collective-permute-start.3 = (bf16[256,512]{1,0:T(8,128)(2,1)S(1)}, bf16[256,512]{1,0:T(8,128)(2,1)S(1)}, u32[]{:S(2)}, u32[]{:S(2)}) collective-permute-start(bf16[256,512]{1,0:T(8,128)(2,1)S(1)} %constant_dynamic-slice_fusion.refs_4_.refs_1_), channel_id=1, source_target_pairs={{0,4},{4,0},{8,12},{12,8},{16,20},{20,16},{24,28},{28,24},{1,5},{5... | collective-permute-start | bytes 786440 | tf_op jit(solution)/shard_map/ppermute | solution.py:623
  46.6 18.7 %collective-permute-start.9 = (bf16[256,512]{1,0:T(8,128)(2,1)S(1)}, bf16[256,512]{1,0:T(8,128)(2,1)S(1)}, u32[]{:S(2)}, u32[]{:S(2)}) collective-permute-start(bf16[256,512]{1,0:T(8,128)(2,1)S(1)} %collective-permute-done.8.refs_10_.refs_7_), channel_id=1, source_target_pairs={{0,4},{4,0},{8,12},{12,8},{16,20},{20,16},{24,28},{28,24},{1,5},{5... | collective-permute-start | bytes 786440 | tf_op jit(solution)/shard_map/ppermute | solution.py:623
  48.1 17.2 %collective-permute-start.7 = (bf16[256,512]{1,0:T(8,128)(2,1)S(1)}, bf16[256,512]{1,0:T(8,128)(2,1)S(1)}, u32[]{:S(2)}, u32[]{:S(2)}) collective-permute-start(bf16[256,512]{1,0:T(8,128)(2,1)S(1)} %collective-permute-done.6.refs_8_.refs_5_), channel_id=1, source_target_pairs={{0,4},{4,0},{8,12},{12,8},{16,20},{20,16},{24,28},{28,24},{1,5},{5... | collective-permute-start | bytes 786440 | tf_op jit(solution)/shard_map/ppermute | solution.py:623
  48.6 17.4 %collective-permute-start.5 = (bf16[256,512]{1,0:T(8,128)(2,1)}, bf16[256,512]{1,0:T(8,128)(2,1)S(1)}, u32[]{:S(2)}, u32[]{:S(2)}) collective-permute-start(bf16[256,512]{1,0:T(8,128)(2,1)} %collective-permute-done.4.refs_6_.refs_3_), channel_id=1, source_target_pairs={{0,4},{4,0},{8,12},{12,8},{16,20},{20,16},{24,28},{28,24},{1,5},{5... | collective-permute-start | bytes 786440 | tf_op jit(solution)/shard_map/ppermute | solution.py:623
  58.4 0.9 copy-start.5
  59.3 0.9 copy-start.7
  60.2 0.9 copy-start.9
  68.5 3.9 %copy-start.2 = (f32[64,2048]{1,0:T(8,128)S(1)}, f32[64,2048]{1,0:T(8,128)}, u32[]{:S(2)}) copy-start(f32[64,2048]{1,0:T(8,128)} %fw.1) | copy-start | bytes 1572868
  68.5 3.9 %copy-start.3 = (f32[232,512]{1,0:T(8,128)S(1)}, f32[232,512]{1,0:T(8,128)}, u32[]{:S(2)}) copy-start(f32[232,512]{1,0:T(8,128)} %constant.32.clone.refs_0_.tab) | copy-start | bytes 1425412
  76.0 6.1 %collective-permute-start.28 = (f32[80,512]{1,0:T(8,128)S(1)}, f32[80,512]{1,0:T(8,128)S(1)}, u32[]{:S(2)}, u32[]{:S(2)}) collective-permute-start(f32[80,512]{1,0:T(8,128)S(1)} %correlate_part.1), channel_id=1, source_target_pairs={{0,4},{4,0},{8,12},{12,8},{16,20},{20,16},{24,28},{28,24},{1,5},{5... | collective-permute-start | bytes 491528 | tf_op jit(solution)/shard_map/ppermute | solution.py:623
  79.5 9.2 %collective-permute-start.20 = (bf16[1,256,512]{2,1,0:T(8,128)(2,1)S(1)}, bf16[1,256,512]{2,1,0:T(8,128)(2,1)S(1)}, u32[]{:S(2)}, u32[]{:S(2)}) collective-permute-start(bf16[1,256,512]{2,1,0:T(8,128)(2,1)S(1)} %get-tuple-element.66), channel_id=1, source_target_pairs={{0,4},{4,0},{8,12},{12,8},{16,20},{20,16},{24,28},{28,24},{1,5},{5... | collective-permute-start | bytes 786440 | tf_op jit(solution)/shard_map/ppermute | solution.py:623
  80.1 14.3 %collective-permute-start.22 = (bf16[1,256,512]{2,1,0:T(8,128)(2,1)S(1)}, bf16[1,256,512]{2,1,0:T(8,128)(2,1)S(1)}, u32[]{:S(2)}, u32[]{:S(2)}) collective-permute-start(bf16[1,256,512]{2,1,0:T(8,128)(2,1)S(1)} %get-tuple-element.68), channel_id=1, source_target_pairs={{0,4},{4,0},{8,12},{12,8},{16,20},{20,16},{24,28},{28,24},{1,5},{5... | collective-permute-start | bytes 786440 | tf_op jit(solution)/shard_map/ppermute | solution.py:623
  81.6 22.3 %collective-permute-start.19 = (bf16[2,256,512]{2,1,0:T(8,128)(2,1)S(1)}, bf16[2,256,512]{2,1,0:T(8,128)(2,1)S(1)}, u32[]{:S(2)}, u32[]{:S(2)}) collective-permute-start(bf16[2,256,512]{2,1,0:T(8,128)(2,1)S(1)} %get-tuple-element.64), channel_id=1, source_target_pairs={{0,4},{4,0},{8,12},{12,8},{16,20},{20,16},{24,28},{28,24},{1,5},{5... | collective-permute-start | bytes 1572872 | tf_op jit(solution)/shard_map/ppermute | solution.py:623
  82.1 23.5 %collective-permute-start.31 = (bf16[80,512]{1,0:T(8,128)(2,1)S(1)}, bf16[80,512]{1,0:T(8,128)(2,1)S(1)}, u32[]{:S(2)}, u32[]{:S(2)}) collective-permute-start(bf16[80,512]{1,0:T(8,128)(2,1)S(1)} %add_convert_fusion.7), channel_id=1, source_target_pairs={{0,24},{4,28},{8,16},{12,20},{16,8},{20,12},{24,0},{28,4},{1,25},{... | collective-permute-start | bytes 245768 | tf_op jit(solution)/shard_map/ppermute | solution.py:623
  84.7 24.7 %collective-permute-start.30 = (bf16[80,512]{1,0:T(8,128)(2,1)S(1)}, bf16[80,512]{1,0:T(8,128)(2,1)S(1)}, u32[]{:S(2)}, u32[]{:S(2)}) collective-permute-start(bf16[80,512]{1,0:T(8,128)(2,1)S(1)} %add_convert_fusion.7), channel_id=1, source_target_pairs={{0,16},{4,20},{8,24},{12,28},{16,0},{20,4},{24,8},{28,12},{1,17},{... | collective-permute-start | bytes 245768 | tf_op jit(solution)/shard_map/ppermute | solution.py:623
  88.7 20.7 %collective-permute-start.29 = (bf16[80,512]{1,0:T(8,128)(2,1)S(1)}, bf16[80,512]{1,0:T(8,128)(2,1)S(1)}, u32[]{:S(2)}, u32[]{:S(2)}) collective-permute-start(bf16[80,512]{1,0:T(8,128)(2,1)S(1)} %add_convert_fusion.7), channel_id=1, source_target_pairs={{0,8},{4,12},{8,0},{12,4},{16,24},{20,28},{24,16},{28,20},{1,9},{5... | collective-permute-start | bytes 245768 | tf_op jit(solution)/shard_map/ppermute | solution.py:623
  94.3 15.7 %collective-permute-start.21 = (bf16[256,512]{1,0:T(8,128)(2,1)S(1)}, bf16[256,512]{1,0:T(8,128)(2,1)S(1)}, u32[]{:S(2)}, u32[]{:S(2)}) collective-permute-start(bf16[256,512]{1,0:T(8,128)(2,1)S(1)} %fusion.4), channel_id=1, source_target_pairs={{0,24},{4,28},{8,16},{12,20},{16,8},{20,12},{24,0},{28,4},{1,25},{... | collective-permute-start | bytes 786440 | tf_op jit(solution)/shard_map/ppermute | solution.py:623
  103.9 13.3 %collective-permute-start.23 = (bf16[256,512]{1,0:T(8,128)(2,1)S(1)}, bf16[256,512]{1,0:T(8,128)(2,1)S(1)}, u32[]{:S(2)}, u32[]{:S(2)}) collective-permute-start(bf16[256,512]{1,0:T(8,128)(2,1)S(1)} %fusion.5), channel_id=1, source_target_pairs={{0,16},{4,20},{8,24},{12,28},{16,0},{20,4},{24,8},{28,12},{1,17},{... | collective-permute-start | bytes 786440 | tf_op jit(solution)/shard_map/ppermute | solution.py:623
  105.7 12.1 %collective-permute-start.24 = (bf16[256,512]{1,0:T(8,128)(2,1)S(1)}, bf16[256,512]{1,0:T(8,128)(2,1)S(1)}, u32[]{:S(2)}, u32[]{:S(2)}) collective-permute-start(bf16[256,512]{1,0:T(8,128)(2,1)S(1)} %fusion.6), channel_id=1, source_target_pairs={{0,8},{4,12},{8,0},{12,4},{16,24},{20,28},{24,16},{28,20},{1,9},{5... | collective-permute-start | bytes 786440 | tf_op jit(solution)/shard_map/ppermute | solution.py:623
  109.4 12.5 %collective-permute-start.17 = (bf16[128,2048]{1,0:T(8,128)(2,1)S(1)}, bf16[128,2048]{1,0:T(8,128)(2,1)S(1)}, u32[]{:S(2)}, u32[]{:S(2)}) collective-permute-start(bf16[128,2048]{1,0:T(8,128)(2,1)S(1)} %get-tuple-element.60), channel_id=1, source_target_pairs={{0,1},{1,0},{2,3},{3,2},{4,5},{5,4},{6,7},{7,6},{8,9},{9,8},{10,11... | collective-permute-start | bytes 1572872 | tf_op jit(solution)/shard_map/ppermute | solution.py:623
  109.5 17.6 %collective-permute-start.13 = (bf16[2,128,512]{2,1,0:T(8,128)(2,1)S(1)}, bf16[2,128,512]{2,1,0:T(8,128)(2,1)S(1)}, u32[]{:S(2)}, u32[]{:S(2)}) collective-permute-start(bf16[2,128,512]{2,1,0:T(8,128)(2,1)S(1)} %get-tuple-element.53), channel_id=1, source_target_pairs={{0,1},{1,0},{2,3},{3,2},{4,5},{5,4},{6,7},{7,6},{8,9},{9,8},{10,11... | collective-permute-start | bytes 786440 | tf_op jit(solution)/shard_map/ppermute | solution.py:623
  110.0 17.1 %collective-permute-start.16 = (bf16[128,2048]{1,0:T(8,128)(2,1)S(1)}, bf16[128,2048]{1,0:T(8,128)(2,1)S(1)}, u32[]{:S(2)}, u32[]{:S(2)}) collective-permute-start(bf16[128,2048]{1,0:T(8,128)(2,1)S(1)} %get-tuple-element.58), channel_id=1, source_target_pairs={{0,1},{1,0},{2,3},{3,2},{4,5},{5,4},{6,7},{7,6},{8,9},{9,8},{10,11... | collective-permute-start | bytes 1572872 | tf_op jit(solution)/shard_map/ppermute | solution.py:623
  117.2 4.2 %collective-permute-start.34 = (bf16[80,512]{1,0:T(8,128)(2,1)S(1)}, bf16[80,512]{1,0:T(8,128)(2,1)S(1)}, u32[]{:S(2)}, u32[]{:S(2)}) collective-permute-start(bf16[80,512]{1,0:T(8,128)(2,1)S(1)} %add_convert_fusion.6.refs_0_), channel_id=1, source_target_pairs={{0,3},{1,2},{2,1},{3,0},{4,7},{5,6},{6,5},{7,4},{8,11},{9,10},{10,... | collective-permute-start | bytes 245768 | tf_op jit(solution)/shard_map/ppermute | solution.py:623
  117.8 5.9 %collective-permute-start.33 = (bf16[80,512]{1,0:T(8,128)(2,1)S(1)}, bf16[80,512]{1,0:T(8,128)(2,1)S(1)}, u32[]{:S(2)}, u32[]{:S(2)}) collective-permute-start(bf16[80,512]{1,0:T(8,128)(2,1)S(1)} %add_convert_fusion.6.refs_0_), channel_id=1, source_target_pairs={{0,2},{1,3},{2,0},{3,1},{4,6},{5,7},{6,4},{7,5},{8,10},{9,11},{10,... | collective-permute-start | bytes 245768 | tf_op jit(solution)/shard_map/ppermute | solution.py:623
  121.4 3.1 %collective-permute-start.32 = (bf16[80,512]{1,0:T(8,128)(2,1)S(1)}, bf16[80,512]{1,0:T(8,128)(2,1)S(1)}, u32[]{:S(2)}, u32[]{:S(2)}) collective-permute-start(bf16[80,512]{1,0:T(8,128)(2,1)S(1)} %add_convert_fusion.6.refs_0_), channel_id=1, source_target_pairs={{0,1},{1,0},{2,3},{3,2},{4,5},{5,4},{6,7},{7,6},{8,9},{9,8},{10,11... | collective-permute-start | bytes 245768 | tf_op jit(solution)/shard_map/ppermute | solution.py:623
  121.8 9.2 %collective-permute-start.26 = (bf16[256,512]{1,0:T(8,128)(2,1)S(1)}, bf16[256,512]{1,0:T(8,128)(2,1)S(1)}, u32[]{:S(2)}, u32[]{:S(2)}) collective-permute-start(bf16[256,512]{1,0:T(8,128)(2,1)S(1)} %fusion.2.refs_0_), channel_id=1, source_target_pairs={{0,2},{1,3},{2,0},{3,1},{4,6},{5,7},{6,4},{7,5},{8,10},{9,11},{10,... | collective-permute-start | bytes 786440 | tf_op jit(solution)/shard_map/ppermute | solution.py:623
  123.7 28.7 %collective-permute-start.18 = (bf16[128,2048]{1,0:T(8,128)(2,1)S(1)}, bf16[128,2048]{1,0:T(8,128)(2,1)S(1)}, u32[]{:S(2)}, u32[]{:S(2)}) collective-permute-start(bf16[128,2048]{1,0:T(8,128)(2,1)S(1)} %add_convert_fusion), channel_id=1, source_target_pairs={{0,2},{1,3},{2,0},{3,1},{4,6},{5,7},{6,4},{7,5},{8,10},{9,11},{10,... | collective-permute-start | bytes 1572872 | tf_op jit(solution)/shard_map/ppermute | solution.py:623
  124.5 23.4 %collective-permute-start.14 = (bf16[2,128,512]{2,1,0:T(8,128)(2,1)S(1)}, bf16[2,128,512]{2,1,0:T(8,128)(2,1)S(1)}, u32[]{:S(2)}, u32[]{:S(2)}) collective-permute-start(bf16[2,128,512]{2,1,0:T(8,128)(2,1)S(1)} %get-tuple-element.54), channel_id=1, source_target_pairs={{0,2},{1,3},{2,0},{3,1},{4,6},{5,7},{6,4},{7,5},{8,10},{9,11},{10,... | collective-permute-start | bytes 786440 | tf_op jit(solution)/shard_map/ppermute | solution.py:623
  127.1 25.3 %collective-permute-start.15 = (bf16[2,128,512]{2,1,0:T(8,128)(2,1)S(1)}, bf16[2,128,512]{2,1,0:T(8,128)(2,1)S(1)}, u32[]{:S(2)}, u32[]{:S(2)}) collective-permute-start(bf16[2,128,512]{2,1,0:T(8,128)(2,1)S(1)} %get-tuple-element.55), channel_id=1, source_target_pairs={{0,3},{1,2},{2,1},{3,0},{4,7},{5,6},{6,5},{7,4},{8,11},{9,10},{10,... | collective-permute-start | bytes 786440 | tf_op jit(solution)/shard_map/ppermute | solution.py:623
  127.1 26.8 %collective-permute-start.25 = (bf16[256,512]{1,0:T(8,128)(2,1)S(1)}, bf16[256,512]{1,0:T(8,128)(2,1)S(1)}, u32[]{:S(2)}, u32[]{:S(2)}) collective-permute-start(bf16[256,512]{1,0:T(8,128)(2,1)S(1)} %fusion.2.refs_0_), channel_id=1, source_target_pairs={{0,1},{1,0},{2,3},{3,2},{4,5},{5,4},{6,7},{7,6},{8,9},{9,8},{10,11... | collective-permute-start | bytes 786440 | tf_op jit(solution)/shard_map/ppermute | solution.py:623
  131.0 23.0 %collective-permute-start.27 = (bf16[256,512]{1,0:T(8,128)(2,1)S(1)}, bf16[256,512]{1,0:T(8,128)(2,1)S(1)}, u32[]{:S(2)}, u32[]{:S(2)}) collective-permute-start(bf16[256,512]{1,0:T(8,128)(2,1)S(1)} %collective-permute-done.26.refs_2_), channel_id=1, source_target_pairs={{0,1},{1,0},{2,3},{3,2},{4,5},{5,4},{6,7},{7,6},{8,9},{9,8},{10,11... | collective-permute-start | bytes 786440 | tf_op jit(solution)/shard_map/ppermute | solution.py:623

commit v7 on v6

--- a/solution.py
+++ b/solution.py
@@ -97,16 +97,16 @@
     return pl.BlockSpec((2, block, width), lambda i, *_: (0, i, 0))
 
 
-def generate(place, table, pos_weight, pos_bias, filter_weight, rows_of, width, block):
+def generate(place, table, pos_weight, pos_bias, filter_weight, rates, skip, width, block):
     highest = lax.Precision.HIGHEST
     length = table.shape[1]
     emb_count, order = pos_weight.shape
     starts = constant_rows(length)
 
     def body(place_ref, *refs):
-        sources = refs[:5]
-        ah, al, th, spec, env_out, hidden_out, cos_out, rows_out, filt, *held, done = refs[5:]
-        tab, pw, pb, fw, vec = held
+        sources = refs[:6]
+        ah, al, th, spec, env_out, hidden_out, cos_out, skip_out, filt, *held, done = refs[6:]
+        tab, pw, pb, fw, rate, skip_row = held
         step = pl.program_id(0)
 
         @pl.when(step == 0)
@@ -122,7 +122,7 @@
                 copy.start()
             for copy in copies:
                 copy.wait()
-            rows_out[...] = vec[...]
+            skip_out[...] = skip_row[...]
             feat = tab[starts[8] : starts[8] + emb_count, :]
             pre = pb[...] + lax.dot_general(
                 feat, pw[...], (((0,), (0,)), ((), ())), precision=highest,
@@ -132,7 +132,10 @@
             hidden_out[...] = hidden
             cos_out[...] = jnp.cos(pre)
             at = lax.broadcasted_iota(jnp.int32, (length, width), 0).astype(f32)
-            env = jnp.exp(-vec[0:1, :] * at) * (1.0 / vec[1:2, :])
+            total = jnp.ones((1, width), f32)
+            for i in range(length.bit_length() - 1):
+                total = total * (1.0 + jnp.exp(rate[...] * (-2.0 * 2**i)))
+            env = jnp.exp(-rate[...] * at) * (1.0 / jnp.sqrt(total))
             env_out[...] = env
             filt[...] = (jnp.dot(hidden, fw[...], precision=highest) * env).astype(bf16)
 
@@ -162,8 +165,8 @@
 
         rows(0, store_both)
         rows(4, store_high)
-        spec[0] = to_spectrum(ah, al, 0, filt[...])
-        spec[1] = to_spectrum(ah, al, 1, filt[...])
+        spec[0] = to_spectrum(ah, al, 0, filt[...]).astype(bf16)
+        spec[1] = to_spectrum(ah, al, 1, filt[...]).astype(bf16)
 
     by_row = pl.BlockSpec((2, block, length), lambda i, *_: (0, i, 0))
     return pl.pallas_call(
@@ -171,19 +174,19 @@
         grid_spec=pltpu.PrefetchScalarGridSpec(
             num_scalar_prefetch=1,
             grid=(length // block,),
-            in_specs=[pl.BlockSpec(memory_space=pltpu.HBM)] * 5,
+            in_specs=[pl.BlockSpec(memory_space=pltpu.HBM)] * 6,
             out_specs=[by_row, by_row, by_row, spectrum_block(width, block)]
             + [whole((length, width)), whole((length, order)), whole((length, order))]
-            + [whole((rows_of.shape[0], width))],
+            + [whole((1, width))],
             scratch_shapes=[VMEM((length, width), bf16)]
             + [VMEM(x.shape, f32) for x in (table, pos_weight, pos_bias)]
-            + [VMEM((order, width), f32), VMEM((rows_of.shape[0], width), f32)]
-            + [pltpu.SemaphoreType.DMA((5,))],
+            + [VMEM((order, width), f32), VMEM((1, width), f32), VMEM((1, width), f32)]
+            + [pltpu.SemaphoreType.DMA((6,))],
         ),
         out_shape=[struct((2, length, length), bf16)] * 3
-        + [struct((2, length, width), f32), struct((length, width), f32)]
+        + [struct((2, length, width), bf16), struct((length, width), f32)]
         + [struct((length, order), f32)] * 2
-        + [struct((rows_of.shape[0], width), f32)],
+        + [struct((1, width), f32)],
         name="generate",
         compiler_params=grant(
             [((6, block, length), 2), ((4, block, width), 4), ((2, length, width), 4)]
@@ -193,7 +196,7 @@
         place,
         *[
             pltpu.with_memory_space_constraint(x, pltpu.HBM)
-            for x in (table, pos_weight, pos_bias, filter_weight, rows_of)
+            for x in (table, pos_weight, pos_bias, filter_weight, rates, skip)
         ],
     )
 
@@ -202,7 +205,7 @@
     return pl.ds(pl.multiple_of((place_ref[0] ^ r) * rows, rows), rows)
 
 
-def convolve(place, signal_rel, cot_rel, filt_spec, tables, rows_of, block):
+def convolve(place, signal_rel, cot_rel, filt_spec, tables, skip, block):
     a_high, a_low, t_high = tables
     count = len(signal_rel)
     local_len, width = cot_rel[0].shape
@@ -222,9 +225,10 @@
 
         re = to_spectrum(ah, al, 0, x[...])
         im = to_spectrum(ah, al, 1, x[...])
-        spec[0] = re
-        spec[1] = im
-        part = from_spectrum(th, re * fs[0] - im * fs[1], re * fs[1] + im * fs[0], length)
+        spec[0] = re.astype(bf16)
+        spec[1] = im.astype(bf16)
+        fr, fi = fs[0].astype(f32), fs[1].astype(f32)
+        part = from_spectrum(th, re * fr - im * fi, re * fi + im * fr, length)
 
         @pl.when(step == 0)
         def _():
@@ -237,7 +241,7 @@
         @pl.when(step == pl.num_programs(0) - 1)
         def _():
             conv = acc[...].astype(bf16).astype(f32)
-            inner_out[...] = conv + skip_ref[2:3, :] * x[...].astype(f32)
+            inner_out[...] = conv + skip_ref[...] * x[...].astype(f32)
             for r in range(count):
                 rows = piece(place_ref, r, local_len)
                 grad_out[rows, :] = (cot[r][...].astype(f32) * inner_out[rows, :]).astype(bf16)
@@ -252,7 +256,7 @@
             in_specs=[cols] * count
             + [whole((local_len, width))] * count
             + [spectrum_block(width, block), by_row, by_row, by_col]
-            + [whole(rows_of.shape)],
+            + [whole(skip.shape)],
             out_specs=[
                 spectrum_block(width, block),
                 whole((length, width)),
@@ -261,7 +265,7 @@
             scratch_shapes=[VMEM((length, width), bf16), VMEM((length, width), f32)],
         ),
         out_shape=[
-            struct((2, length, width), f32),
+            struct((2, length, width), bf16),
             struct((length, width), f32),
             struct((length, width), bf16),
         ],
@@ -269,7 +273,7 @@
         compiler_params=grant(
             [((6, block, length), 2), ((4, block, width), 4), ((3, length, width), 4)], length, width
         ),
-    )(place, *signal_rel, *cot_rel, filt_spec, a_high, a_low, t_high, rows_of)
+    )(place, *signal_rel, *cot_rel, filt_spec, a_high, a_low, t_high, skip)
 
 
 def grant(blocks, length, width):
@@ -328,7 +332,7 @@
         inner_ref = refs[2 * count + dp_count]
         outs = refs[2 * count + dp_count + 1 : -1]
         full = refs[-1]
-        out, inner_grad_out, conv_grad_out, skip_out = outs
+        out, conv_grad_out, skip_out = outs
         for k in range(dp_count):
             start = pl.multiple_of((place_ref[1] ^ k) * rows, rows)
             full[pl.ds(start, rows), :] = weight[k][...]
@@ -341,7 +345,6 @@
             gate = gates[r * local_len : (r + 1) * local_len]
             out[here, :] = (gate * inner_ref[here, :]).astype(bf16)
             inner_grad = cot[r][...].astype(f32) * gate
-            inner_grad_out[here, :] = inner_grad
             conv_grad_out[here, :] = inner_grad.astype(bf16)
             signal = sig[r][:, pl.ds(own, width)].astype(f32)
             skip_sum += jnp.sum(inner_grad * signal, axis=0, keepdims=True)
@@ -350,10 +353,9 @@
     return pl.pallas_call(
         body,
         in_specs=[smem()] + [pl.BlockSpec(memory_space=VMEM)] * (2 * count + dp_count + 1),
-        out_specs=[pl.BlockSpec(memory_space=VMEM)] * 4,
+        out_specs=[pl.BlockSpec(memory_space=VMEM)] * 3,
         out_shape=[
             struct((length, width), bf16),
-            struct((length, width), f32),
             struct((length, width), bf16),
             struct((8, width), f32),
         ],
@@ -370,21 +372,22 @@
 
 
 def correlate_back(
-    place, out, conv_grad, inner_grad, filt_spec, tables, rows_of, count, block
+    place, out, conv_grad, filt_spec, tables, skip, count, block
 ):
     a_high, a_low, t_high = tables
     length, width = conv_grad.shape
     local_len = length // count
 
-    def body(place_ref, out_ref, cg, ig, fs, ah, al, th, skip_ref, *refs):
+    def body(place_ref, out_ref, cg, fs, ah, al, th, skip_ref, *refs):
         pieces = refs[:count]
         spec, back = refs[count:]
         step = pl.program_id(0)
         re = to_spectrum(ah, al, 0, cg[...])
         im = to_spectrum(ah, al, 1, cg[...])
-        spec[0] = re
-        spec[1] = im
-        term = from_spectrum(th, fs[0] * re + fs[1] * im, fs[0] * im - fs[1] * re, length)
+        spec[0] = re.astype(bf16)
+        spec[1] = im.astype(bf16)
+        fr, fi = fs[0].astype(f32), fs[1].astype(f32)
+        term = from_spectrum(th, fr * re + fi * im, fr * im - fi * re, length)
 
         @pl.when(step == 0)
         def _():
@@ -398,7 +401,7 @@
         def _():
             for r in range(count):
                 rows = piece(place_ref, r, local_len)
-                direct = ig[rows, :] * skip_ref[2:3, :]
+                direct = cg[rows, :].astype(f32) * skip_ref[...]
                 pieces[r][0] = out_ref[rows, :]
                 pieces[r][1] = (direct + back[rows, :].astype(bf16).astype(f32)).astype(bf16)
 
@@ -412,23 +415,22 @@
             in_specs=[
                 whole((length, width)),
                 whole((length, width)),
-                whole((length, width)),
                 spec_block,
                 by_row,
                 by_row,
                 by_col,
-                whole(rows_of.shape),
+                whole(skip.shape),
             ],
             out_specs=[whole((2, local_len, width))] * count + [spec_block],
             scratch_shapes=[VMEM((length, width), f32)],
         ),
         out_shape=[struct((2, local_len, width), bf16)] * count
-        + [struct((2, length, width), f32)],
+        + [struct((2, length, width), bf16)],
         name="correlate_back",
         compiler_params=grant(
             [((6, block, length), 2), ((4, block, width), 4), ((3, length, width), 4)], length, width
         ),
-    )(place, out, conv_grad, inner_grad, filt_spec, a_high, a_low, t_high, rows_of)
+    )(place, out, conv_grad, filt_spec, a_high, a_low, t_high, skip)
 
 
 def correlate_part(
@@ -446,9 +448,9 @@
         place_ref, gs, skip_sum_ref, ss, th, env_ref, hid, fw, cp, tab, packed, part,
     ):
         step = pl.program_id(0)
-        term = from_spectrum(
-            th, ss[0] * gs[0] + ss[1] * gs[1], ss[0] * gs[1] - ss[1] * gs[0], length
-        )
+        sr, si = ss[0].astype(f32), ss[1].astype(f32)
+        gr, gi = gs[0].astype(f32), gs[1].astype(f32)
+        term = from_spectrum(th, sr * gr + si * gi, sr * gi - si * gr, length)
 
         @pl.when(step == 0)
         def _():
@@ -672,16 +674,16 @@
     ]
 
     table = jnp.asarray(constants(length, emb_count))
-    rates = decay_rate[None]
-    norm = jnp.sqrt(jnp.expm1(-2.0 * rates * length) / jnp.expm1(-2.0 * rates))
-    rows_of = jnp.concatenate([rates, norm, skip_gain[None]])
-    a_high, a_low, t_high, filt_spec, env, hidden, cos_pre, rows_of = generate(
-        place, table, pos_weight, pos_bias[None], filter_weight, rows_of, width, block
+    if length & (length - 1):
+        raise ValueError("length")
+    a_high, a_low, t_high, filt_spec, env, hidden, cos_pre, skip = generate(
+        place, table, pos_weight, pos_bias[None], filter_weight, decay_rate[None],
+        skip_gain[None], width, block,
     )
     tables = (a_high, a_low, t_high)
 
     signal_spec, inner, gate_grad = convolve(
-        place, signal_rel, cot_rel, filt_spec, tables, rows_of, block
+        place, signal_rel, cot_rel, filt_spec, tables, skip, block
     )
 
     far = list(reversed(range(0, dp_count, 2)))
@@ -706,11 +708,11 @@
         if bit < seq_count:
             live = {r: add_round(live[r], met[r]) for r in met}
 
-    out, inner_grad, conv_grad, skip_sum = gating(
+    out, conv_grad, skip_sum = gating(
         place, signal_rel, weight_rel, cot_rel, inner
     )
     *pieces, grad_spec = correlate_back(
-        place, out, conv_grad, inner_grad, filt_spec, tables, rows_of, seq_count, block
+        place, out, conv_grad, filt_spec, tables, skip, seq_count, block
     )
     pieces = [pieces[0]] + [swap(pieces[r], "seq", r) for r in range(1, seq_count)]
     packed = correlate_part(

time: 156 us -> 157 us (level)
  waiting for transfers between devices: 80.9 us -> 83.7 us
  other arithmetic: 2.84 us -> 0.76 us
    ppermute x35, waiting for transfers between devices: 80.9 us -> 83.7 us  [swap(): return lax.ppermute(value, axis, [(i, i ^ offset) for i in range(count)])]
  transfers between devices with their start and end apart: 35 -> 35, of which waited for: 13 -> 14; matrix products, arithmetic and copies ran while one was open for 3% -> 1% of each run, Pallas kernels for 12% -> 12%
where the time goes in v7:
time: 157 us; the launch traced here: 156 us
  waiting for transfers between devices  83.7 us (53%)
  starting transfers between devices  34.4 us (22%)
  Pallas kernels  30.9 us (20%)
  local copies, waits for them, and re-layouts  5.85 us (4%)
    ppermute x35, waiting for transfers between devices, swap(): return lax.ppermute(value, axis, [(i, i ^ offset) for i in range(count)])  83.7 us
    ppermute x35, starting transfers between devices, swap(): return lax.ppermute(value, axis, [(i, i ^ offset) for i in range(count)])  34.4 us
    pallas_call x1, Pallas kernels, generate(): pl.pallas_call(body, grid_spec=pltpu.PrefetchScalarGridSpec(num_scalar_pr...  6.76 us
    unnamed x20, local copies, waits for them, and re-layouts  4.7 us
    pallas_call x1, Pallas kernels, convolve(): pl.pallas_call(body, grid_spec=pltpu.PrefetchScalarGridSpec(num_scalar_pr...  4.12 us
    pallas_call x1, Pallas kernels, correlate_back(): pl.pallas_call(body, grid_spec=pltpu.PrefetchScalarGridSpec(num_scalar_pr...  3.83 us
    pallas_call x1, Pallas kernels, correlate_part(): pl.pallas_call(body, grid_spec=pltpu.PrefetchScalarGridSpec(num_scalar_pr...  3.63 us
  transfers between devices with their start and end apart: 35, of which 14 were waited for; matrix products, arithmetic and copies ran while one was open for 1% of the time, Pallas kernels for 12%

profile of v7, /device:TPU:0, one launch (start us, length us, event | category | flops | bytes accessed | tf_op | source)
XLA Modules:
  0.0 156.5 jit_solution(14063684543772915576)
XLA Ops:
  0.7 3.0 %collective-permute-start.1 = (bf16[128,2048]{1,0:T(8,128)(2,1)}, bf16[128,2048]{1,0:T(8,128)(2,1)S(1)}, u32[]{:S(2)}, u32[]{:S(2)}) collective-permute-start(bf16[128,2048]{1,0:T(8,128)(2,1)} %bitcast.29), channel_id=1, source_target_pairs={{0,2},{1,3},{2,0},{3,1},{4,6},{5,7},{6,4},{7,5},{8,10},{9,11},{10,... | collective-permute-start | bytes 1572872 | tf_op jit(solution)/shard_map/ppermute | solution.py:625
  3.7 1.1 dynamic-slice_bitcast_fusion
  4.8 0.3 collective-permute-start.12
  5.1 0.4 collective-permute-start.10
  5.5 1.6 collective-permute-start.11
  7.0 9.6 %collective-permute-done.1.refs_2_ = bf16[128,2048]{1,0:T(8,128)(2,1)S(1)} collective-permute-done((bf16[128,2048]{1,0:T(8,128)(2,1)}, bf16[128,2048]{1,0:T(8,128)(2,1)S(1)}, u32[]{:S(2)}, u32[]{:S(2)}) %collective-permute-start.1) | collective-permute-done | bytes 524320 | tf_op jit(solution)/shard_map/ppermute | solution.py:625
  16.7 2.3 %collective-permute-done.12.refs_7_.refs_15_ = bf16[128,512]{1,0:T(8,128)(2,1)S(1)} collective-permute-done((bf16[128,512]{1,0:T(8,128)(2,1)S(1)}, bf16[128,512]{1,0:T(8,128)(2,1)S(1)}, u32[]{:S(2)}, u32[]{:S(2)}) %collective-permute-start.12) | collective-permute-done | bytes 131104 | tf_op jit(solution)/shard_map/ppermute | solution.py:625
  19.0 0.7 copy-done.4
  19.7 3.6 %collective-permute-start.8 = (bf16[256,512]{1,0:T(8,128)(2,1)S(1)}, bf16[256,512]{1,0:T(8,128)(2,1)}, u32[]{:S(2)}, u32[]{:S(2)}) collective-permute-start(bf16[256,512]{1,0:T(8,128)(2,1)S(1)} %constant_dynamic-slice_fusion.refs_4_.refs_1_), channel_id=1, source_target_pairs={{0,24},{4,28},{8,16},{12,20},{16,8},{20,12},{24,0},{28,4},{1,25},{... | collective-permute-start | bytes 786440 | tf_op jit(solution)/shard_map/ppermute | solution.py:625
  23.3 0.7 copy-done.6
  23.9 0.7 copy-done.8
  24.6 0.8 collective-permute-start.4
  25.4 5.5 %collective-permute-done.8.refs_10_.refs_7_ = bf16[256,512]{1,0:T(8,128)(2,1)} collective-permute-done((bf16[256,512]{1,0:T(8,128)(2,1)S(1)}, bf16[256,512]{1,0:T(8,128)(2,1)}, u32[]{:S(2)}, u32[]{:S(2)}) %collective-permute-start.8) | collective-permute-done | bytes 262176 | tf_op jit(solution)/shard_map/ppermute | solution.py:625
  30.9 1.5 collective-permute-start.3
  32.4 14.2 %collective-permute-done.6.refs_8_.refs_5_ = bf16[256,512]{1,0:T(8,128)(2,1)} collective-permute-done((bf16[256,512]{1,0:T(8,128)(2,1)S(1)}, bf16[256,512]{1,0:T(8,128)(2,1)}, u32[]{:S(2)}, u32[]{:S(2)}) %collective-permute-start.6) | collective-permute-done | bytes 262176 | tf_op jit(solution)/shard_map/ppermute | solution.py:625
  46.7 1.5 collective-permute-start.9
  48.2 0.5 collective-permute-start.7
  48.7 1.5 collective-permute-start.5
  50.2 0.1 pad_add_fusion.place_ref
  50.3 6.8 %generate.1 = (bf16[2,512,512]{2,1,0:T(8,128)(2,1)S(1)}, bf16[2,512,512]{2,1,0:T(8,128)(2,1)S(1)}, bf16[2,512,512]{2,1,0:T(8,128)(2,1)S(1)}, bf16[2,512,512]{2,1...) custom-call(s32[2]{0:T(128)S(1)} %pad_add_fusion.place_ref, ...), custom_call_target="tpu_custom_call" | custom-call | tf_op jit(solution)/shard_map/generate/pallas_call | solution.py:172
  57.1 0.9 copy-done.5
  58.0 0.9 copy-done.7
  58.9 0.9 copy-done.9
  59.8 4.1 %convolve.1 = (bf16[2,512,512]{2,1,0:T(8,128)(2,1)S(1)}, f32[512,512]{1,0:T(8,128)S(1)}, bf16[512,512]{1,0:T(8,128)(2,1)S(1)}) custom-call(s32[2]{0:T(128)S(1)} %pad_add_fusion.place_ref, bf16[128,2048]{1,0:T(8,128)(2,1)S(1)} %bitcast.31, bf16[128,2048]{1,0:T(8,128)(2,1)S(1)} %collective-permute-done.refs_1_, ...), custom_call_target="tpu_custom_call" | custom-call | tf_op jit(solution)/shard_map/convolve/pallas_call | solution.py:251
  64.0 2.4 %collective-permute-done.5.refs_7_.refs_4_ = bf16[256,512]{1,0:T(8,128)(2,1)} collective-permute-done((bf16[256,512]{1,0:T(8,128)(2,1)}, bf16[256,512]{1,0:T(8,128)(2,1)}, u32[]{:S(2)}, u32[]{:S(2)}) %collective-permute-start.5) | collective-permute-done | bytes 262176 | tf_op jit(solution)/shard_map/ppermute | solution.py:625
  66.4 3.0 %gating.1 = (bf16[512,512]{1,0:T(8,128)(2,1)S(1)}, bf16[512,512]{1,0:T(8,128)(2,1)S(1)}, f32[8,512]{1,0:T(8,128)S(1)}) custom-call(s32[2]{0:T(128)S(1)} %pad_add_fusion.place_ref, bf16[128,2048]{1,0:T(8,128)(2,1)S(1)} %bitcast.32, bf16[128,2048]{1,0:T(8,128)(2,1)S(1)} %collective-permute-done.refs_1_, bf16[128,2048]{1,0:T(8,128)(2,1)S(1)} %collective-permute-done.1.refs_2_, ...), custom_call_target="tpu_custom_call" | custom-call | tf_op jit(solution)/shard_map/gating/pallas_call | solution.py:353
  69.4 3.8 %correlate_back.1 = (bf16[2,128,512]{2,1,0:T(8,128)(2,1)S(1)}, bf16[2,128,512]{2,1,0:T(8,128)(2,1)S(1)}, bf16[2,128,512]{2,1,0:T(8,128)(2,1)S(1)}, bf16[2,128,51...) custom-call(s32[2]{0:T(128)S(1)} %pad_add_fusion.place_ref, bf16[512,512]{1,0:T(8,128)(2,1)S(1)} %get-tuple-element.48.out_ref, ...), custom_call_target="tpu_custom_call" | custom-call | tf_op jit(solution)/shard_map/correlate_back/pallas_call | solution.py:410
  73.2 3.6 %correlate_part.1 = f32[80,512]{1,0:T(8,128)S(1)} custom-call(s32[2]{0:T(128)S(1)} %pad_add_fusion.place_ref, bf16[2,512,512]{2,1,0:T(8,128)(2,1)S(1)} %get-tuple-element.67.gs, f32[8,512]{1,0:T(8,128)S(1)} %get-tuple-element.68.skip_sum_ref, bf16[2,512,512]{2,1,0:T(8,128)(2,1)S(1)} %get-tuple-element.69.ss, ...), custom_call_target="tpu_custom_call" | custom-call | tf_op jit(solution)/shard_map/correlate_part/pallas_call | solution.py:478
  76.9 1.6 %collective-permute-start.28 = (f32[80,512]{1,0:T(8,128)S(1)}, f32[80,512]{1,0:T(8,128)S(1)}, u32[]{:S(2)}, u32[]{:S(2)}) collective-permute-start(f32[80,512]{1,0:T(8,128)S(1)} %correlate_part.1), channel_id=1, source_target_pairs={{0,4},{4,0},{8,12},{12,8},{16,20},{20,16},{24,28},{28,24},{1,5},{5... | collective-permute-start | bytes 491528 | tf_op jit(solution)/shard_map/ppermute | solution.py:625
  78.5 1.9 %weight_grads.1 = (bf16[1,256,512]{2,1,0:T(8,128)(2,1)S(1)}, bf16[1,256,512]{2,1,0:T(8,128)(2,1)S(1)}, bf16[2,256,512]{2,1,0:T(8,128)(2,1)S(1)}, bf16[1,256,512]...) custom-call(s32[2]{0:T(128)S(1)} %pad_add_fusion.place_ref, ...), custom_call_target="tpu_custom_call" | custom-call | tf_op jit(solution)/shard_map/weight_grads/pallas_call | solution.py:311
  80.3 0.6 collective-permute-start.20
  80.9 1.5 collective-permute-start.22
  82.4 0.5 collective-permute-start.19
  82.9 2.5 %collective-permute-start.31 = (bf16[80,512]{1,0:T(8,128)(2,1)S(1)}, bf16[80,512]{1,0:T(8,128)(2,1)S(1)}, u32[]{:S(2)}, u32[]{:S(2)}) collective-permute-start(bf16[80,512]{1,0:T(8,128)(2,1)S(1)} %add_convert_fusion.7), channel_id=1, source_target_pairs={{0,24},{4,28},{8,16},{12,20},{16,8},{20,12},{24,0},{28,4},{1,25},{... | collective-permute-start | bytes 245768 | tf_op jit(solution)/shard_map/ppermute | solution.py:625
  85.5 4.1 %collective-permute-done.20 = bf16[1,256,512]{2,1,0:T(8,128)(2,1)S(1)} collective-permute-done((bf16[1,256,512]{2,1,0:T(8,128)(2,1)S(1)}, bf16[1,256,512]{2,1,0:T(8,128)(2,1)S(1)}, u32[]{:S(2)}, u32[]{:S(2)}) %collective-permute-start.20) | collective-permute-done | bytes 262176 | tf_op jit(solution)/shard_map/ppermute | solution.py:625
  89.6 0.3 collective-permute-start.29
  90.0 5.2 %collective-permute-done.22 = bf16[1,256,512]{2,1,0:T(8,128)(2,1)S(1)} collective-permute-done((bf16[1,256,512]{2,1,0:T(8,128)(2,1)S(1)}, bf16[1,256,512]{2,1,0:T(8,128)(2,1)S(1)}, u32[]{:S(2)}, u32[]{:S(2)}) %collective-permute-start.22) | collective-permute-done | bytes 262176 | tf_op jit(solution)/shard_map/ppermute | solution.py:625
  95.2 2.5 %collective-permute-start.21 = (bf16[256,512]{1,0:T(8,128)(2,1)S(1)}, bf16[256,512]{1,0:T(8,128)(2,1)S(1)}, u32[]{:S(2)}, u32[]{:S(2)}) collective-permute-start(bf16[256,512]{1,0:T(8,128)(2,1)S(1)} %fusion.4), channel_id=1, source_target_pairs={{0,24},{4,28},{8,16},{12,20},{16,8},{20,12},{24,0},{28,4},{1,25},{... | collective-permute-start | bytes 786440 | tf_op jit(solution)/shard_map/ppermute | solution.py:625
  97.7 7.0 %collective-permute-done.19 = bf16[2,256,512]{2,1,0:T(8,128)(2,1)S(1)} collective-permute-done((bf16[2,256,512]{2,1,0:T(8,128)(2,1)S(1)}, bf16[2,256,512]{2,1,0:T(8,128)(2,1)S(1)}, u32[]{:S(2)}, u32[]{:S(2)}) %collective-permute-start.19) | collective-permute-done | bytes 524320 | tf_op jit(solution)/shard_map/ppermute | solution.py:625
  104.7 1.4 collective-permute-start.23
  106.2 1.7 %collective-permute-start.24 = (bf16[256,512]{1,0:T(8,128)(2,1)S(1)}, bf16[256,512]{1,0:T(8,128)(2,1)S(1)}, u32[]{:S(2)}, u32[]{:S(2)}) collective-permute-start(bf16[256,512]{1,0:T(8,128)(2,1)S(1)} %fusion.6), channel_id=1, source_target_pairs={{0,8},{4,12},{8,0},{12,4},{16,24},{20,28},{24,16},{28,20},{1,9},{5... | collective-permute-start | bytes 786440 | tf_op jit(solution)/shard_map/ppermute | solution.py:625
  107.9 2.7 %through_gate.1 = (bf16[128,2048]{1,0:T(8,128)(2,1)S(1)}, bf16[128,2048]{1,0:T(8,128)(2,1)S(1)}, bf16[128,2048]{1,0:T(8,128)(2,1)S(1)}, bf16[128,2048]{1,0:T(8,128)(2,1)S(1)}) custom-call(s32[2]{0:T(128)S(1)} %pad_add_fusion.place_ref, bf16[512,512]{1,0:T(8,128)(2,1)S(1)} %get-tuple-element.54.refs_0_.refs_4_, ...), custom_call_target="tpu_custom_call" | custom-call | tf_op jit(solution)/shard_map/through_gate/pallas_call | solution.py:529
  110.7 0.1 collective-permute-start.17
  110.8 0.5 collective-permute-start.13
  111.3 0.2 collective-permute-start.16
  111.5 6.5 %collective-permute-done.23 = bf16[256,512]{1,0:T(8,128)(2,1)S(1)} collective-permute-done((bf16[256,512]{1,0:T(8,128)(2,1)S(1)}, bf16[256,512]{1,0:T(8,128)(2,1)S(1)}, u32[]{:S(2)}, u32[]{:S(2)}) %collective-permute-start.23) | collective-permute-done | bytes 262176 | tf_op jit(solution)/shard_map/ppermute | solution.py:625
  118.0 0.4 collective-permute-start.34
  118.4 1.4 collective-permute-start.33
  119.8 0.2 fusion.2.refs_0_
  120.0 2.4 %collective-permute-done.34.refs_3_ = bf16[80,512]{1,0:T(8,128)(2,1)S(1)} collective-permute-done((bf16[80,512]{1,0:T(8,128)(2,1)S(1)}, bf16[80,512]{1,0:T(8,128)(2,1)S(1)}, u32[]{:S(2)}, u32[]{:S(2)}) %collective-permute-start.34) | collective-permute-done | bytes 81952 | tf_op jit(solution)/shard_map/ppermute | solution.py:625
  122.4 0.4 collective-permute-start.32
  122.8 1.3 collective-permute-start.26
  124.1 0.1 add_convert_fusion
  124.3 0.2 collective-permute-done.33.refs_2_
  124.5 0.6 collective-permute-start.18
  125.1 1.4 collective-permute-start.14
  126.5 1.4 finish.1
  127.9 0.7 collective-permute-start.25
  128.6 3.3 %collective-permute-done.26.refs_2_ = bf16[256,512]{1,0:T(8,128)(2,1)S(1)} collective-permute-done((bf16[256,512]{1,0:T(8,128)(2,1)S(1)}, bf16[256,512]{1,0:T(8,128)(2,1)S(1)}, u32[]{:S(2)}, u32[]{:S(2)}) %collective-permute-start.26) | collective-permute-done | bytes 262176 | tf_op jit(solution)/shard_map/ppermute | solution.py:625
  132.0 0.1 add_convert_fusion.1.refs_4_
  132.1 16.7 %collective-permute-done.14.refs_2_ = bf16[2,128,512]{2,1,0:T(8,128)(2,1)S(1)} collective-permute-done((bf16[2,128,512]{2,1,0:T(8,128)(2,1)S(1)}, bf16[2,128,512]{2,1,0:T(8,128)(2,1)S(1)}, u32[]{:S(2)}, u32[]{:S(2)}) %collective-permute-start.14) | collective-permute-done | bytes 262176 | tf_op jit(solution)/shard_map/ppermute | solution.py:625
  148.8 4.0 %collective-permute-done.15.refs_3_ = bf16[2,128,512]{2,1,0:T(8,128)(2,1)S(1)} collective-permute-done((bf16[2,128,512]{2,1,0:T(8,128)(2,1)S(1)}, bf16[2,128,512]{2,1,0:T(8,128)(2,1)S(1)}, u32[]{:S(2)}, u32[]{:S(2)}) %collective-permute-start.15) | collective-permute-done | bytes 262176 | tf_op jit(solution)/shard_map/ppermute | solution.py:625
  152.8 1.6 %combine.1 = (bf16[128,2048]{1,0:T(8,128)(2,1)}, bf16[128,2048]{1,0:T(8,128)(2,1)}) custom-call(s32[2]{0:T(128)S(1)} %pad_add_fusion.place_ref, bf16[2,128,512]{2,1,0:T(8,128)(2,1)S(1)} %get-tuple-element.50.refs_0_, bf16[2,128,512]{2,1,0:T(8,128)(2,1)S(1)} %collective-permute-done.13.refs_1_, bf16[2,128,512]{2,1,0:T(8,128)(2,1)S(1)} %collective-permute-done.14.refs_2_, ...), custom_call_target="tpu_custom_call" | custom-call | tf_op jit(solution)/shard_map/combine/pallas_call | solution.py:551
  154.5 2.0 %assemble.1 = f32[256,2048]{1,0:T(8,128)} custom-call(s32[2]{0:T(128)S(1)} %pad_add_fusion.place_ref, bf16[256,512]{1,0:T(8,128)(2,1)S(1)} %fusion.2.refs_0_, bf16[256,512]{1,0:T(8,128)(2,1)S(1)} %collective-permute-done.25.refs_1_, bf16[256,512]{1,0:T(8,128)(2,1)S(1)} %collective-permute-done.26.refs_2_, bf16[256,512]{1,0:T(8,128)(2,1)S(1)} %collective-permute-done.27.refs_3_), custom_call_target="tpu_custom_call" | custom-call | tf_op jit(solution)/shard_map/assemble/pallas_call | solution.py:571
  (47 shorter events, 0.4 us)
Async XLA Ops:
  0.6 16.0 %copy-start = (bf16[256,2048]{1,0:T(8,128)(2,1)S(1)}, bf16[256,2048]{1,0:T(8,128)(2,1)}, u32[]{:S(2)}) copy-start(bf16[256,2048]{1,0:T(8,128)(2,1)} %param.10) | copy-start | bytes 3145732
  0.6 56.4 %copy-start.1 = (bf16[1,128,2048]{2,1,0:T(8,128)(2,1)S(1)}, bf16[1,128,2048]{2,1,0:T(8,128)(2,1)}, u32[]{:S(2)}) copy-start(bf16[1,128,2048]{2,1,0:T(8,128)(2,1)} %param.9) | copy-start | bytes 1572868
  0.7 16.0 %collective-permute-start.1 = (bf16[128,2048]{1,0:T(8,128)(2,1)}, bf16[128,2048]{1,0:T(8,128)(2,1)S(1)}, u32[]{:S(2)}, u32[]{:S(2)}) collective-permute-start(bf16[128,2048]{1,0:T(8,128)(2,1)} %bitcast.29), channel_id=1, source_target_pairs={{0,2},{1,3},{2,0},{3,1},{4,6},{5,7},{6,4},{7,5},{8,10},{9,11},{10,... | collective-permute-start | bytes 1572872 | tf_op jit(solution)/shard_map/ppermute | solution.py:625
  3.7 45.0 %collective-permute-start = (bf16[128,2048]{1,0:T(8,128)(2,1)}, bf16[128,2048]{1,0:T(8,128)(2,1)S(1)}, u32[]{:S(2)}, u32[]{:S(2)}) collective-permute-start(bf16[128,2048]{1,0:T(8,128)(2,1)} %bitcast.30), channel_id=1, source_target_pairs={{0,1},{1,0},{2,3},{3,2},{4,5},{5,4},{6,7},{7,6},{8,9},{9,8},{10,11... | collective-permute-start | bytes 1572872 | tf_op jit(solution)/shard_map/ppermute | solution.py:625
  4.8 14.2 %collective-permute-start.12 = (bf16[128,512]{1,0:T(8,128)(2,1)S(1)}, bf16[128,512]{1,0:T(8,128)(2,1)S(1)}, u32[]{:S(2)}, u32[]{:S(2)}) collective-permute-start(bf16[128,512]{1,0:T(8,128)(2,1)S(1)} %get-tuple-element.77), channel_id=1, source_target_pairs={{0,3},{1,2},{2,1},{3,0},{4,7},{5,6},{6,5},{7,4},{8,11},{9,10},{10,... | collective-permute-start | bytes 393224 | tf_op jit(solution)/shard_map/ppermute | solution.py:625
  5.1 18.2 %collective-permute-start.10 = (bf16[128,512]{1,0:T(8,128)(2,1)S(1)}, bf16[128,512]{1,0:T(8,128)(2,1)S(1)}, u32[]{:S(2)}, u32[]{:S(2)}) collective-permute-start(bf16[128,512]{1,0:T(8,128)(2,1)S(1)} %get-tuple-element.78), channel_id=1, source_target_pairs={{0,1},{1,0},{2,3},{3,2},{4,5},{5,4},{6,7},{7,6},{8,9},{9,8},{10,11... | collective-permute-start | bytes 393224 | tf_op jit(solution)/shard_map/ppermute | solution.py:625
  5.5 18.5 %collective-permute-start.11 = (bf16[128,512]{1,0:T(8,128)(2,1)S(1)}, bf16[128,512]{1,0:T(8,128)(2,1)S(1)}, u32[]{:S(2)}, u32[]{:S(2)}) collective-permute-start(bf16[128,512]{1,0:T(8,128)(2,1)S(1)} %get-tuple-element.80), channel_id=1, source_target_pairs={{0,2},{1,3},{2,0},{3,1},{4,6},{5,7},{6,4},{7,5},{8,10},{9,11},{10,... | collective-permute-start | bytes 393224 | tf_op jit(solution)/shard_map/ppermute | solution.py:625
  16.7 40.4 %collective-permute-start.2 = (bf16[128,2048]{1,0:T(8,128)(2,1)S(1)}, bf16[128,2048]{1,0:T(8,128)(2,1)S(1)}, u32[]{:S(2)}, u32[]{:S(2)}) collective-permute-start(bf16[128,2048]{1,0:T(8,128)(2,1)S(1)} %collective-permute-done.1.refs_2_), channel_id=1, source_target_pairs={{0,1},{1,0},{2,3},{3,2},{4,5},{5,4},{6,7},{7,6},{8,9},{9,8},{10,11... | collective-permute-start | bytes 1572872 | tf_op jit(solution)/shard_map/ppermute | solution.py:625
  19.0 0.7 copy-start.4
  19.7 11.2 %collective-permute-start.8 = (bf16[256,512]{1,0:T(8,128)(2,1)S(1)}, bf16[256,512]{1,0:T(8,128)(2,1)}, u32[]{:S(2)}, u32[]{:S(2)}) collective-permute-start(bf16[256,512]{1,0:T(8,128)(2,1)S(1)} %constant_dynamic-slice_fusion.refs_4_.refs_1_), channel_id=1, source_target_pairs={{0,24},{4,28},{8,16},{12,20},{16,8},{20,12},{24,0},{28,4},{1,25},{... | collective-permute-start | bytes 786440 | tf_op jit(solution)/shard_map/ppermute | solution.py:625
  23.3 0.7 copy-start.6
  23.9 22.7 %collective-permute-start.6 = (bf16[256,512]{1,0:T(8,128)(2,1)S(1)}, bf16[256,512]{1,0:T(8,128)(2,1)}, u32[]{:S(2)}, u32[]{:S(2)}) collective-permute-start(bf16[256,512]{1,0:T(8,128)(2,1)S(1)} %constant_dynamic-slice_fusion.refs_4_.refs_1_), channel_id=1, source_target_pairs={{0,16},{4,20},{8,24},{12,28},{16,0},{20,4},{24,8},{28,12},{1,17},{... | collective-permute-start | bytes 786440 | tf_op jit(solution)/shard_map/ppermute | solution.py:625
  23.9 0.7 copy-start.8
  24.6 23.6 %collective-permute-start.4 = (bf16[256,512]{1,0:T(8,128)(2,1)S(1)}, bf16[256,512]{1,0:T(8,128)(2,1)}, u32[]{:S(2)}, u32[]{:S(2)}) collective-permute-start(bf16[256,512]{1,0:T(8,128)(2,1)S(1)} %constant_dynamic-slice_fusion.refs_4_.refs_1_), channel_id=1, source_target_pairs={{0,8},{4,12},{8,0},{12,4},{16,24},{20,28},{24,16},{28,20},{1,9},{5... | collective-permute-start | bytes 786440 | tf_op jit(solution)/shard_map/ppermute | solution.py:625
  30.9 33.0 %collective-permute-start.3 = (bf16[256,512]{1,0:T(8,128)(2,1)S(1)}, bf16[256,512]{1,0:T(8,128)(2,1)}, u32[]{:S(2)}, u32[]{:S(2)}) collective-permute-start(bf16[256,512]{1,0:T(8,128)(2,1)S(1)} %constant_dynamic-slice_fusion.refs_4_.refs_1_), channel_id=1, source_target_pairs={{0,4},{4,0},{8,12},{12,8},{16,20},{20,16},{24,28},{28,24},{1,5},{5... | collective-permute-start | bytes 786440 | tf_op jit(solution)/shard_map/ppermute | solution.py:625
  46.7 17.3 %collective-permute-start.9 = (bf16[256,512]{1,0:T(8,128)(2,1)}, bf16[256,512]{1,0:T(8,128)(2,1)}, u32[]{:S(2)}, u32[]{:S(2)}) collective-permute-start(bf16[256,512]{1,0:T(8,128)(2,1)} %collective-permute-done.8.refs_10_.refs_7_), channel_id=1, source_target_pairs={{0,4},{4,0},{8,12},{12,8},{16,20},{20,16},{24,28},{28,24},{1,5},{5... | collective-permute-start | bytes 786440 | tf_op jit(solution)/shard_map/ppermute | solution.py:625
  48.2 15.8 %collective-permute-start.7 = (bf16[256,512]{1,0:T(8,128)(2,1)}, bf16[256,512]{1,0:T(8,128)(2,1)}, u32[]{:S(2)}, u32[]{:S(2)}) collective-permute-start(bf16[256,512]{1,0:T(8,128)(2,1)} %collective-permute-done.6.refs_8_.refs_5_), channel_id=1, source_target_pairs={{0,4},{4,0},{8,12},{12,8},{16,20},{20,16},{24,28},{28,24},{1,5},{5... | collective-permute-start | bytes 786440 | tf_op jit(solution)/shard_map/ppermute | solution.py:625
  48.7 17.7 %collective-permute-start.5 = (bf16[256,512]{1,0:T(8,128)(2,1)}, bf16[256,512]{1,0:T(8,128)(2,1)}, u32[]{:S(2)}, u32[]{:S(2)}) collective-permute-start(bf16[256,512]{1,0:T(8,128)(2,1)} %collective-permute-done.4.refs_6_.refs_3_), channel_id=1, source_target_pairs={{0,4},{4,0},{8,12},{12,8},{16,20},{20,16},{24,28},{28,24},{1,5},{5... | collective-permute-start | bytes 786440 | tf_op jit(solution)/shard_map/ppermute | solution.py:625
  57.1 0.9 copy-start.5
  58.0 0.9 copy-start.7
  58.9 0.9 copy-start.9
  69.3 3.9 %copy-start.2 = (f32[64,2048]{1,0:T(8,128)S(1)}, f32[64,2048]{1,0:T(8,128)}, u32[]{:S(2)}) copy-start(f32[64,2048]{1,0:T(8,128)} %fw.1) | copy-start | bytes 1572868
  69.4 3.9 %copy-start.3 = (f32[232,512]{1,0:T(8,128)S(1)}, f32[232,512]{1,0:T(8,128)}, u32[]{:S(2)}) copy-start(f32[232,512]{1,0:T(8,128)} %constant.27.clone.refs_0_.tab) | copy-start | bytes 1425412
  76.9 6.0 %collective-permute-start.28 = (f32[80,512]{1,0:T(8,128)S(1)}, f32[80,512]{1,0:T(8,128)S(1)}, u32[]{:S(2)}, u32[]{:S(2)}) collective-permute-start(f32[80,512]{1,0:T(8,128)S(1)} %correlate_part.1), channel_id=1, source_target_pairs={{0,4},{4,0},{8,12},{12,8},{16,20},{20,16},{24,28},{28,24},{1,5},{5... | collective-permute-start | bytes 491528 | tf_op jit(solution)/shard_map/ppermute | solution.py:625
  80.3 9.2 %collective-permute-start.20 = (bf16[1,256,512]{2,1,0:T(8,128)(2,1)S(1)}, bf16[1,256,512]{2,1,0:T(8,128)(2,1)S(1)}, u32[]{:S(2)}, u32[]{:S(2)}) collective-permute-start(bf16[1,256,512]{2,1,0:T(8,128)(2,1)S(1)} %get-tuple-element.64), channel_id=1, source_target_pairs={{0,4},{4,0},{8,12},{12,8},{16,20},{20,16},{24,28},{28,24},{1,5},{5... | collective-permute-start | bytes 786440 | tf_op jit(solution)/shard_map/ppermute | solution.py:625
  80.9 14.3 %collective-permute-start.22 = (bf16[1,256,512]{2,1,0:T(8,128)(2,1)S(1)}, bf16[1,256,512]{2,1,0:T(8,128)(2,1)S(1)}, u32[]{:S(2)}, u32[]{:S(2)}) collective-permute-start(bf16[1,256,512]{2,1,0:T(8,128)(2,1)S(1)} %get-tuple-element.66), channel_id=1, source_target_pairs={{0,4},{4,0},{8,12},{12,8},{16,20},{20,16},{24,28},{28,24},{1,5},{5... | collective-permute-start | bytes 786440 | tf_op jit(solution)/shard_map/ppermute | solution.py:625
  82.4 22.3 %collective-permute-start.19 = (bf16[2,256,512]{2,1,0:T(8,128)(2,1)S(1)}, bf16[2,256,512]{2,1,0:T(8,128)(2,1)S(1)}, u32[]{:S(2)}, u32[]{:S(2)}) collective-permute-start(bf16[2,256,512]{2,1,0:T(8,128)(2,1)S(1)} %get-tuple-element.62), channel_id=1, source_target_pairs={{0,4},{4,0},{8,12},{12,8},{16,20},{20,16},{24,28},{28,24},{1,5},{5... | collective-permute-start | bytes 1572872 | tf_op jit(solution)/shard_map/ppermute | solution.py:625
  82.9 23.2 %collective-permute-start.31 = (bf16[80,512]{1,0:T(8,128)(2,1)S(1)}, bf16[80,512]{1,0:T(8,128)(2,1)S(1)}, u32[]{:S(2)}, u32[]{:S(2)}) collective-permute-start(bf16[80,512]{1,0:T(8,128)(2,1)S(1)} %add_convert_fusion.7), channel_id=1, source_target_pairs={{0,24},{4,28},{8,16},{12,20},{16,8},{20,12},{24,0},{28,4},{1,25},{... | collective-permute-start | bytes 245768 | tf_op jit(solution)/shard_map/ppermute | solution.py:625
  85.5 25.2 %collective-permute-start.30 = (bf16[80,512]{1,0:T(8,128)(2,1)S(1)}, bf16[80,512]{1,0:T(8,128)(2,1)S(1)}, u32[]{:S(2)}, u32[]{:S(2)}) collective-permute-start(bf16[80,512]{1,0:T(8,128)(2,1)S(1)} %add_convert_fusion.7), channel_id=1, source_target_pairs={{0,16},{4,20},{8,24},{12,28},{16,0},{20,4},{24,8},{28,12},{1,17},{... | collective-permute-start | bytes 245768 | tf_op jit(solution)/shard_map/ppermute | solution.py:625
  89.6 21.2 %collective-permute-start.29 = (bf16[80,512]{1,0:T(8,128)(2,1)S(1)}, bf16[80,512]{1,0:T(8,128)(2,1)S(1)}, u32[]{:S(2)}, u32[]{:S(2)}) collective-permute-start(bf16[80,512]{1,0:T(8,128)(2,1)S(1)} %add_convert_fusion.7), channel_id=1, source_target_pairs={{0,8},{4,12},{8,0},{12,4},{16,24},{20,28},{24,16},{28,20},{1,9},{5... | collective-permute-start | bytes 245768 | tf_op jit(solution)/shard_map/ppermute | solution.py:625
  95.2 16.1 %collective-permute-start.21 = (bf16[256,512]{1,0:T(8,128)(2,1)S(1)}, bf16[256,512]{1,0:T(8,128)(2,1)S(1)}, u32[]{:S(2)}, u32[]{:S(2)}) collective-permute-start(bf16[256,512]{1,0:T(8,128)(2,1)S(1)} %fusion.4), channel_id=1, source_target_pairs={{0,24},{4,28},{8,16},{12,20},{16,8},{20,12},{24,0},{28,4},{1,25},{... | collective-permute-start | bytes 786440 | tf_op jit(solution)/shard_map/ppermute | solution.py:625
  104.7 13.2 %collective-permute-start.23 = (bf16[256,512]{1,0:T(8,128)(2,1)S(1)}, bf16[256,512]{1,0:T(8,128)(2,1)S(1)}, u32[]{:S(2)}, u32[]{:S(2)}) collective-permute-start(bf16[256,512]{1,0:T(8,128)(2,1)S(1)} %fusion.5), channel_id=1, source_target_pairs={{0,16},{4,20},{8,24},{12,28},{16,0},{20,4},{24,8},{28,12},{1,17},{... | collective-permute-start | bytes 786440 | tf_op jit(solution)/shard_map/ppermute | solution.py:625
  106.2 12.2 %collective-permute-start.24 = (bf16[256,512]{1,0:T(8,128)(2,1)S(1)}, bf16[256,512]{1,0:T(8,128)(2,1)S(1)}, u32[]{:S(2)}, u32[]{:S(2)}) collective-permute-start(bf16[256,512]{1,0:T(8,128)(2,1)S(1)} %fusion.6), channel_id=1, source_target_pairs={{0,8},{4,12},{8,0},{12,4},{16,24},{20,28},{24,16},{28,20},{1,9},{5... | collective-permute-start | bytes 786440 | tf_op jit(solution)/shard_map/ppermute | solution.py:625
  110.7 12.1 %collective-permute-start.17 = (bf16[128,2048]{1,0:T(8,128)(2,1)S(1)}, bf16[128,2048]{1,0:T(8,128)(2,1)S(1)}, u32[]{:S(2)}, u32[]{:S(2)}) collective-permute-start(bf16[128,2048]{1,0:T(8,128)(2,1)S(1)} %get-tuple-element.58), channel_id=1, source_target_pairs={{0,1},{1,0},{2,3},{3,2},{4,5},{5,4},{6,7},{7,6},{8,9},{9,8},{10,11... | collective-permute-start | bytes 1572872 | tf_op jit(solution)/shard_map/ppermute | solution.py:625
  110.8 17.1 %collective-permute-start.13 = (bf16[2,128,512]{2,1,0:T(8,128)(2,1)S(1)}, bf16[2,128,512]{2,1,0:T(8,128)(2,1)S(1)}, u32[]{:S(2)}, u32[]{:S(2)}) collective-permute-start(bf16[2,128,512]{2,1,0:T(8,128)(2,1)S(1)} %get-tuple-element.51), channel_id=1, source_target_pairs={{0,1},{1,0},{2,3},{3,2},{4,5},{5,4},{6,7},{7,6},{8,9},{9,8},{10,11... | collective-permute-start | bytes 786440 | tf_op jit(solution)/shard_map/ppermute | solution.py:625
  111.3 16.6 %collective-permute-start.16 = (bf16[128,2048]{1,0:T(8,128)(2,1)S(1)}, bf16[128,2048]{1,0:T(8,128)(2,1)S(1)}, u32[]{:S(2)}, u32[]{:S(2)}) collective-permute-start(bf16[128,2048]{1,0:T(8,128)(2,1)S(1)} %get-tuple-element.56), channel_id=1, source_target_pairs={{0,1},{1,0},{2,3},{3,2},{4,5},{5,4},{6,7},{7,6},{8,9},{9,8},{10,11... | collective-permute-start | bytes 1572872 | tf_op jit(solution)/shard_map/ppermute | solution.py:625
  118.0 4.4 %collective-permute-start.34 = (bf16[80,512]{1,0:T(8,128)(2,1)S(1)}, bf16[80,512]{1,0:T(8,128)(2,1)S(1)}, u32[]{:S(2)}, u32[]{:S(2)}) collective-permute-start(bf16[80,512]{1,0:T(8,128)(2,1)S(1)} %add_convert_fusion.6.refs_0_), channel_id=1, source_target_pairs={{0,3},{1,2},{2,1},{3,0},{4,7},{5,6},{6,5},{7,4},{8,11},{9,10},{10,... | collective-permute-start | bytes 245768 | tf_op jit(solution)/shard_map/ppermute | solution.py:625
  118.4 6.0 %collective-permute-start.33 = (bf16[80,512]{1,0:T(8,128)(2,1)S(1)}, bf16[80,512]{1,0:T(8,128)(2,1)S(1)}, u32[]{:S(2)}, u32[]{:S(2)}) collective-permute-start(bf16[80,512]{1,0:T(8,128)(2,1)S(1)} %add_convert_fusion.6.refs_0_), channel_id=1, source_target_pairs={{0,2},{1,3},{2,0},{3,1},{4,6},{5,7},{6,4},{7,5},{8,10},{9,11},{10,... | collective-permute-start | bytes 245768 | tf_op jit(solution)/shard_map/ppermute | solution.py:625
  122.4 2.7 %collective-permute-start.32 = (bf16[80,512]{1,0:T(8,128)(2,1)S(1)}, bf16[80,512]{1,0:T(8,128)(2,1)S(1)}, u32[]{:S(2)}, u32[]{:S(2)}) collective-permute-start(bf16[80,512]{1,0:T(8,128)(2,1)S(1)} %add_convert_fusion.6.refs_0_), channel_id=1, source_target_pairs={{0,1},{1,0},{2,3},{3,2},{4,5},{5,4},{6,7},{7,6},{8,9},{9,8},{10,11... | collective-permute-start | bytes 245768 | tf_op jit(solution)/shard_map/ppermute | solution.py:625
  122.8 9.2 %collective-permute-start.26 = (bf16[256,512]{1,0:T(8,128)(2,1)S(1)}, bf16[256,512]{1,0:T(8,128)(2,1)S(1)}, u32[]{:S(2)}, u32[]{:S(2)}) collective-permute-start(bf16[256,512]{1,0:T(8,128)(2,1)S(1)} %fusion.2.refs_0_), channel_id=1, source_target_pairs={{0,2},{1,3},{2,0},{3,1},{4,6},{5,7},{6,4},{7,5},{8,10},{9,11},{10,... | collective-permute-start | bytes 786440 | tf_op jit(solution)/shard_map/ppermute | solution.py:625
  124.5 28.4 %collective-permute-start.18 = (bf16[128,2048]{1,0:T(8,128)(2,1)S(1)}, bf16[128,2048]{1,0:T(8,128)(2,1)S(1)}, u32[]{:S(2)}, u32[]{:S(2)}) collective-permute-start(bf16[128,2048]{1,0:T(8,128)(2,1)S(1)} %add_convert_fusion), channel_id=1, source_target_pairs={{0,2},{1,3},{2,0},{3,1},{4,6},{5,7},{6,4},{7,5},{8,10},{9,11},{10,... | collective-permute-start | bytes 1572872 | tf_op jit(solution)/shard_map/ppermute | solution.py:625
  125.1 23.7 %collective-permute-start.14 = (bf16[2,128,512]{2,1,0:T(8,128)(2,1)S(1)}, bf16[2,128,512]{2,1,0:T(8,128)(2,1)S(1)}, u32[]{:S(2)}, u32[]{:S(2)}) collective-permute-start(bf16[2,128,512]{2,1,0:T(8,128)(2,1)S(1)} %get-tuple-element.52), channel_id=1, source_target_pairs={{0,2},{1,3},{2,0},{3,1},{4,6},{5,7},{6,4},{7,5},{8,10},{9,11},{10,... | collective-permute-start | bytes 786440 | tf_op jit(solution)/shard_map/ppermute | solution.py:625
  127.9 25.0 %collective-permute-start.15 = (bf16[2,128,512]{2,1,0:T(8,128)(2,1)S(1)}, bf16[2,128,512]{2,1,0:T(8,128)(2,1)S(1)}, u32[]{:S(2)}, u32[]{:S(2)}) collective-permute-start(bf16[2,128,512]{2,1,0:T(8,128)(2,1)S(1)} %get-tuple-element.53), channel_id=1, source_target_pairs={{0,3},{1,2},{2,1},{3,0},{4,7},{5,6},{6,5},{7,4},{8,11},{9,10},{10,... | collective-permute-start | bytes 786440 | tf_op jit(solution)/shard_map/ppermute | solution.py:625
  127.9 26.6 %collective-permute-start.25 = (bf16[256,512]{1,0:T(8,128)(2,1)S(1)}, bf16[256,512]{1,0:T(8,128)(2,1)S(1)}, u32[]{:S(2)}, u32[]{:S(2)}) collective-permute-start(bf16[256,512]{1,0:T(8,128)(2,1)S(1)} %fusion.2.refs_0_), channel_id=1, source_target_pairs={{0,1},{1,0},{2,3},{3,2},{4,5},{5,4},{6,7},{7,6},{8,9},{9,8},{10,11... | collective-permute-start | bytes 786440 | tf_op jit(solution)/shard_map/ppermute | solution.py:625
  132.0 22.5 %collective-permute-start.27 = (bf16[256,512]{1,0:T(8,128)(2,1)S(1)}, bf16[256,512]{1,0:T(8,128)(2,1)S(1)}, u32[]{:S(2)}, u32[]{:S(2)}) collective-permute-start(bf16[256,512]{1,0:T(8,128)(2,1)S(1)} %collective-permute-done.26.refs_2_), channel_id=1, source_target_pairs={{0,1},{1,0},{2,3},{3,2},{4,5},{5,4},{6,7},{7,6},{8,9},{9,8},{10,11... | collective-permute-start | bytes 786440 | tf_op jit(solution)/shard_map/ppermute | solution.py:625

commit v8 on v7

--- a/solution.py
+++ b/solution.py
@@ -165,8 +165,8 @@
 
         rows(0, store_both)
         rows(4, store_high)
-        spec[0] = to_spectrum(ah, al, 0, filt[...]).astype(bf16)
-        spec[1] = to_spectrum(ah, al, 1, filt[...]).astype(bf16)
+        spec[0] = to_spectrum(ah, al, 0, filt[...])
+        spec[1] = to_spectrum(ah, al, 1, filt[...])
 
     by_row = pl.BlockSpec((2, block, length), lambda i, *_: (0, i, 0))
     return pl.pallas_call(
@@ -184,7 +184,7 @@
             + [pltpu.SemaphoreType.DMA((6,))],
         ),
         out_shape=[struct((2, length, length), bf16)] * 3
-        + [struct((2, length, width), bf16), struct((length, width), f32)]
+        + [struct((2, length, width), f32), struct((length, width), f32)]
         + [struct((length, order), f32)] * 2
         + [struct((1, width), f32)],
         name="generate",
@@ -225,9 +225,9 @@
 
         re = to_spectrum(ah, al, 0, x[...])
         im = to_spectrum(ah, al, 1, x[...])
-        spec[0] = re.astype(bf16)
-        spec[1] = im.astype(bf16)
-        fr, fi = fs[0].astype(f32), fs[1].astype(f32)
+        spec[0] = re
+        spec[1] = im
+        fr, fi = fs[0], fs[1]
         part = from_spectrum(th, re * fr - im * fi, re * fi + im * fr, length)
 
         @pl.when(step == 0)
@@ -265,7 +265,7 @@
             scratch_shapes=[VMEM((length, width), bf16), VMEM((length, width), f32)],
         ),
         out_shape=[
-            struct((2, length, width), bf16),
+            struct((2, length, width), f32),
             struct((length, width), f32),
             struct((length, width), bf16),
         ],
@@ -384,9 +384,9 @@
         step = pl.program_id(0)
         re = to_spectrum(ah, al, 0, cg[...])
         im = to_spectrum(ah, al, 1, cg[...])
-        spec[0] = re.astype(bf16)
-        spec[1] = im.astype(bf16)
-        fr, fi = fs[0].astype(f32), fs[1].astype(f32)
+        spec[0] = re
+        spec[1] = im
+        fr, fi = fs[0], fs[1]
         term = from_spectrum(th, fr * re + fi * im, fr * im - fi * re, length)
 
         @pl.when(step == 0)
@@ -425,7 +425,7 @@
             scratch_shapes=[VMEM((length, width), f32)],
         ),
         out_shape=[struct((2, local_len, width), bf16)] * count
-        + [struct((2, length, width), bf16)],
+        + [struct((2, length, width), f32)],
         name="correlate_back",
         compiler_params=grant(
             [((6, block, length), 2), ((4, block, width), 4), ((3, length, width), 4)], length, width
@@ -448,8 +448,8 @@
         place_ref, gs, skip_sum_ref, ss, th, env_ref, hid, fw, cp, tab, packed, part,
     ):
         step = pl.program_id(0)
-        sr, si = ss[0].astype(f32), ss[1].astype(f32)
-        gr, gi = gs[0].astype(f32), gs[1].astype(f32)
+        sr, si = ss[0], ss[1]
+        gr, gi = gs[0], gs[1]
         term = from_spectrum(th, sr * gr + si * gi, sr * gi - si * gr, length)
 
         @pl.when(step == 0)
@@ -558,39 +558,22 @@
     )(place, *pieces, near_part, far_part)
 
 
-def assemble(place, pieces, kind):
+def finish(place, pieces, row_pieces, order, emb_count):
     count = len(pieces)
-    rows, width = pieces[0].shape
-
-    def body(place_ref, *refs):
-        out = refs[count]
-        for r in range(count):
-            start = pl.multiple_of((place_ref[0] ^ r) * width, width)
-            out[:, pl.ds(start, width)] = refs[r][...].astype(kind)
-
-    return pl.pallas_call(
-        body,
-        in_specs=[smem()] + [pl.BlockSpec(memory_space=VMEM)] * count,
-        out_specs=pl.BlockSpec(memory_space=VMEM),
-        out_shape=struct((rows, width * count), kind),
-        name="assemble",
-        compiler_params=grant([((rows, 2 * width * count), 4)], rows, width),
-    )(place, *pieces)
-
-
-def finish(place, pieces, order, emb_count):
-    count = len(pieces)
+    block_rows = row_pieces[0].shape[0]
     rows, width = pieces[0].shape
     table_rows = 8 * (emb_count // 8 + 1)
     _, per_group = packed_rows(order, table_rows, width)
 
     def body(place_ref, *refs):
-        filter_out, skip_out, pos_out, bias_out = refs[count:]
+        parts = refs[count : 2 * count]
+        filter_out, skip_out, pos_out, bias_out, weight_out = refs[2 * count :]
         for r in range(count):
             cols = pl.ds(pl.multiple_of((place_ref[0] ^ r) * width, width), width)
             values = refs[r][...].astype(f32)
             filter_out[:, cols] = values[:order, :]
             skip_out[:, cols] = values[order : order + 1, :]
+            weight_out[:, cols] = parts[r][...].astype(f32)
         tails = [refs[r][...].astype(f32)[order + 8 :, :] for r in range(count)]
         while len(tails) > 1:
             tails = [tails[i] + tails[i + 1] for i in range(0, len(tails), 2)]
@@ -607,17 +590,18 @@
 
     return pl.pallas_call(
         body,
-        in_specs=[smem()] + [pl.BlockSpec(memory_space=VMEM)] * count,
-        out_specs=[pl.BlockSpec(memory_space=VMEM)] * 4,
+        in_specs=[smem()] + [pl.BlockSpec(memory_space=VMEM)] * (2 * count),
+        out_specs=[pl.BlockSpec(memory_space=VMEM)] * 5,
         out_shape=[
             struct((order, width * count), f32),
             struct((1, width * count), f32),
             struct((emb_count, order), f32),
             struct((1, order), f32),
+            struct((block_rows, width * count), f32),
         ],
         name="finish",
-        compiler_params=grant([((rows, 2 * width * count), 4)], rows, width),
-    )(place, *pieces)
+        compiler_params=grant([((rows + block_rows, 2 * width * count), 4)], rows, width),
+    )(place, *pieces, *row_pieces)
 
 
 def swap(value, axis, offset):
@@ -697,7 +681,6 @@
             sums[k] = add_round(weight_parts[len(pairs) + i][at], met[at])
     row_sum = add_round(sums[0], *[swap(sums[k], "dp", k) for k in far[:-1]])
     row_rel = gather_rel(row_sum, "seq")
-    grad_gate_weight = assemble(place, row_rel, f32)
 
     back_rel = through_gate(place, gate_grad, weight_rel, seq_count)
     live = {r: back_rel[r] for r in range(seq_count)}
@@ -729,8 +712,8 @@
         terms = [terms[i] + terms[i + 1] for i in range(0, len(terms), 2)]
     packed = terms[0].astype(bf16)
     packed_rel = [packed] + [swap(packed, "seq", r) for r in range(1, seq_count)]
-    grad_filter_weight, grad_skip, grad_pos_weight, grad_pos_bias = finish(
-        place, packed_rel, order, emb_count
+    grad_filter_weight, grad_skip, grad_pos_weight, grad_pos_bias, grad_gate_weight = finish(
+        place, packed_rel, row_rel, order, emb_count
     )
     return (
         output[None],

time: 157 us -> 152 us (0.968)
  waiting for transfers between devices: 83.7 us -> 67.4 us
  starting transfers between devices: 34.4 us -> 46.7 us
    ppermute x35, waiting for transfers between devices: 83.7 us -> 67.4 us  [swap(): return lax.ppermute(value, axis, [(i, i ^ offset) for i in range(count)])]
    ppermute x35, starting transfers between devices: 34.4 us -> 46.7 us  [swap(): return lax.ppermute(value, axis, [(i, i ^ offset) for i in range(count)])]
    pallas_call x1 -> x0, Pallas kernels: 2 us -> none  [assemble(): pl.pallas_call(body, in_specs=[smem()] + [pl.BlockSpec(memory_space=VMEM)...]
  transfers between devices with their start and end apart: 35 -> 35, of which waited for: 14 -> 11; matrix products, arithmetic and copies ran while one was open for 1% -> 1% of each run, Pallas kernels for 12% -> 11%
where the time goes in v8:
time: 152 us
  waiting for transfers between devices  67.4 us (44%)
  starting transfers between devices  46.7 us (31%)
  Pallas kernels  29.8 us (20%)
  local copies, waits for them, and re-layouts  5.84 us (4%)
    ppermute x35, waiting for transfers between devices, swap(): return lax.ppermute(value, axis, [(i, i ^ offset) for i in range(count)])  67.4 us
    ppermute x35, starting transfers between devices, swap(): return lax.ppermute(value, axis, [(i, i ^ offset) for i in range(count)])  46.7 us
    pallas_call x1, Pallas kernels, generate(): pl.pallas_call(body, grid_spec=pltpu.PrefetchScalarGridSpec(num_scalar_pr...  6.82 us
    unnamed x20, local copies, waits for them, and re-layouts  4.69 us
    pallas_call x1, Pallas kernels, convolve(): pl.pallas_call(body, grid_spec=pltpu.PrefetchScalarGridSpec(num_scalar_pr...  4.14 us
    pallas_call x1, Pallas kernels, correlate_back(): pl.pallas_call(body, grid_spec=pltpu.PrefetchScalarGridSpec(num_scalar_pr...  3.84 us
    pallas_call x1, Pallas kernels, correlate_part(): pl.pallas_call(body, grid_spec=pltpu.PrefetchScalarGridSpec(num_scalar_pr...  3.67 us
  transfers between devices with their start and end apart: 35, of which 11 were waited for; matrix products, arithmetic and copies ran while one was open for 1% of the time, Pallas kernels for 11%

profile of v8, /device:TPU:0, one launch (start us, length us, event | category | flops | bytes accessed | tf_op | source)
XLA Modules:
  0.0 151.6 jit_solution(2168265593514289890)
XLA Ops:
  0.7 3.0 %collective-permute-start.1 = (bf16[128,2048]{1,0:T(8,128)(2,1)}, bf16[128,2048]{1,0:T(8,128)(2,1)S(1)}, u32[]{:S(2)}, u32[]{:S(2)}) collective-permute-start(bf16[128,2048]{1,0:T(8,128)(2,1)} %bitcast.29), channel_id=1, source_target_pairs={{0,2},{1,3},{2,0},{3,1},{4,6},{5,7},{6,4},{7,5},{8,10},{9,11},{10,... | collective-permute-start | bytes 1572872 | tf_op jit(solution)/shard_map/ppermute | solution.py:609
  3.7 1.1 dynamic-slice_bitcast_fusion
  4.8 0.6 collective-permute-start.10
  5.4 0.1 collective-permute-start.11
  5.5 1.4 collective-permute-start.12
  6.8 9.8 %collective-permute-done.1.refs_2_ = bf16[128,2048]{1,0:T(8,128)(2,1)S(1)} collective-permute-done((bf16[128,2048]{1,0:T(8,128)(2,1)}, bf16[128,2048]{1,0:T(8,128)(2,1)S(1)}, u32[]{:S(2)}, u32[]{:S(2)}) %collective-permute-start.1) | collective-permute-done | bytes 524320 | tf_op jit(solution)/shard_map/ppermute | solution.py:609
  16.7 0.6 copy-done.4
  17.4 2.1 %collective-permute-start.4 = (bf16[256,512]{1,0:T(8,128)(2,1)S(1)}, bf16[256,512]{1,0:T(8,128)(2,1)}, u32[]{:S(2)}, u32[]{:S(2)}) collective-permute-start(bf16[256,512]{1,0:T(8,128)(2,1)S(1)} %constant_dynamic-slice_fusion.refs_4_.refs_1_), channel_id=1, source_target_pairs={{0,8},{4,12},{8,0},{12,4},{16,24},{20,28},{24,16},{28,20},{1,9},{5... | collective-permute-start | bytes 786440 | tf_op jit(solution)/shard_map/ppermute | solution.py:609
  19.5 0.7 copy-done.6
  20.1 3.1 %collective-permute-start.6 = (bf16[256,512]{1,0:T(8,128)(2,1)S(1)}, bf16[256,512]{1,0:T(8,128)(2,1)}, u32[]{:S(2)}, u32[]{:S(2)}) collective-permute-start(bf16[256,512]{1,0:T(8,128)(2,1)S(1)} %constant_dynamic-slice_fusion.refs_4_.refs_1_), channel_id=1, source_target_pairs={{0,16},{4,20},{8,24},{12,28},{16,0},{20,4},{24,8},{28,12},{1,17},{... | collective-permute-start | bytes 786440 | tf_op jit(solution)/shard_map/ppermute | solution.py:609
  23.3 0.7 copy-done.8
  23.9 1.3 collective-permute-start.8
  25.3 6.1 %collective-permute-done.4.refs_6_.refs_3_ = bf16[256,512]{1,0:T(8,128)(2,1)} collective-permute-done((bf16[256,512]{1,0:T(8,128)(2,1)S(1)}, bf16[256,512]{1,0:T(8,128)(2,1)}, u32[]{:S(2)}, u32[]{:S(2)}) %collective-permute-start.4) | collective-permute-done | bytes 262176 | tf_op jit(solution)/shard_map/ppermute | solution.py:609
  31.3 1.5 %collective-permute-start.3 = (bf16[256,512]{1,0:T(8,128)(2,1)S(1)}, bf16[256,512]{1,0:T(8,128)(2,1)}, u32[]{:S(2)}, u32[]{:S(2)}) collective-permute-start(bf16[256,512]{1,0:T(8,128)(2,1)S(1)} %constant_dynamic-slice_fusion.refs_4_.refs_1_), channel_id=1, source_target_pairs={{0,4},{4,0},{8,12},{12,8},{16,20},{20,16},{24,28},{28,24},{1,5},{5... | collective-permute-start | bytes 786440 | tf_op jit(solution)/shard_map/ppermute | solution.py:609
  32.9 8.9 %collective-permute-done.6.refs_8_.refs_5_ = bf16[256,512]{1,0:T(8,128)(2,1)} collective-permute-done((bf16[256,512]{1,0:T(8,128)(2,1)S(1)}, bf16[256,512]{1,0:T(8,128)(2,1)}, u32[]{:S(2)}, u32[]{:S(2)}) %collective-permute-start.6) | collective-permute-done | bytes 262176 | tf_op jit(solution)/shard_map/ppermute | solution.py:609
  41.8 1.8 %collective-permute-start.5 = (bf16[256,512]{1,0:T(8,128)(2,1)}, bf16[256,512]{1,0:T(8,128)(2,1)}, u32[]{:S(2)}, u32[]{:S(2)}) collective-permute-start(bf16[256,512]{1,0:T(8,128)(2,1)} %collective-permute-done.4.refs_6_.refs_3_), channel_id=1, source_target_pairs={{0,4},{4,0},{8,12},{12,8},{16,20},{20,16},{24,28},{28,24},{1,5},{5... | collective-permute-start | bytes 786440 | tf_op jit(solution)/shard_map/ppermute | solution.py:609
  43.6 0.2 collective-permute-start.7
  43.8 1.8 %collective-permute-start.9 = (bf16[256,512]{1,0:T(8,128)(2,1)}, bf16[256,512]{1,0:T(8,128)(2,1)}, u32[]{:S(2)}, u32[]{:S(2)}) collective-permute-start(bf16[256,512]{1,0:T(8,128)(2,1)} %collective-permute-done.8.refs_10_.refs_7_), channel_id=1, source_target_pairs={{0,4},{4,0},{8,12},{12,8},{16,20},{20,16},{24,28},{28,24},{1,5},{5... | collective-permute-start | bytes 786440 | tf_op jit(solution)/shard_map/ppermute | solution.py:609
  45.6 0.1 pad_add_fusion.place_ref
  45.7 6.8 %generate.1 = (bf16[2,512,512]{2,1,0:T(8,128)(2,1)S(1)}, bf16[2,512,512]{2,1,0:T(8,128)(2,1)S(1)}, bf16[2,512,512]{2,1,0:T(8,128)(2,1)S(1)}, f32[2,512,512]{2,1,...) custom-call(s32[2]{0:T(128)S(1)} %pad_add_fusion.place_ref, ...), custom_call_target="tpu_custom_call" | custom-call | tf_op jit(solution)/shard_map/generate/pallas_call | solution.py:172
  52.6 0.9 copy-done.5
  53.5 0.9 copy-done.7
  54.4 0.9 copy-done.9
  55.3 4.1 %convolve.1 = (f32[2,512,512]{2,1,0:T(8,128)S(1)}, f32[512,512]{1,0:T(8,128)S(1)}, bf16[512,512]{1,0:T(8,128)(2,1)S(1)}) custom-call(s32[2]{0:T(128)S(1)} %pad_add_fusion.place_ref, bf16[128,2048]{1,0:T(8,128)(2,1)S(1)} %bitcast.31, bf16[128,2048]{1,0:T(8,128)(2,1)S(1)} %collective-permute-done.refs_1_, ...), custom_call_target="tpu_custom_call" | custom-call | tf_op jit(solution)/shard_map/convolve/pallas_call | solution.py:251
  59.5 3.0 %gating.1 = (bf16[512,512]{1,0:T(8,128)(2,1)S(1)}, bf16[512,512]{1,0:T(8,128)(2,1)S(1)}, f32[8,512]{1,0:T(8,128)S(1)}) custom-call(s32[2]{0:T(128)S(1)} %pad_add_fusion.place_ref, bf16[128,2048]{1,0:T(8,128)(2,1)S(1)} %bitcast.32, bf16[128,2048]{1,0:T(8,128)(2,1)S(1)} %collective-permute-done.refs_1_, bf16[128,2048]{1,0:T(8,128)(2,1)S(1)} %collective-permute-done.1.refs_2_, ...), custom_call_target="tpu_custom_call" | custom-call | tf_op jit(solution)/shard_map/gating/pallas_call | solution.py:353
  62.5 3.8 %correlate_back.1 = (bf16[2,128,512]{2,1,0:T(8,128)(2,1)S(1)}, bf16[2,128,512]{2,1,0:T(8,128)(2,1)S(1)}, bf16[2,128,512]{2,1,0:T(8,128)(2,1)S(1)}, bf16[2,128,512]{2,1,0:T(8,128)(2,1)S(1)}, f32[2,512,512]{2,1,0:T(8,128)S(1)}) custom-call(s32[2]{0:T(128)S(1)} %pad_add_fusion.place_ref, bf16[512,512]{1,0:T(8,128)(2,1)S(1)} %get-tuple-element.49.out_ref, ...), custom_call_target="tpu_custom_call" | custom-call | tf_op jit(solution)/shard_map/correlate_back/pallas_call | solution.py:410
  66.3 3.7 %correlate_part.1 = f32[80,512]{1,0:T(8,128)S(1)} custom-call(s32[2]{0:T(128)S(1)} %pad_add_fusion.place_ref, f32[2,512,512]{2,1,0:T(8,128)S(1)} %get-tuple-element.62.gs, f32[8,512]{1,0:T(8,128)S(1)} %get-tuple-element.63.skip_sum_ref, f32[2,512,512]{2,1,0:T(8,128)S(1)} %get-tuple-element.64.ss, bf16[2,512,512]{2,1,0:T(8,128)(2,1)S(1)} %get-tuple-element.46.refs_11_.th, ...), custom_call_target="tpu_custom_call" | custom-call | tf_op jit(solution)/shard_map/correlate_part/pallas_call | solution.py:478
  70.0 0.3 collective-permute-start.19
  70.3 1.9 %weight_grads.1 = (bf16[1,256,512]{2,1,0:T(8,128)(2,1)S(1)}, bf16[1,256,512]{2,1,0:T(8,128)(2,1)S(1)}, bf16[2,256,512]{2,1,0:T(8,128)(2,1)S(1)}, bf16[1,256,512]...) custom-call(s32[2]{0:T(128)S(1)} %pad_add_fusion.place_ref, ...), custom_call_target="tpu_custom_call" | custom-call | tf_op jit(solution)/shard_map/weight_grads/pallas_call | solution.py:311
  72.2 1.9 %collective-permute-start.27 = (bf16[1,256,512]{2,1,0:T(8,128)(2,1)S(1)}, bf16[1,256,512]{2,1,0:T(8,128)(2,1)S(1)}, u32[]{:S(2)}, u32[]{:S(2)}) collective-permute-start(bf16[1,256,512]{2,1,0:T(8,128)(2,1)S(1)} %get-tuple-element.71), channel_id=1, source_target_pairs={{0,4},{4,0},{8,12},{12,8},{16,20},{20,16},{24,28},{28,24},{1,5},{5... | collective-permute-start | bytes 786440 | tf_op jit(solution)/shard_map/ppermute | solution.py:609
  74.0 0.2 collective-permute-start.29
  74.3 1.8 %collective-permute-start.26 = (bf16[2,256,512]{2,1,0:T(8,128)(2,1)S(1)}, bf16[2,256,512]{2,1,0:T(8,128)(2,1)S(1)}, u32[]{:S(2)}, u32[]{:S(2)}) collective-permute-start(bf16[2,256,512]{2,1,0:T(8,128)(2,1)S(1)} %get-tuple-element.69), channel_id=1, source_target_pairs={{0,4},{4,0},{8,12},{12,8},{16,20},{20,16},{24,28},{28,24},{1,5},{5... | collective-permute-start | bytes 1572872 | tf_op jit(solution)/shard_map/ppermute | solution.py:609
  76.1 2.7 %through_gate.1 = (bf16[128,2048]{1,0:T(8,128)(2,1)S(1)}, bf16[128,2048]{1,0:T(8,128)(2,1)S(1)}, bf16[128,2048]{1,0:T(8,128)(2,1)S(1)}, bf16[128,2048]{1,0:T(8,128)(2,1)S(1)}) custom-call(s32[2]{0:T(128)S(1)} %pad_add_fusion.place_ref, bf16[512,512]{1,0:T(8,128)(2,1)S(1)} %get-tuple-element.55.refs_0_.refs_4_, ...), custom_call_target="tpu_custom_call" | custom-call | tf_op jit(solution)/shard_map/through_gate/pallas_call | solution.py:529
  78.8 0.1 collective-permute-start.17
  78.9 3.5 %collective-permute-start.20 = (bf16[80,512]{1,0:T(8,128)(2,1)S(1)}, bf16[80,512]{1,0:T(8,128)(2,1)S(1)}, u32[]{:S(2)}, u32[]{:S(2)}) collective-permute-start(bf16[80,512]{1,0:T(8,128)(2,1)S(1)} %add_convert_fusion.7), channel_id=1, source_target_pairs={{0,8},{4,12},{8,0},{12,4},{16,24},{20,28},{24,16},{28,20},{1,9},{5... | collective-permute-start | bytes 245768 | tf_op jit(solution)/shard_map/ppermute | solution.py:609
  82.4 0.3 collective-permute-done.27
  82.8 4.5 %collective-permute-start.21 = (bf16[80,512]{1,0:T(8,128)(2,1)S(1)}, bf16[80,512]{1,0:T(8,128)(2,1)S(1)}, u32[]{:S(2)}, u32[]{:S(2)}) collective-permute-start(bf16[80,512]{1,0:T(8,128)(2,1)S(1)} %add_convert_fusion.7), channel_id=1, source_target_pairs={{0,16},{4,20},{8,24},{12,28},{16,0},{20,4},{24,8},{28,12},{1,17},{... | collective-permute-start | bytes 245768 | tf_op jit(solution)/shard_map/ppermute | solution.py:609
  87.2 0.1 fusion.4
  87.3 1.1 collective-permute-done.29
  88.4 2.9 %collective-permute-start.22 = (bf16[80,512]{1,0:T(8,128)(2,1)S(1)}, bf16[80,512]{1,0:T(8,128)(2,1)S(1)}, u32[]{:S(2)}, u32[]{:S(2)}) collective-permute-start(bf16[80,512]{1,0:T(8,128)(2,1)S(1)} %add_convert_fusion.7), channel_id=1, source_target_pairs={{0,24},{4,28},{8,16},{12,20},{16,8},{20,12},{24,0},{28,4},{1,25},{... | collective-permute-start | bytes 245768 | tf_op jit(solution)/shard_map/ppermute | solution.py:609
  91.3 0.1 fusion.5
  91.4 4.2 %collective-permute-done.26 = bf16[2,256,512]{2,1,0:T(8,128)(2,1)S(1)} collective-permute-done((bf16[2,256,512]{2,1,0:T(8,128)(2,1)S(1)}, bf16[2,256,512]{2,1,0:T(8,128)(2,1)S(1)}, u32[]{:S(2)}, u32[]{:S(2)}) %collective-permute-start.26) | collective-permute-done | bytes 524320 | tf_op jit(solution)/shard_map/ppermute | solution.py:609
  95.6 1.3 collective-permute-start.28
  97.0 5.9 %collective-permute-start.30 = (bf16[256,512]{1,0:T(8,128)(2,1)S(1)}, bf16[256,512]{1,0:T(8,128)(2,1)S(1)}, u32[]{:S(2)}, u32[]{:S(2)}) collective-permute-start(bf16[256,512]{1,0:T(8,128)(2,1)S(1)} %fusion.5), channel_id=1, source_target_pairs={{0,16},{4,20},{8,24},{12,28},{16,0},{20,4},{24,8},{28,12},{1,17},{... | collective-permute-start | bytes 786440 | tf_op jit(solution)/shard_map/ppermute | solution.py:609
  102.9 0.1 add_convert_fusion
  103.1 0.1 collective-permute-start.16
  103.2 0.5 collective-permute-start.13
  103.6 1.1 collective-permute-done.28
  104.8 1.5 collective-permute-start.14
  106.3 14.4 %collective-permute-done.30 = bf16[256,512]{1,0:T(8,128)(2,1)S(1)} collective-permute-done((bf16[256,512]{1,0:T(8,128)(2,1)S(1)}, bf16[256,512]{1,0:T(8,128)(2,1)S(1)}, u32[]{:S(2)}, u32[]{:S(2)}) %collective-permute-start.30) | collective-permute-done | bytes 262176 | tf_op jit(solution)/shard_map/ppermute | solution.py:609
  120.6 1.1 collective-permute-start.15
  121.7 0.5 collective-permute-start.18
  122.3 0.2 fusion.2.refs_4_
  122.5 1.6 %collective-permute-start.33 = (bf16[256,512]{1,0:T(8,128)(2,1)S(1)}, bf16[256,512]{1,0:T(8,128)(2,1)S(1)}, u32[]{:S(2)}, u32[]{:S(2)}) collective-permute-start(bf16[256,512]{1,0:T(8,128)(2,1)S(1)} %fusion.2.refs_4_), channel_id=1, source_target_pairs={{0,2},{1,3},{2,0},{3,1},{4,6},{5,7},{6,4},{7,5},{8,10},{9,11},{10,... | collective-permute-start | bytes 786440 | tf_op jit(solution)/shard_map/ppermute | solution.py:609
  124.1 0.1 collective-permute-start.23
  124.2 4.9 %collective-permute-done.15.refs_3_ = bf16[2,128,512]{2,1,0:T(8,128)(2,1)S(1)} collective-permute-done((bf16[2,128,512]{2,1,0:T(8,128)(2,1)S(1)}, bf16[2,128,512]{2,1,0:T(8,128)(2,1)S(1)}, u32[]{:S(2)}, u32[]{:S(2)}) %collective-permute-start.15) | collective-permute-done | bytes 262176 | tf_op jit(solution)/shard_map/ppermute | solution.py:609
  129.0 1.5 collective-permute-start.24
  130.5 0.1 collective-permute-start.25
  130.6 15.7 %collective-permute-done.33.refs_6_ = bf16[256,512]{1,0:T(8,128)(2,1)S(1)} collective-permute-done((bf16[256,512]{1,0:T(8,128)(2,1)S(1)}, bf16[256,512]{1,0:T(8,128)(2,1)S(1)}, u32[]{:S(2)}, u32[]{:S(2)}) %collective-permute-start.33) | collective-permute-done | bytes 262176 | tf_op jit(solution)/shard_map/ppermute | solution.py:609
  146.3 0.5 collective-permute-start.34
  146.8 0.1 add_convert_fusion.1.refs_4_
  146.9 1.6 %combine.1 = (bf16[128,2048]{1,0:T(8,128)(2,1)}, bf16[128,2048]{1,0:T(8,128)(2,1)}) custom-call(s32[2]{0:T(128)S(1)} %pad_add_fusion.place_ref, bf16[2,128,512]{2,1,0:T(8,128)(2,1)S(1)} %get-tuple-element.51.refs_0_, bf16[2,128,512]{2,1,0:T(8,128)(2,1)S(1)} %collective-permute-done.13.refs_1_, bf16[2,128,512]{2,1,0:T(8,128)(2,1)S(1)} %collective-permute-done.14.refs_2_, ...), custom_call_target="tpu_custom_call" | custom-call | tf_op jit(solution)/shard_map/combine/pallas_call | solution.py:551
  148.5 0.9 collective-permute-done.25.refs_3_
  149.4 2.2 %finish.1 = (f32[64,2048]{1,0:T(8,128)}, f32[1,2048]{1,0:T(1,128)}, f32[33,64]{1,0:T(8,128)}, f32[1,64]{1,0:T(1,128)}, f32[256,2048]{1,0:T(8,128)}) custom-call(s32[2]{0:T(128)S(1)} %pad_add_fusion.place_ref, bf16[80,512]{1,0:T(8,128)(2,1)S(1)} %add_convert_fusion.6.refs_0_, bf16[80,512]{1,0:T(8,128)(2,1)S(1)} %collective-permute-done.23.refs_1_, ...), custom_call_target="tpu_custom_call" | custom-call | tf_op jit(solution)/shard_map/finish/pallas_call | solution.py:591
  (46 shorter events, 0.3 us)
Async XLA Ops:
  0.6 16.0 %copy-start = (bf16[256,2048]{1,0:T(8,128)(2,1)S(1)}, bf16[256,2048]{1,0:T(8,128)(2,1)}, u32[]{:S(2)}) copy-start(bf16[256,2048]{1,0:T(8,128)(2,1)} %param.10) | copy-start | bytes 3145732
  0.6 51.9 %copy-start.1 = (bf16[1,128,2048]{2,1,0:T(8,128)(2,1)S(1)}, bf16[1,128,2048]{2,1,0:T(8,128)(2,1)}, u32[]{:S(2)}) copy-start(bf16[1,128,2048]{2,1,0:T(8,128)(2,1)} %param.9) | copy-start | bytes 1572868
  0.7 16.0 %collective-permute-start.1 = (bf16[128,2048]{1,0:T(8,128)(2,1)}, bf16[128,2048]{1,0:T(8,128)(2,1)S(1)}, u32[]{:S(2)}, u32[]{:S(2)}) collective-permute-start(bf16[128,2048]{1,0:T(8,128)(2,1)} %bitcast.29), channel_id=1, source_target_pairs={{0,2},{1,3},{2,0},{3,1},{4,6},{5,7},{6,4},{7,5},{8,10},{9,11},{10,... | collective-permute-start | bytes 1572872 | tf_op jit(solution)/shard_map/ppermute | solution.py:609
  3.7 40.1 %collective-permute-start = (bf16[128,2048]{1,0:T(8,128)(2,1)}, bf16[128,2048]{1,0:T(8,128)(2,1)S(1)}, u32[]{:S(2)}, u32[]{:S(2)}) collective-permute-start(bf16[128,2048]{1,0:T(8,128)(2,1)} %bitcast.30), channel_id=1, source_target_pairs={{0,1},{1,0},{2,3},{3,2},{4,5},{5,4},{6,7},{7,6},{8,9},{9,8},{10,11... | collective-permute-start | bytes 1572872 | tf_op jit(solution)/shard_map/ppermute | solution.py:609
  4.8 11.9 %collective-permute-start.10 = (bf16[128,512]{1,0:T(8,128)(2,1)S(1)}, bf16[128,512]{1,0:T(8,128)(2,1)S(1)}, u32[]{:S(2)}, u32[]{:S(2)}) collective-permute-start(bf16[128,512]{1,0:T(8,128)(2,1)S(1)} %get-tuple-element.80), channel_id=1, source_target_pairs={{0,1},{1,0},{2,3},{3,2},{4,5},{5,4},{6,7},{7,6},{8,9},{9,8},{10,11... | collective-permute-start | bytes 393224 | tf_op jit(solution)/shard_map/ppermute | solution.py:609
  5.4 14.1 %collective-permute-start.11 = (bf16[128,512]{1,0:T(8,128)(2,1)S(1)}, bf16[128,512]{1,0:T(8,128)(2,1)S(1)}, u32[]{:S(2)}, u32[]{:S(2)}) collective-permute-start(bf16[128,512]{1,0:T(8,128)(2,1)S(1)} %get-tuple-element.82), channel_id=1, source_target_pairs={{0,2},{1,3},{2,0},{3,1},{4,6},{5,7},{6,4},{7,5},{8,10},{9,11},{10,... | collective-permute-start | bytes 393224 | tf_op jit(solution)/shard_map/ppermute | solution.py:609
  5.5 17.8 %collective-permute-start.12 = (bf16[128,512]{1,0:T(8,128)(2,1)S(1)}, bf16[128,512]{1,0:T(8,128)(2,1)S(1)}, u32[]{:S(2)}, u32[]{:S(2)}) collective-permute-start(bf16[128,512]{1,0:T(8,128)(2,1)S(1)} %get-tuple-element.79), channel_id=1, source_target_pairs={{0,3},{1,2},{2,1},{3,0},{4,7},{5,6},{6,5},{7,4},{8,11},{9,10},{10,... | collective-permute-start | bytes 393224 | tf_op jit(solution)/shard_map/ppermute | solution.py:609
  16.7 35.9 %collective-permute-start.2 = (bf16[128,2048]{1,0:T(8,128)(2,1)S(1)}, bf16[128,2048]{1,0:T(8,128)(2,1)S(1)}, u32[]{:S(2)}, u32[]{:S(2)}) collective-permute-start(bf16[128,2048]{1,0:T(8,128)(2,1)S(1)} %collective-permute-done.1.refs_2_), channel_id=1, source_target_pairs={{0,1},{1,0},{2,3},{3,2},{4,5},{5,4},{6,7},{7,6},{8,9},{9,8},{10,11... | collective-permute-start | bytes 1572872 | tf_op jit(solution)/shard_map/ppermute | solution.py:609
  16.7 0.7 copy-start.4
  17.4 13.9 %collective-permute-start.4 = (bf16[256,512]{1,0:T(8,128)(2,1)S(1)}, bf16[256,512]{1,0:T(8,128)(2,1)}, u32[]{:S(2)}, u32[]{:S(2)}) collective-permute-start(bf16[256,512]{1,0:T(8,128)(2,1)S(1)} %constant_dynamic-slice_fusion.refs_4_.refs_1_), channel_id=1, source_target_pairs={{0,8},{4,12},{8,0},{12,4},{16,24},{20,28},{24,16},{28,20},{1,9},{5... | collective-permute-start | bytes 786440 | tf_op jit(solution)/shard_map/ppermute | solution.py:609
  19.5 0.7 copy-start.6
  20.1 21.7 %collective-permute-start.6 = (bf16[256,512]{1,0:T(8,128)(2,1)S(1)}, bf16[256,512]{1,0:T(8,128)(2,1)}, u32[]{:S(2)}, u32[]{:S(2)}) collective-permute-start(bf16[256,512]{1,0:T(8,128)(2,1)S(1)} %constant_dynamic-slice_fusion.refs_4_.refs_1_), channel_id=1, source_target_pairs={{0,16},{4,20},{8,24},{12,28},{16,0},{20,4},{24,8},{28,12},{1,17},{... | collective-permute-start | bytes 786440 | tf_op jit(solution)/shard_map/ppermute | solution.py:609
  23.3 0.7 copy-start.8
  23.9 19.7 %collective-permute-start.8 = (bf16[256,512]{1,0:T(8,128)(2,1)S(1)}, bf16[256,512]{1,0:T(8,128)(2,1)}, u32[]{:S(2)}, u32[]{:S(2)}) collective-permute-start(bf16[256,512]{1,0:T(8,128)(2,1)S(1)} %constant_dynamic-slice_fusion.refs_4_.refs_1_), channel_id=1, source_target_pairs={{0,24},{4,28},{8,16},{12,20},{16,8},{20,12},{24,0},{28,4},{1,25},{... | collective-permute-start | bytes 786440 | tf_op jit(solution)/shard_map/ppermute | solution.py:609
  31.3 28.1 %collective-permute-start.3 = (bf16[256,512]{1,0:T(8,128)(2,1)S(1)}, bf16[256,512]{1,0:T(8,128)(2,1)}, u32[]{:S(2)}, u32[]{:S(2)}) collective-permute-start(bf16[256,512]{1,0:T(8,128)(2,1)S(1)} %constant_dynamic-slice_fusion.refs_4_.refs_1_), channel_id=1, source_target_pairs={{0,4},{4,0},{8,12},{12,8},{16,20},{20,16},{24,28},{28,24},{1,5},{5... | collective-permute-start | bytes 786440 | tf_op jit(solution)/shard_map/ppermute | solution.py:609
  41.8 17.7 %collective-permute-start.5 = (bf16[256,512]{1,0:T(8,128)(2,1)}, bf16[256,512]{1,0:T(8,128)(2,1)}, u32[]{:S(2)}, u32[]{:S(2)}) collective-permute-start(bf16[256,512]{1,0:T(8,128)(2,1)} %collective-permute-done.4.refs_6_.refs_3_), channel_id=1, source_target_pairs={{0,4},{4,0},{8,12},{12,8},{16,20},{20,16},{24,28},{28,24},{1,5},{5... | collective-permute-start | bytes 786440 | tf_op jit(solution)/shard_map/ppermute | solution.py:609
  43.6 15.9 %collective-permute-start.7 = (bf16[256,512]{1,0:T(8,128)(2,1)}, bf16[256,512]{1,0:T(8,128)(2,1)}, u32[]{:S(2)}, u32[]{:S(2)}) collective-permute-start(bf16[256,512]{1,0:T(8,128)(2,1)} %collective-permute-done.6.refs_8_.refs_5_), channel_id=1, source_target_pairs={{0,4},{4,0},{8,12},{12,8},{16,20},{20,16},{24,28},{28,24},{1,5},{5... | collective-permute-start | bytes 786440 | tf_op jit(solution)/shard_map/ppermute | solution.py:609
  43.8 15.6 %collective-permute-start.9 = (bf16[256,512]{1,0:T(8,128)(2,1)}, bf16[256,512]{1,0:T(8,128)(2,1)}, u32[]{:S(2)}, u32[]{:S(2)}) collective-permute-start(bf16[256,512]{1,0:T(8,128)(2,1)} %collective-permute-done.8.refs_10_.refs_7_), channel_id=1, source_target_pairs={{0,4},{4,0},{8,12},{12,8},{16,20},{20,16},{24,28},{28,24},{1,5},{5... | collective-permute-start | bytes 786440 | tf_op jit(solution)/shard_map/ppermute | solution.py:609
  52.6 0.9 copy-start.5
  53.5 0.9 copy-start.7
  54.4 0.9 copy-start.9
  62.4 3.9 %copy-start.2 = (f32[64,2048]{1,0:T(8,128)S(1)}, f32[64,2048]{1,0:T(8,128)}, u32[]{:S(2)}) copy-start(f32[64,2048]{1,0:T(8,128)} %fw.1) | copy-start | bytes 1572868
  62.5 3.9 %copy-start.3 = (f32[232,512]{1,0:T(8,128)S(1)}, f32[232,512]{1,0:T(8,128)}, u32[]{:S(2)}) copy-start(f32[232,512]{1,0:T(8,128)} %constant.27.clone.refs_0_.tab) | copy-start | bytes 1425412
  70.0 8.9 %collective-permute-start.19 = (f32[80,512]{1,0:T(8,128)S(1)}, f32[80,512]{1,0:T(8,128)S(1)}, u32[]{:S(2)}, u32[]{:S(2)}) collective-permute-start(f32[80,512]{1,0:T(8,128)S(1)} %correlate_part.1), channel_id=1, source_target_pairs={{0,4},{4,0},{8,12},{12,8},{16,20},{20,16},{24,28},{28,24},{1,5},{5... | collective-permute-start | bytes 491528 | tf_op jit(solution)/shard_map/ppermute | solution.py:609
  72.2 10.6 %collective-permute-start.27 = (bf16[1,256,512]{2,1,0:T(8,128)(2,1)S(1)}, bf16[1,256,512]{2,1,0:T(8,128)(2,1)S(1)}, u32[]{:S(2)}, u32[]{:S(2)}) collective-permute-start(bf16[1,256,512]{2,1,0:T(8,128)(2,1)S(1)} %get-tuple-element.71), channel_id=1, source_target_pairs={{0,4},{4,0},{8,12},{12,8},{16,20},{20,16},{24,28},{28,24},{1,5},{5... | collective-permute-start | bytes 786440 | tf_op jit(solution)/shard_map/ppermute | solution.py:609
  74.0 14.4 %collective-permute-start.29 = (bf16[1,256,512]{2,1,0:T(8,128)(2,1)S(1)}, bf16[1,256,512]{2,1,0:T(8,128)(2,1)S(1)}, u32[]{:S(2)}, u32[]{:S(2)}) collective-permute-start(bf16[1,256,512]{2,1,0:T(8,128)(2,1)S(1)} %get-tuple-element.73), channel_id=1, source_target_pairs={{0,4},{4,0},{8,12},{12,8},{16,20},{20,16},{24,28},{28,24},{1,5},{5... | collective-permute-start | bytes 786440 | tf_op jit(solution)/shard_map/ppermute | solution.py:609
  74.3 21.3 %collective-permute-start.26 = (bf16[2,256,512]{2,1,0:T(8,128)(2,1)S(1)}, bf16[2,256,512]{2,1,0:T(8,128)(2,1)S(1)}, u32[]{:S(2)}, u32[]{:S(2)}) collective-permute-start(bf16[2,256,512]{2,1,0:T(8,128)(2,1)S(1)} %get-tuple-element.69), channel_id=1, source_target_pairs={{0,4},{4,0},{8,12},{12,8},{16,20},{20,16},{24,28},{28,24},{1,5},{5... | collective-permute-start | bytes 1572872 | tf_op jit(solution)/shard_map/ppermute | solution.py:609
  78.8 24.1 %collective-permute-start.17 = (bf16[128,2048]{1,0:T(8,128)(2,1)S(1)}, bf16[128,2048]{1,0:T(8,128)(2,1)S(1)}, u32[]{:S(2)}, u32[]{:S(2)}) collective-permute-start(bf16[128,2048]{1,0:T(8,128)(2,1)S(1)} %get-tuple-element.59), channel_id=1, source_target_pairs={{0,1},{1,0},{2,3},{3,2},{4,5},{5,4},{6,7},{7,6},{8,9},{9,8},{10,11... | collective-permute-start | bytes 1572872 | tf_op jit(solution)/shard_map/ppermute | solution.py:609
  78.9 18.1 %collective-permute-start.20 = (bf16[80,512]{1,0:T(8,128)(2,1)S(1)}, bf16[80,512]{1,0:T(8,128)(2,1)S(1)}, u32[]{:S(2)}, u32[]{:S(2)}) collective-permute-start(bf16[80,512]{1,0:T(8,128)(2,1)S(1)} %add_convert_fusion.7), channel_id=1, source_target_pairs={{0,8},{4,12},{8,0},{12,4},{16,24},{20,28},{24,16},{28,20},{1,9},{5... | collective-permute-start | bytes 245768 | tf_op jit(solution)/shard_map/ppermute | solution.py:609
  82.8 20.3 %collective-permute-start.21 = (bf16[80,512]{1,0:T(8,128)(2,1)S(1)}, bf16[80,512]{1,0:T(8,128)(2,1)S(1)}, u32[]{:S(2)}, u32[]{:S(2)}) collective-permute-start(bf16[80,512]{1,0:T(8,128)(2,1)S(1)} %add_convert_fusion.7), channel_id=1, source_target_pairs={{0,16},{4,20},{8,24},{12,28},{16,0},{20,4},{24,8},{28,12},{1,17},{... | collective-permute-start | bytes 245768 | tf_op jit(solution)/shard_map/ppermute | solution.py:609
  88.4 14.8 %collective-permute-start.22 = (bf16[80,512]{1,0:T(8,128)(2,1)S(1)}, bf16[80,512]{1,0:T(8,128)(2,1)S(1)}, u32[]{:S(2)}, u32[]{:S(2)}) collective-permute-start(bf16[80,512]{1,0:T(8,128)(2,1)S(1)} %add_convert_fusion.7), channel_id=1, source_target_pairs={{0,24},{4,28},{8,16},{12,20},{16,8},{20,12},{24,0},{28,4},{1,25},{... | collective-permute-start | bytes 245768 | tf_op jit(solution)/shard_map/ppermute | solution.py:609
  95.6 9.2 %collective-permute-start.28 = (bf16[256,512]{1,0:T(8,128)(2,1)S(1)}, bf16[256,512]{1,0:T(8,128)(2,1)S(1)}, u32[]{:S(2)}, u32[]{:S(2)}) collective-permute-start(bf16[256,512]{1,0:T(8,128)(2,1)S(1)} %fusion.4), channel_id=1, source_target_pairs={{0,24},{4,28},{8,16},{12,20},{16,8},{20,12},{24,0},{28,4},{1,25},{... | collective-permute-start | bytes 786440 | tf_op jit(solution)/shard_map/ppermute | solution.py:609
  97.0 23.6 %collective-permute-start.30 = (bf16[256,512]{1,0:T(8,128)(2,1)S(1)}, bf16[256,512]{1,0:T(8,128)(2,1)S(1)}, u32[]{:S(2)}, u32[]{:S(2)}) collective-permute-start(bf16[256,512]{1,0:T(8,128)(2,1)S(1)} %fusion.5), channel_id=1, source_target_pairs={{0,16},{4,20},{8,24},{12,28},{16,0},{20,4},{24,8},{28,12},{1,17},{... | collective-permute-start | bytes 786440 | tf_op jit(solution)/shard_map/ppermute | solution.py:609
  102.9 18.8 %collective-permute-start.31 = (bf16[256,512]{1,0:T(8,128)(2,1)S(1)}, bf16[256,512]{1,0:T(8,128)(2,1)S(1)}, u32[]{:S(2)}, u32[]{:S(2)}) collective-permute-start(bf16[256,512]{1,0:T(8,128)(2,1)S(1)} %fusion.6), channel_id=1, source_target_pairs={{0,8},{4,12},{8,0},{12,4},{16,24},{20,28},{24,16},{28,20},{1,9},{5... | collective-permute-start | bytes 786440 | tf_op jit(solution)/shard_map/ppermute | solution.py:609
  103.1 27.5 %collective-permute-start.16 = (bf16[128,2048]{1,0:T(8,128)(2,1)S(1)}, bf16[128,2048]{1,0:T(8,128)(2,1)S(1)}, u32[]{:S(2)}, u32[]{:S(2)}) collective-permute-start(bf16[128,2048]{1,0:T(8,128)(2,1)S(1)} %get-tuple-element.57), channel_id=1, source_target_pairs={{0,1},{1,0},{2,3},{3,2},{4,5},{5,4},{6,7},{7,6},{8,9},{9,8},{10,11... | collective-permute-start | bytes 1572872 | tf_op jit(solution)/shard_map/ppermute | solution.py:609
  103.2 19.3 %collective-permute-start.13 = (bf16[2,128,512]{2,1,0:T(8,128)(2,1)S(1)}, bf16[2,128,512]{2,1,0:T(8,128)(2,1)S(1)}, u32[]{:S(2)}, u32[]{:S(2)}) collective-permute-start(bf16[2,128,512]{2,1,0:T(8,128)(2,1)S(1)} %get-tuple-element.52), channel_id=1, source_target_pairs={{0,1},{1,0},{2,3},{3,2},{4,5},{5,4},{6,7},{7,6},{8,9},{9,8},{10,11... | collective-permute-start | bytes 786440 | tf_op jit(solution)/shard_map/ppermute | solution.py:609
  104.8 19.3 %collective-permute-start.14 = (bf16[2,128,512]{2,1,0:T(8,128)(2,1)S(1)}, bf16[2,128,512]{2,1,0:T(8,128)(2,1)S(1)}, u32[]{:S(2)}, u32[]{:S(2)}) collective-permute-start(bf16[2,128,512]{2,1,0:T(8,128)(2,1)S(1)} %get-tuple-element.53), channel_id=1, source_target_pairs={{0,2},{1,3},{2,0},{3,1},{4,6},{5,7},{6,4},{7,5},{8,10},{9,11},{10,... | collective-permute-start | bytes 786440 | tf_op jit(solution)/shard_map/ppermute | solution.py:609
  120.6 8.4 %collective-permute-start.15 = (bf16[2,128,512]{2,1,0:T(8,128)(2,1)S(1)}, bf16[2,128,512]{2,1,0:T(8,128)(2,1)S(1)}, u32[]{:S(2)}, u32[]{:S(2)}) collective-permute-start(bf16[2,128,512]{2,1,0:T(8,128)(2,1)S(1)} %get-tuple-element.54), channel_id=1, source_target_pairs={{0,3},{1,2},{2,1},{3,0},{4,7},{5,6},{6,5},{7,4},{8,11},{9,10},{10,... | collective-permute-start | bytes 786440 | tf_op jit(solution)/shard_map/ppermute | solution.py:609
  121.7 24.5 %collective-permute-start.18 = (bf16[128,2048]{1,0:T(8,128)(2,1)S(1)}, bf16[128,2048]{1,0:T(8,128)(2,1)S(1)}, u32[]{:S(2)}, u32[]{:S(2)}) collective-permute-start(bf16[128,2048]{1,0:T(8,128)(2,1)S(1)} %add_convert_fusion), channel_id=1, source_target_pairs={{0,2},{1,3},{2,0},{3,1},{4,6},{5,7},{6,4},{7,5},{8,10},{9,11},{10,... | collective-permute-start | bytes 1572872 | tf_op jit(solution)/shard_map/ppermute | solution.py:609
  122.5 23.8 %collective-permute-start.33 = (bf16[256,512]{1,0:T(8,128)(2,1)S(1)}, bf16[256,512]{1,0:T(8,128)(2,1)S(1)}, u32[]{:S(2)}, u32[]{:S(2)}) collective-permute-start(bf16[256,512]{1,0:T(8,128)(2,1)S(1)} %fusion.2.refs_4_), channel_id=1, source_target_pairs={{0,2},{1,3},{2,0},{3,1},{4,6},{5,7},{6,4},{7,5},{8,10},{9,11},{10,... | collective-permute-start | bytes 786440 | tf_op jit(solution)/shard_map/ppermute | solution.py:609
  124.1 24.5 %collective-permute-start.23 = (bf16[80,512]{1,0:T(8,128)(2,1)S(1)}, bf16[80,512]{1,0:T(8,128)(2,1)S(1)}, u32[]{:S(2)}, u32[]{:S(2)}) collective-permute-start(bf16[80,512]{1,0:T(8,128)(2,1)S(1)} %add_convert_fusion.6.refs_0_), channel_id=1, source_target_pairs={{0,1},{1,0},{2,3},{3,2},{4,5},{5,4},{6,7},{7,6},{8,9},{9,8},{10,11... | collective-permute-start | bytes 245768 | tf_op jit(solution)/shard_map/ppermute | solution.py:609
  129.0 19.5 %collective-permute-start.24 = (bf16[80,512]{1,0:T(8,128)(2,1)S(1)}, bf16[80,512]{1,0:T(8,128)(2,1)S(1)}, u32[]{:S(2)}, u32[]{:S(2)}) collective-permute-start(bf16[80,512]{1,0:T(8,128)(2,1)S(1)} %add_convert_fusion.6.refs_0_), channel_id=1, source_target_pairs={{0,2},{1,3},{2,0},{3,1},{4,6},{5,7},{6,4},{7,5},{8,10},{9,11},{10,... | collective-permute-start | bytes 245768 | tf_op jit(solution)/shard_map/ppermute | solution.py:609
  130.5 18.9 %collective-permute-start.25 = (bf16[80,512]{1,0:T(8,128)(2,1)S(1)}, bf16[80,512]{1,0:T(8,128)(2,1)S(1)}, u32[]{:S(2)}, u32[]{:S(2)}) collective-permute-start(bf16[80,512]{1,0:T(8,128)(2,1)S(1)} %add_convert_fusion.6.refs_0_), channel_id=1, source_target_pairs={{0,3},{1,2},{2,1},{3,0},{4,7},{5,6},{6,5},{7,4},{8,11},{9,10},{10,... | collective-permute-start | bytes 245768 | tf_op jit(solution)/shard_map/ppermute | solution.py:609
  146.3 3.1 %collective-permute-start.32 = (bf16[256,512]{1,0:T(8,128)(2,1)S(1)}, bf16[256,512]{1,0:T(8,128)(2,1)S(1)}, u32[]{:S(2)}, u32[]{:S(2)}) collective-permute-start(bf16[256,512]{1,0:T(8,128)(2,1)S(1)} %fusion.2.refs_4_), channel_id=1, source_target_pairs={{0,1},{1,0},{2,3},{3,2},{4,5},{5,4},{6,7},{7,6},{8,9},{9,8},{10,11... | collective-permute-start | bytes 786440 | tf_op jit(solution)/shard_map/ppermute | solution.py:609
  146.3 3.1 %collective-permute-start.34 = (bf16[256,512]{1,0:T(8,128)(2,1)S(1)}, bf16[256,512]{1,0:T(8,128)(2,1)S(1)}, u32[]{:S(2)}, u32[]{:S(2)}) collective-permute-start(bf16[256,512]{1,0:T(8,128)(2,1)S(1)} %collective-permute-done.33.refs_6_), channel_id=1, source_target_pairs={{0,1},{1,0},{2,3},{3,2},{4,5},{5,4},{6,7},{7,6},{8,9},{9,8},{10,11... | collective-permute-start | bytes 786440 | tf_op jit(solution)/shard_map/ppermute | solution.py:609
